TPU v7x, 256 devices: a whole 4x4x8 slice. The times are simulated.
256 devices in a mesh: tok: 64 (over z_hi, x, y), head: 4 (over z_lo, core).
Axes of the slice: x: 4, y: 4, z: 8 (z_hi: 4, z_lo: 2; z = z_hi * 2 + z_lo), core: 2. Of those that a mesh axis runs over, the one named last changes fastest.
Arguments:
- queries: bfloat16 [16384, 2560], P('tok', 'head'), may hold values from -140 to 140
- keys: bfloat16 [2048, 2560], P('tok', 'head'), may hold values from -6 to 6
- values: bfloat16 [2048, 2560], P('tok', 'head'), may hold values from -6 to 6
- query_tan: bfloat16 [16384, 2560], P('tok', 'head'), may hold values from -6 to 6
- key_tan: bfloat16 [2048, 2560], P('tok', 'head'), may hold values from -6 to 6
- value_tan: bfloat16 [2048, 2560], P('tok', 'head'), may hold values from -6 to 6
- out_weight: bfloat16 [2560, 5120], P('head'), may hold values from -0.3125 to 0.3125
Outputs:
- output: bfloat16 [16384, 5120], P('tok', 'head')
- output_tan: bfloat16 [16384, 5120], P('tok', 'head')
All inputs are finite; a program needn't handle non-finite values.
Results may differ from a plain program's by a relative error of at most 0.012.
Values may be sent and summed in bfloat16 or wider, within the bound.
No kernel may reach another device: no remote copies, remote signals or barrier semaphores. Data moves between devices by JAX's collectives and lax.ppermute only.
A program may use at most 128 MiB of HBM per device.

v0:
```python
import functools

import jax
import jax.numpy as jnp
from jax import lax
from jax.experimental import pallas as pl
from jax.experimental.pallas import tpu as pltpu
from jax.sharding import PartitionSpec as P


HD = 128
SCALE = HD**-0.5
EXP2_SCALE = SCALE * 1.4426950408889634
NT = (((1,), (1,)), ((), ()))
ZH, NX, NY, ZL, CORES = 4, 4, 4, 2, 2
SLOTS = (0, NY, 1, 2, 3)
AXES = ("tok", "head")


VMEM = pl.BlockSpec(memory_space=pltpu.VMEM)
SMEM = pl.BlockSpec(memory_space=pltpu.SMEM)
HBM = pl.BlockSpec(memory_space=pltpu.HBM)
BF16 = jnp.bfloat16
F32 = jnp.float32


def shift(array, zh=0, x=0, y=0, zl=0, core=0):
    pairs = []
    for index in range(ZH * NX * NY * ZL * CORES):
        rest, c = divmod(index, CORES)
        rest, b = divmod(rest, ZL)
        rest, j = divmod(rest, NY)
        a, i = divmod(rest, NX)
        to = ((a + zh) % ZH, (i + x) % NX, (j + y) % NY, (b + zl) % ZL, (c + core) % CORES)
        target = (((to[0] * NX + to[1]) * NY + to[2]) * ZL + to[3]) * CORES + to[4]
        pairs.append((index, target))
    return lax.ppermute(array, AXES, pairs)


def across(array):
    pairs = []
    for index in range(ZH * NX * NY * ZL * CORES):
        rest, c = divmod(index, CORES)
        rest, b = divmod(rest, ZL)
        a, xy = divmod(rest, NX * NY)
        to = (a + 1) % ZH if b else (a - 1) % ZH
        pairs.append((index, ((to * NX * NY + xy) * ZL + 1 - b) * CORES + 1 - c))
    return lax.ppermute(array, AXES, pairs)


def call(kernel, outs, *operands, flops=0, specs=None, limit=16, **kwargs):
    return called(kernel, outs, operands, flops, specs, limit, kwargs)


def called(kernel, outs, operands, flops, specs, limit, kwargs):
    return pl.pallas_call(
        kernel,
        out_shape=outs,
        in_specs=specs or [VMEM] * len(operands),
        out_specs=jax.tree.map(lambda _: VMEM, outs),
        compiler_params=pltpu.CompilerParams(vmem_limit_bytes=limit << 20),
        cost_estimate=pl.CostEstimate(
            flops=flops,
            transcendentals=0,
            bytes_accessed=sum(o.size * o.dtype.itemsize for o in operands),
        ),
        **kwargs,
    )(*operands)


def fetch(source_refs, held_ref, sems):
    copies = [
        pltpu.make_async_copy(ref, held_ref.at[slot], sems.at[slot]) for slot, ref in enumerate(source_refs)
    ]
    for copy in copies:
        copy.start()
    for copy in copies:
        copy.wait()


def pack_keys_kernel(k_ref, dk_ref, v_ref, dv_ref, out_ref, held_ref, sems):
    fetch((k_ref, dk_ref, v_ref, dv_ref), held_ref, sems)
    for head in range(out_ref.shape[0]):
        for slot in range(4):
            out_ref[head, :, slot * HD : (slot + 1) * HD] = held_ref[slot, :, head * HD : (head + 1) * HD]


def pack_queries_kernel(y_ref, q_ref, dq_ref, *refs):
    out_refs, (held_ref, sems) = refs[:-2], refs[-2:]
    fetch((dq_ref, q_ref), held_ref, sems)
    for k, out_ref in enumerate(out_refs):
        head = lax.rem(y_ref[0] + k, NY) if k < NY else NY
        lanes = pl.ds(pl.multiple_of(head * HD, HD), HD)
        out_ref[:, :HD] = held_ref[0, :, lanes]
        out_ref[:, HD:] = held_ref[1, :, lanes]


def split_keys_kernel(y_ref, *refs):
    pieces, out_refs = refs[:ZH], refs[ZH:]
    for k, out_ref in enumerate(out_refs):
        head = lax.rem(y_ref[0] + k, NY) if k < NY else NY
        for z, piece in enumerate(pieces):
            rows = piece.shape[1]
            out_ref[z * rows : (z + 1) * rows, :] = piece[head]


def attend(both, key_refs, state):
    query = both[:, HD:]
    for ref in key_refs:
        keys = ref[:, : 2 * HD]
        values = ref[:, 2 * HD :]
        scores = lax.dot_general(query, keys[:, :HD], NT, preferred_element_type=F32)
        tangent = lax.dot_general(both, keys, NT, preferred_element_type=F32)
        top = jnp.max(scores, axis=1, keepdims=True)
        if state is None:
            peak = jnp.broadcast_to(top, (scores.shape[0], HD))
        else:
            peak_old, total, total_tan, numer, numer_tan = state
            peak = jnp.maximum(peak_old, top)
            fade = jnp.exp2((peak_old - peak) * EXP2_SCALE)
        expo = jnp.exp2((scores - peak[:, :1]) * EXP2_SCALE)
        expo_tan = expo * tangent
        cuts = range(0, scores.shape[1], HD)
        add = sum(expo[:, c : c + HD] for c in cuts)
        add_tan = sum(expo_tan[:, c : c + HD] for c in cuts)
        pair = jnp.dot(expo.astype(BF16), values, preferred_element_type=F32)
        single = jnp.dot(expo_tan.astype(BF16), values[:, :HD], preferred_element_type=F32)
        if state is None:
            state = (peak, add, add_tan, pair, single)
        else:
            state = (
                peak,
                total * fade + add,
                total_tan * fade + add_tan,
                numer * jnp.concatenate([fade, fade], axis=1) + pair,
                numer_tan * fade + single,
            )
    return state


def finish(state):
    _, total, total_tan, numer, numer_tan = state
    inverse = 1.0 / jnp.sum(total, axis=1, keepdims=True)
    total_tan = jnp.sum(total_tan, axis=1, keepdims=True) * SCALE
    attended = numer[:, :HD] * inverse
    attended_tan = (numer_tan * SCALE + numer[:, HD:] - attended * total_tan) * inverse
    return jnp.concatenate([attended, attended_tan], axis=0).astype(BF16)


def load_state(ref, tile):
    cut = [ref[tile, :, c * HD : (c + 1) * HD] for c in range(3)]
    return (*cut, ref[tile, :, 3 * HD : 5 * HD], ref[tile, :, 5 * HD :])


def attend_kernel(tiles, first, joined, *refs):
    queries, refs = refs[: len(tiles)], refs[len(tiles) :]
    (shared, own), refs = refs[:2], refs[2:]
    if not first:
        state_in, refs = refs[0], refs[1:]
    for place, tile in enumerate(tiles):
        state = None if first else load_state(state_in, tile)
        state = attend(queries[place][...], [shared if tile < NY else own], state)
        if joined is None:
            refs[0][tile] = jnp.concatenate(state, axis=1)
        elif joined:
            refs[0][:, place * HD : (place + 1) * HD] = finish(state)
        else:
            refs[place][...] = finish(state)


def attend_step(blocks, shared, own, state, tiles=tuple(range(NY + 1)), joined=None):
    rows = blocks[0].shape[0]
    if joined is None:
        outs = [jax.ShapeDtypeStruct((NY + 1, rows, 6 * HD), F32)]
    elif joined:
        outs = [jax.ShapeDtypeStruct((2 * rows, len(tiles) * HD), BF16)]
    else:
        outs = [jax.ShapeDtypeStruct((2 * rows, HD), BF16)] * len(tiles)
    carried = [] if state is None else [state]
    found = call(
        functools.partial(attend_kernel, tiles, state is None, joined),
        outs,
        *[blocks[tile] for tile in tiles],
        shared,
        own,
        *carried,
        flops=len(tiles) * rows * shared.shape[0] * 1792,
    )
    return found if joined is False else found[0]


def cut_weight_kernel(y_ref, place_ref, w_ref, *refs):
    out_refs, sems = refs[:-1], refs[-1]
    columns = out_refs[0].shape[1]
    copies = []
    for flip, out_ref in enumerate(out_refs):
        block = lax.bitwise_xor(place_ref[0], flip)
        lanes = pl.ds(pl.multiple_of(block * columns, HD), columns)
        for slot, k in enumerate(SLOTS):
            head = lax.rem(y_ref[0] + k, NY) if k < NY else NY
            source = w_ref.at[pl.ds(pl.multiple_of(head * HD, HD), HD), lanes]
            target = out_ref.at[slot * HD : (slot + 1) * HD]
            copies.append(pltpu.make_async_copy(source, target, sems.at[flip, slot]))
    for copy in copies:
        copy.start()
    for copy in copies:
        copy.wait()


def project_first_kernel(*refs):
    weights, out_ref = refs[6:10], refs[10]
    own, far_rows = 2 * HD, 5 * HD
    total = None
    for ref, weight, low, high in (
        (refs[0], weights[0], 0, own),
        (refs[1], weights[0], own, far_rows),
        (refs[2], weights[1], 0, own),
        (refs[3], weights[1], own, far_rows),
        (refs[4], weights[2], 0, own),
        (refs[5], weights[3], 0, own),
    ):
        part = jnp.dot(ref[...], weight[low:high, :], preferred_element_type=F32)
        total = part if total is None else total + part
    out_ref[...] = total


def project_last_kernel(a_ref, b_ref, w_ref, u_ref, sum_ref, out_ref, tan_ref):
    rows, tile = out_ref.shape
    depth = a_ref.shape[1]
    lanes = pl.ds(pl.multiple_of(pl.program_id(0) * tile, tile), tile)
    weights = pl.ds(w_ref.shape[0] - depth, depth)
    for ref, half in ((out_ref, pl.ds(0, rows)), (tan_ref, pl.ds(rows, rows))):
        total = (
            sum_ref[half, lanes]
            + jnp.dot(a_ref[half, :], w_ref[weights, lanes], preferred_element_type=F32)
            + jnp.dot(b_ref[half, :], u_ref[weights, lanes], preferred_element_type=F32)
        )
        ref[...] = total.astype(BF16)


def project_last(near, far, weight_near, weight_far, partial):
    rows, columns = partial.shape
    tile = 256
    half = pl.BlockSpec((rows // 2, tile), lambda j: (0, j))
    return pl.pallas_call(
        project_last_kernel,
        grid=(columns // tile,),
        in_specs=[VMEM] * 5,
        out_specs=[half, half],
        out_shape=[jax.ShapeDtypeStruct((rows // 2, columns), BF16)] * 2,
        name="project_last",
        compiler_params=pltpu.CompilerParams(vmem_limit_bytes=16 << 20),
    )(near, far, weight_near, weight_far, partial)


def shard_step(queries, keys, values, query_tan, key_tan, value_tan, out_weight):
    rows, width = queries.shape
    heads = width // HD
    slab = keys.shape[0]
    columns = out_weight.shape[1] // (ZL * CORES)
    y = (lax.axis_index("tok") % NY).astype(jnp.int32).reshape(1)
    place = lax.axis_index("head").astype(jnp.int32).reshape(1)
    with_index = [SMEM] + [VMEM] * 8
    out_weight = pltpu.with_memory_space_constraint(out_weight, pltpu.HBM)
    keys, values, query_tan, key_tan, value_tan, queries = (
        pltpu.with_memory_space_constraint(array, pltpu.HBM)
        for array in (keys, values, query_tan, key_tan, value_tan, queries)
    )

    packed = call(
        pack_keys_kernel,
        jax.ShapeDtypeStruct((heads, slab, 4 * HD), BF16),
        keys,
        key_tan,
        values,
        value_tan,
        specs=[HBM] * 4,
        scratch_shapes=[pltpu.VMEM((4, slab, width), BF16), pltpu.SemaphoreType.DMA((4,))],
    )
    pieces = [packed] + [shift(packed, zh=k) for k in (1, 3, 2)]

    sends = call(
        pack_queries_kernel,
        [jax.ShapeDtypeStruct((rows, 2 * HD), BF16)] * (NY + 1),
        y,
        queries,
        query_tan,
        specs=[SMEM, HBM, HBM],
        scratch_shapes=[pltpu.VMEM((2, rows, width), BF16), pltpu.SemaphoreType.DMA((2,))],
    )
    blocks = [sends[0]] + [shift(sends[k], y=k) for k in (1, 2, 3)] + [sends[NY]]

    place, _ = lax.optimization_barrier((place, sends[1]))
    cuts = call(
        cut_weight_kernel,
        [jax.ShapeDtypeStruct((width, columns), BF16)] * (ZL * CORES),
        y,
        place,
        out_weight,
        specs=[SMEM, SMEM, HBM],
        scratch_shapes=[pltpu.SemaphoreType.DMA((ZL * CORES, NY + 1))],
    )
    pieces, cuts = lax.optimization_barrier((pieces, cuts))

    split = call(
        split_keys_kernel,
        [jax.ShapeDtypeStruct((ZH * slab, 4 * HD), BF16)] * (NY + 1),
        y,
        *pieces,
        specs=with_index[: ZH + 1],
    )
    shared = jnp.concatenate([split[0]] + [shift(split[k], y=k) for k in (1, 3, 2)])
    own = jnp.concatenate([split[NY]] + [shift(split[NY], x=k) for k in (1, 3, 2)])
    shared_far = [shift(shared, x=k) for k in (1, 3, 2)]
    own_far = [shift(own, y=k) for k in (1, 3, 2)]

    cuts, _ = lax.optimization_barrier((cuts, split[0]))
    weight_core = shift(cuts[1], core=1)
    weight_near = shift(cuts[2], zl=1)
    weight_far = across(cuts[3])

    state = attend_step(blocks, shared, own, None)
    for k in range(2):
        state = attend_step(blocks, shared_far[k], own_far[k], state)
    others = attend_step(blocks, shared_far[2], own_far[2], state, (1, 2, 3), False)
    own_far[2], _ = lax.optimization_barrier((own_far[2], others[0]))
    mine = [attend_step(blocks, shared_far[2], own_far[2], state, (0, NY), True)]
    back = [shift(others[k - 1], y=-k) for k in (1, 2, 3)]
    mine.append(jnp.concatenate(back, axis=1))

    near = [shift(mine[n], zl=1) for n in range(2)]
    sibling = [shift(mine[n], core=1) for n in range(2)]
    far = shift(near[0], core=1)
    partial = call(
        project_first_kernel,
        jax.ShapeDtypeStruct((2 * rows, columns), F32),
        *mine,
        *sibling,
        near[0],
        far,
        cuts[0],
        weight_core,
        weight_near,
        weight_far,
        flops=10 * rows * width * columns,
    )
    last, partial = lax.optimization_barrier((near[1], partial))
    far = shift(last, core=1)
    return tuple(project_last(last, far, weight_near, weight_far, partial))


def solution(mesh):
    spec = P("tok", "head")
    return jax.shard_map(
        shard_step,
        mesh=mesh,
        in_specs=(spec,) * 6 + (P("head", None),),
        out_specs=(spec, spec),
        check_vma=False,
    )
```

profile of v0, /device:TPU:1, one launch (start us, length us, event | category | flops | bytes accessed | tf_op | source)
XLA Modules:
  0.0 133.1 jit_solution(15087439350352923479)
XLA Ops:
  0.6 0.9 shard_map.87.refs_0_
  1.5 3.9 %collective-permute-start.3 = (bf16[5,32,512]{2,1,0:T(8,128)(2,1)S(1)}, bf16[5,32,512]{2,1,0:T(8,128)(2,1)S(1)}, u32[]{:S(2)}, u32[]{:S(2)}) collective-permute-start(bf16[5,32,512]{2,1,0:T(8,128)(2,1)S(1)} %shard_map.87.refs_0_), channel_id=1, source_target_pairs={{0,64},{1,65},{2,66},{3,67},{4,68},{5,69},{6,70},{7,71},{8,72},{9,... | collective-permute-start | bytes 491528 | tf_op jit(solution)/shard_map/ppermute | solution.py:37
  5.4 3.1 %collective-permute-start.4 = (bf16[5,32,512]{2,1,0:T(8,128)(2,1)S(1)}, bf16[5,32,512]{2,1,0:T(8,128)(2,1)S(1)}, u32[]{:S(2)}, u32[]{:S(2)}) collective-permute-start(bf16[5,32,512]{2,1,0:T(8,128)(2,1)S(1)} %shard_map.87.refs_0_), channel_id=1, source_target_pairs={{0,192},{1,193},{2,194},{3,195},{4,196},{5,197},{6,198},{7,199},{8... | collective-permute-start | bytes 491528 | tf_op jit(solution)/shard_map/ppermute | solution.py:37
  8.5 4.4 %collective-permute-start.5 = (bf16[5,32,512]{2,1,0:T(8,128)(2,1)S(1)}, bf16[5,32,512]{2,1,0:T(8,128)(2,1)S(1)}, u32[]{:S(2)}, u32[]{:S(2)}) collective-permute-start(bf16[5,32,512]{2,1,0:T(8,128)(2,1)S(1)} %shard_map.87.refs_0_), channel_id=1, source_target_pairs={{0,128},{1,129},{2,130},{3,131},{4,132},{5,133},{6,134},{7,135},{8... | collective-permute-start | bytes 491528 | tf_op jit(solution)/shard_map/ppermute | solution.py:37
  12.9 1.2 shard_map.86
  14.1 3.1 %shard_map.88 = (bf16[640,1280]{1,0:T(8,128)(2,1)S(1)}, bf16[640,1280]{1,0:T(8,128)(2,1)S(1)}, bf16[640,1280]{1,0:T(8,128)(2,1)S(1)}, bf16[640,1280]{1,0:T(8,128)(2,1)S(1)}) custom-call(s32[1]{0:T(128)} %bitcast.y_ref, s32[1]{0:T(128)} %bitcast.1.place_ref, bf16[640,5120]{1,0:T(8,128)(2,1)} %w_ref.1), custom_call_target="tpu_custom_call" | custom-call | bytes 6553608 | tf_op jit(solution)/shard_map/pallas_call | solution.py:56
  17.2 3.8 %collective-permute-done.4.refs_2_ = bf16[5,32,512]{2,1,0:T(8,128)(2,1)S(1)} collective-permute-done((bf16[5,32,512]{2,1,0:T(8,128)(2,1)S(1)}, bf16[5,32,512]{2,1,0:T(8,128)(2,1)S(1)}, u32[]{:S(2)}, u32[]{:S(2)}) %collective-permute-start.4) | collective-permute-done | bytes 163872 | tf_op jit(solution)/shard_map/ppermute | solution.py:37
  21.0 0.9 collective-permute-done.5.refs_3_
  21.9 1.3 collective-permute-start.10
  23.2 1.5 %collective-permute-start.11 = (bf16[128,512]{1,0:T(8,128)(2,1)S(1)}, bf16[128,512]{1,0:T(8,128)(2,1)S(1)}, u32[]{:S(2)}, u32[]{:S(2)}) collective-permute-start(bf16[128,512]{1,0:T(8,128)(2,1)S(1)} %get-tuple-element.51), channel_id=1, source_target_pairs={{0,48},{1,49},{2,50},{3,51},{4,52},{5,53},{6,54},{7,55},{8,56},{9,... | collective-permute-start | bytes 393224 | tf_op jit(solution)/shard_map/ppermute | solution.py:37
  24.7 1.5 %collective-permute-start.12 = (bf16[128,512]{1,0:T(8,128)(2,1)S(1)}, bf16[128,512]{1,0:T(8,128)(2,1)S(1)}, u32[]{:S(2)}, u32[]{:S(2)}) collective-permute-start(bf16[128,512]{1,0:T(8,128)(2,1)S(1)} %get-tuple-element.51), channel_id=1, source_target_pairs={{0,32},{1,33},{2,34},{3,35},{4,36},{5,37},{6,38},{7,39},{8,40},{9,... | collective-permute-start | bytes 393224 | tf_op jit(solution)/shard_map/ppermute | solution.py:37
  26.3 1.4 %collective-permute-start.6 = (bf16[128,512]{1,0:T(8,128)(2,1)S(1)}, bf16[128,512]{1,0:T(8,128)(2,1)S(1)}, u32[]{:S(2)}, u32[]{:S(2)}) collective-permute-start(bf16[128,512]{1,0:T(8,128)(2,1)S(1)} %get-tuple-element.48), channel_id=1, source_target_pairs={{0,4},{1,5},{2,6},{3,7},{4,8},{5,9},{6,10},{7,11},{8,12},{9,13},{1... | collective-permute-start | bytes 393224 | tf_op jit(solution)/shard_map/ppermute | solution.py:37
  27.6 1.5 %collective-permute-start.7 = (bf16[128,512]{1,0:T(8,128)(2,1)S(1)}, bf16[128,512]{1,0:T(8,128)(2,1)S(1)}, u32[]{:S(2)}, u32[]{:S(2)}) collective-permute-start(bf16[128,512]{1,0:T(8,128)(2,1)S(1)} %get-tuple-element.49), channel_id=1, source_target_pairs={{0,12},{1,13},{2,14},{3,15},{4,0},{5,1},{6,2},{7,3},{8,4},{9,5},{1... | collective-permute-start | bytes 393224 | tf_op jit(solution)/shard_map/ppermute | solution.py:37
  29.2 1.6 %collective-permute-start.8 = (bf16[128,512]{1,0:T(8,128)(2,1)S(1)}, bf16[128,512]{1,0:T(8,128)(2,1)S(1)}, u32[]{:S(2)}, u32[]{:S(2)}) collective-permute-start(bf16[128,512]{1,0:T(8,128)(2,1)S(1)} %get-tuple-element.50), channel_id=1, source_target_pairs={{0,8},{1,9},{2,10},{3,11},{4,12},{5,13},{6,14},{7,15},{8,0},{9,1},... | collective-permute-start | bytes 393224 | tf_op jit(solution)/shard_map/ppermute | solution.py:37
  30.8 0.7 collective-permute-start.17
  31.8 2.8 %collective-permute-done.8 = bf16[128,512]{1,0:T(8,128)(2,1)S(1)} collective-permute-done((bf16[128,512]{1,0:T(8,128)(2,1)S(1)}, bf16[128,512]{1,0:T(8,128)(2,1)S(1)}, u32[]{:S(2)}, u32[]{:S(2)}) %collective-permute-start.8) | collective-permute-done | bytes 131104 | tf_op jit(solution)/shard_map/ppermute | solution.py:37
  34.9 1.4 %collective-permute-start.15 = (bf16[512,512]{1,0:T(8,128)(2,1)S(1)}, bf16[512,512]{1,0:T(8,128)(2,1)S(1)}, u32[]{:S(2)}, u32[]{:S(2)}) collective-permute-start(bf16[512,512]{1,0:T(8,128)(2,1)S(1)} %constant_dynamic-update-slice_fusion.4.refs_6_), channel_id=1, source_target_pairs={{0,12},{1,13},{2,14},{3,15},{4,0},{5,1},{6,2},{7,3},{8,4},{9,5},{1... | collective-permute-start | bytes 1572872 | tf_op jit(solution)/shard_map/ppermute | solution.py:37
  36.3 2.6 %collective-permute-start.14 = (bf16[512,512]{1,0:T(8,128)(2,1)S(1)}, bf16[512,512]{1,0:T(8,128)(2,1)S(1)}, u32[]{:S(2)}, u32[]{:S(2)}) collective-permute-start(bf16[512,512]{1,0:T(8,128)(2,1)S(1)} %constant_dynamic-update-slice_fusion.refs_5_), channel_id=1, source_target_pairs={{0,48},{1,49},{2,50},{3,51},{4,52},{5,53},{6,54},{7,55},{8,56},{9,... | collective-permute-start | bytes 1572872 | tf_op jit(solution)/shard_map/ppermute | solution.py:37
  38.9 9.4 %collective-permute-done.refs_1_.refs_0_ = bf16[256,256]{1,0:T(8,128)(2,1)S(1)} collective-permute-done((bf16[256,256]{1,0:T(8,128)(2,1)S(1)}, bf16[256,256]{1,0:T(8,128)(2,1)S(1)}, u32[]{:S(2)}, u32[]{:S(2)}) %collective-permute-start) | collective-permute-done | bytes 131104 | tf_op jit(solution)/shard_map/ppermute | solution.py:37
  48.4 2.0 %collective-permute-start.1 = (bf16[256,256]{1,0:T(8,128)(2,1)S(1)}, bf16[256,256]{1,0:T(8,128)(2,1)S(1)}, u32[]{:S(2)}, u32[]{:S(2)}) collective-permute-start(bf16[256,256]{1,0:T(8,128)(2,1)S(1)} %get-tuple-element.36), channel_id=1, source_target_pairs={{0,8},{1,9},{2,10},{3,11},{4,12},{5,13},{6,14},{7,15},{8,0},{9,1},... | collective-permute-start | bytes 393224 | tf_op jit(solution)/shard_map/ppermute | solution.py:37
  50.4 3.3 %collective-permute-done.1.refs_2_.refs_1_ = bf16[256,256]{1,0:T(8,128)(2,1)S(1)} collective-permute-done((bf16[256,256]{1,0:T(8,128)(2,1)S(1)}, bf16[256,256]{1,0:T(8,128)(2,1)S(1)}, u32[]{:S(2)}, u32[]{:S(2)}) %collective-permute-start.1) | collective-permute-done | bytes 131104 | tf_op jit(solution)/shard_map/ppermute | solution.py:37
  53.7 1.3 collective-permute-start.2
  55.0 3.0 %collective-permute-done.2.refs_3_.refs_2_ = bf16[256,256]{1,0:T(8,128)(2,1)S(1)} collective-permute-done((bf16[256,256]{1,0:T(8,128)(2,1)S(1)}, bf16[256,256]{1,0:T(8,128)(2,1)S(1)}, u32[]{:S(2)}, u32[]{:S(2)}) %collective-permute-start.2) | collective-permute-done | bytes 131104 | tf_op jit(solution)/shard_map/ppermute | solution.py:37
  58.0 1.9 %collective-permute-start.13 = (bf16[512,512]{1,0:T(8,128)(2,1)S(1)}, bf16[512,512]{1,0:T(8,128)(2,1)S(1)}, u32[]{:S(2)}, u32[]{:S(2)}) collective-permute-start(bf16[512,512]{1,0:T(8,128)(2,1)S(1)} %constant_dynamic-update-slice_fusion.4.refs_6_), channel_id=1, source_target_pairs={{0,8},{1,9},{2,10},{3,11},{4,12},{5,13},{6,14},{7,15},{8,0},{9,1},... | collective-permute-start | bytes 1572872 | tf_op jit(solution)/shard_map/ppermute | solution.py:37
  59.9 1.4 %collective-permute-start.9 = (bf16[512,512]{1,0:T(8,128)(2,1)S(1)}, bf16[512,512]{1,0:T(8,128)(2,1)S(1)}, u32[]{:S(2)}, u32[]{:S(2)}) collective-permute-start(bf16[512,512]{1,0:T(8,128)(2,1)S(1)} %constant_dynamic-update-slice_fusion.refs_5_), channel_id=1, source_target_pairs={{0,32},{1,33},{2,34},{3,35},{4,36},{5,37},{6,38},{7,39},{8,40},{9,... | collective-permute-start | bytes 1572872 | tf_op jit(solution)/shard_map/ppermute | solution.py:37
  61.3 9.6 %collective-permute-start.26 = (bf16[640,1280]{1,0:T(8,128)(2,1)S(1)}, bf16[640,1280]{1,0:T(8,128)(2,1)S(1)}, u32[]{:S(2)}, u32[]{:S(2)}) collective-permute-start(bf16[640,1280]{1,0:T(8,128)(2,1)S(1)} %get-tuple-element.63), channel_id=1, source_target_pairs={{0,1},{1,0},{2,3},{3,2},{4,5},{5,4},{6,7},{7,6},{8,9},{9,8},{10,11... | collective-permute-start | bytes 4915208 | tf_op jit(solution)/shard_map/ppermute | solution.py:37
  70.9 2.0 %collective-permute-start.27 = (bf16[640,1280]{1,0:T(8,128)(2,1)S(1)}, bf16[640,1280]{1,0:T(8,128)(2,1)S(1)}, u32[]{:S(2)}, u32[]{:S(2)}) collective-permute-start(bf16[640,1280]{1,0:T(8,128)(2,1)S(1)} %get-tuple-element.64), channel_id=1, source_target_pairs={{0,2},{1,3},{2,0},{3,1},{4,6},{5,7},{6,4},{7,5},{8,10},{9,11},{10,... | collective-permute-start | bytes 4915208 | tf_op jit(solution)/shard_map/ppermute | solution.py:37
  72.9 2.1 %shard_map.90.refs_7_ = f32[5,256,768]{2,1,0:T(8,128)S(1)} custom-call(bf16[256,256]{1,0:T(8,128)(2,1)S(1)} %get-tuple-element.52.refs_0_, bf16[256,256]{1,0:T(8,128)(2,1)S(1)} %collective-permute-done.refs_1_.refs_0_, bf16[256,256]{1,0:T(8,128)(2,1)S(1)} %collective-permute-done.1.refs_2_.refs_1_, ...), custom_call_target="tpu_custom_call" | custom-call | flops 1174405120 | bytes 1703936 | tf_op jit(solution)/shard_map/pallas_call | solution.py:56
  75.0 2.7 %shard_map.91.refs_7_ = f32[5,256,768]{2,1,0:T(8,128)S(1)} custom-call(bf16[256,256]{1,0:T(8,128)(2,1)S(1)} %get-tuple-element.52.refs_0_, bf16[256,256]{1,0:T(8,128)(2,1)S(1)} %collective-permute-done.refs_1_.refs_0_, bf16[256,256]{1,0:T(8,128)(2,1)S(1)} %collective-permute-done.1.refs_2_.refs_1_, ...), custom_call_target="tpu_custom_call" | custom-call | flops 1174405120 | bytes 5636096 | tf_op jit(solution)/shard_map/pallas_call | solution.py:56
  77.8 2.7 %shard_map.92.refs_5_.refs_4_ = f32[5,256,768]{2,1,0:T(8,128)S(1)} custom-call(bf16[256,256]{1,0:T(8,128)(2,1)S(1)} %get-tuple-element.52.refs_0_, bf16[256,256]{1,0:T(8,128)(2,1)S(1)} %collective-permute-done.refs_1_.refs_0_, bf16[256,256]{1,0:T(8,128)(2,1)S(1)} %collective-permute-done.1.refs_2_.refs_1_, ...), custom_call_target="tpu_custom_call" | custom-call | flops 1174405120 | bytes 5636096 | tf_op jit(solution)/shard_map/pallas_call | solution.py:56
  80.5 1.8 %shard_map.93 = (bf16[512,128]{1,0:T(8,128)(2,1)S(1)}, bf16[512,128]{1,0:T(8,128)(2,1)S(1)}, bf16[512,128]{1,0:T(8,128)(2,1)S(1)}) custom-call(bf16[256,256]{1,0:T(8,128)(2,1)S(1)} %collective-permute-done.refs_1_.refs_0_, bf16[256,256]{1,0:T(8,128)(2,1)S(1)} %collective-permute-done.1.refs_2_.refs_1_, ...), custom_call_target="tpu_custom_call" | custom-call | flops 704643072 | bytes 5373952 | tf_op jit(solution)/shard_map/pallas_call | solution.py:56
  82.2 1.6 %collective-permute-start.18 = (bf16[512,128]{1,0:T(8,128)(2,1)S(1)}, bf16[512,128]{1,0:T(8,128)(2,1)S(1)}, u32[]{:S(2)}, u32[]{:S(2)}) collective-permute-start(bf16[512,128]{1,0:T(8,128)(2,1)S(1)} %get-tuple-element.54), channel_id=1, source_target_pairs={{0,12},{1,13},{2,14},{3,15},{4,0},{5,1},{6,2},{7,3},{8,4},{9,5},{1... | collective-permute-start | bytes 393224 | tf_op jit(solution)/shard_map/ppermute | solution.py:37
  83.8 2.6 %collective-permute-start.19 = (bf16[512,128]{1,0:T(8,128)(2,1)S(1)}, bf16[512,128]{1,0:T(8,128)(2,1)S(1)}, u32[]{:S(2)}, u32[]{:S(2)}) collective-permute-start(bf16[512,128]{1,0:T(8,128)(2,1)S(1)} %get-tuple-element.55), channel_id=1, source_target_pairs={{0,8},{1,9},{2,10},{3,11},{4,12},{5,13},{6,14},{7,15},{8,0},{9,1},... | collective-permute-start | bytes 393224 | tf_op jit(solution)/shard_map/ppermute | solution.py:37
  86.5 1.2 shard_map.94.refs_0_
  87.7 0.7 collective-permute-done.18
  88.4 4.0 %collective-permute-start.20 = (bf16[512,128]{1,0:T(8,128)(2,1)S(1)}, bf16[512,128]{1,0:T(8,128)(2,1)S(1)}, u32[]{:S(2)}, u32[]{:S(2)}) collective-permute-start(bf16[512,128]{1,0:T(8,128)(2,1)S(1)} %get-tuple-element.56), channel_id=1, source_target_pairs={{0,4},{1,5},{2,6},{3,7},{4,8},{5,9},{6,10},{7,11},{8,12},{9,13},{1... | collective-permute-start | bytes 393224 | tf_op jit(solution)/shard_map/ppermute | solution.py:37
  92.5 1.2 collective-permute-start.24
  93.7 0.7 collective-permute-done.20
  94.4 1.9 %collective-permute-start.23 = (bf16[512,384]{1,0:T(8,128)(2,1)S(1)}, bf16[512,384]{1,0:T(8,128)(2,1)S(1)}, u32[]{:S(2)}, u32[]{:S(2)}) collective-permute-start(bf16[512,384]{1,0:T(8,128)(2,1)S(1)} %constant_dynamic-update-slice_fusion.8.refs_1_), channel_id=1, source_target_pairs={{0,1},{1,0},{2,3},{3,2},{4,5},{5,4},{6,7},{7,6},{8,9},{9,8},{10,11... | collective-permute-start | bytes 1179656 | tf_op jit(solution)/shard_map/ppermute | solution.py:37
  96.3 18.3 %collective-permute-done.24.refs_4_ = bf16[512,256]{1,0:T(8,128)(2,1)S(1)} collective-permute-done((bf16[512,256]{1,0:T(8,128)(2,1)S(1)}, bf16[512,256]{1,0:T(8,128)(2,1)S(1)}, u32[]{:S(2)}, u32[]{:S(2)}) %collective-permute-start.24) | collective-permute-done | bytes 262176 | tf_op jit(solution)/shard_map/ppermute | solution.py:37
  114.6 0.7 collective-permute-start.22
  115.3 1.2 collective-permute-done.22.refs_2_
  116.8 1.5 %collective-permute-start.21 = (bf16[512,384]{1,0:T(8,128)(2,1)S(1)}, bf16[512,384]{1,0:T(8,128)(2,1)S(1)}, u32[]{:S(2)}, u32[]{:S(2)}) collective-permute-start(bf16[512,384]{1,0:T(8,128)(2,1)S(1)} %constant_dynamic-update-slice_fusion.8.refs_1_), channel_id=1, source_target_pairs={{0,2},{1,3},{2,0},{3,1},{4,6},{5,7},{6,4},{7,5},{8,10},{9,11},{10,... | collective-permute-start | bytes 1179656 | tf_op jit(solution)/shard_map/ppermute | solution.py:37
  118.3 2.9 %shard_map.95.sum_ref = f32[512,1280]{1,0:T(8,128)S(1)} custom-call(bf16[512,256]{1,0:T(8,128)(2,1)S(1)} %shard_map.94.refs_0_, bf16[512,384]{1,0:T(8,128)(2,1)S(1)} %constant_dynamic-update-slice_fusion.8.refs_1_, bf16[512,256]{1,0:T(8,128)(2,1)S(1)} %collective-permute-done.22.refs_2_, bf16[512,384]{1,0:T(8,128)(2,1)S(1)} %collective-permute-done.23.refs_3_, ...), custom_call_target="tpu_custom_call" | custom-call | flops 2097152000 | bytes 8388608 | tf_op jit(solution)/shard_map/pallas_call | solution.py:56
  121.2 6.2 %collective-permute-done.21.a_ref = bf16[512,384]{1,0:T(8,128)(2,1)S(1)} collective-permute-done((bf16[512,384]{1,0:T(8,128)(2,1)S(1)}, bf16[512,384]{1,0:T(8,128)(2,1)S(1)}, u32[]{:S(2)}, u32[]{:S(2)}) %collective-permute-start.21) | collective-permute-done | bytes 393248 | tf_op jit(solution)/shard_map/ppermute | solution.py:37
  127.4 1.0 collective-permute-start.29
  128.4 1.3 %collective-permute-done.29.b_ref = bf16[512,384]{1,0:T(8,128)(2,1)S(1)} collective-permute-done((bf16[512,384]{1,0:T(8,128)(2,1)S(1)}, bf16[512,384]{1,0:T(8,128)(2,1)S(1)}, u32[]{:S(2)}, u32[]{:S(2)}) %collective-permute-start.29) | collective-permute-done | bytes 393248 | tf_op jit(solution)/shard_map/ppermute | solution.py:37
  129.7 3.4 %project_last.1 = (bf16[256,1280]{1,0:T(8,128)(2,1)}, bf16[256,1280]{1,0:T(8,128)(2,1)}) custom-call(bf16[512,384]{1,0:T(8,128)(2,1)S(1)} %collective-permute-done.21.a_ref, bf16[512,384]{1,0:T(8,128)(2,1)S(1)} %collective-permute-done.29.b_ref, bf16[640,1280]{1,0:T(8,128)(2,1)S(1)} %collective-permute-done.27.refs_8_.w_ref, ...), custom_call_target="tpu_custom_call" | custom-call | tf_op jit(solution)/shard_map/project_last/pallas_call | solution.py:245
  (34 shorter events, 1.2 us)
Async XLA Ops:
  1.5 15.7 %collective-permute-start.3 = (bf16[5,32,512]{2,1,0:T(8,128)(2,1)S(1)}, bf16[5,32,512]{2,1,0:T(8,128)(2,1)S(1)}, u32[]{:S(2)}, u32[]{:S(2)}) collective-permute-start(bf16[5,32,512]{2,1,0:T(8,128)(2,1)S(1)} %shard_map.87.refs_0_), channel_id=1, source_target_pairs={{0,64},{1,65},{2,66},{3,67},{4,68},{5,69},{6,70},{7,71},{8,72},{9,... | collective-permute-start | bytes 491528 | tf_op jit(solution)/shard_map/ppermute | solution.py:37
  5.4 15.5 %collective-permute-start.4 = (bf16[5,32,512]{2,1,0:T(8,128)(2,1)S(1)}, bf16[5,32,512]{2,1,0:T(8,128)(2,1)S(1)}, u32[]{:S(2)}, u32[]{:S(2)}) collective-permute-start(bf16[5,32,512]{2,1,0:T(8,128)(2,1)S(1)} %shard_map.87.refs_0_), channel_id=1, source_target_pairs={{0,192},{1,193},{2,194},{3,195},{4,196},{5,197},{6,198},{7,199},{8... | collective-permute-start | bytes 491528 | tf_op jit(solution)/shard_map/ppermute | solution.py:37
  8.5 13.3 %collective-permute-start.5 = (bf16[5,32,512]{2,1,0:T(8,128)(2,1)S(1)}, bf16[5,32,512]{2,1,0:T(8,128)(2,1)S(1)}, u32[]{:S(2)}, u32[]{:S(2)}) collective-permute-start(bf16[5,32,512]{2,1,0:T(8,128)(2,1)S(1)} %shard_map.87.refs_0_), channel_id=1, source_target_pairs={{0,128},{1,129},{2,130},{3,131},{4,132},{5,133},{6,134},{7,135},{8... | collective-permute-start | bytes 491528 | tf_op jit(solution)/shard_map/ppermute | solution.py:37
  21.9 7.3 %collective-permute-start.10 = (bf16[128,512]{1,0:T(8,128)(2,1)S(1)}, bf16[128,512]{1,0:T(8,128)(2,1)S(1)}, u32[]{:S(2)}, u32[]{:S(2)}) collective-permute-start(bf16[128,512]{1,0:T(8,128)(2,1)S(1)} %get-tuple-element.51), channel_id=1, source_target_pairs={{0,16},{1,17},{2,18},{3,19},{4,20},{5,21},{6,22},{7,23},{8,24},{9,... | collective-permute-start | bytes 393224 | tf_op jit(solution)/shard_map/ppermute | solution.py:37
  23.2 7.6 %collective-permute-start.11 = (bf16[128,512]{1,0:T(8,128)(2,1)S(1)}, bf16[128,512]{1,0:T(8,128)(2,1)S(1)}, u32[]{:S(2)}, u32[]{:S(2)}) collective-permute-start(bf16[128,512]{1,0:T(8,128)(2,1)S(1)} %get-tuple-element.51), channel_id=1, source_target_pairs={{0,48},{1,49},{2,50},{3,51},{4,52},{5,53},{6,54},{7,55},{8,56},{9,... | collective-permute-start | bytes 393224 | tf_op jit(solution)/shard_map/ppermute | solution.py:37
  24.7 6.1 %collective-permute-start.12 = (bf16[128,512]{1,0:T(8,128)(2,1)S(1)}, bf16[128,512]{1,0:T(8,128)(2,1)S(1)}, u32[]{:S(2)}, u32[]{:S(2)}) collective-permute-start(bf16[128,512]{1,0:T(8,128)(2,1)S(1)} %get-tuple-element.51), channel_id=1, source_target_pairs={{0,32},{1,33},{2,34},{3,35},{4,36},{5,37},{6,38},{7,39},{8,40},{9,... | collective-permute-start | bytes 393224 | tf_op jit(solution)/shard_map/ppermute | solution.py:37
  26.3 5.5 %collective-permute-start.6 = (bf16[128,512]{1,0:T(8,128)(2,1)S(1)}, bf16[128,512]{1,0:T(8,128)(2,1)S(1)}, u32[]{:S(2)}, u32[]{:S(2)}) collective-permute-start(bf16[128,512]{1,0:T(8,128)(2,1)S(1)} %get-tuple-element.48), channel_id=1, source_target_pairs={{0,4},{1,5},{2,6},{3,7},{4,8},{5,9},{6,10},{7,11},{8,12},{9,13},{1... | collective-permute-start | bytes 393224 | tf_op jit(solution)/shard_map/ppermute | solution.py:37
  27.6 4.1 %collective-permute-start.7 = (bf16[128,512]{1,0:T(8,128)(2,1)S(1)}, bf16[128,512]{1,0:T(8,128)(2,1)S(1)}, u32[]{:S(2)}, u32[]{:S(2)}) collective-permute-start(bf16[128,512]{1,0:T(8,128)(2,1)S(1)} %get-tuple-element.49), channel_id=1, source_target_pairs={{0,12},{1,13},{2,14},{3,15},{4,0},{5,1},{6,2},{7,3},{8,4},{9,5},{1... | collective-permute-start | bytes 393224 | tf_op jit(solution)/shard_map/ppermute | solution.py:37
  29.2 5.4 %collective-permute-start.8 = (bf16[128,512]{1,0:T(8,128)(2,1)S(1)}, bf16[128,512]{1,0:T(8,128)(2,1)S(1)}, u32[]{:S(2)}, u32[]{:S(2)}) collective-permute-start(bf16[128,512]{1,0:T(8,128)(2,1)S(1)} %get-tuple-element.50), channel_id=1, source_target_pairs={{0,8},{1,9},{2,10},{3,11},{4,12},{5,13},{6,14},{7,15},{8,0},{9,1},... | collective-permute-start | bytes 393224 | tf_op jit(solution)/shard_map/ppermute | solution.py:37
  30.8 29.1 %collective-permute-start.17 = (bf16[512,512]{1,0:T(8,128)(2,1)S(1)}, bf16[512,512]{1,0:T(8,128)(2,1)S(1)}, u32[]{:S(2)}, u32[]{:S(2)}) collective-permute-start(bf16[512,512]{1,0:T(8,128)(2,1)S(1)} %constant_dynamic-update-slice_fusion.4.refs_6_), channel_id=1, source_target_pairs={{0,4},{1,5},{2,6},{3,7},{4,8},{5,9},{6,10},{7,11},{8,12},{9,13},{1... | collective-permute-start | bytes 1572872 | tf_op jit(solution)/shard_map/ppermute | solution.py:37
  34.6 26.8 %collective-permute-start.16 = (bf16[512,512]{1,0:T(8,128)(2,1)S(1)}, bf16[512,512]{1,0:T(8,128)(2,1)S(1)}, u32[]{:S(2)}, u32[]{:S(2)}) collective-permute-start(bf16[512,512]{1,0:T(8,128)(2,1)S(1)} %constant_dynamic-update-slice_fusion.refs_5_), channel_id=1, source_target_pairs={{0,16},{1,17},{2,18},{3,19},{4,20},{5,21},{6,22},{7,23},{8,24},{9,... | collective-permute-start | bytes 1572872 | tf_op jit(solution)/shard_map/ppermute | solution.py:37
  34.9 36.0 %collective-permute-start.15 = (bf16[512,512]{1,0:T(8,128)(2,1)S(1)}, bf16[512,512]{1,0:T(8,128)(2,1)S(1)}, u32[]{:S(2)}, u32[]{:S(2)}) collective-permute-start(bf16[512,512]{1,0:T(8,128)(2,1)S(1)} %constant_dynamic-update-slice_fusion.4.refs_6_), channel_id=1, source_target_pairs={{0,12},{1,13},{2,14},{3,15},{4,0},{5,1},{6,2},{7,3},{8,4},{9,5},{1... | collective-permute-start | bytes 1572872 | tf_op jit(solution)/shard_map/ppermute | solution.py:37
  36.3 36.6 %collective-permute-start.14 = (bf16[512,512]{1,0:T(8,128)(2,1)S(1)}, bf16[512,512]{1,0:T(8,128)(2,1)S(1)}, u32[]{:S(2)}, u32[]{:S(2)}) collective-permute-start(bf16[512,512]{1,0:T(8,128)(2,1)S(1)} %constant_dynamic-update-slice_fusion.refs_5_), channel_id=1, source_target_pairs={{0,48},{1,49},{2,50},{3,51},{4,52},{5,53},{6,54},{7,55},{8,56},{9,... | collective-permute-start | bytes 1572872 | tf_op jit(solution)/shard_map/ppermute | solution.py:37
  38.9 9.4 %collective-permute-start = (bf16[256,256]{1,0:T(8,128)(2,1)S(1)}, bf16[256,256]{1,0:T(8,128)(2,1)S(1)}, u32[]{:S(2)}, u32[]{:S(2)}) collective-permute-start(bf16[256,256]{1,0:T(8,128)(2,1)S(1)} %get-tuple-element.35), channel_id=1, source_target_pairs={{0,4},{1,5},{2,6},{3,7},{4,8},{5,9},{6,10},{7,11},{8,12},{9,13},{1... | collective-permute-start | bytes 393224 | tf_op jit(solution)/shard_map/ppermute | solution.py:37
  48.4 5.3 %collective-permute-start.1 = (bf16[256,256]{1,0:T(8,128)(2,1)S(1)}, bf16[256,256]{1,0:T(8,128)(2,1)S(1)}, u32[]{:S(2)}, u32[]{:S(2)}) collective-permute-start(bf16[256,256]{1,0:T(8,128)(2,1)S(1)} %get-tuple-element.36), channel_id=1, source_target_pairs={{0,8},{1,9},{2,10},{3,11},{4,12},{5,13},{6,14},{7,15},{8,0},{9,1},... | collective-permute-start | bytes 393224 | tf_op jit(solution)/shard_map/ppermute | solution.py:37
  53.7 4.3 %collective-permute-start.2 = (bf16[256,256]{1,0:T(8,128)(2,1)S(1)}, bf16[256,256]{1,0:T(8,128)(2,1)S(1)}, u32[]{:S(2)}, u32[]{:S(2)}) collective-permute-start(bf16[256,256]{1,0:T(8,128)(2,1)S(1)} %get-tuple-element.37), channel_id=1, source_target_pairs={{0,12},{1,13},{2,14},{3,15},{4,0},{5,1},{6,2},{7,3},{8,4},{9,5},{1... | collective-permute-start | bytes 393224 | tf_op jit(solution)/shard_map/ppermute | solution.py:37
  58.0 22.5 %collective-permute-start.13 = (bf16[512,512]{1,0:T(8,128)(2,1)S(1)}, bf16[512,512]{1,0:T(8,128)(2,1)S(1)}, u32[]{:S(2)}, u32[]{:S(2)}) collective-permute-start(bf16[512,512]{1,0:T(8,128)(2,1)S(1)} %constant_dynamic-update-slice_fusion.4.refs_6_), channel_id=1, source_target_pairs={{0,8},{1,9},{2,10},{3,11},{4,12},{5,13},{6,14},{7,15},{8,0},{9,1},... | collective-permute-start | bytes 1572872 | tf_op jit(solution)/shard_map/ppermute | solution.py:37
  59.9 20.6 %collective-permute-start.9 = (bf16[512,512]{1,0:T(8,128)(2,1)S(1)}, bf16[512,512]{1,0:T(8,128)(2,1)S(1)}, u32[]{:S(2)}, u32[]{:S(2)}) collective-permute-start(bf16[512,512]{1,0:T(8,128)(2,1)S(1)} %constant_dynamic-update-slice_fusion.refs_5_), channel_id=1, source_target_pairs={{0,32},{1,33},{2,34},{3,35},{4,36},{5,37},{6,38},{7,39},{8,40},{9,... | collective-permute-start | bytes 1572872 | tf_op jit(solution)/shard_map/ppermute | solution.py:37
  61.3 57.0 %collective-permute-start.26 = (bf16[640,1280]{1,0:T(8,128)(2,1)S(1)}, bf16[640,1280]{1,0:T(8,128)(2,1)S(1)}, u32[]{:S(2)}, u32[]{:S(2)}) collective-permute-start(bf16[640,1280]{1,0:T(8,128)(2,1)S(1)} %get-tuple-element.63), channel_id=1, source_target_pairs={{0,1},{1,0},{2,3},{3,2},{4,5},{5,4},{6,7},{7,6},{8,9},{9,8},{10,11... | collective-permute-start | bytes 4915208 | tf_op jit(solution)/shard_map/ppermute | solution.py:37
  70.9 47.4 %collective-permute-start.27 = (bf16[640,1280]{1,0:T(8,128)(2,1)S(1)}, bf16[640,1280]{1,0:T(8,128)(2,1)S(1)}, u32[]{:S(2)}, u32[]{:S(2)}) collective-permute-start(bf16[640,1280]{1,0:T(8,128)(2,1)S(1)} %get-tuple-element.64), channel_id=1, source_target_pairs={{0,2},{1,3},{2,0},{3,1},{4,6},{5,7},{6,4},{7,5},{8,10},{9,11},{10,... | collective-permute-start | bytes 4915208 | tf_op jit(solution)/shard_map/ppermute | solution.py:37
  72.9 45.4 %collective-permute-start.28 = (bf16[640,1280]{1,0:T(8,128)(2,1)S(1)}, bf16[640,1280]{1,0:T(8,128)(2,1)S(1)}, u32[]{:S(2)}, u32[]{:S(2)}) collective-permute-start(bf16[640,1280]{1,0:T(8,128)(2,1)S(1)} %get-tuple-element.65), channel_id=1, source_target_pairs={{0,195},{1,194},{2,65},{3,64},{4,199},{5,198},{6,69},{7,68},{8,203... | collective-permute-start | bytes 4915208 | tf_op jit(solution)/shard_map/ppermute | solution.py:48
  82.2 6.2 %collective-permute-start.18 = (bf16[512,128]{1,0:T(8,128)(2,1)S(1)}, bf16[512,128]{1,0:T(8,128)(2,1)S(1)}, u32[]{:S(2)}, u32[]{:S(2)}) collective-permute-start(bf16[512,128]{1,0:T(8,128)(2,1)S(1)} %get-tuple-element.54), channel_id=1, source_target_pairs={{0,12},{1,13},{2,14},{3,15},{4,0},{5,1},{6,2},{7,3},{8,4},{9,5},{1... | collective-permute-start | bytes 393224 | tf_op jit(solution)/shard_map/ppermute | solution.py:37
  83.8 8.6 %collective-permute-start.19 = (bf16[512,128]{1,0:T(8,128)(2,1)S(1)}, bf16[512,128]{1,0:T(8,128)(2,1)S(1)}, u32[]{:S(2)}, u32[]{:S(2)}) collective-permute-start(bf16[512,128]{1,0:T(8,128)(2,1)S(1)} %get-tuple-element.55), channel_id=1, source_target_pairs={{0,8},{1,9},{2,10},{3,11},{4,12},{5,13},{6,14},{7,15},{8,0},{9,1},... | collective-permute-start | bytes 393224 | tf_op jit(solution)/shard_map/ppermute | solution.py:37
  88.4 5.9 %collective-permute-start.20 = (bf16[512,128]{1,0:T(8,128)(2,1)S(1)}, bf16[512,128]{1,0:T(8,128)(2,1)S(1)}, u32[]{:S(2)}, u32[]{:S(2)}) collective-permute-start(bf16[512,128]{1,0:T(8,128)(2,1)S(1)} %get-tuple-element.56), channel_id=1, source_target_pairs={{0,4},{1,5},{2,6},{3,7},{4,8},{5,9},{6,10},{7,11},{8,12},{9,13},{1... | collective-permute-start | bytes 393224 | tf_op jit(solution)/shard_map/ppermute | solution.py:37
  92.5 22.2 %collective-permute-start.24 = (bf16[512,256]{1,0:T(8,128)(2,1)S(1)}, bf16[512,256]{1,0:T(8,128)(2,1)S(1)}, u32[]{:S(2)}, u32[]{:S(2)}) collective-permute-start(bf16[512,256]{1,0:T(8,128)(2,1)S(1)} %shard_map.94.refs_0_), channel_id=1, source_target_pairs={{0,2},{1,3},{2,0},{3,1},{4,6},{5,7},{6,4},{7,5},{8,10},{9,11},{10,... | collective-permute-start | bytes 786440 | tf_op jit(solution)/shard_map/ppermute | solution.py:37
  94.4 22.4 %collective-permute-start.23 = (bf16[512,384]{1,0:T(8,128)(2,1)S(1)}, bf16[512,384]{1,0:T(8,128)(2,1)S(1)}, u32[]{:S(2)}, u32[]{:S(2)}) collective-permute-start(bf16[512,384]{1,0:T(8,128)(2,1)S(1)} %constant_dynamic-update-slice_fusion.8.refs_1_), channel_id=1, source_target_pairs={{0,1},{1,0},{2,3},{3,2},{4,5},{5,4},{6,7},{7,6},{8,9},{9,8},{10,11... | collective-permute-start | bytes 1179656 | tf_op jit(solution)/shard_map/ppermute | solution.py:37
  114.6 1.8 %collective-permute-start.22 = (bf16[512,256]{1,0:T(8,128)(2,1)S(1)}, bf16[512,256]{1,0:T(8,128)(2,1)S(1)}, u32[]{:S(2)}, u32[]{:S(2)}) collective-permute-start(bf16[512,256]{1,0:T(8,128)(2,1)S(1)} %shard_map.94.refs_0_), channel_id=1, source_target_pairs={{0,1},{1,0},{2,3},{3,2},{4,5},{5,4},{6,7},{7,6},{8,9},{9,8},{10,11... | collective-permute-start | bytes 786440 | tf_op jit(solution)/shard_map/ppermute | solution.py:37
  116.5 1.8 %collective-permute-start.25 = (bf16[512,256]{1,0:T(8,128)(2,1)S(1)}, bf16[512,256]{1,0:T(8,128)(2,1)S(1)}, u32[]{:S(2)}, u32[]{:S(2)}) collective-permute-start(bf16[512,256]{1,0:T(8,128)(2,1)S(1)} %collective-permute-done.24.refs_4_), channel_id=1, source_target_pairs={{0,1},{1,0},{2,3},{3,2},{4,5},{5,4},{6,7},{7,6},{8,9},{9,8},{10,11... | collective-permute-start | bytes 786440 | tf_op jit(solution)/shard_map/ppermute | solution.py:37
  116.8 10.5 %collective-permute-start.21 = (bf16[512,384]{1,0:T(8,128)(2,1)S(1)}, bf16[512,384]{1,0:T(8,128)(2,1)S(1)}, u32[]{:S(2)}, u32[]{:S(2)}) collective-permute-start(bf16[512,384]{1,0:T(8,128)(2,1)S(1)} %constant_dynamic-update-slice_fusion.8.refs_1_), channel_id=1, source_target_pairs={{0,2},{1,3},{2,0},{3,1},{4,6},{5,7},{6,4},{7,5},{8,10},{9,11},{10,... | collective-permute-start | bytes 1179656 | tf_op jit(solution)/shard_map/ppermute | solution.py:37
  127.4 2.3 %collective-permute-start.29 = (bf16[512,384]{1,0:T(8,128)(2,1)S(1)}, bf16[512,384]{1,0:T(8,128)(2,1)S(1)}, u32[]{:S(2)}, u32[]{:S(2)}) collective-permute-start(bf16[512,384]{1,0:T(8,128)(2,1)S(1)} %collective-permute-done.21.a_ref), channel_id=1, source_target_pairs={{0,1},{1,0},{2,3},{3,2},{4,5},{5,4},{6,7},{7,6},{8,9},{9,8},{10,11... | collective-permute-start | bytes 1179656 | tf_op jit(solution)/shard_map/ppermute | solution.py:37
where the time goes:
time: 135 us; the launch traced here: 133 us
  starting transfers between devices  58.3 us (43%)
  waiting for transfers between devices  51.9 us (38%)
  Pallas kernels  22 us (16%)
    ppermute x29, starting transfers between devices, shift(): return lax.ppermute(array, AXES, pairs)  58.3 us
    ppermute x29, waiting for transfers between devices, shift(): return lax.ppermute(array, AXES, pairs)  51.9 us
    pallas_call x10, Pallas kernels, called(): pl.pallas_call(kernel, out_shape=outs, in_specs=specs or [VMEM] * len(ope...  18.6 us
    pallas_call x1, Pallas kernels, project_last(): pl.pallas_call(project_last_kernel, grid=(columns // tile,), in_specs=[VM...  3.41 us
  transfers between devices with their start and end apart: 30, of which 13 were waited for; matrix products, arithmetic and copies ran while one was open for 0% of the time, Pallas kernels for 13%

commit v1 on v0

--- a/solution.py
+++ b/solution.py
@@ -24,13 +24,14 @@
 F32 = jnp.float32
 
 
-def shift(array, zh=0, x=0, y=0, zl=0, core=0):
+def shift(array, zh=0, swap=0, ring=0, zl=0, core=0):
     pairs = []
     for index in range(ZH * NX * NY * ZL * CORES):
         rest, c = divmod(index, CORES)
         rest, b = divmod(rest, ZL)
         rest, j = divmod(rest, NY)
         a, i = divmod(rest, NX)
+        x, y = (swap, ring) if c else (ring, swap)
         to = ((a + zh) % ZH, (i + x) % NX, (j + y) % NY, (b + zl) % ZL, (c + core) % CORES)
         target = (((to[0] * NX + to[1]) * NY + to[2]) * ZL + to[3]) * CORES + to[4]
         pairs.append((index, target))
@@ -98,10 +99,19 @@
 def split_keys_kernel(y_ref, *refs):
     pieces, out_refs = refs[:ZH], refs[ZH:]
     for k, out_ref in enumerate(out_refs):
-        head = lax.rem(y_ref[0] + k, NY) if k < NY else NY
-        for z, piece in enumerate(pieces):
-            rows = piece.shape[1]
-            out_ref[z * rows : (z + 1) * rows, :] = piece[head]
+        for half, head in enumerate((lax.rem(y_ref[0] + k, NY), NY)):
+            for z, piece in enumerate(pieces):
+                rows = piece.shape[1]
+                start = (half * ZH + z) * rows
+                out_ref[start : start + rows, :] = piece[head]
+
+
+def join_keys_kernel(*refs):
+    pieces, out_refs = refs[:NY], refs[NY:]
+    rows = pieces[0].shape[0] // 2
+    for half, out_ref in enumerate(out_refs):
+        for k, piece in enumerate(pieces):
+            out_ref[k * rows : (k + 1) * rows, :] = piece[half * rows : (half + 1) * rows, :]
 
 
 def attend(both, key_refs, state):
@@ -258,8 +268,9 @@
     heads = width // HD
     slab = keys.shape[0]
     columns = out_weight.shape[1] // (ZL * CORES)
-    y = (lax.axis_index("tok") % NY).astype(jnp.int32).reshape(1)
     place = lax.axis_index("head").astype(jnp.int32).reshape(1)
+    tok = lax.axis_index("tok").astype(jnp.int32).reshape(1)
+    y = jnp.where(place % CORES == 0, tok % NY, tok // NY % NX)
     with_index = [SMEM] + [VMEM] * 8
     out_weight = pltpu.with_memory_space_constraint(out_weight, pltpu.HBM)
     keys, values, query_tan, key_tan, value_tan, queries = (
@@ -288,7 +299,7 @@
         specs=[SMEM, HBM, HBM],
         scratch_shapes=[pltpu.VMEM((2, rows, width), BF16), pltpu.SemaphoreType.DMA((2,))],
     )
-    blocks = [sends[0]] + [shift(sends[k], y=k) for k in (1, 2, 3)] + [sends[NY]]
+    blocks = [sends[0]] + [shift(sends[k], swap=k) for k in (1, 2, 3)] + [sends[NY]]
 
     place, _ = lax.optimization_barrier((place, sends[1]))
     cuts = call(
@@ -304,28 +315,33 @@
 
     split = call(
         split_keys_kernel,
-        [jax.ShapeDtypeStruct((ZH * slab, 4 * HD), BF16)] * (NY + 1),
+        [jax.ShapeDtypeStruct((2 * ZH * slab, 4 * HD), BF16)] * NY,
         y,
         *pieces,
         specs=with_index[: ZH + 1],
     )
-    shared = jnp.concatenate([split[0]] + [shift(split[k], y=k) for k in (1, 3, 2)])
-    own = jnp.concatenate([split[NY]] + [shift(split[NY], x=k) for k in (1, 3, 2)])
-    shared_far = [shift(shared, x=k) for k in (1, 3, 2)]
-    own_far = [shift(own, y=k) for k in (1, 3, 2)]
-
     cuts, _ = lax.optimization_barrier((cuts, split[0]))
-    weight_core = shift(cuts[1], core=1)
     weight_near = shift(cuts[2], zl=1)
     weight_far = across(cuts[3])
-
-    state = attend_step(blocks, shared, own, None)
-    for k in range(2):
-        state = attend_step(blocks, shared_far[k], own_far[k], state)
-    others = attend_step(blocks, shared_far[2], own_far[2], state, (1, 2, 3), False)
-    own_far[2], _ = lax.optimization_barrier((own_far[2], others[0]))
-    mine = [attend_step(blocks, shared_far[2], own_far[2], state, (0, NY), True)]
-    back = [shift(others[k - 1], y=-k) for k in (1, 2, 3)]
+    weight_core = shift(cuts[1], core=1)
+
+    own = call(
+        join_keys_kernel,
+        [jax.ShapeDtypeStruct((NY * ZH * slab, 4 * HD), BF16)] * 2,
+        split[0],
+        *[shift(split[k], swap=k) for k in (1, 3, 2)],
+    )
+    left = [shift(own[0], ring=1), shift(own[1], ring=1)]
+    right = [shift(own[0], ring=-1), shift(own[1], ring=-1)]
+    opposite = [shift(left[0], ring=1), shift(right[1], ring=-1)]
+
+    state = attend_step(blocks, own[0], own[1], None)
+    state = attend_step(blocks, left[0], right[1], state)
+    state = attend_step(blocks, right[0], left[1], state)
+    others = attend_step(blocks, opposite[0], opposite[1], state, (1, 2, 3), False)
+    opposite[1], _ = lax.optimization_barrier((opposite[1], others[0]))
+    mine = [attend_step(blocks, opposite[0], opposite[1], state, (0, NY), True)]
+    back = [shift(others[k - 1], swap=-k) for k in (1, 2, 3)]
     mine.append(jnp.concatenate(back, axis=1))
 
     near = [shift(mine[n], zl=1) for n in range(2)]

time: 135 us -> 118 us (0.87)
  waiting for transfers between devices: 51.9 us -> 42.9 us
  starting transfers between devices: 58.3 us -> 51.3 us
    ppermute x29 -> x26, waiting for transfers between devices: 51.9 us -> 42.9 us  [shift(): return lax.ppermute(array, AXES, pairs)]
    ppermute x29 -> x26, starting transfers between devices: 58.3 us -> 51.3 us  [shift(): return lax.ppermute(array, AXES, pairs)]
    pallas_call x10 -> x11, Pallas kernels: 18.6 us -> 18.7 us  [called(): pl.pallas_call(kernel, out_shape=outs, in_specs=specs or [VMEM] * len(ope...]
  transfers between devices with their start and end apart: 30 -> 27, of which waited for: 13 -> 13; matrix products, arithmetic and copies ran while one was open for 0% -> 0% of each run, Pallas kernels for 13% -> 15%
where the time goes in v1:
time: 118 us; the launch traced here: 117 us
  starting transfers between devices  51.3 us (43%)
  waiting for transfers between devices  42.9 us (36%)
  Pallas kernels  22.1 us (19%)
    ppermute x26, starting transfers between devices, shift(): return lax.ppermute(array, AXES, pairs)  51.3 us
    ppermute x26, waiting for transfers between devices, shift(): return lax.ppermute(array, AXES, pairs)  42.9 us
    pallas_call x11, Pallas kernels, called(): pl.pallas_call(kernel, out_shape=outs, in_specs=specs or [VMEM] * len(ope...  18.7 us
    pallas_call x1, Pallas kernels, project_last(): pl.pallas_call(project_last_kernel, grid=(columns // tile,), in_specs=[VM...  3.41 us
  transfers between devices with their start and end apart: 27, of which 13 were waited for; matrix products, arithmetic and copies ran while one was open for 0% of the time, Pallas kernels for 15%

profile of v1, /device:TPU:1, one launch (start us, length us, event | category | flops | bytes accessed | tf_op | source)
XLA Modules:
  0.0 117.2 jit_solution(12207930852391195286)
XLA Ops:
  0.6 0.9 shard_map.87.refs_0_
  1.5 3.9 %collective-permute-start.3 = (bf16[5,32,512]{2,1,0:T(8,128)(2,1)S(1)}, bf16[5,32,512]{2,1,0:T(8,128)(2,1)S(1)}, u32[]{:S(2)}, u32[]{:S(2)}) collective-permute-start(bf16[5,32,512]{2,1,0:T(8,128)(2,1)S(1)} %shard_map.87.refs_0_), channel_id=1, source_target_pairs={{0,64},{1,65},{2,66},{3,67},{4,68},{5,69},{6,70},{7,71},{8,72},{9,... | collective-permute-start | bytes 491528 | tf_op jit(solution)/shard_map/ppermute | solution.py:38
  5.4 3.1 %collective-permute-start.4 = (bf16[5,32,512]{2,1,0:T(8,128)(2,1)S(1)}, bf16[5,32,512]{2,1,0:T(8,128)(2,1)S(1)}, u32[]{:S(2)}, u32[]{:S(2)}) collective-permute-start(bf16[5,32,512]{2,1,0:T(8,128)(2,1)S(1)} %shard_map.87.refs_0_), channel_id=1, source_target_pairs={{0,192},{1,193},{2,194},{3,195},{4,196},{5,197},{6,198},{7,199},{8... | collective-permute-start | bytes 491528 | tf_op jit(solution)/shard_map/ppermute | solution.py:38
  8.5 4.4 %collective-permute-start.5 = (bf16[5,32,512]{2,1,0:T(8,128)(2,1)S(1)}, bf16[5,32,512]{2,1,0:T(8,128)(2,1)S(1)}, u32[]{:S(2)}, u32[]{:S(2)}) collective-permute-start(bf16[5,32,512]{2,1,0:T(8,128)(2,1)S(1)} %shard_map.87.refs_0_), channel_id=1, source_target_pairs={{0,128},{1,129},{2,130},{3,131},{4,132},{5,133},{6,134},{7,135},{8... | collective-permute-start | bytes 491528 | tf_op jit(solution)/shard_map/ppermute | solution.py:38
  12.9 1.2 %shard_map.86 = (bf16[256,256]{1,0:T(8,128)(2,1)S(1)}, bf16[256,256]{1,0:T(8,128)(2,1)S(1)}, bf16[256,256]{1,0:T(8,128)(2,1)S(1)}, bf16[256,256]{1,0:T(8,128)(2,1)S(1)}, bf16[256,256]{1,0:T(8,128)(2,1)S(1)}) custom-call(s32[1]{0:T(128)S(6)} %select_n.27.y_ref, bf16[256,640]{1,0:T(8,128)(2,1)} %q_ref.1, bf16[256,640]{1,0:T(8,128)(2,1)} %dq_ref.1), custom_call_target="tpu_custom_call" | custom-call | bytes 655364 | tf_op jit(solution)/shard_map/pallas_call | solution.py:57
  14.1 3.1 %shard_map.88 = (bf16[640,1280]{1,0:T(8,128)(2,1)S(1)}, bf16[640,1280]{1,0:T(8,128)(2,1)S(1)}, bf16[640,1280]{1,0:T(8,128)(2,1)S(1)}, bf16[640,1280]{1,0:T(8,128)(2,1)S(1)}) custom-call(s32[1]{0:T(128)S(6)} %select_n.27.y_ref, s32[1]{0:T(128)} %bitcast.place_ref, bf16[640,5120]{1,0:T(8,128)(2,1)} %w_ref.1), custom_call_target="tpu_custom_call" | custom-call | bytes 6553608 | tf_op jit(solution)/shard_map/pallas_call | solution.py:57
  17.2 3.8 %collective-permute-done.4.refs_2_ = bf16[5,32,512]{2,1,0:T(8,128)(2,1)S(1)} collective-permute-done((bf16[5,32,512]{2,1,0:T(8,128)(2,1)S(1)}, bf16[5,32,512]{2,1,0:T(8,128)(2,1)S(1)}, u32[]{:S(2)}, u32[]{:S(2)}) %collective-permute-start.4) | collective-permute-done | bytes 163872 | tf_op jit(solution)/shard_map/ppermute | solution.py:38
  21.0 0.9 collective-permute-done.5.refs_3_
  21.8 0.1 shard_map.89
  21.9 1.3 %collective-permute-start.6 = (bf16[256,512]{1,0:T(8,128)(2,1)S(1)}, bf16[256,512]{1,0:T(8,128)(2,1)S(1)}, u32[]{:S(2)}, u32[]{:S(2)}) collective-permute-start(bf16[256,512]{1,0:T(8,128)(2,1)S(1)} %get-tuple-element.49), channel_id=1, source_target_pairs={{0,4},{1,17},{2,6},{3,19},{4,8},{5,21},{6,10},{7,23},{8,12},{9,25}... | collective-permute-start | bytes 786440 | tf_op jit(solution)/shard_map/ppermute | solution.py:38
  23.2 1.5 %collective-permute-start.7 = (bf16[256,512]{1,0:T(8,128)(2,1)S(1)}, bf16[256,512]{1,0:T(8,128)(2,1)S(1)}, u32[]{:S(2)}, u32[]{:S(2)}) collective-permute-start(bf16[256,512]{1,0:T(8,128)(2,1)S(1)} %get-tuple-element.50), channel_id=1, source_target_pairs={{0,12},{1,49},{2,14},{3,51},{4,0},{5,53},{6,2},{7,55},{8,4},{9,57}... | collective-permute-start | bytes 786440 | tf_op jit(solution)/shard_map/ppermute | solution.py:38
  24.6 1.5 %collective-permute-start.8 = (bf16[256,512]{1,0:T(8,128)(2,1)S(1)}, bf16[256,512]{1,0:T(8,128)(2,1)S(1)}, u32[]{:S(2)}, u32[]{:S(2)}) collective-permute-start(bf16[256,512]{1,0:T(8,128)(2,1)S(1)} %get-tuple-element.51), channel_id=1, source_target_pairs={{0,8},{1,33},{2,10},{3,35},{4,12},{5,37},{6,14},{7,39},{8,0},{9,41... | collective-permute-start | bytes 786440 | tf_op jit(solution)/shard_map/ppermute | solution.py:38
  26.2 2.2 %collective-permute-done.6.refs_1_ = bf16[256,512]{1,0:T(8,128)(2,1)S(1)} collective-permute-done((bf16[256,512]{1,0:T(8,128)(2,1)S(1)}, bf16[256,512]{1,0:T(8,128)(2,1)S(1)}, u32[]{:S(2)}, u32[]{:S(2)}) %collective-permute-start.6) | collective-permute-done | bytes 262176 | tf_op jit(solution)/shard_map/ppermute | solution.py:38
  28.4 3.8 %collective-permute-done.8.refs_3_ = bf16[256,512]{1,0:T(8,128)(2,1)S(1)} collective-permute-done((bf16[256,512]{1,0:T(8,128)(2,1)S(1)}, bf16[256,512]{1,0:T(8,128)(2,1)S(1)}, u32[]{:S(2)}, u32[]{:S(2)}) %collective-permute-start.8) | collective-permute-done | bytes 262176 | tf_op jit(solution)/shard_map/ppermute | solution.py:38
  32.2 0.1 shard_map.90
  32.3 3.1 %collective-permute-start.11 = (bf16[512,512]{1,0:T(8,128)(2,1)S(1)}, bf16[512,512]{1,0:T(8,128)(2,1)S(1)}, u32[]{:S(2)}, u32[]{:S(2)}) collective-permute-start(bf16[512,512]{1,0:T(8,128)(2,1)S(1)} %get-tuple-element.53.refs_6_), channel_id=1, source_target_pairs={{0,48},{1,13},{2,50},{3,15},{4,52},{5,1},{6,54},{7,3},{8,56},{9,5}... | collective-permute-start | bytes 1572872 | tf_op jit(solution)/shard_map/ppermute | solution.py:38
  35.4 0.9 collective-permute-start
  36.2 2.0 %collective-permute-start.1 = (bf16[256,256]{1,0:T(8,128)(2,1)S(1)}, bf16[256,256]{1,0:T(8,128)(2,1)S(1)}, u32[]{:S(2)}, u32[]{:S(2)}) collective-permute-start(bf16[256,256]{1,0:T(8,128)(2,1)S(1)} %get-tuple-element.37), channel_id=1, source_target_pairs={{0,8},{1,33},{2,10},{3,35},{4,12},{5,37},{6,14},{7,39},{8,0},{9,41... | collective-permute-start | bytes 393224 | tf_op jit(solution)/shard_map/ppermute | solution.py:38
  38.3 2.7 %collective-permute-start.13 = (bf16[512,512]{1,0:T(8,128)(2,1)S(1)}, bf16[512,512]{1,0:T(8,128)(2,1)S(1)}, u32[]{:S(2)}, u32[]{:S(2)}) collective-permute-start(bf16[512,512]{1,0:T(8,128)(2,1)S(1)} %get-tuple-element.52.refs_5_), channel_id=1, source_target_pairs={{0,48},{1,13},{2,50},{3,15},{4,52},{5,1},{6,54},{7,3},{8,56},{9,5}... | collective-permute-start | bytes 1572872 | tf_op jit(solution)/shard_map/ppermute | solution.py:38
  40.9 1.1 collective-permute-done.1.refs_2_.refs_1_
  42.0 2.5 %collective-permute-start.2 = (bf16[256,256]{1,0:T(8,128)(2,1)S(1)}, bf16[256,256]{1,0:T(8,128)(2,1)S(1)}, u32[]{:S(2)}, u32[]{:S(2)}) collective-permute-start(bf16[256,256]{1,0:T(8,128)(2,1)S(1)} %get-tuple-element.38), channel_id=1, source_target_pairs={{0,12},{1,49},{2,14},{3,51},{4,0},{5,53},{6,2},{7,55},{8,4},{9,57}... | collective-permute-start | bytes 393224 | tf_op jit(solution)/shard_map/ppermute | solution.py:38
  44.6 3.3 %collective-permute-done.2.refs_3_.refs_2_ = bf16[256,256]{1,0:T(8,128)(2,1)S(1)} collective-permute-done((bf16[256,256]{1,0:T(8,128)(2,1)S(1)}, bf16[256,256]{1,0:T(8,128)(2,1)S(1)}, u32[]{:S(2)}, u32[]{:S(2)}) %collective-permute-start.2) | collective-permute-done | bytes 131104 | tf_op jit(solution)/shard_map/ppermute | solution.py:38
  47.9 8.0 %collective-permute-start.23 = (bf16[640,1280]{1,0:T(8,128)(2,1)S(1)}, bf16[640,1280]{1,0:T(8,128)(2,1)S(1)}, u32[]{:S(2)}, u32[]{:S(2)}) collective-permute-start(bf16[640,1280]{1,0:T(8,128)(2,1)S(1)} %get-tuple-element.65), channel_id=1, source_target_pairs={{0,1},{1,0},{2,3},{3,2},{4,5},{5,4},{6,7},{7,6},{8,9},{9,8},{10,11... | collective-permute-start | bytes 4915208 | tf_op jit(solution)/shard_map/ppermute | solution.py:38
  55.8 2.6 %collective-permute-start.24 = (bf16[640,1280]{1,0:T(8,128)(2,1)S(1)}, bf16[640,1280]{1,0:T(8,128)(2,1)S(1)}, u32[]{:S(2)}, u32[]{:S(2)}) collective-permute-start(bf16[640,1280]{1,0:T(8,128)(2,1)S(1)} %get-tuple-element.66), channel_id=1, source_target_pairs={{0,2},{1,3},{2,0},{3,1},{4,6},{5,7},{6,4},{7,5},{8,10},{9,11},{10,... | collective-permute-start | bytes 4915208 | tf_op jit(solution)/shard_map/ppermute | solution.py:38
  58.4 0.3 collective-permute-start.10
  58.7 2.7 %collective-permute-start.12 = (bf16[512,512]{1,0:T(8,128)(2,1)S(1)}, bf16[512,512]{1,0:T(8,128)(2,1)S(1)}, u32[]{:S(2)}, u32[]{:S(2)}) collective-permute-start(bf16[512,512]{1,0:T(8,128)(2,1)S(1)} %collective-permute-done.11.refs_6_), channel_id=1, source_target_pairs={{0,48},{1,13},{2,50},{3,15},{4,52},{5,1},{6,54},{7,3},{8,56},{9,5}... | collective-permute-start | bytes 1572872 | tf_op jit(solution)/shard_map/ppermute | solution.py:38
  61.4 2.1 %shard_map.91.refs_7_ = f32[5,256,768]{2,1,0:T(8,128)S(1)} custom-call(bf16[256,256]{1,0:T(8,128)(2,1)S(1)} %get-tuple-element.54.refs_0_, bf16[256,256]{1,0:T(8,128)(2,1)S(1)} %collective-permute-done.refs_1_.refs_0_, bf16[256,256]{1,0:T(8,128)(2,1)S(1)} %collective-permute-done.1.refs_2_.refs_1_, ...), custom_call_target="tpu_custom_call" | custom-call | flops 1174405120 | bytes 1703936 | tf_op jit(solution)/shard_map/pallas_call | solution.py:57
  63.5 2.7 %shard_map.92.refs_7_ = f32[5,256,768]{2,1,0:T(8,128)S(1)} custom-call(bf16[256,256]{1,0:T(8,128)(2,1)S(1)} %get-tuple-element.54.refs_0_, bf16[256,256]{1,0:T(8,128)(2,1)S(1)} %collective-permute-done.refs_1_.refs_0_, bf16[256,256]{1,0:T(8,128)(2,1)S(1)} %collective-permute-done.1.refs_2_.refs_1_, ...), custom_call_target="tpu_custom_call" | custom-call | flops 1174405120 | bytes 5636096 | tf_op jit(solution)/shard_map/pallas_call | solution.py:57
  66.2 2.7 %shard_map.93.refs_5_.refs_4_ = f32[5,256,768]{2,1,0:T(8,128)S(1)} custom-call(bf16[256,256]{1,0:T(8,128)(2,1)S(1)} %get-tuple-element.54.refs_0_, bf16[256,256]{1,0:T(8,128)(2,1)S(1)} %collective-permute-done.refs_1_.refs_0_, bf16[256,256]{1,0:T(8,128)(2,1)S(1)} %collective-permute-done.1.refs_2_.refs_1_, ...), custom_call_target="tpu_custom_call" | custom-call | flops 1174405120 | bytes 5636096 | tf_op jit(solution)/shard_map/pallas_call | solution.py:57
  68.9 1.8 %shard_map.94 = (bf16[512,128]{1,0:T(8,128)(2,1)S(1)}, bf16[512,128]{1,0:T(8,128)(2,1)S(1)}, bf16[512,128]{1,0:T(8,128)(2,1)S(1)}) custom-call(bf16[256,256]{1,0:T(8,128)(2,1)S(1)} %collective-permute-done.refs_1_.refs_0_, bf16[256,256]{1,0:T(8,128)(2,1)S(1)} %collective-permute-done.1.refs_2_.refs_1_, ...), custom_call_target="tpu_custom_call" | custom-call | flops 704643072 | bytes 5373952 | tf_op jit(solution)/shard_map/pallas_call | solution.py:57
  70.7 2.5 %collective-permute-start.15 = (bf16[512,128]{1,0:T(8,128)(2,1)S(1)}, bf16[512,128]{1,0:T(8,128)(2,1)S(1)}, u32[]{:S(2)}, u32[]{:S(2)}) collective-permute-start(bf16[512,128]{1,0:T(8,128)(2,1)S(1)} %get-tuple-element.56), channel_id=1, source_target_pairs={{0,12},{1,49},{2,14},{3,51},{4,0},{5,53},{6,2},{7,55},{8,4},{9,57}... | collective-permute-start | bytes 393224 | tf_op jit(solution)/shard_map/ppermute | solution.py:38
  73.2 0.7 collective-permute-start.16
  73.9 1.3 %collective-permute-done.15 = bf16[512,128]{1,0:T(8,128)(2,1)S(1)} collective-permute-done((bf16[512,128]{1,0:T(8,128)(2,1)S(1)}, bf16[512,128]{1,0:T(8,128)(2,1)S(1)}, u32[]{:S(2)}, u32[]{:S(2)}) %collective-permute-start.15) | collective-permute-done | bytes 131104 | tf_op jit(solution)/shard_map/ppermute | solution.py:38
  75.2 1.0 collective-permute-start.17
  76.1 1.2 %shard_map.95.refs_0_ = bf16[512,256]{1,0:T(8,128)(2,1)S(1)} custom-call(bf16[256,256]{1,0:T(8,128)(2,1)S(1)} %get-tuple-element.54.refs_0_, bf16[256,256]{1,0:T(8,128)(2,1)S(1)} %get-tuple-element.55.refs_4_.refs_1_, bf16[512,512]{1,0:T(8,128)(2,1)S(1)} %collective-permute-done.10.refs_3_.refs_2_, ...), custom_call_target="tpu_custom_call" | custom-call | flops 469762048 | bytes 5242880 | tf_op jit(solution)/shard_map/pallas_call | solution.py:57
  77.4 1.5 %collective-permute-done.16 = bf16[512,128]{1,0:T(8,128)(2,1)S(1)} collective-permute-done((bf16[512,128]{1,0:T(8,128)(2,1)S(1)}, bf16[512,128]{1,0:T(8,128)(2,1)S(1)}, u32[]{:S(2)}, u32[]{:S(2)}) %collective-permute-start.16) | collective-permute-done | bytes 131104 | tf_op jit(solution)/shard_map/ppermute | solution.py:38
  78.8 1.4 %collective-permute-start.21 = (bf16[512,256]{1,0:T(8,128)(2,1)S(1)}, bf16[512,256]{1,0:T(8,128)(2,1)S(1)}, u32[]{:S(2)}, u32[]{:S(2)}) collective-permute-start(bf16[512,256]{1,0:T(8,128)(2,1)S(1)} %shard_map.95.refs_0_), channel_id=1, source_target_pairs={{0,2},{1,3},{2,0},{3,1},{4,6},{5,7},{6,4},{7,5},{8,10},{9,11},{10,... | collective-permute-start | bytes 786440 | tf_op jit(solution)/shard_map/ppermute | solution.py:38
  80.3 2.3 %collective-permute-done.17 = bf16[512,128]{1,0:T(8,128)(2,1)S(1)} collective-permute-done((bf16[512,128]{1,0:T(8,128)(2,1)S(1)}, bf16[512,128]{1,0:T(8,128)(2,1)S(1)}, u32[]{:S(2)}, u32[]{:S(2)}) %collective-permute-start.17) | collective-permute-done | bytes 131104 | tf_op jit(solution)/shard_map/ppermute | solution.py:38
  82.6 2.0 %collective-permute-start.19 = (bf16[512,256]{1,0:T(8,128)(2,1)S(1)}, bf16[512,256]{1,0:T(8,128)(2,1)S(1)}, u32[]{:S(2)}, u32[]{:S(2)}) collective-permute-start(bf16[512,256]{1,0:T(8,128)(2,1)S(1)} %shard_map.95.refs_0_), channel_id=1, source_target_pairs={{0,1},{1,0},{2,3},{3,2},{4,5},{5,4},{6,7},{7,6},{8,9},{9,8},{10,11... | collective-permute-start | bytes 786440 | tf_op jit(solution)/shard_map/ppermute | solution.py:38
  84.7 15.5 %collective-permute-done.21.refs_4_ = bf16[512,256]{1,0:T(8,128)(2,1)S(1)} collective-permute-done((bf16[512,256]{1,0:T(8,128)(2,1)S(1)}, bf16[512,256]{1,0:T(8,128)(2,1)S(1)}, u32[]{:S(2)}, u32[]{:S(2)}) %collective-permute-start.21) | collective-permute-done | bytes 262176 | tf_op jit(solution)/shard_map/ppermute | solution.py:38
  100.2 0.6 collective-permute-start.20
  100.8 1.5 %collective-permute-start.18 = (bf16[512,384]{1,0:T(8,128)(2,1)S(1)}, bf16[512,384]{1,0:T(8,128)(2,1)S(1)}, u32[]{:S(2)}, u32[]{:S(2)}) collective-permute-start(bf16[512,384]{1,0:T(8,128)(2,1)S(1)} %constant_dynamic-update-slice_fusion.refs_1_), channel_id=1, source_target_pairs={{0,2},{1,3},{2,0},{3,1},{4,6},{5,7},{6,4},{7,5},{8,10},{9,11},{10,... | collective-permute-start | bytes 1179656 | tf_op jit(solution)/shard_map/ppermute | solution.py:38
  102.3 0.2 collective-permute-done.22.refs_5_
  102.5 2.9 %shard_map.96.sum_ref = f32[512,1280]{1,0:T(8,128)S(1)} custom-call(bf16[512,256]{1,0:T(8,128)(2,1)S(1)} %shard_map.95.refs_0_, bf16[512,384]{1,0:T(8,128)(2,1)S(1)} %constant_dynamic-update-slice_fusion.refs_1_, bf16[512,256]{1,0:T(8,128)(2,1)S(1)} %collective-permute-done.19.refs_2_, bf16[512,384]{1,0:T(8,128)(2,1)S(1)} %collective-permute-done.20.refs_3_, ...), custom_call_target="tpu_custom_call" | custom-call | flops 2097152000 | bytes 8388608 | tf_op jit(solution)/shard_map/pallas_call | solution.py:57
  105.4 5.8 %collective-permute-done.18.a_ref = bf16[512,384]{1,0:T(8,128)(2,1)S(1)} collective-permute-done((bf16[512,384]{1,0:T(8,128)(2,1)S(1)}, bf16[512,384]{1,0:T(8,128)(2,1)S(1)}, u32[]{:S(2)}, u32[]{:S(2)}) %collective-permute-start.18) | collective-permute-done | bytes 393248 | tf_op jit(solution)/shard_map/ppermute | solution.py:38
  111.1 1.3 %collective-permute-start.26 = (bf16[512,384]{1,0:T(8,128)(2,1)S(1)}, bf16[512,384]{1,0:T(8,128)(2,1)S(1)}, u32[]{:S(2)}, u32[]{:S(2)}) collective-permute-start(bf16[512,384]{1,0:T(8,128)(2,1)S(1)} %collective-permute-done.18.a_ref), channel_id=1, source_target_pairs={{0,1},{1,0},{2,3},{3,2},{4,5},{5,4},{6,7},{7,6},{8,9},{9,8},{10,11... | collective-permute-start | bytes 1179656 | tf_op jit(solution)/shard_map/ppermute | solution.py:38
  112.4 1.3 %collective-permute-done.26.b_ref = bf16[512,384]{1,0:T(8,128)(2,1)S(1)} collective-permute-done((bf16[512,384]{1,0:T(8,128)(2,1)S(1)}, bf16[512,384]{1,0:T(8,128)(2,1)S(1)}, u32[]{:S(2)}, u32[]{:S(2)}) %collective-permute-start.26) | collective-permute-done | bytes 393248 | tf_op jit(solution)/shard_map/ppermute | solution.py:38
  113.8 3.4 %project_last.1 = (bf16[256,1280]{1,0:T(8,128)(2,1)}, bf16[256,1280]{1,0:T(8,128)(2,1)}) custom-call(bf16[512,384]{1,0:T(8,128)(2,1)S(1)} %collective-permute-done.18.a_ref, bf16[512,384]{1,0:T(8,128)(2,1)S(1)} %collective-permute-done.26.b_ref, bf16[640,1280]{1,0:T(8,128)(2,1)S(1)} %collective-permute-done.24.refs_8_.w_ref, ...), custom_call_target="tpu_custom_call" | custom-call | tf_op jit(solution)/shard_map/project_last/pallas_call | solution.py:255
  (21 shorter events, 0.1 us)
Async XLA Ops:
  1.5 15.7 %collective-permute-start.3 = (bf16[5,32,512]{2,1,0:T(8,128)(2,1)S(1)}, bf16[5,32,512]{2,1,0:T(8,128)(2,1)S(1)}, u32[]{:S(2)}, u32[]{:S(2)}) collective-permute-start(bf16[5,32,512]{2,1,0:T(8,128)(2,1)S(1)} %shard_map.87.refs_0_), channel_id=1, source_target_pairs={{0,64},{1,65},{2,66},{3,67},{4,68},{5,69},{6,70},{7,71},{8,72},{9,... | collective-permute-start | bytes 491528 | tf_op jit(solution)/shard_map/ppermute | solution.py:38
  5.4 15.5 %collective-permute-start.4 = (bf16[5,32,512]{2,1,0:T(8,128)(2,1)S(1)}, bf16[5,32,512]{2,1,0:T(8,128)(2,1)S(1)}, u32[]{:S(2)}, u32[]{:S(2)}) collective-permute-start(bf16[5,32,512]{2,1,0:T(8,128)(2,1)S(1)} %shard_map.87.refs_0_), channel_id=1, source_target_pairs={{0,192},{1,193},{2,194},{3,195},{4,196},{5,197},{6,198},{7,199},{8... | collective-permute-start | bytes 491528 | tf_op jit(solution)/shard_map/ppermute | solution.py:38
  8.5 13.3 %collective-permute-start.5 = (bf16[5,32,512]{2,1,0:T(8,128)(2,1)S(1)}, bf16[5,32,512]{2,1,0:T(8,128)(2,1)S(1)}, u32[]{:S(2)}, u32[]{:S(2)}) collective-permute-start(bf16[5,32,512]{2,1,0:T(8,128)(2,1)S(1)} %shard_map.87.refs_0_), channel_id=1, source_target_pairs={{0,128},{1,129},{2,130},{3,131},{4,132},{5,133},{6,134},{7,135},{8... | collective-permute-start | bytes 491528 | tf_op jit(solution)/shard_map/ppermute | solution.py:38
  21.9 6.5 %collective-permute-start.6 = (bf16[256,512]{1,0:T(8,128)(2,1)S(1)}, bf16[256,512]{1,0:T(8,128)(2,1)S(1)}, u32[]{:S(2)}, u32[]{:S(2)}) collective-permute-start(bf16[256,512]{1,0:T(8,128)(2,1)S(1)} %get-tuple-element.49), channel_id=1, source_target_pairs={{0,4},{1,17},{2,6},{3,19},{4,8},{5,21},{6,10},{7,23},{8,12},{9,25}... | collective-permute-start | bytes 786440 | tf_op jit(solution)/shard_map/ppermute | solution.py:38
  23.2 5.2 %collective-permute-start.7 = (bf16[256,512]{1,0:T(8,128)(2,1)S(1)}, bf16[256,512]{1,0:T(8,128)(2,1)S(1)}, u32[]{:S(2)}, u32[]{:S(2)}) collective-permute-start(bf16[256,512]{1,0:T(8,128)(2,1)S(1)} %get-tuple-element.50), channel_id=1, source_target_pairs={{0,12},{1,49},{2,14},{3,51},{4,0},{5,53},{6,2},{7,55},{8,4},{9,57}... | collective-permute-start | bytes 786440 | tf_op jit(solution)/shard_map/ppermute | solution.py:38
  24.6 7.5 %collective-permute-start.8 = (bf16[256,512]{1,0:T(8,128)(2,1)S(1)}, bf16[256,512]{1,0:T(8,128)(2,1)S(1)}, u32[]{:S(2)}, u32[]{:S(2)}) collective-permute-start(bf16[256,512]{1,0:T(8,128)(2,1)S(1)} %get-tuple-element.51), channel_id=1, source_target_pairs={{0,8},{1,33},{2,10},{3,35},{4,12},{5,37},{6,14},{7,39},{8,0},{9,41... | collective-permute-start | bytes 786440 | tf_op jit(solution)/shard_map/ppermute | solution.py:38
  32.3 23.6 %collective-permute-start.11 = (bf16[512,512]{1,0:T(8,128)(2,1)S(1)}, bf16[512,512]{1,0:T(8,128)(2,1)S(1)}, u32[]{:S(2)}, u32[]{:S(2)}) collective-permute-start(bf16[512,512]{1,0:T(8,128)(2,1)S(1)} %get-tuple-element.53.refs_6_), channel_id=1, source_target_pairs={{0,48},{1,13},{2,50},{3,15},{4,52},{5,1},{6,54},{7,3},{8,56},{9,5}... | collective-permute-start | bytes 1572872 | tf_op jit(solution)/shard_map/ppermute | solution.py:38
  35.4 23.0 %collective-permute-start.9 = (bf16[512,512]{1,0:T(8,128)(2,1)S(1)}, bf16[512,512]{1,0:T(8,128)(2,1)S(1)}, u32[]{:S(2)}, u32[]{:S(2)}) collective-permute-start(bf16[512,512]{1,0:T(8,128)(2,1)S(1)} %get-tuple-element.52.refs_5_), channel_id=1, source_target_pairs={{0,16},{1,5},{2,18},{3,7},{4,20},{5,9},{6,22},{7,11},{8,24},{9,13}... | collective-permute-start | bytes 1572872 | tf_op jit(solution)/shard_map/ppermute | solution.py:38
  35.4 5.6 %collective-permute-start = (bf16[256,256]{1,0:T(8,128)(2,1)S(1)}, bf16[256,256]{1,0:T(8,128)(2,1)S(1)}, u32[]{:S(2)}, u32[]{:S(2)}) collective-permute-start(bf16[256,256]{1,0:T(8,128)(2,1)S(1)} %get-tuple-element.36), channel_id=1, source_target_pairs={{0,4},{1,17},{2,6},{3,19},{4,8},{5,21},{6,10},{7,23},{8,12},{9,25}... | collective-permute-start | bytes 393224 | tf_op jit(solution)/shard_map/ppermute | solution.py:38
  36.2 5.8 %collective-permute-start.1 = (bf16[256,256]{1,0:T(8,128)(2,1)S(1)}, bf16[256,256]{1,0:T(8,128)(2,1)S(1)}, u32[]{:S(2)}, u32[]{:S(2)}) collective-permute-start(bf16[256,256]{1,0:T(8,128)(2,1)S(1)} %get-tuple-element.37), channel_id=1, source_target_pairs={{0,8},{1,33},{2,10},{3,35},{4,12},{5,37},{6,14},{7,39},{8,0},{9,41... | collective-permute-start | bytes 393224 | tf_op jit(solution)/shard_map/ppermute | solution.py:38
  38.3 20.1 %collective-permute-start.13 = (bf16[512,512]{1,0:T(8,128)(2,1)S(1)}, bf16[512,512]{1,0:T(8,128)(2,1)S(1)}, u32[]{:S(2)}, u32[]{:S(2)}) collective-permute-start(bf16[512,512]{1,0:T(8,128)(2,1)S(1)} %get-tuple-element.52.refs_5_), channel_id=1, source_target_pairs={{0,48},{1,13},{2,50},{3,15},{4,52},{5,1},{6,54},{7,3},{8,56},{9,5}... | collective-permute-start | bytes 1572872 | tf_op jit(solution)/shard_map/ppermute | solution.py:38
  40.9 17.8 %collective-permute-start.14 = (bf16[512,512]{1,0:T(8,128)(2,1)S(1)}, bf16[512,512]{1,0:T(8,128)(2,1)S(1)}, u32[]{:S(2)}, u32[]{:S(2)}) collective-permute-start(bf16[512,512]{1,0:T(8,128)(2,1)S(1)} %get-tuple-element.53.refs_6_), channel_id=1, source_target_pairs={{0,16},{1,5},{2,18},{3,7},{4,20},{5,9},{6,22},{7,11},{8,24},{9,13}... | collective-permute-start | bytes 1572872 | tf_op jit(solution)/shard_map/ppermute | solution.py:38
  42.0 5.8 %collective-permute-start.2 = (bf16[256,256]{1,0:T(8,128)(2,1)S(1)}, bf16[256,256]{1,0:T(8,128)(2,1)S(1)}, u32[]{:S(2)}, u32[]{:S(2)}) collective-permute-start(bf16[256,256]{1,0:T(8,128)(2,1)S(1)} %get-tuple-element.38), channel_id=1, source_target_pairs={{0,12},{1,49},{2,14},{3,51},{4,0},{5,53},{6,2},{7,55},{8,4},{9,57}... | collective-permute-start | bytes 393224 | tf_op jit(solution)/shard_map/ppermute | solution.py:38
  47.9 52.9 %collective-permute-start.23 = (bf16[640,1280]{1,0:T(8,128)(2,1)S(1)}, bf16[640,1280]{1,0:T(8,128)(2,1)S(1)}, u32[]{:S(2)}, u32[]{:S(2)}) collective-permute-start(bf16[640,1280]{1,0:T(8,128)(2,1)S(1)} %get-tuple-element.65), channel_id=1, source_target_pairs={{0,1},{1,0},{2,3},{3,2},{4,5},{5,4},{6,7},{7,6},{8,9},{9,8},{10,11... | collective-permute-start | bytes 4915208 | tf_op jit(solution)/shard_map/ppermute | solution.py:38
  55.8 46.5 %collective-permute-start.24 = (bf16[640,1280]{1,0:T(8,128)(2,1)S(1)}, bf16[640,1280]{1,0:T(8,128)(2,1)S(1)}, u32[]{:S(2)}, u32[]{:S(2)}) collective-permute-start(bf16[640,1280]{1,0:T(8,128)(2,1)S(1)} %get-tuple-element.66), channel_id=1, source_target_pairs={{0,2},{1,3},{2,0},{3,1},{4,6},{5,7},{6,4},{7,5},{8,10},{9,11},{10,... | collective-permute-start | bytes 4915208 | tf_op jit(solution)/shard_map/ppermute | solution.py:38
  58.4 43.9 %collective-permute-start.25 = (bf16[640,1280]{1,0:T(8,128)(2,1)S(1)}, bf16[640,1280]{1,0:T(8,128)(2,1)S(1)}, u32[]{:S(2)}, u32[]{:S(2)}) collective-permute-start(bf16[640,1280]{1,0:T(8,128)(2,1)S(1)} %get-tuple-element.67), channel_id=1, source_target_pairs={{0,195},{1,194},{2,65},{3,64},{4,199},{5,198},{6,69},{7,68},{8,203... | collective-permute-start | bytes 4915208 | tf_op jit(solution)/shard_map/ppermute | solution.py:49
  58.4 10.5 %collective-permute-start.10 = (bf16[512,512]{1,0:T(8,128)(2,1)S(1)}, bf16[512,512]{1,0:T(8,128)(2,1)S(1)}, u32[]{:S(2)}, u32[]{:S(2)}) collective-permute-start(bf16[512,512]{1,0:T(8,128)(2,1)S(1)} %collective-permute-done.9.refs_5_), channel_id=1, source_target_pairs={{0,16},{1,5},{2,18},{3,7},{4,20},{5,9},{6,22},{7,11},{8,24},{9,13}... | collective-permute-start | bytes 1572872 | tf_op jit(solution)/shard_map/ppermute | solution.py:38
  58.7 10.2 %collective-permute-start.12 = (bf16[512,512]{1,0:T(8,128)(2,1)S(1)}, bf16[512,512]{1,0:T(8,128)(2,1)S(1)}, u32[]{:S(2)}, u32[]{:S(2)}) collective-permute-start(bf16[512,512]{1,0:T(8,128)(2,1)S(1)} %collective-permute-done.11.refs_6_), channel_id=1, source_target_pairs={{0,48},{1,13},{2,50},{3,15},{4,52},{5,1},{6,54},{7,3},{8,56},{9,5}... | collective-permute-start | bytes 1572872 | tf_op jit(solution)/shard_map/ppermute | solution.py:38
  70.7 4.5 %collective-permute-start.15 = (bf16[512,128]{1,0:T(8,128)(2,1)S(1)}, bf16[512,128]{1,0:T(8,128)(2,1)S(1)}, u32[]{:S(2)}, u32[]{:S(2)}) collective-permute-start(bf16[512,128]{1,0:T(8,128)(2,1)S(1)} %get-tuple-element.56), channel_id=1, source_target_pairs={{0,12},{1,49},{2,14},{3,51},{4,0},{5,53},{6,2},{7,55},{8,4},{9,57}... | collective-permute-start | bytes 393224 | tf_op jit(solution)/shard_map/ppermute | solution.py:38
  73.2 5.6 %collective-permute-start.16 = (bf16[512,128]{1,0:T(8,128)(2,1)S(1)}, bf16[512,128]{1,0:T(8,128)(2,1)S(1)}, u32[]{:S(2)}, u32[]{:S(2)}) collective-permute-start(bf16[512,128]{1,0:T(8,128)(2,1)S(1)} %get-tuple-element.57), channel_id=1, source_target_pairs={{0,8},{1,33},{2,10},{3,35},{4,12},{5,37},{6,14},{7,39},{8,0},{9,41... | collective-permute-start | bytes 393224 | tf_op jit(solution)/shard_map/ppermute | solution.py:38
  75.2 7.4 %collective-permute-start.17 = (bf16[512,128]{1,0:T(8,128)(2,1)S(1)}, bf16[512,128]{1,0:T(8,128)(2,1)S(1)}, u32[]{:S(2)}, u32[]{:S(2)}) collective-permute-start(bf16[512,128]{1,0:T(8,128)(2,1)S(1)} %get-tuple-element.58), channel_id=1, source_target_pairs={{0,4},{1,17},{2,6},{3,19},{4,8},{5,21},{6,10},{7,23},{8,12},{9,25}... | collective-permute-start | bytes 393224 | tf_op jit(solution)/shard_map/ppermute | solution.py:38
  78.8 21.4 %collective-permute-start.21 = (bf16[512,256]{1,0:T(8,128)(2,1)S(1)}, bf16[512,256]{1,0:T(8,128)(2,1)S(1)}, u32[]{:S(2)}, u32[]{:S(2)}) collective-permute-start(bf16[512,256]{1,0:T(8,128)(2,1)S(1)} %shard_map.95.refs_0_), channel_id=1, source_target_pairs={{0,2},{1,3},{2,0},{3,1},{4,6},{5,7},{6,4},{7,5},{8,10},{9,11},{10,... | collective-permute-start | bytes 786440 | tf_op jit(solution)/shard_map/ppermute | solution.py:38
  82.6 18.2 %collective-permute-start.19 = (bf16[512,256]{1,0:T(8,128)(2,1)S(1)}, bf16[512,256]{1,0:T(8,128)(2,1)S(1)}, u32[]{:S(2)}, u32[]{:S(2)}) collective-permute-start(bf16[512,256]{1,0:T(8,128)(2,1)S(1)} %shard_map.95.refs_0_), channel_id=1, source_target_pairs={{0,1},{1,0},{2,3},{3,2},{4,5},{5,4},{6,7},{7,6},{8,9},{9,8},{10,11... | collective-permute-start | bytes 786440 | tf_op jit(solution)/shard_map/ppermute | solution.py:38
  100.2 2.3 %collective-permute-start.20 = (bf16[512,384]{1,0:T(8,128)(2,1)S(1)}, bf16[512,384]{1,0:T(8,128)(2,1)S(1)}, u32[]{:S(2)}, u32[]{:S(2)}) collective-permute-start(bf16[512,384]{1,0:T(8,128)(2,1)S(1)} %constant_dynamic-update-slice_fusion.refs_1_), channel_id=1, source_target_pairs={{0,1},{1,0},{2,3},{3,2},{4,5},{5,4},{6,7},{7,6},{8,9},{9,8},{10,11... | collective-permute-start | bytes 1179656 | tf_op jit(solution)/shard_map/ppermute | solution.py:38
  100.8 1.7 %collective-permute-start.22 = (bf16[512,256]{1,0:T(8,128)(2,1)S(1)}, bf16[512,256]{1,0:T(8,128)(2,1)S(1)}, u32[]{:S(2)}, u32[]{:S(2)}) collective-permute-start(bf16[512,256]{1,0:T(8,128)(2,1)S(1)} %collective-permute-done.21.refs_4_), channel_id=1, source_target_pairs={{0,1},{1,0},{2,3},{3,2},{4,5},{5,4},{6,7},{7,6},{8,9},{9,8},{10,11... | collective-permute-start | bytes 786440 | tf_op jit(solution)/shard_map/ppermute | solution.py:38
  100.8 10.3 %collective-permute-start.18 = (bf16[512,384]{1,0:T(8,128)(2,1)S(1)}, bf16[512,384]{1,0:T(8,128)(2,1)S(1)}, u32[]{:S(2)}, u32[]{:S(2)}) collective-permute-start(bf16[512,384]{1,0:T(8,128)(2,1)S(1)} %constant_dynamic-update-slice_fusion.refs_1_), channel_id=1, source_target_pairs={{0,2},{1,3},{2,0},{3,1},{4,6},{5,7},{6,4},{7,5},{8,10},{9,11},{10,... | collective-permute-start | bytes 1179656 | tf_op jit(solution)/shard_map/ppermute | solution.py:38
  111.1 2.6 %collective-permute-start.26 = (bf16[512,384]{1,0:T(8,128)(2,1)S(1)}, bf16[512,384]{1,0:T(8,128)(2,1)S(1)}, u32[]{:S(2)}, u32[]{:S(2)}) collective-permute-start(bf16[512,384]{1,0:T(8,128)(2,1)S(1)} %collective-permute-done.18.a_ref), channel_id=1, source_target_pairs={{0,1},{1,0},{2,3},{3,2},{4,5},{5,4},{6,7},{7,6},{8,9},{9,8},{10,11... | collective-permute-start | bytes 1179656 | tf_op jit(solution)/shard_map/ppermute | solution.py:38

commit v2 on v1

--- a/solution.py
+++ b/solution.py
@@ -175,7 +175,9 @@
         elif joined:
             refs[0][:, place * HD : (place + 1) * HD] = finish(state)
         else:
-            refs[place][...] = finish(state)
+            done = finish(state)
+            refs[place][...] = done
+            refs[-1][:, place * HD : (place + 1) * HD] = done
 
 
 def attend_step(blocks, shared, own, state, tiles=tuple(range(NY + 1)), joined=None):
@@ -186,6 +188,7 @@
         outs = [jax.ShapeDtypeStruct((2 * rows, len(tiles) * HD), BF16)]
     else:
         outs = [jax.ShapeDtypeStruct((2 * rows, HD), BF16)] * len(tiles)
+        outs.append(jax.ShapeDtypeStruct((2 * rows, len(tiles) * HD), BF16))
     carried = [] if state is None else [state]
     found = call(
         functools.partial(attend_kernel, tiles, state is None, joined),
@@ -217,50 +220,43 @@
         copy.wait()
 
 
+def project_sum(refs, weights, lanes=slice(None)):
+    own = refs[0].shape[1]
+    total = None
+    for place, ref in enumerate(refs):
+        start = own * (place % 2)
+        rows = slice(start, start + ref.shape[1])
+        part = jnp.dot(ref[...], weights[place // 2][rows, lanes], preferred_element_type=F32)
+        total = part if total is None else total + part
+    return total
+
+
 def project_first_kernel(*refs):
-    weights, out_ref = refs[6:10], refs[10]
-    own, far_rows = 2 * HD, 5 * HD
-    total = None
-    for ref, weight, low, high in (
-        (refs[0], weights[0], 0, own),
-        (refs[1], weights[0], own, far_rows),
-        (refs[2], weights[1], 0, own),
-        (refs[3], weights[1], own, far_rows),
-        (refs[4], weights[2], 0, own),
-        (refs[5], weights[3], 0, own),
-    ):
-        part = jnp.dot(ref[...], weight[low:high, :], preferred_element_type=F32)
-        total = part if total is None else total + part
-    out_ref[...] = total
-
-
-def project_last_kernel(a_ref, b_ref, w_ref, u_ref, sum_ref, out_ref, tan_ref):
+    refs[6][...] = project_sum(refs[:4], refs[4:6])
+
+
+def project_last_kernel(*refs):
+    sum_ref, out_ref, tan_ref = refs[6:]
     rows, tile = out_ref.shape
-    depth = a_ref.shape[1]
     lanes = pl.ds(pl.multiple_of(pl.program_id(0) * tile, tile), tile)
-    weights = pl.ds(w_ref.shape[0] - depth, depth)
-    for ref, half in ((out_ref, pl.ds(0, rows)), (tan_ref, pl.ds(rows, rows))):
-        total = (
-            sum_ref[half, lanes]
-            + jnp.dot(a_ref[half, :], w_ref[weights, lanes], preferred_element_type=F32)
-            + jnp.dot(b_ref[half, :], u_ref[weights, lanes], preferred_element_type=F32)
-        )
-        ref[...] = total.astype(BF16)
-
-
-def project_last(near, far, weight_near, weight_far, partial):
-    rows, columns = partial.shape
+    total = sum_ref[:, lanes] + project_sum(refs[:4], refs[4:6], lanes)
+    out_ref[...] = total[:rows].astype(BF16)
+    tan_ref[...] = total[rows:].astype(BF16)
+
+
+def project_last(*operands):
+    rows, columns = operands[-1].shape
     tile = 256
     half = pl.BlockSpec((rows // 2, tile), lambda j: (0, j))
     return pl.pallas_call(
         project_last_kernel,
         grid=(columns // tile,),
-        in_specs=[VMEM] * 5,
+        in_specs=[VMEM] * len(operands),
         out_specs=[half, half],
         out_shape=[jax.ShapeDtypeStruct((rows // 2, columns), BF16)] * 2,
         name="project_last",
         compiler_params=pltpu.CompilerParams(vmem_limit_bytes=16 << 20),
-    )(near, far, weight_near, weight_far, partial)
+    )(*operands)
 
 
 def shard_step(queries, keys, values, query_tan, key_tan, value_tan, out_weight):
@@ -338,31 +334,28 @@
     state = attend_step(blocks, own[0], own[1], None)
     state = attend_step(blocks, left[0], right[1], state)
     state = attend_step(blocks, right[0], left[1], state)
-    others = attend_step(blocks, opposite[0], opposite[1], state, (1, 2, 3), False)
+    others = attend_step(blocks, opposite[0], opposite[0], state, (1, 2, 3), False)
     opposite[1], _ = lax.optimization_barrier((opposite[1], others[0]))
     mine = [attend_step(blocks, opposite[0], opposite[1], state, (0, NY), True)]
     back = [shift(others[k - 1], swap=-k) for k in (1, 2, 3)]
     mine.append(jnp.concatenate(back, axis=1))
 
-    near = [shift(mine[n], zl=1) for n in range(2)]
     sibling = [shift(mine[n], core=1) for n in range(2)]
-    far = shift(near[0], core=1)
     partial = call(
         project_first_kernel,
         jax.ShapeDtypeStruct((2 * rows, columns), F32),
         *mine,
         *sibling,
-        near[0],
-        far,
         cuts[0],
         weight_core,
-        weight_near,
-        weight_far,
-        flops=10 * rows * width * columns,
-    )
-    last, partial = lax.optimization_barrier((near[1], partial))
-    far = shift(last, core=1)
-    return tuple(project_last(last, far, weight_near, weight_far, partial))
+        flops=8 * rows * width * columns,
+    )
+
+    crossed = shift(others[NY - 1], zl=1)
+    handed = [shift(crossed[:, (k - 1) * HD : k * HD], swap=-k) for k in (1, 2, 3)]
+    near = [shift(mine[0], zl=1), jnp.concatenate(handed, axis=1)]
+    far = [shift(near[n], core=1) for n in range(2)]
+    return tuple(project_last(*near, *far, weight_near, weight_far, partial))
 
 
 def solution(mesh):

time: 118 us -> 132 us (1.12)
  waiting for transfers between devices: 42.9 us -> 58.7 us
    ppermute x26 -> x29, waiting for transfers between devices: 42.9 us -> 58.7 us  [shift(): return lax.ppermute(array, AXES, pairs)]
    ppermute x26 -> x29, starting transfers between devices: 51.3 us -> 49.7 us  [shift(): return lax.ppermute(array, AXES, pairs)]
  transfers between devices with their start and end apart: 27 -> 30, of which waited for: 13 -> 14; matrix products, arithmetic and copies ran while one was open for 0% -> 0% of each run, Pallas kernels for 15% -> 13%
where the time goes in v2:
time: 132 us
  waiting for transfers between devices  58.7 us (44%)
  starting transfers between devices  50 us (38%)
  Pallas kernels  21.8 us (17%)
    ppermute x29, waiting for transfers between devices, shift(): return lax.ppermute(array, AXES, pairs)  58.7 us
    ppermute x29, starting transfers between devices, shift(): return lax.ppermute(array, AXES, pairs)  49.7 us
    pallas_call x11, Pallas kernels, called(): pl.pallas_call(kernel, out_shape=outs, in_specs=specs or [VMEM] * len(ope...  18 us
    pallas_call x1, Pallas kernels, project_last(): pl.pallas_call(project_last_kernel, grid=(columns // tile,), in_specs=[VM...  3.82 us
  transfers between devices with their start and end apart: 30, of which 14 were waited for; matrix products, arithmetic and copies ran while one was open for 0% of the time, Pallas kernels for 13%

profile of v2, /device:TPU:1, one launch (start us, length us, event | category | flops | bytes accessed | tf_op | source)
XLA Modules:
  0.0 131.6 jit_solution(12314464431921911474)
XLA Ops:
  0.6 0.9 shard_map.87.refs_0_
  1.5 3.9 %collective-permute-start = (bf16[5,32,512]{2,1,0:T(8,128)(2,1)S(1)}, bf16[5,32,512]{2,1,0:T(8,128)(2,1)S(1)}, u32[]{:S(2)}, u32[]{:S(2)}) collective-permute-start(bf16[5,32,512]{2,1,0:T(8,128)(2,1)S(1)} %shard_map.87.refs_0_), channel_id=1, source_target_pairs={{0,64},{1,65},{2,66},{3,67},{4,68},{5,69},{6,70},{7,71},{8,72},{9,... | collective-permute-start | bytes 491528 | tf_op jit(solution)/shard_map/ppermute | solution.py:38
  5.4 3.1 %collective-permute-start.1 = (bf16[5,32,512]{2,1,0:T(8,128)(2,1)S(1)}, bf16[5,32,512]{2,1,0:T(8,128)(2,1)S(1)}, u32[]{:S(2)}, u32[]{:S(2)}) collective-permute-start(bf16[5,32,512]{2,1,0:T(8,128)(2,1)S(1)} %shard_map.87.refs_0_), channel_id=1, source_target_pairs={{0,192},{1,193},{2,194},{3,195},{4,196},{5,197},{6,198},{7,199},{8... | collective-permute-start | bytes 491528 | tf_op jit(solution)/shard_map/ppermute | solution.py:38
  8.5 4.4 %collective-permute-start.2 = (bf16[5,32,512]{2,1,0:T(8,128)(2,1)S(1)}, bf16[5,32,512]{2,1,0:T(8,128)(2,1)S(1)}, u32[]{:S(2)}, u32[]{:S(2)}) collective-permute-start(bf16[5,32,512]{2,1,0:T(8,128)(2,1)S(1)} %shard_map.87.refs_0_), channel_id=1, source_target_pairs={{0,128},{1,129},{2,130},{3,131},{4,132},{5,133},{6,134},{7,135},{8... | collective-permute-start | bytes 491528 | tf_op jit(solution)/shard_map/ppermute | solution.py:38
  12.9 1.2 shard_map.86
  14.1 3.1 %shard_map.88 = (bf16[640,1280]{1,0:T(8,128)(2,1)S(1)}, bf16[640,1280]{1,0:T(8,128)(2,1)S(1)}, bf16[640,1280]{1,0:T(8,128)(2,1)S(1)}, bf16[640,1280]{1,0:T(8,128)(2,1)S(1)}) custom-call(s32[1]{0:T(128)S(6)} %select_n.27.y_ref, s32[1]{0:T(128)} %bitcast.place_ref, bf16[640,5120]{1,0:T(8,128)(2,1)} %w_ref.1), custom_call_target="tpu_custom_call" | custom-call | bytes 6553608 | tf_op jit(solution)/shard_map/pallas_call | solution.py:57
  17.2 3.8 %collective-permute-done.1.refs_2_ = bf16[5,32,512]{2,1,0:T(8,128)(2,1)S(1)} collective-permute-done((bf16[5,32,512]{2,1,0:T(8,128)(2,1)S(1)}, bf16[5,32,512]{2,1,0:T(8,128)(2,1)S(1)}, u32[]{:S(2)}, u32[]{:S(2)}) %collective-permute-start.1) | collective-permute-done | bytes 163872 | tf_op jit(solution)/shard_map/ppermute | solution.py:38
  21.0 0.9 collective-permute-done.2.refs_3_
  21.9 1.3 collective-permute-start.3
  23.2 1.5 %collective-permute-start.4 = (bf16[256,512]{1,0:T(8,128)(2,1)S(1)}, bf16[256,512]{1,0:T(8,128)(2,1)S(1)}, u32[]{:S(2)}, u32[]{:S(2)}) collective-permute-start(bf16[256,512]{1,0:T(8,128)(2,1)S(1)} %get-tuple-element.49), channel_id=1, source_target_pairs={{0,12},{1,49},{2,14},{3,51},{4,0},{5,53},{6,2},{7,55},{8,4},{9,57}... | collective-permute-start | bytes 786440 | tf_op jit(solution)/shard_map/ppermute | solution.py:38
  24.6 1.5 %collective-permute-start.5 = (bf16[256,512]{1,0:T(8,128)(2,1)S(1)}, bf16[256,512]{1,0:T(8,128)(2,1)S(1)}, u32[]{:S(2)}, u32[]{:S(2)}) collective-permute-start(bf16[256,512]{1,0:T(8,128)(2,1)S(1)} %get-tuple-element.50), channel_id=1, source_target_pairs={{0,8},{1,33},{2,10},{3,35},{4,12},{5,37},{6,14},{7,39},{8,0},{9,41... | collective-permute-start | bytes 786440 | tf_op jit(solution)/shard_map/ppermute | solution.py:38
  26.2 2.2 %collective-permute-done.3.refs_1_ = bf16[256,512]{1,0:T(8,128)(2,1)S(1)} collective-permute-done((bf16[256,512]{1,0:T(8,128)(2,1)S(1)}, bf16[256,512]{1,0:T(8,128)(2,1)S(1)}, u32[]{:S(2)}, u32[]{:S(2)}) %collective-permute-start.3) | collective-permute-done | bytes 262176 | tf_op jit(solution)/shard_map/ppermute | solution.py:38
  28.4 3.8 %collective-permute-done.5.refs_3_ = bf16[256,512]{1,0:T(8,128)(2,1)S(1)} collective-permute-done((bf16[256,512]{1,0:T(8,128)(2,1)S(1)}, bf16[256,512]{1,0:T(8,128)(2,1)S(1)}, u32[]{:S(2)}, u32[]{:S(2)}) %collective-permute-start.5) | collective-permute-done | bytes 262176 | tf_op jit(solution)/shard_map/ppermute | solution.py:38
  32.3 1.4 %collective-permute-start.6 = (bf16[512,512]{1,0:T(8,128)(2,1)S(1)}, bf16[512,512]{1,0:T(8,128)(2,1)S(1)}, u32[]{:S(2)}, u32[]{:S(2)}) collective-permute-start(bf16[512,512]{1,0:T(8,128)(2,1)S(1)} %get-tuple-element.51.refs_5_), channel_id=1, source_target_pairs={{0,16},{1,5},{2,18},{3,7},{4,20},{5,9},{6,22},{7,11},{8,24},{9,13}... | collective-permute-start | bytes 1572872 | tf_op jit(solution)/shard_map/ppermute | solution.py:38
  33.6 1.8 %collective-permute-start.8 = (bf16[512,512]{1,0:T(8,128)(2,1)S(1)}, bf16[512,512]{1,0:T(8,128)(2,1)S(1)}, u32[]{:S(2)}, u32[]{:S(2)}) collective-permute-start(bf16[512,512]{1,0:T(8,128)(2,1)S(1)} %get-tuple-element.52.refs_6_), channel_id=1, source_target_pairs={{0,48},{1,13},{2,50},{3,15},{4,52},{5,1},{6,54},{7,3},{8,56},{9,5}... | collective-permute-start | bytes 1572872 | tf_op jit(solution)/shard_map/ppermute | solution.py:38
  35.5 0.9 collective-permute-start.10
  36.3 1.4 %collective-permute-start.13 = (bf16[512,512]{1,0:T(8,128)(2,1)S(1)}, bf16[512,512]{1,0:T(8,128)(2,1)S(1)}, u32[]{:S(2)}, u32[]{:S(2)}) collective-permute-start(bf16[512,512]{1,0:T(8,128)(2,1)S(1)} %get-tuple-element.51.refs_5_), channel_id=1, source_target_pairs={{0,48},{1,13},{2,50},{3,15},{4,52},{5,1},{6,54},{7,3},{8,56},{9,5}... | collective-permute-start | bytes 1572872 | tf_op jit(solution)/shard_map/ppermute | solution.py:38
  37.8 2.7 %collective-permute-done.10.refs_1_.refs_0_ = bf16[256,256]{1,0:T(8,128)(2,1)S(1)} collective-permute-done((bf16[256,256]{1,0:T(8,128)(2,1)S(1)}, bf16[256,256]{1,0:T(8,128)(2,1)S(1)}, u32[]{:S(2)}, u32[]{:S(2)}) %collective-permute-start.10) | collective-permute-done | bytes 131104 | tf_op jit(solution)/shard_map/ppermute | solution.py:38
  40.5 1.7 %collective-permute-done.6.refs_5_ = bf16[512,512]{1,0:T(8,128)(2,1)S(1)} collective-permute-done((bf16[512,512]{1,0:T(8,128)(2,1)S(1)}, bf16[512,512]{1,0:T(8,128)(2,1)S(1)}, u32[]{:S(2)}, u32[]{:S(2)}) %collective-permute-start.6) | collective-permute-done | bytes 524320 | tf_op jit(solution)/shard_map/ppermute | solution.py:38
  42.3 5.0 %collective-permute-done.11.refs_2_.refs_1_ = bf16[256,256]{1,0:T(8,128)(2,1)S(1)} collective-permute-done((bf16[256,256]{1,0:T(8,128)(2,1)S(1)}, bf16[256,256]{1,0:T(8,128)(2,1)S(1)}, u32[]{:S(2)}, u32[]{:S(2)}) %collective-permute-start.11) | collective-permute-done | bytes 131104 | tf_op jit(solution)/shard_map/ppermute | solution.py:38
  47.2 0.5 collective-permute-start.12
  47.7 5.0 %collective-permute-done.12.refs_3_.refs_2_ = bf16[256,256]{1,0:T(8,128)(2,1)S(1)} collective-permute-done((bf16[256,256]{1,0:T(8,128)(2,1)S(1)}, bf16[256,256]{1,0:T(8,128)(2,1)S(1)}, u32[]{:S(2)}, u32[]{:S(2)}) %collective-permute-start.12) | collective-permute-done | bytes 131104 | tf_op jit(solution)/shard_map/ppermute | solution.py:38
  52.7 7.9 %collective-permute-start.29 = (bf16[640,1280]{1,0:T(8,128)(2,1)S(1)}, bf16[640,1280]{1,0:T(8,128)(2,1)S(1)}, u32[]{:S(2)}, u32[]{:S(2)}) collective-permute-start(bf16[640,1280]{1,0:T(8,128)(2,1)S(1)} %get-tuple-element.67), channel_id=1, source_target_pairs={{0,1},{1,0},{2,3},{3,2},{4,5},{5,4},{6,7},{7,6},{8,9},{9,8},{10,11... | collective-permute-start | bytes 4915208 | tf_op jit(solution)/shard_map/ppermute | solution.py:38
  60.6 0.9 collective-permute-start.9
  61.5 2.1 %shard_map.91.refs_7_ = f32[5,256,768]{2,1,0:T(8,128)S(1)} custom-call(bf16[256,256]{1,0:T(8,128)(2,1)S(1)} %get-tuple-element.35.refs_0_, bf16[256,256]{1,0:T(8,128)(2,1)S(1)} %collective-permute-done.10.refs_1_.refs_0_, bf16[256,256]{1,0:T(8,128)(2,1)S(1)} %collective-permute-done.11.refs_2_.refs_1_, ...), custom_call_target="tpu_custom_call" | custom-call | flops 1174405120 | bytes 1703936 | tf_op jit(solution)/shard_map/pallas_call | solution.py:57
  63.7 2.7 %shard_map.92.refs_7_ = f32[5,256,768]{2,1,0:T(8,128)S(1)} custom-call(bf16[256,256]{1,0:T(8,128)(2,1)S(1)} %get-tuple-element.35.refs_0_, bf16[256,256]{1,0:T(8,128)(2,1)S(1)} %collective-permute-done.10.refs_1_.refs_0_, bf16[256,256]{1,0:T(8,128)(2,1)S(1)} %collective-permute-done.11.refs_2_.refs_1_, ...), custom_call_target="tpu_custom_call" | custom-call | flops 1174405120 | bytes 5636096 | tf_op jit(solution)/shard_map/pallas_call | solution.py:57
  66.4 2.7 %shard_map.93.refs_5_.refs_4_ = f32[5,256,768]{2,1,0:T(8,128)S(1)} custom-call(bf16[256,256]{1,0:T(8,128)(2,1)S(1)} %get-tuple-element.35.refs_0_, bf16[256,256]{1,0:T(8,128)(2,1)S(1)} %collective-permute-done.10.refs_1_.refs_0_, bf16[256,256]{1,0:T(8,128)(2,1)S(1)} %collective-permute-done.11.refs_2_.refs_1_, ...), custom_call_target="tpu_custom_call" | custom-call | flops 1174405120 | bytes 5636096 | tf_op jit(solution)/shard_map/pallas_call | solution.py:57
  69.1 1.8 %shard_map.94 = (bf16[512,128]{1,0:T(8,128)(2,1)S(1)}, bf16[512,128]{1,0:T(8,128)(2,1)S(1)}, bf16[512,128]{1,0:T(8,128)(2,1)S(1)}, bf16[512,384]{1,0:T(8,128)(2,1)S(1)}) custom-call(bf16[256,256]{1,0:T(8,128)(2,1)S(1)} %collective-permute-done.10.refs_1_.refs_0_, bf16[256,256]{1,0:T(8,128)(2,1)S(1)} %collective-permute-done.11.refs_2_.refs_1_, ...), custom_call_target="tpu_custom_call" | custom-call | flops 704643072 | bytes 5373952 | tf_op jit(solution)/shard_map/pallas_call | solution.py:57
  70.9 3.9 %collective-permute-start.16 = (bf16[512,384]{1,0:T(8,128)(2,1)S(1)}, bf16[512,384]{1,0:T(8,128)(2,1)S(1)}, u32[]{:S(2)}, u32[]{:S(2)}) collective-permute-start(bf16[512,384]{1,0:T(8,128)(2,1)S(1)} %get-tuple-element.57), channel_id=1, source_target_pairs={{0,2},{1,3},{2,0},{3,1},{4,6},{5,7},{6,4},{7,5},{8,10},{9,11},{10,... | collective-permute-start | bytes 1179656 | tf_op jit(solution)/shard_map/ppermute | solution.py:38
  74.8 0.1 collective-permute-start.22
  74.9 0.3 collective-permute-start.23
  75.1 1.0 collective-permute-start.24
  76.1 3.1 %collective-permute-done.24 = bf16[512,128]{1,0:T(8,128)(2,1)S(1)} collective-permute-done((bf16[512,128]{1,0:T(8,128)(2,1)S(1)}, bf16[512,128]{1,0:T(8,128)(2,1)S(1)}, u32[]{:S(2)}, u32[]{:S(2)}) %collective-permute-start.24) | collective-permute-done | bytes 131104 | tf_op jit(solution)/shard_map/ppermute | solution.py:38
  79.3 1.2 collective-permute-start.25
  80.5 1.2 shard_map.95.refs_0_
  81.7 2.9 %collective-permute-done.25 = bf16[512,128]{1,0:T(8,128)(2,1)S(1)} collective-permute-done((bf16[512,128]{1,0:T(8,128)(2,1)S(1)}, bf16[512,128]{1,0:T(8,128)(2,1)S(1)}, u32[]{:S(2)}, u32[]{:S(2)}) %collective-permute-start.25) | collective-permute-done | bytes 131104 | tf_op jit(solution)/shard_map/ppermute | solution.py:38
  84.6 0.5 collective-permute-start.26
  85.1 2.1 %collective-permute-start.27 = (bf16[512,256]{1,0:T(8,128)(2,1)S(1)}, bf16[512,256]{1,0:T(8,128)(2,1)S(1)}, u32[]{:S(2)}, u32[]{:S(2)}) collective-permute-start(bf16[512,256]{1,0:T(8,128)(2,1)S(1)} %shard_map.95.refs_0_), channel_id=1, source_target_pairs={{0,1},{1,0},{2,3},{3,2},{4,5},{5,4},{6,7},{7,6},{8,9},{9,8},{10,11... | collective-permute-start | bytes 786440 | tf_op jit(solution)/shard_map/ppermute | solution.py:38
  87.3 2.6 %collective-permute-done.26 = bf16[512,128]{1,0:T(8,128)(2,1)S(1)} collective-permute-done((bf16[512,128]{1,0:T(8,128)(2,1)S(1)}, bf16[512,128]{1,0:T(8,128)(2,1)S(1)}, u32[]{:S(2)}, u32[]{:S(2)}) %collective-permute-start.26) | collective-permute-done | bytes 131104 | tf_op jit(solution)/shard_map/ppermute | solution.py:38
  89.9 1.3 collective-permute-start.17
  91.4 2.7 %collective-permute-done.17 = bf16[512,128]{1,0:T(8,128)(2,1)S(1)} collective-permute-done((bf16[512,128]{1,0:T(8,128)(2,1)S(1)}, bf16[512,128]{1,0:T(8,128)(2,1)S(1)}, u32[]{:S(2)}, u32[]{:S(2)}) %collective-permute-start.17) | collective-permute-done | bytes 131104 | tf_op jit(solution)/shard_map/ppermute | solution.py:38
  94.1 2.6 %collective-permute-done.18 = bf16[512,128]{1,0:T(8,128)(2,1)S(1)} collective-permute-done((bf16[512,128]{1,0:T(8,128)(2,1)S(1)}, bf16[512,128]{1,0:T(8,128)(2,1)S(1)}, u32[]{:S(2)}, u32[]{:S(2)}) %collective-permute-start.18) | collective-permute-done | bytes 131104 | tf_op jit(solution)/shard_map/ppermute | solution.py:38
  96.6 3.6 %collective-permute-start.15 = (bf16[512,256]{1,0:T(8,128)(2,1)S(1)}, bf16[512,256]{1,0:T(8,128)(2,1)S(1)}, u32[]{:S(2)}, u32[]{:S(2)}) collective-permute-start(bf16[512,256]{1,0:T(8,128)(2,1)S(1)} %shard_map.95.refs_0_), channel_id=1, source_target_pairs={{0,2},{1,3},{2,0},{3,1},{4,6},{5,7},{6,4},{7,5},{8,10},{9,11},{10,... | collective-permute-start | bytes 786440 | tf_op jit(solution)/shard_map/ppermute | solution.py:38
  100.2 4.3 %collective-permute-start.28 = (bf16[512,384]{1,0:T(8,128)(2,1)S(1)}, bf16[512,384]{1,0:T(8,128)(2,1)S(1)}, u32[]{:S(2)}, u32[]{:S(2)}) collective-permute-start(bf16[512,384]{1,0:T(8,128)(2,1)S(1)} %constant_dynamic-update-slice_fusion.3.refs_1_), channel_id=1, source_target_pairs={{0,1},{1,0},{2,3},{3,2},{4,5},{5,4},{6,7},{7,6},{8,9},{9,8},{10,11... | collective-permute-start | bytes 1179656 | tf_op jit(solution)/shard_map/ppermute | solution.py:38
  104.6 19.8 %collective-permute-done.15.refs_0_ = bf16[512,256]{1,0:T(8,128)(2,1)S(1)} collective-permute-done((bf16[512,256]{1,0:T(8,128)(2,1)S(1)}, bf16[512,256]{1,0:T(8,128)(2,1)S(1)}, u32[]{:S(2)}, u32[]{:S(2)}) %collective-permute-start.15) | collective-permute-done | bytes 262176 | tf_op jit(solution)/shard_map/ppermute | solution.py:38
  124.4 1.2 collective-permute-start.21
  125.6 2.2 %shard_map.96.refs_6_ = f32[512,1280]{1,0:T(8,128)S(1)} custom-call(bf16[512,256]{1,0:T(8,128)(2,1)S(1)} %shard_map.95.refs_0_, bf16[512,384]{1,0:T(8,128)(2,1)S(1)} %constant_dynamic-update-slice_fusion.3.refs_1_, bf16[512,256]{1,0:T(8,128)(2,1)S(1)} %collective-permute-done.27.refs_2_, bf16[512,384]{1,0:T(8,128)(2,1)S(1)} %collective-permute-done.28.refs_3_, ...), custom_call_target="tpu_custom_call" | custom-call | flops 1677721600 | bytes 4587520 | tf_op jit(solution)/shard_map/pallas_call | solution.py:57
  127.8 3.8 %project_last.1 = (bf16[256,1280]{1,0:T(8,128)(2,1)}, bf16[256,1280]{1,0:T(8,128)(2,1)}) custom-call(bf16[512,256]{1,0:T(8,128)(2,1)S(1)} %collective-permute-done.15.refs_0_, bf16[512,384]{1,0:T(8,128)(2,1)S(1)} %constant_dynamic-update-slice_fusion.refs_1_, bf16[512,256]{1,0:T(8,128)(2,1)S(1)} %collective-permute-done.20.refs_2_, ...), custom_call_target="tpu_custom_call" | custom-call | tf_op jit(solution)/shard_map/project_last/pallas_call | solution.py:251
  (31 shorter events, 0.6 us)
Async XLA Ops:
  1.5 15.7 %collective-permute-start = (bf16[5,32,512]{2,1,0:T(8,128)(2,1)S(1)}, bf16[5,32,512]{2,1,0:T(8,128)(2,1)S(1)}, u32[]{:S(2)}, u32[]{:S(2)}) collective-permute-start(bf16[5,32,512]{2,1,0:T(8,128)(2,1)S(1)} %shard_map.87.refs_0_), channel_id=1, source_target_pairs={{0,64},{1,65},{2,66},{3,67},{4,68},{5,69},{6,70},{7,71},{8,72},{9,... | collective-permute-start | bytes 491528 | tf_op jit(solution)/shard_map/ppermute | solution.py:38
  5.4 15.5 %collective-permute-start.1 = (bf16[5,32,512]{2,1,0:T(8,128)(2,1)S(1)}, bf16[5,32,512]{2,1,0:T(8,128)(2,1)S(1)}, u32[]{:S(2)}, u32[]{:S(2)}) collective-permute-start(bf16[5,32,512]{2,1,0:T(8,128)(2,1)S(1)} %shard_map.87.refs_0_), channel_id=1, source_target_pairs={{0,192},{1,193},{2,194},{3,195},{4,196},{5,197},{6,198},{7,199},{8... | collective-permute-start | bytes 491528 | tf_op jit(solution)/shard_map/ppermute | solution.py:38
  8.5 13.3 %collective-permute-start.2 = (bf16[5,32,512]{2,1,0:T(8,128)(2,1)S(1)}, bf16[5,32,512]{2,1,0:T(8,128)(2,1)S(1)}, u32[]{:S(2)}, u32[]{:S(2)}) collective-permute-start(bf16[5,32,512]{2,1,0:T(8,128)(2,1)S(1)} %shard_map.87.refs_0_), channel_id=1, source_target_pairs={{0,128},{1,129},{2,130},{3,131},{4,132},{5,133},{6,134},{7,135},{8... | collective-permute-start | bytes 491528 | tf_op jit(solution)/shard_map/ppermute | solution.py:38
  21.9 6.5 %collective-permute-start.3 = (bf16[256,512]{1,0:T(8,128)(2,1)S(1)}, bf16[256,512]{1,0:T(8,128)(2,1)S(1)}, u32[]{:S(2)}, u32[]{:S(2)}) collective-permute-start(bf16[256,512]{1,0:T(8,128)(2,1)S(1)} %get-tuple-element.48), channel_id=1, source_target_pairs={{0,4},{1,17},{2,6},{3,19},{4,8},{5,21},{6,10},{7,23},{8,12},{9,25}... | collective-permute-start | bytes 786440 | tf_op jit(solution)/shard_map/ppermute | solution.py:38
  23.2 5.2 %collective-permute-start.4 = (bf16[256,512]{1,0:T(8,128)(2,1)S(1)}, bf16[256,512]{1,0:T(8,128)(2,1)S(1)}, u32[]{:S(2)}, u32[]{:S(2)}) collective-permute-start(bf16[256,512]{1,0:T(8,128)(2,1)S(1)} %get-tuple-element.49), channel_id=1, source_target_pairs={{0,12},{1,49},{2,14},{3,51},{4,0},{5,53},{6,2},{7,55},{8,4},{9,57}... | collective-permute-start | bytes 786440 | tf_op jit(solution)/shard_map/ppermute | solution.py:38
  24.6 7.5 %collective-permute-start.5 = (bf16[256,512]{1,0:T(8,128)(2,1)S(1)}, bf16[256,512]{1,0:T(8,128)(2,1)S(1)}, u32[]{:S(2)}, u32[]{:S(2)}) collective-permute-start(bf16[256,512]{1,0:T(8,128)(2,1)S(1)} %get-tuple-element.50), channel_id=1, source_target_pairs={{0,8},{1,33},{2,10},{3,35},{4,12},{5,37},{6,14},{7,39},{8,0},{9,41... | collective-permute-start | bytes 786440 | tf_op jit(solution)/shard_map/ppermute | solution.py:38
  32.3 10.0 %collective-permute-start.6 = (bf16[512,512]{1,0:T(8,128)(2,1)S(1)}, bf16[512,512]{1,0:T(8,128)(2,1)S(1)}, u32[]{:S(2)}, u32[]{:S(2)}) collective-permute-start(bf16[512,512]{1,0:T(8,128)(2,1)S(1)} %get-tuple-element.51.refs_5_), channel_id=1, source_target_pairs={{0,16},{1,5},{2,18},{3,7},{4,20},{5,9},{6,22},{7,11},{8,24},{9,13}... | collective-permute-start | bytes 1572872 | tf_op jit(solution)/shard_map/ppermute | solution.py:38
  33.6 27.0 %collective-permute-start.8 = (bf16[512,512]{1,0:T(8,128)(2,1)S(1)}, bf16[512,512]{1,0:T(8,128)(2,1)S(1)}, u32[]{:S(2)}, u32[]{:S(2)}) collective-permute-start(bf16[512,512]{1,0:T(8,128)(2,1)S(1)} %get-tuple-element.52.refs_6_), channel_id=1, source_target_pairs={{0,48},{1,13},{2,50},{3,15},{4,52},{5,1},{6,54},{7,3},{8,56},{9,5}... | collective-permute-start | bytes 1572872 | tf_op jit(solution)/shard_map/ppermute | solution.py:38
  35.5 5.0 %collective-permute-start.10 = (bf16[256,256]{1,0:T(8,128)(2,1)S(1)}, bf16[256,256]{1,0:T(8,128)(2,1)S(1)}, u32[]{:S(2)}, u32[]{:S(2)}) collective-permute-start(bf16[256,256]{1,0:T(8,128)(2,1)S(1)} %get-tuple-element.37), channel_id=1, source_target_pairs={{0,4},{1,17},{2,6},{3,19},{4,8},{5,21},{6,10},{7,23},{8,12},{9,25}... | collective-permute-start | bytes 393224 | tf_op jit(solution)/shard_map/ppermute | solution.py:38
  36.3 30.0 %collective-permute-start.13 = (bf16[512,512]{1,0:T(8,128)(2,1)S(1)}, bf16[512,512]{1,0:T(8,128)(2,1)S(1)}, u32[]{:S(2)}, u32[]{:S(2)}) collective-permute-start(bf16[512,512]{1,0:T(8,128)(2,1)S(1)} %get-tuple-element.51.refs_5_), channel_id=1, source_target_pairs={{0,48},{1,13},{2,50},{3,15},{4,52},{5,1},{6,54},{7,3},{8,56},{9,5}... | collective-permute-start | bytes 1572872 | tf_op jit(solution)/shard_map/ppermute | solution.py:38
  37.7 28.7 %collective-permute-start.14 = (bf16[512,512]{1,0:T(8,128)(2,1)S(1)}, bf16[512,512]{1,0:T(8,128)(2,1)S(1)}, u32[]{:S(2)}, u32[]{:S(2)}) collective-permute-start(bf16[512,512]{1,0:T(8,128)(2,1)S(1)} %get-tuple-element.52.refs_6_), channel_id=1, source_target_pairs={{0,16},{1,5},{2,18},{3,7},{4,20},{5,9},{6,22},{7,11},{8,24},{9,13}... | collective-permute-start | bytes 1572872 | tf_op jit(solution)/shard_map/ppermute | solution.py:38
  40.5 6.7 %collective-permute-start.11 = (bf16[256,256]{1,0:T(8,128)(2,1)S(1)}, bf16[256,256]{1,0:T(8,128)(2,1)S(1)}, u32[]{:S(2)}, u32[]{:S(2)}) collective-permute-start(bf16[256,256]{1,0:T(8,128)(2,1)S(1)} %get-tuple-element.53), channel_id=1, source_target_pairs={{0,8},{1,33},{2,10},{3,35},{4,12},{5,37},{6,14},{7,39},{8,0},{9,41... | collective-permute-start | bytes 393224 | tf_op jit(solution)/shard_map/ppermute | solution.py:38
  42.2 26.9 %collective-permute-start.7 = (bf16[512,512]{1,0:T(8,128)(2,1)S(1)}, bf16[512,512]{1,0:T(8,128)(2,1)S(1)}, u32[]{:S(2)}, u32[]{:S(2)}) collective-permute-start(bf16[512,512]{1,0:T(8,128)(2,1)S(1)} %collective-permute-done.6.refs_5_), channel_id=1, source_target_pairs={{0,16},{1,5},{2,18},{3,7},{4,20},{5,9},{6,22},{7,11},{8,24},{9,13}... | collective-permute-start | bytes 1572872 | tf_op jit(solution)/shard_map/ppermute | solution.py:38
  47.2 5.5 %collective-permute-start.12 = (bf16[256,256]{1,0:T(8,128)(2,1)S(1)}, bf16[256,256]{1,0:T(8,128)(2,1)S(1)}, u32[]{:S(2)}, u32[]{:S(2)}) collective-permute-start(bf16[256,256]{1,0:T(8,128)(2,1)S(1)} %get-tuple-element.54), channel_id=1, source_target_pairs={{0,12},{1,49},{2,14},{3,51},{4,0},{5,53},{6,2},{7,55},{8,4},{9,57}... | collective-permute-start | bytes 393224 | tf_op jit(solution)/shard_map/ppermute | solution.py:38
  52.7 72.8 %collective-permute-start.29 = (bf16[640,1280]{1,0:T(8,128)(2,1)S(1)}, bf16[640,1280]{1,0:T(8,128)(2,1)S(1)}, u32[]{:S(2)}, u32[]{:S(2)}) collective-permute-start(bf16[640,1280]{1,0:T(8,128)(2,1)S(1)} %get-tuple-element.67), channel_id=1, source_target_pairs={{0,1},{1,0},{2,3},{3,2},{4,5},{5,4},{6,7},{7,6},{8,9},{9,8},{10,11... | collective-permute-start | bytes 4915208 | tf_op jit(solution)/shard_map/ppermute | solution.py:38
  60.6 14.5 %collective-permute-start.9 = (bf16[512,512]{1,0:T(8,128)(2,1)S(1)}, bf16[512,512]{1,0:T(8,128)(2,1)S(1)}, u32[]{:S(2)}, u32[]{:S(2)}) collective-permute-start(bf16[512,512]{1,0:T(8,128)(2,1)S(1)} %collective-permute-done.8.refs_6_), channel_id=1, source_target_pairs={{0,48},{1,13},{2,50},{3,15},{4,52},{5,1},{6,54},{7,3},{8,56},{9,5}... | collective-permute-start | bytes 1572872 | tf_op jit(solution)/shard_map/ppermute | solution.py:38
  70.9 14.2 %collective-permute-start.16 = (bf16[512,384]{1,0:T(8,128)(2,1)S(1)}, bf16[512,384]{1,0:T(8,128)(2,1)S(1)}, u32[]{:S(2)}, u32[]{:S(2)}) collective-permute-start(bf16[512,384]{1,0:T(8,128)(2,1)S(1)} %get-tuple-element.57), channel_id=1, source_target_pairs={{0,2},{1,3},{2,0},{3,1},{4,6},{5,7},{6,4},{7,5},{8,10},{9,11},{10,... | collective-permute-start | bytes 1179656 | tf_op jit(solution)/shard_map/ppermute | solution.py:38
  74.8 53.0 %collective-permute-start.22 = (bf16[640,1280]{1,0:T(8,128)(2,1)S(1)}, bf16[640,1280]{1,0:T(8,128)(2,1)S(1)}, u32[]{:S(2)}, u32[]{:S(2)}) collective-permute-start(bf16[640,1280]{1,0:T(8,128)(2,1)S(1)} %get-tuple-element.62), channel_id=1, source_target_pairs={{0,2},{1,3},{2,0},{3,1},{4,6},{5,7},{6,4},{7,5},{8,10},{9,11},{10,... | collective-permute-start | bytes 4915208 | tf_op jit(solution)/shard_map/ppermute | solution.py:38
  74.9 52.9 %collective-permute-start.23 = (bf16[640,1280]{1,0:T(8,128)(2,1)S(1)}, bf16[640,1280]{1,0:T(8,128)(2,1)S(1)}, u32[]{:S(2)}, u32[]{:S(2)}) collective-permute-start(bf16[640,1280]{1,0:T(8,128)(2,1)S(1)} %get-tuple-element.63), channel_id=1, source_target_pairs={{0,195},{1,194},{2,65},{3,64},{4,199},{5,198},{6,69},{7,68},{8,203... | collective-permute-start | bytes 4915208 | tf_op jit(solution)/shard_map/ppermute | solution.py:49
  75.1 4.1 %collective-permute-start.24 = (bf16[512,128]{1,0:T(8,128)(2,1)S(1)}, bf16[512,128]{1,0:T(8,128)(2,1)S(1)}, u32[]{:S(2)}, u32[]{:S(2)}) collective-permute-start(bf16[512,128]{1,0:T(8,128)(2,1)S(1)} %get-tuple-element.55), channel_id=1, source_target_pairs={{0,12},{1,49},{2,14},{3,51},{4,0},{5,53},{6,2},{7,55},{8,4},{9,57}... | collective-permute-start | bytes 393224 | tf_op jit(solution)/shard_map/ppermute | solution.py:38
  79.3 5.3 %collective-permute-start.25 = (bf16[512,128]{1,0:T(8,128)(2,1)S(1)}, bf16[512,128]{1,0:T(8,128)(2,1)S(1)}, u32[]{:S(2)}, u32[]{:S(2)}) collective-permute-start(bf16[512,128]{1,0:T(8,128)(2,1)S(1)} %get-tuple-element.64), channel_id=1, source_target_pairs={{0,8},{1,33},{2,10},{3,35},{4,12},{5,37},{6,14},{7,39},{8,0},{9,41... | collective-permute-start | bytes 393224 | tf_op jit(solution)/shard_map/ppermute | solution.py:38
  84.6 5.3 %collective-permute-start.26 = (bf16[512,128]{1,0:T(8,128)(2,1)S(1)}, bf16[512,128]{1,0:T(8,128)(2,1)S(1)}, u32[]{:S(2)}, u32[]{:S(2)}) collective-permute-start(bf16[512,128]{1,0:T(8,128)(2,1)S(1)} %get-tuple-element.65), channel_id=1, source_target_pairs={{0,4},{1,17},{2,6},{3,19},{4,8},{5,21},{6,10},{7,23},{8,12},{9,25}... | collective-permute-start | bytes 393224 | tf_op jit(solution)/shard_map/ppermute | solution.py:38
  85.1 6.1 %collective-permute-start.27 = (bf16[512,256]{1,0:T(8,128)(2,1)S(1)}, bf16[512,256]{1,0:T(8,128)(2,1)S(1)}, u32[]{:S(2)}, u32[]{:S(2)}) collective-permute-start(bf16[512,256]{1,0:T(8,128)(2,1)S(1)} %shard_map.95.refs_0_), channel_id=1, source_target_pairs={{0,1},{1,0},{2,3},{3,2},{4,5},{5,4},{6,7},{7,6},{8,9},{9,8},{10,11... | collective-permute-start | bytes 786440 | tf_op jit(solution)/shard_map/ppermute | solution.py:38
  89.9 4.1 %collective-permute-start.17 = (bf16[512,128]{1,0:T(8,128)(2,1)S(1)}, bf16[512,128]{1,0:T(8,128)(2,1)S(1)}, u32[]{:S(2)}, u32[]{:S(2)}) collective-permute-start(bf16[512,128]{1,0:T(8,128)(2,1)S(1)} %get-tuple-element.70), channel_id=1, source_target_pairs={{0,12},{1,49},{2,14},{3,51},{4,0},{5,53},{6,2},{7,55},{8,4},{9,57}... | collective-permute-start | bytes 393224 | tf_op jit(solution)/shard_map/ppermute | solution.py:38
  91.2 5.4 %collective-permute-start.18 = (bf16[512,128]{1,0:T(8,128)(2,1)S(1)}, bf16[512,128]{1,0:T(8,128)(2,1)S(1)}, u32[]{:S(2)}, u32[]{:S(2)}) collective-permute-start(bf16[512,128]{1,0:T(8,128)(2,1)S(1)} %get-tuple-element.69), channel_id=1, source_target_pairs={{0,8},{1,33},{2,10},{3,35},{4,12},{5,37},{6,14},{7,39},{8,0},{9,41... | collective-permute-start | bytes 393224 | tf_op jit(solution)/shard_map/ppermute | solution.py:38
  94.0 6.2 %collective-permute-start.19 = (bf16[512,128]{1,0:T(8,128)(2,1)S(1)}, bf16[512,128]{1,0:T(8,128)(2,1)S(1)}, u32[]{:S(2)}, u32[]{:S(2)}) collective-permute-start(bf16[512,128]{1,0:T(8,128)(2,1)S(1)} %get-tuple-element.68), channel_id=1, source_target_pairs={{0,4},{1,17},{2,6},{3,19},{4,8},{5,21},{6,10},{7,23},{8,12},{9,25}... | collective-permute-start | bytes 393224 | tf_op jit(solution)/shard_map/ppermute | solution.py:38
  96.6 27.7 %collective-permute-start.15 = (bf16[512,256]{1,0:T(8,128)(2,1)S(1)}, bf16[512,256]{1,0:T(8,128)(2,1)S(1)}, u32[]{:S(2)}, u32[]{:S(2)}) collective-permute-start(bf16[512,256]{1,0:T(8,128)(2,1)S(1)} %shard_map.95.refs_0_), channel_id=1, source_target_pairs={{0,2},{1,3},{2,0},{3,1},{4,6},{5,7},{6,4},{7,5},{8,10},{9,11},{10,... | collective-permute-start | bytes 786440 | tf_op jit(solution)/shard_map/ppermute | solution.py:38
  100.2 25.3 %collective-permute-start.28 = (bf16[512,384]{1,0:T(8,128)(2,1)S(1)}, bf16[512,384]{1,0:T(8,128)(2,1)S(1)}, u32[]{:S(2)}, u32[]{:S(2)}) collective-permute-start(bf16[512,384]{1,0:T(8,128)(2,1)S(1)} %constant_dynamic-update-slice_fusion.3.refs_1_), channel_id=1, source_target_pairs={{0,1},{1,0},{2,3},{3,2},{4,5},{5,4},{6,7},{7,6},{8,9},{9,8},{10,11... | collective-permute-start | bytes 1179656 | tf_op jit(solution)/shard_map/ppermute | solution.py:38
  124.4 3.4 %collective-permute-start.21 = (bf16[512,384]{1,0:T(8,128)(2,1)S(1)}, bf16[512,384]{1,0:T(8,128)(2,1)S(1)}, u32[]{:S(2)}, u32[]{:S(2)}) collective-permute-start(bf16[512,384]{1,0:T(8,128)(2,1)S(1)} %constant_dynamic-update-slice_fusion.refs_1_), channel_id=1, source_target_pairs={{0,1},{1,0},{2,3},{3,2},{4,5},{5,4},{6,7},{7,6},{8,9},{9,8},{10,11... | collective-permute-start | bytes 1179656 | tf_op jit(solution)/shard_map/ppermute | solution.py:38
  125.6 2.2 %collective-permute-start.20 = (bf16[512,256]{1,0:T(8,128)(2,1)S(1)}, bf16[512,256]{1,0:T(8,128)(2,1)S(1)}, u32[]{:S(2)}, u32[]{:S(2)}) collective-permute-start(bf16[512,256]{1,0:T(8,128)(2,1)S(1)} %collective-permute-done.15.refs_0_), channel_id=1, source_target_pairs={{0,1},{1,0},{2,3},{3,2},{4,5},{5,4},{6,7},{7,6},{8,9},{9,8},{10,11... | collective-permute-start | bytes 786440 | tf_op jit(solution)/shard_map/ppermute | solution.py:38

commit v3 on v2

--- a/solution.py
+++ b/solution.py
@@ -38,14 +38,14 @@
     return lax.ppermute(array, AXES, pairs)
 
 
-def across(array):
+def across(array, core=0):
     pairs = []
     for index in range(ZH * NX * NY * ZL * CORES):
         rest, c = divmod(index, CORES)
         rest, b = divmod(rest, ZL)
         a, xy = divmod(rest, NX * NY)
         to = (a + 1) % ZH if b else (a - 1) % ZH
-        pairs.append((index, ((to * NX * NY + xy) * ZL + 1 - b) * CORES + 1 - c))
+        pairs.append((index, ((to * NX * NY + xy) * ZL + 1 - b) * CORES + (c + core) % CORES))
     return lax.ppermute(array, AXES, pairs)
 
 
@@ -175,9 +175,7 @@
         elif joined:
             refs[0][:, place * HD : (place + 1) * HD] = finish(state)
         else:
-            done = finish(state)
-            refs[place][...] = done
-            refs[-1][:, place * HD : (place + 1) * HD] = done
+            refs[place][...] = finish(state)
 
 
 def attend_step(blocks, shared, own, state, tiles=tuple(range(NY + 1)), joined=None):
@@ -188,7 +186,6 @@
         outs = [jax.ShapeDtypeStruct((2 * rows, len(tiles) * HD), BF16)]
     else:
         outs = [jax.ShapeDtypeStruct((2 * rows, HD), BF16)] * len(tiles)
-        outs.append(jax.ShapeDtypeStruct((2 * rows, len(tiles) * HD), BF16))
     carried = [] if state is None else [state]
     found = call(
         functools.partial(attend_kernel, tiles, state is None, joined),
@@ -206,13 +203,16 @@
     out_refs, sems = refs[:-1], refs[-1]
     columns = out_refs[0].shape[1]
     copies = []
-    for flip, out_ref in enumerate(out_refs):
+    for flip in range(ZL * CORES):
         block = lax.bitwise_xor(place_ref[0], flip)
         lanes = pl.ds(pl.multiple_of(block * columns, HD), columns)
         for slot, k in enumerate(SLOTS):
             head = lax.rem(y_ref[0] + k, NY) if k < NY else NY
             source = w_ref.at[pl.ds(pl.multiple_of(head * HD, HD), HD), lanes]
-            target = out_ref.at[slot * HD : (slot + 1) * HD]
+            if flip == ZL and slot == NY:
+                target = out_refs[-1]
+            else:
+                target = out_refs[flip].at[slot * HD : (slot + 1) * HD]
             copies.append(pltpu.make_async_copy(source, target, sems.at[flip, slot]))
     for copy in copies:
         copy.start()
@@ -220,26 +220,43 @@
         copy.wait()
 
 
-def project_sum(refs, weights, lanes=slice(None)):
-    own = refs[0].shape[1]
+def project_sum(pairs, lanes=slice(None)):
     total = None
-    for place, ref in enumerate(refs):
-        start = own * (place % 2)
-        rows = slice(start, start + ref.shape[1])
-        part = jnp.dot(ref[...], weights[place // 2][rows, lanes], preferred_element_type=F32)
+    for ref, columns, weight, row in pairs:
+        low, high = columns
+        rows = slice(row, row + high - low)
+        part = jnp.dot(ref[:, low:high], weight[rows, lanes], preferred_element_type=F32)
         total = part if total is None else total + part
     return total
 
 
-def project_first_kernel(*refs):
-    refs[6][...] = project_sum(refs[:4], refs[4:6])
-
-
-def project_last_kernel(*refs):
-    sum_ref, out_ref, tan_ref = refs[6:]
+OWN, REST, MOST = (0, 2 * HD), (0, 3 * HD), (0, 2 * HD)
+
+
+def project_first_kernel(a_ref, b_ref, c_ref, d_ref, wa_ref, wb_ref, wc_ref, wm_ref, wd_ref, out_ref):
+    out_ref[...] = project_sum(
+        (
+            (a_ref, OWN, wa_ref, 0),
+            (b_ref, OWN, wb_ref, 0),
+            (c_ref, MOST, wc_ref, 2 * HD),
+            (c_ref, (2 * HD, 3 * HD), wm_ref, 0),
+            (d_ref, REST, wd_ref, 2 * HD),
+        )
+    )
+
+
+def project_last_kernel(a_ref, b_ref, c_ref, d_ref, wa_ref, wb_ref, wc_ref, wd_ref, sum_ref, out_ref, tan_ref):
     rows, tile = out_ref.shape
     lanes = pl.ds(pl.multiple_of(pl.program_id(0) * tile, tile), tile)
-    total = sum_ref[:, lanes] + project_sum(refs[:4], refs[4:6], lanes)
+    total = sum_ref[:, lanes] + project_sum(
+        (
+            (a_ref, REST, wa_ref, 2 * HD),
+            (b_ref, REST, wb_ref, 2 * HD),
+            (c_ref, OWN, wc_ref, 0),
+            (d_ref, OWN, wd_ref, 0),
+        ),
+        lanes,
+    )
     out_ref[...] = total[:rows].astype(BF16)
     tan_ref[...] = total[rows:].astype(BF16)
 
@@ -300,7 +317,10 @@
     place, _ = lax.optimization_barrier((place, sends[1]))
     cuts = call(
         cut_weight_kernel,
-        [jax.ShapeDtypeStruct((width, columns), BF16)] * (ZL * CORES),
+        [
+            jax.ShapeDtypeStruct((depth, columns), BF16)
+            for depth in (width, width, width - HD, width, HD)
+        ],
         y,
         place,
         out_weight,
@@ -318,7 +338,8 @@
     )
     cuts, _ = lax.optimization_barrier((cuts, split[0]))
     weight_near = shift(cuts[2], zl=1)
-    weight_far = across(cuts[3])
+    weight_far = across(cuts[3], core=1)
+    weight_more = across(cuts[4])
     weight_core = shift(cuts[1], core=1)
 
     own = call(
@@ -336,26 +357,31 @@
     state = attend_step(blocks, right[0], left[1], state)
     others = attend_step(blocks, opposite[0], opposite[0], state, (1, 2, 3), False)
     opposite[1], _ = lax.optimization_barrier((opposite[1], others[0]))
-    mine = [attend_step(blocks, opposite[0], opposite[1], state, (0, NY), True)]
-    back = [shift(others[k - 1], swap=-k) for k in (1, 2, 3)]
-    mine.append(jnp.concatenate(back, axis=1))
-
+    kept = attend_step(blocks, opposite[0], opposite[1], state, (0, NY), True)
+
+    near = [
+        shift(kept, zl=1),
+        jnp.concatenate([shift(others[k - 1], swap=-k, zl=1) for k in (1, 2, 3)], axis=1),
+    ]
+    mine = [kept, jnp.concatenate([shift(others[k - 1], swap=-k) for k in (1, 2, 3)], axis=1)]
     sibling = [shift(mine[n], core=1) for n in range(2)]
+    far = [shift(near[n], core=1) for n in range(2)]
+    weights = (cuts[0], weight_core, weight_near)
     partial = call(
         project_first_kernel,
         jax.ShapeDtypeStruct((2 * rows, columns), F32),
-        *mine,
-        *sibling,
-        cuts[0],
-        weight_core,
+        mine[0],
+        sibling[0],
+        near[1],
+        far[1],
+        *weights,
+        weight_more,
+        weight_far,
         flops=8 * rows * width * columns,
     )
-
-    crossed = shift(others[NY - 1], zl=1)
-    handed = [shift(crossed[:, (k - 1) * HD : k * HD], swap=-k) for k in (1, 2, 3)]
-    near = [shift(mine[0], zl=1), jnp.concatenate(handed, axis=1)]
-    far = [shift(near[n], core=1) for n in range(2)]
-    return tuple(project_last(*near, *far, weight_near, weight_far, partial))
+    return tuple(
+        project_last(mine[1], sibling[1], near[0], far[0], *weights, weight_far, partial)
+    )
 
 
 def solution(mesh):

time: 132 us -> 132 us (level)
  starting transfers between devices: 50 us -> 61.8 us
  waiting for transfers between devices: 58.7 us -> 47.5 us
    ppermute x29 -> x28, waiting for transfers between devices: 58.7 us -> 18.7 us  [shift(): return lax.ppermute(array, AXES, pairs)]
    ppermute x1 -> x2, waiting for transfers between devices: 0.01 us -> 28.8 us  [across(): return lax.ppermute(array, AXES, pairs)]
    ppermute x29 -> x28, starting transfers between devices: 49.7 us -> 59 us  [shift(): return lax.ppermute(array, AXES, pairs)]
    ppermute x1 -> x2, starting transfers between devices: 0.29 us -> 2.84 us  [across(): return lax.ppermute(array, AXES, pairs)]
  transfers between devices with their start and end apart: 30 -> 30, of which waited for: 14 -> 11; matrix products, arithmetic and copies ran while one was open for 0% -> 0% of each run, Pallas kernels for 13% -> 13%
where the time goes in v3:
time: 132 us
  starting transfers between devices  61.8 us (47%)
  waiting for transfers between devices  47.5 us (36%)
  Pallas kernels  21.8 us (17%)
    ppermute x28, starting transfers between devices, shift(): return lax.ppermute(array, AXES, pairs)  59 us
    ppermute x2, waiting for transfers between devices, across(): return lax.ppermute(array, AXES, pairs)  28.8 us
    ppermute x28, waiting for transfers between devices, shift(): return lax.ppermute(array, AXES, pairs)  18.7 us
    pallas_call x11, Pallas kernels, called(): pl.pallas_call(kernel, out_shape=outs, in_specs=specs or [VMEM] * len(ope...  18 us
    pallas_call x1, Pallas kernels, project_last(): pl.pallas_call(project_last_kernel, grid=(columns // tile,), in_specs=[VM...  3.82 us
    ppermute x2, starting transfers between devices, across(): return lax.ppermute(array, AXES, pairs)  2.84 us
  transfers between devices with their start and end apart: 30, of which 11 were waited for; matrix products, arithmetic and copies ran while one was open for 0% of the time, Pallas kernels for 13%

profile of v3, /device:TPU:1, one launch (start us, length us, event | category | flops | bytes accessed | tf_op | source)
XLA Modules:
  0.0 132.1 jit_solution(2962386109788880232)
XLA Ops:
  0.6 0.9 shard_map.87.refs_0_
  1.5 3.9 %collective-permute-start.3 = (bf16[5,32,512]{2,1,0:T(8,128)(2,1)S(1)}, bf16[5,32,512]{2,1,0:T(8,128)(2,1)S(1)}, u32[]{:S(2)}, u32[]{:S(2)}) collective-permute-start(bf16[5,32,512]{2,1,0:T(8,128)(2,1)S(1)} %shard_map.87.refs_0_), channel_id=1, source_target_pairs={{0,64},{1,65},{2,66},{3,67},{4,68},{5,69},{6,70},{7,71},{8,72},{9,... | collective-permute-start | bytes 491528 | tf_op jit(solution)/shard_map/ppermute | solution.py:38
  5.4 3.1 %collective-permute-start.4 = (bf16[5,32,512]{2,1,0:T(8,128)(2,1)S(1)}, bf16[5,32,512]{2,1,0:T(8,128)(2,1)S(1)}, u32[]{:S(2)}, u32[]{:S(2)}) collective-permute-start(bf16[5,32,512]{2,1,0:T(8,128)(2,1)S(1)} %shard_map.87.refs_0_), channel_id=1, source_target_pairs={{0,192},{1,193},{2,194},{3,195},{4,196},{5,197},{6,198},{7,199},{8... | collective-permute-start | bytes 491528 | tf_op jit(solution)/shard_map/ppermute | solution.py:38
  8.5 4.4 %collective-permute-start.5 = (bf16[5,32,512]{2,1,0:T(8,128)(2,1)S(1)}, bf16[5,32,512]{2,1,0:T(8,128)(2,1)S(1)}, u32[]{:S(2)}, u32[]{:S(2)}) collective-permute-start(bf16[5,32,512]{2,1,0:T(8,128)(2,1)S(1)} %shard_map.87.refs_0_), channel_id=1, source_target_pairs={{0,128},{1,129},{2,130},{3,131},{4,132},{5,133},{6,134},{7,135},{8... | collective-permute-start | bytes 491528 | tf_op jit(solution)/shard_map/ppermute | solution.py:38
  12.9 1.2 shard_map.86
  14.1 3.1 %shard_map.88 = (bf16[640,1280]{1,0:T(8,128)(2,1)S(1)}, bf16[640,1280]{1,0:T(8,128)(2,1)S(1)}, bf16[512,1280]{1,0:T(8,128)(2,1)S(1)}, bf16[640,1280]{1,0:T(8,128)(2,1)S(1)}, bf16[128,1280]{1,0:T(8,128)(2,1)S(1)}) custom-call(s32[1]{0:T(128)S(6)} %select_n.27.y_ref, s32[1]{0:T(128)} %bitcast.place_ref, bf16[640,5120]{1,0:T(8,128)(2,1)} %w_ref.1), custom_call_target="tpu_custom_call" | custom-call | bytes 6553608 | tf_op jit(solution)/shard_map/pallas_call | solution.py:57
  17.2 3.7 %collective-permute-done.4.refs_2_ = bf16[5,32,512]{2,1,0:T(8,128)(2,1)S(1)} collective-permute-done((bf16[5,32,512]{2,1,0:T(8,128)(2,1)S(1)}, bf16[5,32,512]{2,1,0:T(8,128)(2,1)S(1)}, u32[]{:S(2)}, u32[]{:S(2)}) %collective-permute-start.4) | collective-permute-done | bytes 163872 | tf_op jit(solution)/shard_map/ppermute | solution.py:38
  21.0 0.9 collective-permute-done.5.refs_3_
  21.9 1.3 collective-permute-start.6
  23.2 1.5 %collective-permute-start.7 = (bf16[256,512]{1,0:T(8,128)(2,1)S(1)}, bf16[256,512]{1,0:T(8,128)(2,1)S(1)}, u32[]{:S(2)}, u32[]{:S(2)}) collective-permute-start(bf16[256,512]{1,0:T(8,128)(2,1)S(1)} %get-tuple-element.52), channel_id=1, source_target_pairs={{0,12},{1,49},{2,14},{3,51},{4,0},{5,53},{6,2},{7,55},{8,4},{9,57}... | collective-permute-start | bytes 786440 | tf_op jit(solution)/shard_map/ppermute | solution.py:38
  24.6 1.5 %collective-permute-start.8 = (bf16[256,512]{1,0:T(8,128)(2,1)S(1)}, bf16[256,512]{1,0:T(8,128)(2,1)S(1)}, u32[]{:S(2)}, u32[]{:S(2)}) collective-permute-start(bf16[256,512]{1,0:T(8,128)(2,1)S(1)} %get-tuple-element.53), channel_id=1, source_target_pairs={{0,8},{1,33},{2,10},{3,35},{4,12},{5,37},{6,14},{7,39},{8,0},{9,41... | collective-permute-start | bytes 786440 | tf_op jit(solution)/shard_map/ppermute | solution.py:38
  26.2 2.2 %collective-permute-done.6.refs_1_ = bf16[256,512]{1,0:T(8,128)(2,1)S(1)} collective-permute-done((bf16[256,512]{1,0:T(8,128)(2,1)S(1)}, bf16[256,512]{1,0:T(8,128)(2,1)S(1)}, u32[]{:S(2)}, u32[]{:S(2)}) %collective-permute-start.6) | collective-permute-done | bytes 262176 | tf_op jit(solution)/shard_map/ppermute | solution.py:38
  28.4 3.8 %collective-permute-done.8.refs_3_ = bf16[256,512]{1,0:T(8,128)(2,1)S(1)} collective-permute-done((bf16[256,512]{1,0:T(8,128)(2,1)S(1)}, bf16[256,512]{1,0:T(8,128)(2,1)S(1)}, u32[]{:S(2)}, u32[]{:S(2)}) %collective-permute-start.8) | collective-permute-done | bytes 262176 | tf_op jit(solution)/shard_map/ppermute | solution.py:38
  32.3 1.4 %collective-permute-start.9 = (bf16[512,512]{1,0:T(8,128)(2,1)S(1)}, bf16[512,512]{1,0:T(8,128)(2,1)S(1)}, u32[]{:S(2)}, u32[]{:S(2)}) collective-permute-start(bf16[512,512]{1,0:T(8,128)(2,1)S(1)} %get-tuple-element.54.refs_5_), channel_id=1, source_target_pairs={{0,16},{1,5},{2,18},{3,7},{4,20},{5,9},{6,22},{7,11},{8,24},{9,13}... | collective-permute-start | bytes 1572872 | tf_op jit(solution)/shard_map/ppermute | solution.py:38
  33.6 0.9 collective-permute-start
  34.5 2.0 %collective-permute-start.1 = (bf16[256,256]{1,0:T(8,128)(2,1)S(1)}, bf16[256,256]{1,0:T(8,128)(2,1)S(1)}, u32[]{:S(2)}, u32[]{:S(2)}) collective-permute-start(bf16[256,256]{1,0:T(8,128)(2,1)S(1)} %get-tuple-element.38), channel_id=1, source_target_pairs={{0,8},{1,33},{2,10},{3,35},{4,12},{5,37},{6,14},{7,39},{8,0},{9,41... | collective-permute-start | bytes 393224 | tf_op jit(solution)/shard_map/ppermute | solution.py:38
  36.5 1.8 %collective-permute-start.13 = (bf16[512,512]{1,0:T(8,128)(2,1)S(1)}, bf16[512,512]{1,0:T(8,128)(2,1)S(1)}, u32[]{:S(2)}, u32[]{:S(2)}) collective-permute-start(bf16[512,512]{1,0:T(8,128)(2,1)S(1)} %get-tuple-element.57.refs_6_), channel_id=1, source_target_pairs={{0,48},{1,13},{2,50},{3,15},{4,52},{5,1},{6,54},{7,3},{8,56},{9,5}... | collective-permute-start | bytes 1572872 | tf_op jit(solution)/shard_map/ppermute | solution.py:38
  38.4 1.4 %collective-permute-start.11 = (bf16[512,512]{1,0:T(8,128)(2,1)S(1)}, bf16[512,512]{1,0:T(8,128)(2,1)S(1)}, u32[]{:S(2)}, u32[]{:S(2)}) collective-permute-start(bf16[512,512]{1,0:T(8,128)(2,1)S(1)} %get-tuple-element.54.refs_5_), channel_id=1, source_target_pairs={{0,48},{1,13},{2,50},{3,15},{4,52},{5,1},{6,54},{7,3},{8,56},{9,5}... | collective-permute-start | bytes 1572872 | tf_op jit(solution)/shard_map/ppermute | solution.py:38
  39.7 0.4 collective-permute-start.2
  40.1 0.2 collective-permute-done.1.refs_2_.refs_1_
  40.3 1.3 collective-permute-start.12
  41.6 2.3 %collective-permute-done.2.refs_3_.refs_2_ = bf16[256,256]{1,0:T(8,128)(2,1)S(1)} collective-permute-done((bf16[256,256]{1,0:T(8,128)(2,1)S(1)}, bf16[256,256]{1,0:T(8,128)(2,1)S(1)}, u32[]{:S(2)}, u32[]{:S(2)}) %collective-permute-start.2) | collective-permute-done | bytes 131104 | tf_op jit(solution)/shard_map/ppermute | solution.py:38
  43.8 6.5 %collective-permute-start.22 = (bf16[512,1280]{1,0:T(8,128)(2,1)S(1)}, bf16[512,1280]{1,0:T(8,128)(2,1)S(1)}, u32[]{:S(2)}, u32[]{:S(2)}) collective-permute-start(bf16[512,1280]{1,0:T(8,128)(2,1)S(1)} %get-tuple-element.69), channel_id=1, source_target_pairs={{0,2},{1,3},{2,0},{3,1},{4,6},{5,7},{6,4},{7,5},{8,10},{9,11},{10,... | collective-permute-start | bytes 3932168 | tf_op jit(solution)/shard_map/ppermute | solution.py:38
  50.3 0.3 collective-permute-start.10
  50.6 7.0 %collective-permute-start.21 = (bf16[640,1280]{1,0:T(8,128)(2,1)S(1)}, bf16[640,1280]{1,0:T(8,128)(2,1)S(1)}, u32[]{:S(2)}, u32[]{:S(2)}) collective-permute-start(bf16[640,1280]{1,0:T(8,128)(2,1)S(1)} %get-tuple-element.68), channel_id=1, source_target_pairs={{0,1},{1,0},{2,3},{3,2},{4,5},{5,4},{6,7},{7,6},{8,9},{9,8},{10,11... | collective-permute-start | bytes 4915208 | tf_op jit(solution)/shard_map/ppermute | solution.py:38
  57.6 2.1 %collective-permute-start.18 = (bf16[512,512]{1,0:T(8,128)(2,1)S(1)}, bf16[512,512]{1,0:T(8,128)(2,1)S(1)}, u32[]{:S(2)}, u32[]{:S(2)}) collective-permute-start(bf16[512,512]{1,0:T(8,128)(2,1)S(1)} %collective-permute-done.13.refs_6_), channel_id=1, source_target_pairs={{0,48},{1,13},{2,50},{3,15},{4,52},{5,1},{6,54},{7,3},{8,56},{9,5}... | collective-permute-start | bytes 1572872 | tf_op jit(solution)/shard_map/ppermute | solution.py:38
  59.8 2.1 %shard_map.91.refs_7_ = f32[5,256,768]{2,1,0:T(8,128)S(1)} custom-call(bf16[256,256]{1,0:T(8,128)(2,1)S(1)} %get-tuple-element.55.refs_0_, bf16[256,256]{1,0:T(8,128)(2,1)S(1)} %collective-permute-done.refs_1_.refs_0_, bf16[256,256]{1,0:T(8,128)(2,1)S(1)} %collective-permute-done.1.refs_2_.refs_1_, ...), custom_call_target="tpu_custom_call" | custom-call | flops 1174405120 | bytes 1703936 | tf_op jit(solution)/shard_map/pallas_call | solution.py:57
  61.9 2.8 %collective-permute-start.29 = (bf16[128,1280]{1,0:T(8,128)(2,1)S(1)}, bf16[128,1280]{1,0:T(8,128)(2,1)S(1)}, u32[]{:S(2)}, u32[]{:S(2)}) collective-permute-start(bf16[128,1280]{1,0:T(8,128)(2,1)S(1)} %get-tuple-element.71), channel_id=1, source_target_pairs={{0,194},{1,195},{2,64},{3,65},{4,198},{5,199},{6,68},{7,69},{8,202... | collective-permute-start | bytes 983048 | tf_op jit(solution)/shard_map/ppermute | solution.py:49
  64.7 2.7 %shard_map.92.refs_7_ = f32[5,256,768]{2,1,0:T(8,128)S(1)} custom-call(bf16[256,256]{1,0:T(8,128)(2,1)S(1)} %get-tuple-element.55.refs_0_, bf16[256,256]{1,0:T(8,128)(2,1)S(1)} %collective-permute-done.refs_1_.refs_0_, bf16[256,256]{1,0:T(8,128)(2,1)S(1)} %collective-permute-done.1.refs_2_.refs_1_, ...), custom_call_target="tpu_custom_call" | custom-call | flops 1174405120 | bytes 5636096 | tf_op jit(solution)/shard_map/pallas_call | solution.py:57
  67.4 2.7 %shard_map.93.refs_5_.refs_4_ = f32[5,256,768]{2,1,0:T(8,128)S(1)} custom-call(bf16[256,256]{1,0:T(8,128)(2,1)S(1)} %get-tuple-element.55.refs_0_, bf16[256,256]{1,0:T(8,128)(2,1)S(1)} %collective-permute-done.refs_1_.refs_0_, bf16[256,256]{1,0:T(8,128)(2,1)S(1)} %collective-permute-done.1.refs_2_.refs_1_, ...), custom_call_target="tpu_custom_call" | custom-call | flops 1174405120 | bytes 5636096 | tf_op jit(solution)/shard_map/pallas_call | solution.py:57
  70.1 1.8 %shard_map.94 = (bf16[512,128]{1,0:T(8,128)(2,1)S(1)}, bf16[512,128]{1,0:T(8,128)(2,1)S(1)}, bf16[512,128]{1,0:T(8,128)(2,1)S(1)}) custom-call(bf16[256,256]{1,0:T(8,128)(2,1)S(1)} %collective-permute-done.refs_1_.refs_0_, bf16[256,256]{1,0:T(8,128)(2,1)S(1)} %collective-permute-done.1.refs_2_.refs_1_, ...), custom_call_target="tpu_custom_call" | custom-call | flops 704643072 | bytes 5373952 | tf_op jit(solution)/shard_map/pallas_call | solution.py:57
  71.9 2.7 %collective-permute-start.25 = (bf16[512,128]{1,0:T(8,128)(2,1)S(1)}, bf16[512,128]{1,0:T(8,128)(2,1)S(1)}, u32[]{:S(2)}, u32[]{:S(2)}) collective-permute-start(bf16[512,128]{1,0:T(8,128)(2,1)S(1)} %get-tuple-element.58), channel_id=1, source_target_pairs={{0,14},{1,51},{2,12},{3,49},{4,2},{5,55},{6,0},{7,53},{8,6},{9,59}... | collective-permute-start | bytes 393224 | tf_op jit(solution)/shard_map/ppermute | solution.py:38
  74.6 28.8 %collective-permute-done.29.wm_ref = bf16[128,1280]{1,0:T(8,128)(2,1)S(1)} collective-permute-done((bf16[128,1280]{1,0:T(8,128)(2,1)S(1)}, bf16[128,1280]{1,0:T(8,128)(2,1)S(1)}, u32[]{:S(2)}, u32[]{:S(2)}) %collective-permute-start.29) | collective-permute-done | bytes 327712 | tf_op jit(solution)/shard_map/ppermute | solution.py:49
  103.4 1.8 %collective-permute-start.14 = (bf16[512,128]{1,0:T(8,128)(2,1)S(1)}, bf16[512,128]{1,0:T(8,128)(2,1)S(1)}, u32[]{:S(2)}, u32[]{:S(2)}) collective-permute-start(bf16[512,128]{1,0:T(8,128)(2,1)S(1)} %get-tuple-element.58), channel_id=1, source_target_pairs={{0,12},{1,49},{2,14},{3,51},{4,0},{5,53},{6,2},{7,55},{8,4},{9,57}... | collective-permute-start | bytes 393224 | tf_op jit(solution)/shard_map/ppermute | solution.py:38
  105.2 1.2 shard_map.95.a_ref
  106.4 2.8 %collective-permute-start.26 = (bf16[512,128]{1,0:T(8,128)(2,1)S(1)}, bf16[512,128]{1,0:T(8,128)(2,1)S(1)}, u32[]{:S(2)}, u32[]{:S(2)}) collective-permute-start(bf16[512,128]{1,0:T(8,128)(2,1)S(1)} %get-tuple-element.59), channel_id=1, source_target_pairs={{0,10},{1,35},{2,8},{3,33},{4,14},{5,39},{6,12},{7,37},{8,2},{9,43... | collective-permute-start | bytes 393224 | tf_op jit(solution)/shard_map/ppermute | solution.py:38
  109.2 1.0 collective-permute-start.27
  110.2 2.6 %collective-permute-start.15 = (bf16[512,128]{1,0:T(8,128)(2,1)S(1)}, bf16[512,128]{1,0:T(8,128)(2,1)S(1)}, u32[]{:S(2)}, u32[]{:S(2)}) collective-permute-start(bf16[512,128]{1,0:T(8,128)(2,1)S(1)} %get-tuple-element.59), channel_id=1, source_target_pairs={{0,8},{1,33},{2,10},{3,35},{4,12},{5,37},{6,14},{7,39},{8,0},{9,41... | collective-permute-start | bytes 393224 | tf_op jit(solution)/shard_map/ppermute | solution.py:38
  112.9 1.3 collective-permute-done.26
  114.2 2.2 %collective-permute-done.27 = bf16[512,128]{1,0:T(8,128)(2,1)S(1)} collective-permute-done((bf16[512,128]{1,0:T(8,128)(2,1)S(1)}, bf16[512,128]{1,0:T(8,128)(2,1)S(1)}, u32[]{:S(2)}, u32[]{:S(2)}) %collective-permute-start.27) | collective-permute-done | bytes 131104 | tf_op jit(solution)/shard_map/ppermute | solution.py:38
  116.4 0.8 collective-permute-start.24
  117.3 1.3 collective-permute-start.19
  118.5 0.7 collective-permute-done.16
  119.2 2.4 %collective-permute-start.28 = (bf16[512,384]{1,0:T(8,128)(2,1)S(1)}, bf16[512,384]{1,0:T(8,128)(2,1)S(1)}, u32[]{:S(2)}, u32[]{:S(2)}) collective-permute-start(bf16[512,384]{1,0:T(8,128)(2,1)S(1)} %constant_dynamic-update-slice_fusion.3.c_ref), channel_id=1, source_target_pairs={{0,1},{1,0},{2,3},{3,2},{4,5},{5,4},{6,7},{7,6},{8,9},{9,8},{10,11... | collective-permute-start | bytes 1179656 | tf_op jit(solution)/shard_map/ppermute | solution.py:38
  121.7 1.4 %collective-permute-done.19.c_ref = bf16[512,256]{1,0:T(8,128)(2,1)S(1)} collective-permute-done((bf16[512,256]{1,0:T(8,128)(2,1)S(1)}, bf16[512,256]{1,0:T(8,128)(2,1)S(1)}, u32[]{:S(2)}, u32[]{:S(2)}) %collective-permute-start.19) | collective-permute-done | bytes 262176 | tf_op jit(solution)/shard_map/ppermute | solution.py:38
  123.1 3.0 %collective-permute-start.20 = (bf16[512,256]{1,0:T(8,128)(2,1)S(1)}, bf16[512,256]{1,0:T(8,128)(2,1)S(1)}, u32[]{:S(2)}, u32[]{:S(2)}) collective-permute-start(bf16[512,256]{1,0:T(8,128)(2,1)S(1)} %collective-permute-done.19.c_ref), channel_id=1, source_target_pairs={{0,1},{1,0},{2,3},{3,2},{4,5},{5,4},{6,7},{7,6},{8,9},{9,8},{10,11... | collective-permute-start | bytes 786440 | tf_op jit(solution)/shard_map/ppermute | solution.py:38
  126.1 2.2 %shard_map.96.sum_ref = f32[512,1280]{1,0:T(8,128)S(1)} custom-call(bf16[512,256]{1,0:T(8,128)(2,1)S(1)} %shard_map.95.a_ref, bf16[512,256]{1,0:T(8,128)(2,1)S(1)} %collective-permute-done.24.b_ref, bf16[512,384]{1,0:T(8,128)(2,1)S(1)} %constant_dynamic-update-slice_fusion.3.c_ref, bf16[512,384]{1,0:T(8,128)(2,1)S(1)} %collective-permute-done.28.d_ref, ...), custom_call_target="tpu_custom_call" | custom-call | flops 1677721600 | bytes 7864320 | tf_op jit(solution)/shard_map/pallas_call | solution.py:57
  128.3 3.8 %project_last.1 = (bf16[256,1280]{1,0:T(8,128)(2,1)}, bf16[256,1280]{1,0:T(8,128)(2,1)}) custom-call(bf16[512,384]{1,0:T(8,128)(2,1)S(1)} %constant_dynamic-update-slice_fusion.a_ref, bf16[512,384]{1,0:T(8,128)(2,1)S(1)} %collective-permute-done.17.b_ref, bf16[512,256]{1,0:T(8,128)(2,1)S(1)} %collective-permute-done.19.c_ref, ...), custom_call_target="tpu_custom_call" | custom-call | tf_op jit(solution)/shard_map/project_last/pallas_call | solution.py:268
  (30 shorter events, 0.5 us)
Async XLA Ops:
  1.5 15.7 %collective-permute-start.3 = (bf16[5,32,512]{2,1,0:T(8,128)(2,1)S(1)}, bf16[5,32,512]{2,1,0:T(8,128)(2,1)S(1)}, u32[]{:S(2)}, u32[]{:S(2)}) collective-permute-start(bf16[5,32,512]{2,1,0:T(8,128)(2,1)S(1)} %shard_map.87.refs_0_), channel_id=1, source_target_pairs={{0,64},{1,65},{2,66},{3,67},{4,68},{5,69},{6,70},{7,71},{8,72},{9,... | collective-permute-start | bytes 491528 | tf_op jit(solution)/shard_map/ppermute | solution.py:38
  5.4 15.5 %collective-permute-start.4 = (bf16[5,32,512]{2,1,0:T(8,128)(2,1)S(1)}, bf16[5,32,512]{2,1,0:T(8,128)(2,1)S(1)}, u32[]{:S(2)}, u32[]{:S(2)}) collective-permute-start(bf16[5,32,512]{2,1,0:T(8,128)(2,1)S(1)} %shard_map.87.refs_0_), channel_id=1, source_target_pairs={{0,192},{1,193},{2,194},{3,195},{4,196},{5,197},{6,198},{7,199},{8... | collective-permute-start | bytes 491528 | tf_op jit(solution)/shard_map/ppermute | solution.py:38
  8.5 13.3 %collective-permute-start.5 = (bf16[5,32,512]{2,1,0:T(8,128)(2,1)S(1)}, bf16[5,32,512]{2,1,0:T(8,128)(2,1)S(1)}, u32[]{:S(2)}, u32[]{:S(2)}) collective-permute-start(bf16[5,32,512]{2,1,0:T(8,128)(2,1)S(1)} %shard_map.87.refs_0_), channel_id=1, source_target_pairs={{0,128},{1,129},{2,130},{3,131},{4,132},{5,133},{6,134},{7,135},{8... | collective-permute-start | bytes 491528 | tf_op jit(solution)/shard_map/ppermute | solution.py:38
  21.9 6.5 %collective-permute-start.6 = (bf16[256,512]{1,0:T(8,128)(2,1)S(1)}, bf16[256,512]{1,0:T(8,128)(2,1)S(1)}, u32[]{:S(2)}, u32[]{:S(2)}) collective-permute-start(bf16[256,512]{1,0:T(8,128)(2,1)S(1)} %get-tuple-element.51), channel_id=1, source_target_pairs={{0,4},{1,17},{2,6},{3,19},{4,8},{5,21},{6,10},{7,23},{8,12},{9,25}... | collective-permute-start | bytes 786440 | tf_op jit(solution)/shard_map/ppermute | solution.py:38
  23.2 5.2 %collective-permute-start.7 = (bf16[256,512]{1,0:T(8,128)(2,1)S(1)}, bf16[256,512]{1,0:T(8,128)(2,1)S(1)}, u32[]{:S(2)}, u32[]{:S(2)}) collective-permute-start(bf16[256,512]{1,0:T(8,128)(2,1)S(1)} %get-tuple-element.52), channel_id=1, source_target_pairs={{0,12},{1,49},{2,14},{3,51},{4,0},{5,53},{6,2},{7,55},{8,4},{9,57}... | collective-permute-start | bytes 786440 | tf_op jit(solution)/shard_map/ppermute | solution.py:38
  24.6 7.5 %collective-permute-start.8 = (bf16[256,512]{1,0:T(8,128)(2,1)S(1)}, bf16[256,512]{1,0:T(8,128)(2,1)S(1)}, u32[]{:S(2)}, u32[]{:S(2)}) collective-permute-start(bf16[256,512]{1,0:T(8,128)(2,1)S(1)} %get-tuple-element.53), channel_id=1, source_target_pairs={{0,8},{1,33},{2,10},{3,35},{4,12},{5,37},{6,14},{7,39},{8,0},{9,41... | collective-permute-start | bytes 786440 | tf_op jit(solution)/shard_map/ppermute | solution.py:38
  32.3 18.1 %collective-permute-start.9 = (bf16[512,512]{1,0:T(8,128)(2,1)S(1)}, bf16[512,512]{1,0:T(8,128)(2,1)S(1)}, u32[]{:S(2)}, u32[]{:S(2)}) collective-permute-start(bf16[512,512]{1,0:T(8,128)(2,1)S(1)} %get-tuple-element.54.refs_5_), channel_id=1, source_target_pairs={{0,16},{1,5},{2,18},{3,7},{4,20},{5,9},{6,22},{7,11},{8,24},{9,13}... | collective-permute-start | bytes 1572872 | tf_op jit(solution)/shard_map/ppermute | solution.py:38
  33.6 6.1 %collective-permute-start = (bf16[256,256]{1,0:T(8,128)(2,1)S(1)}, bf16[256,256]{1,0:T(8,128)(2,1)S(1)}, u32[]{:S(2)}, u32[]{:S(2)}) collective-permute-start(bf16[256,256]{1,0:T(8,128)(2,1)S(1)} %get-tuple-element.37), channel_id=1, source_target_pairs={{0,4},{1,17},{2,6},{3,19},{4,8},{5,21},{6,10},{7,23},{8,12},{9,25}... | collective-permute-start | bytes 393224 | tf_op jit(solution)/shard_map/ppermute | solution.py:38
  34.5 5.8 %collective-permute-start.1 = (bf16[256,256]{1,0:T(8,128)(2,1)S(1)}, bf16[256,256]{1,0:T(8,128)(2,1)S(1)}, u32[]{:S(2)}, u32[]{:S(2)}) collective-permute-start(bf16[256,256]{1,0:T(8,128)(2,1)S(1)} %get-tuple-element.38), channel_id=1, source_target_pairs={{0,8},{1,33},{2,10},{3,35},{4,12},{5,37},{6,14},{7,39},{8,0},{9,41... | collective-permute-start | bytes 393224 | tf_op jit(solution)/shard_map/ppermute | solution.py:38
  36.5 14.1 %collective-permute-start.13 = (bf16[512,512]{1,0:T(8,128)(2,1)S(1)}, bf16[512,512]{1,0:T(8,128)(2,1)S(1)}, u32[]{:S(2)}, u32[]{:S(2)}) collective-permute-start(bf16[512,512]{1,0:T(8,128)(2,1)S(1)} %get-tuple-element.57.refs_6_), channel_id=1, source_target_pairs={{0,48},{1,13},{2,50},{3,15},{4,52},{5,1},{6,54},{7,3},{8,56},{9,5}... | collective-permute-start | bytes 1572872 | tf_op jit(solution)/shard_map/ppermute | solution.py:38
  38.4 19.2 %collective-permute-start.11 = (bf16[512,512]{1,0:T(8,128)(2,1)S(1)}, bf16[512,512]{1,0:T(8,128)(2,1)S(1)}, u32[]{:S(2)}, u32[]{:S(2)}) collective-permute-start(bf16[512,512]{1,0:T(8,128)(2,1)S(1)} %get-tuple-element.54.refs_5_), channel_id=1, source_target_pairs={{0,48},{1,13},{2,50},{3,15},{4,52},{5,1},{6,54},{7,3},{8,56},{9,5}... | collective-permute-start | bytes 1572872 | tf_op jit(solution)/shard_map/ppermute | solution.py:38
  39.7 4.1 %collective-permute-start.2 = (bf16[256,256]{1,0:T(8,128)(2,1)S(1)}, bf16[256,256]{1,0:T(8,128)(2,1)S(1)}, u32[]{:S(2)}, u32[]{:S(2)}) collective-permute-start(bf16[256,256]{1,0:T(8,128)(2,1)S(1)} %get-tuple-element.39), channel_id=1, source_target_pairs={{0,12},{1,49},{2,14},{3,51},{4,0},{5,53},{6,2},{7,55},{8,4},{9,57}... | collective-permute-start | bytes 393224 | tf_op jit(solution)/shard_map/ppermute | solution.py:38
  40.3 17.3 %collective-permute-start.12 = (bf16[512,512]{1,0:T(8,128)(2,1)S(1)}, bf16[512,512]{1,0:T(8,128)(2,1)S(1)}, u32[]{:S(2)}, u32[]{:S(2)}) collective-permute-start(bf16[512,512]{1,0:T(8,128)(2,1)S(1)} %get-tuple-element.57.refs_6_), channel_id=1, source_target_pairs={{0,16},{1,5},{2,18},{3,7},{4,20},{5,9},{6,22},{7,11},{8,24},{9,13}... | collective-permute-start | bytes 1572872 | tf_op jit(solution)/shard_map/ppermute | solution.py:38
  43.8 66.4 %collective-permute-start.22 = (bf16[512,1280]{1,0:T(8,128)(2,1)S(1)}, bf16[512,1280]{1,0:T(8,128)(2,1)S(1)}, u32[]{:S(2)}, u32[]{:S(2)}) collective-permute-start(bf16[512,1280]{1,0:T(8,128)(2,1)S(1)} %get-tuple-element.69), channel_id=1, source_target_pairs={{0,2},{1,3},{2,0},{3,1},{4,6},{5,7},{6,4},{7,5},{8,10},{9,11},{10,... | collective-permute-start | bytes 3932168 | tf_op jit(solution)/shard_map/ppermute | solution.py:38
  50.3 11.5 %collective-permute-start.10 = (bf16[512,512]{1,0:T(8,128)(2,1)S(1)}, bf16[512,512]{1,0:T(8,128)(2,1)S(1)}, u32[]{:S(2)}, u32[]{:S(2)}) collective-permute-start(bf16[512,512]{1,0:T(8,128)(2,1)S(1)} %collective-permute-done.9.refs_5_), channel_id=1, source_target_pairs={{0,16},{1,5},{2,18},{3,7},{4,20},{5,9},{6,22},{7,11},{8,24},{9,13}... | collective-permute-start | bytes 1572872 | tf_op jit(solution)/shard_map/ppermute | solution.py:38
  50.6 75.5 %collective-permute-start.21 = (bf16[640,1280]{1,0:T(8,128)(2,1)S(1)}, bf16[640,1280]{1,0:T(8,128)(2,1)S(1)}, u32[]{:S(2)}, u32[]{:S(2)}) collective-permute-start(bf16[640,1280]{1,0:T(8,128)(2,1)S(1)} %get-tuple-element.68), channel_id=1, source_target_pairs={{0,1},{1,0},{2,3},{3,2},{4,5},{5,4},{6,7},{7,6},{8,9},{9,8},{10,11... | collective-permute-start | bytes 4915208 | tf_op jit(solution)/shard_map/ppermute | solution.py:38
  57.6 68.5 %collective-permute-start.23 = (bf16[640,1280]{1,0:T(8,128)(2,1)S(1)}, bf16[640,1280]{1,0:T(8,128)(2,1)S(1)}, u32[]{:S(2)}, u32[]{:S(2)}) collective-permute-start(bf16[640,1280]{1,0:T(8,128)(2,1)S(1)} %get-tuple-element.70), channel_id=1, source_target_pairs={{0,195},{1,194},{2,65},{3,64},{4,199},{5,198},{6,69},{7,68},{8,203... | collective-permute-start | bytes 4915208 | tf_op jit(solution)/shard_map/ppermute | solution.py:49
  57.6 14.3 %collective-permute-start.18 = (bf16[512,512]{1,0:T(8,128)(2,1)S(1)}, bf16[512,512]{1,0:T(8,128)(2,1)S(1)}, u32[]{:S(2)}, u32[]{:S(2)}) collective-permute-start(bf16[512,512]{1,0:T(8,128)(2,1)S(1)} %collective-permute-done.13.refs_6_), channel_id=1, source_target_pairs={{0,48},{1,13},{2,50},{3,15},{4,52},{5,1},{6,54},{7,3},{8,56},{9,5}... | collective-permute-start | bytes 1572872 | tf_op jit(solution)/shard_map/ppermute | solution.py:38
  61.9 41.5 %collective-permute-start.29 = (bf16[128,1280]{1,0:T(8,128)(2,1)S(1)}, bf16[128,1280]{1,0:T(8,128)(2,1)S(1)}, u32[]{:S(2)}, u32[]{:S(2)}) collective-permute-start(bf16[128,1280]{1,0:T(8,128)(2,1)S(1)} %get-tuple-element.71), channel_id=1, source_target_pairs={{0,194},{1,195},{2,64},{3,65},{4,198},{5,199},{6,68},{7,69},{8,202... | collective-permute-start | bytes 983048 | tf_op jit(solution)/shard_map/ppermute | solution.py:49
  71.9 34.5 %collective-permute-start.25 = (bf16[512,128]{1,0:T(8,128)(2,1)S(1)}, bf16[512,128]{1,0:T(8,128)(2,1)S(1)}, u32[]{:S(2)}, u32[]{:S(2)}) collective-permute-start(bf16[512,128]{1,0:T(8,128)(2,1)S(1)} %get-tuple-element.58), channel_id=1, source_target_pairs={{0,14},{1,51},{2,12},{3,49},{4,2},{5,55},{6,0},{7,53},{8,6},{9,59}... | collective-permute-start | bytes 393224 | tf_op jit(solution)/shard_map/ppermute | solution.py:38
  103.4 5.9 %collective-permute-start.14 = (bf16[512,128]{1,0:T(8,128)(2,1)S(1)}, bf16[512,128]{1,0:T(8,128)(2,1)S(1)}, u32[]{:S(2)}, u32[]{:S(2)}) collective-permute-start(bf16[512,128]{1,0:T(8,128)(2,1)S(1)} %get-tuple-element.58), channel_id=1, source_target_pairs={{0,12},{1,49},{2,14},{3,51},{4,0},{5,53},{6,2},{7,55},{8,4},{9,57}... | collective-permute-start | bytes 393224 | tf_op jit(solution)/shard_map/ppermute | solution.py:38
  106.4 7.7 %collective-permute-start.26 = (bf16[512,128]{1,0:T(8,128)(2,1)S(1)}, bf16[512,128]{1,0:T(8,128)(2,1)S(1)}, u32[]{:S(2)}, u32[]{:S(2)}) collective-permute-start(bf16[512,128]{1,0:T(8,128)(2,1)S(1)} %get-tuple-element.59), channel_id=1, source_target_pairs={{0,10},{1,35},{2,8},{3,33},{4,14},{5,39},{6,12},{7,37},{8,2},{9,43... | collective-permute-start | bytes 393224 | tf_op jit(solution)/shard_map/ppermute | solution.py:38
  109.2 7.2 %collective-permute-start.27 = (bf16[512,128]{1,0:T(8,128)(2,1)S(1)}, bf16[512,128]{1,0:T(8,128)(2,1)S(1)}, u32[]{:S(2)}, u32[]{:S(2)}) collective-permute-start(bf16[512,128]{1,0:T(8,128)(2,1)S(1)} %get-tuple-element.60), channel_id=1, source_target_pairs={{0,6},{1,19},{2,4},{3,17},{4,10},{5,23},{6,8},{7,21},{8,14},{9,27}... | collective-permute-start | bytes 393224 | tf_op jit(solution)/shard_map/ppermute | solution.py:38
  110.2 7.0 %collective-permute-start.15 = (bf16[512,128]{1,0:T(8,128)(2,1)S(1)}, bf16[512,128]{1,0:T(8,128)(2,1)S(1)}, u32[]{:S(2)}, u32[]{:S(2)}) collective-permute-start(bf16[512,128]{1,0:T(8,128)(2,1)S(1)} %get-tuple-element.59), channel_id=1, source_target_pairs={{0,8},{1,33},{2,10},{3,35},{4,12},{5,37},{6,14},{7,39},{8,0},{9,41... | collective-permute-start | bytes 393224 | tf_op jit(solution)/shard_map/ppermute | solution.py:38
  114.2 5.0 %collective-permute-start.16 = (bf16[512,128]{1,0:T(8,128)(2,1)S(1)}, bf16[512,128]{1,0:T(8,128)(2,1)S(1)}, u32[]{:S(2)}, u32[]{:S(2)}) collective-permute-start(bf16[512,128]{1,0:T(8,128)(2,1)S(1)} %get-tuple-element.60), channel_id=1, source_target_pairs={{0,4},{1,17},{2,6},{3,19},{4,8},{5,21},{6,10},{7,23},{8,12},{9,25}... | collective-permute-start | bytes 393224 | tf_op jit(solution)/shard_map/ppermute | solution.py:38
  116.4 5.2 %collective-permute-start.24 = (bf16[512,256]{1,0:T(8,128)(2,1)S(1)}, bf16[512,256]{1,0:T(8,128)(2,1)S(1)}, u32[]{:S(2)}, u32[]{:S(2)}) collective-permute-start(bf16[512,256]{1,0:T(8,128)(2,1)S(1)} %shard_map.95.a_ref), channel_id=1, source_target_pairs={{0,1},{1,0},{2,3},{3,2},{4,5},{5,4},{6,7},{7,6},{8,9},{9,8},{10,11... | collective-permute-start | bytes 786440 | tf_op jit(solution)/shard_map/ppermute | solution.py:38
  117.3 5.9 %collective-permute-start.19 = (bf16[512,256]{1,0:T(8,128)(2,1)S(1)}, bf16[512,256]{1,0:T(8,128)(2,1)S(1)}, u32[]{:S(2)}, u32[]{:S(2)}) collective-permute-start(bf16[512,256]{1,0:T(8,128)(2,1)S(1)} %shard_map.95.a_ref), channel_id=1, source_target_pairs={{0,2},{1,3},{2,0},{3,1},{4,6},{5,7},{6,4},{7,5},{8,10},{9,11},{10,... | collective-permute-start | bytes 786440 | tf_op jit(solution)/shard_map/ppermute | solution.py:38
  119.2 6.9 %collective-permute-start.28 = (bf16[512,384]{1,0:T(8,128)(2,1)S(1)}, bf16[512,384]{1,0:T(8,128)(2,1)S(1)}, u32[]{:S(2)}, u32[]{:S(2)}) collective-permute-start(bf16[512,384]{1,0:T(8,128)(2,1)S(1)} %constant_dynamic-update-slice_fusion.3.c_ref), channel_id=1, source_target_pairs={{0,1},{1,0},{2,3},{3,2},{4,5},{5,4},{6,7},{7,6},{8,9},{9,8},{10,11... | collective-permute-start | bytes 1179656 | tf_op jit(solution)/shard_map/ppermute | solution.py:38
  121.6 6.7 %collective-permute-start.17 = (bf16[512,384]{1,0:T(8,128)(2,1)S(1)}, bf16[512,384]{1,0:T(8,128)(2,1)S(1)}, u32[]{:S(2)}, u32[]{:S(2)}) collective-permute-start(bf16[512,384]{1,0:T(8,128)(2,1)S(1)} %constant_dynamic-update-slice_fusion.a_ref), channel_id=1, source_target_pairs={{0,1},{1,0},{2,3},{3,2},{4,5},{5,4},{6,7},{7,6},{8,9},{9,8},{10,11... | collective-permute-start | bytes 1179656 | tf_op jit(solution)/shard_map/ppermute | solution.py:38
  123.1 5.2 %collective-permute-start.20 = (bf16[512,256]{1,0:T(8,128)(2,1)S(1)}, bf16[512,256]{1,0:T(8,128)(2,1)S(1)}, u32[]{:S(2)}, u32[]{:S(2)}) collective-permute-start(bf16[512,256]{1,0:T(8,128)(2,1)S(1)} %collective-permute-done.19.c_ref), channel_id=1, source_target_pairs={{0,1},{1,0},{2,3},{3,2},{4,5},{5,4},{6,7},{7,6},{8,9},{9,8},{10,11... | collective-permute-start | bytes 786440 | tf_op jit(solution)/shard_map/ppermute | solution.py:38

commit v4 on v3

--- a/solution.py
+++ b/solution.py
@@ -114,38 +114,35 @@
             out_ref[k * rows : (k + 1) * rows, :] = piece[half * rows : (half + 1) * rows, :]
 
 
-def attend(both, key_refs, state):
+def attend(both, key_ref, state):
     query = both[:, HD:]
-    for ref in key_refs:
-        keys = ref[:, : 2 * HD]
-        values = ref[:, 2 * HD :]
-        scores = lax.dot_general(query, keys[:, :HD], NT, preferred_element_type=F32)
-        tangent = lax.dot_general(both, keys, NT, preferred_element_type=F32)
-        top = jnp.max(scores, axis=1, keepdims=True)
-        if state is None:
-            peak = jnp.broadcast_to(top, (scores.shape[0], HD))
-        else:
-            peak_old, total, total_tan, numer, numer_tan = state
-            peak = jnp.maximum(peak_old, top)
-            fade = jnp.exp2((peak_old - peak) * EXP2_SCALE)
-        expo = jnp.exp2((scores - peak[:, :1]) * EXP2_SCALE)
-        expo_tan = expo * tangent
-        cuts = range(0, scores.shape[1], HD)
-        add = sum(expo[:, c : c + HD] for c in cuts)
-        add_tan = sum(expo_tan[:, c : c + HD] for c in cuts)
-        pair = jnp.dot(expo.astype(BF16), values, preferred_element_type=F32)
-        single = jnp.dot(expo_tan.astype(BF16), values[:, :HD], preferred_element_type=F32)
-        if state is None:
-            state = (peak, add, add_tan, pair, single)
-        else:
-            state = (
-                peak,
-                total * fade + add,
-                total_tan * fade + add_tan,
-                numer * jnp.concatenate([fade, fade], axis=1) + pair,
-                numer_tan * fade + single,
-            )
-    return state
+    keys = key_ref[:, : 2 * HD]
+    values = key_ref[:, 2 * HD :]
+    scores = lax.dot_general(query, keys[:, :HD], NT, preferred_element_type=F32)
+    tangent = lax.dot_general(both, keys, NT, preferred_element_type=F32)
+    top = jnp.max(scores, axis=1, keepdims=True)
+    if state is None:
+        peak = jnp.broadcast_to(top, (scores.shape[0], HD))
+    else:
+        peak_old, total, total_tan, numer, numer_tan = state
+        peak = jnp.maximum(peak_old, top)
+        fade = jnp.exp2((peak_old - peak) * EXP2_SCALE)
+    expo = jnp.exp2((scores - peak[:, :1]) * EXP2_SCALE)
+    expo_tan = expo * tangent
+    cuts = range(0, scores.shape[1], HD)
+    add = sum(expo[:, c : c + HD] for c in cuts)
+    add_tan = sum(expo_tan[:, c : c + HD] for c in cuts)
+    pair = jnp.dot(expo.astype(BF16), values, preferred_element_type=F32)
+    single = jnp.dot(expo_tan.astype(BF16), values[:, :HD], preferred_element_type=F32)
+    if state is None:
+        return peak, add, add_tan, pair, single
+    return (
+        peak,
+        total * fade + add,
+        total_tan * fade + add_tan,
+        numer * jnp.concatenate([fade, fade], axis=1) + pair,
+        numer_tan * fade + single,
+    )
 
 
 def finish(state):
@@ -154,49 +151,54 @@
     total_tan = jnp.sum(total_tan, axis=1, keepdims=True) * SCALE
     attended = numer[:, :HD] * inverse
     attended_tan = (numer_tan * SCALE + numer[:, HD:] - attended * total_tan) * inverse
-    return jnp.concatenate([attended, attended_tan], axis=0).astype(BF16)
-
-
-def load_state(ref, tile):
-    cut = [ref[tile, :, c * HD : (c + 1) * HD] for c in range(3)]
-    return (*cut, ref[tile, :, 3 * HD : 5 * HD], ref[tile, :, 5 * HD :])
-
-
-def attend_kernel(tiles, first, joined, *refs):
-    queries, refs = refs[: len(tiles)], refs[len(tiles) :]
-    (shared, own), refs = refs[:2], refs[2:]
-    if not first:
-        state_in, refs = refs[0], refs[1:]
-    for place, tile in enumerate(tiles):
-        state = None if first else load_state(state_in, tile)
-        state = attend(queries[place][...], [shared if tile < NY else own], state)
-        if joined is None:
-            refs[0][tile] = jnp.concatenate(state, axis=1)
-        elif joined:
-            refs[0][:, place * HD : (place + 1) * HD] = finish(state)
-        else:
-            refs[place][...] = finish(state)
-
-
-def attend_step(blocks, shared, own, state, tiles=tuple(range(NY + 1)), joined=None):
-    rows = blocks[0].shape[0]
-    if joined is None:
-        outs = [jax.ShapeDtypeStruct((NY + 1, rows, 6 * HD), F32)]
-    elif joined:
-        outs = [jax.ShapeDtypeStruct((2 * rows, len(tiles) * HD), BF16)]
-    else:
-        outs = [jax.ShapeDtypeStruct((2 * rows, HD), BF16)] * len(tiles)
-    carried = [] if state is None else [state]
-    found = call(
-        functools.partial(attend_kernel, tiles, state is None, joined),
-        outs,
-        *[blocks[tile] for tile in tiles],
-        shared,
-        own,
-        *carried,
-        flops=len(tiles) * rows * shared.shape[0] * 1792,
-    )
-    return found if joined is False else found[0]
+    return attended.astype(BF16), attended_tan.astype(BF16)
+
+
+def load_state(ref, rows):
+    cut = [ref[rows, c * HD : (c + 1) * HD] for c in range(3)]
+    return (*cut, ref[rows, 3 * HD : 5 * HD], ref[rows, 5 * HD :])
+
+
+def attend_kernel(first, shared_ref, own_ref, shared_keys, own_keys, *refs):
+    sides = ((shared_ref, shared_keys, refs[-2]), (own_ref, own_keys, refs[-1]))
+    for side, (query, keys, out_ref) in enumerate(sides):
+        state = None if first else load_state(refs[side], slice(None))
+        out_ref[...] = jnp.concatenate(attend(query[...], keys, state), axis=1)
+
+
+def attend_step(queries, keys, state):
+    rows = [query.shape[0] for query in queries]
+    return call(
+        functools.partial(attend_kernel, not state),
+        [jax.ShapeDtypeStruct((n, 6 * HD), F32) for n in rows],
+        *queries,
+        *keys,
+        *state,
+        flops=sum(rows) * keys[0].shape[0] * 1792,
+    )
+
+
+def attend_others_kernel(query_ref, keys, state_ref, *out_refs):
+    rows = out_refs[0].shape[0] // 2
+    most = slice(0, rows * len(out_refs))
+    attended, attended_tan = finish(attend(query_ref[most, :], keys, load_state(state_ref, most)))
+    for place, ref in enumerate(out_refs):
+        ref[:rows, :] = attended[place * rows : (place + 1) * rows]
+        ref[rows:, :] = attended_tan[place * rows : (place + 1) * rows]
+
+
+def attend_kept_kernel(shared_ref, own_ref, shared_keys, own_keys, shared_state, own_state, out_ref):
+    rows = own_ref.shape[0]
+    start = shared_ref.shape[0] - rows
+    sides = (
+        (shared_ref, shared_keys, shared_state, slice(start, start + rows)),
+        (own_ref, own_keys, own_state, slice(0, rows)),
+    )
+    for side, (query, keys, state, part) in enumerate(sides):
+        lanes = slice(side * HD, (side + 1) * HD)
+        attended, attended_tan = finish(attend(query[part, :], keys, load_state(state, part)))
+        out_ref[:rows, lanes] = attended
+        out_ref[rows:, lanes] = attended_tan
 
 
 def cut_weight_kernel(y_ref, place_ref, w_ref, *refs):
@@ -220,57 +222,65 @@
         copy.wait()
 
 
-def project_sum(pairs, lanes=slice(None)):
+def project_sum(operands, terms, lanes=slice(None)):
     total = None
-    for ref, columns, weight, row in pairs:
-        low, high = columns
-        rows = slice(row, row + high - low)
-        part = jnp.dot(ref[:, low:high], weight[rows, lanes], preferred_element_type=F32)
+    for ref, low, high, weight, row in terms:
+        part = jnp.dot(
+            operands[ref][:, low:high],
+            operands[weight][row : row + high - low, lanes],
+            preferred_element_type=F32,
+        )
         total = part if total is None else total + part
     return total
 
 
-OWN, REST, MOST = (0, 2 * HD), (0, 3 * HD), (0, 2 * HD)
-
-
-def project_first_kernel(a_ref, b_ref, c_ref, d_ref, wa_ref, wb_ref, wc_ref, wm_ref, wd_ref, out_ref):
-    out_ref[...] = project_sum(
-        (
-            (a_ref, OWN, wa_ref, 0),
-            (b_ref, OWN, wb_ref, 0),
-            (c_ref, MOST, wc_ref, 2 * HD),
-            (c_ref, (2 * HD, 3 * HD), wm_ref, 0),
-            (d_ref, REST, wd_ref, 2 * HD),
-        )
-    )
-
-
-def project_last_kernel(a_ref, b_ref, c_ref, d_ref, wa_ref, wb_ref, wc_ref, wd_ref, sum_ref, out_ref, tan_ref):
-    rows, tile = out_ref.shape
-    lanes = pl.ds(pl.multiple_of(pl.program_id(0) * tile, tile), tile)
-    total = sum_ref[:, lanes] + project_sum(
-        (
-            (a_ref, REST, wa_ref, 2 * HD),
-            (b_ref, REST, wb_ref, 2 * HD),
-            (c_ref, OWN, wc_ref, 0),
-            (d_ref, OWN, wd_ref, 0),
-        ),
-        lanes,
-    )
-    out_ref[...] = total[:rows].astype(BF16)
-    tan_ref[...] = total[rows:].astype(BF16)
-
-
-def project_last(*operands):
+def project_kernel(terms, *refs):
+    out_ref = refs[-1]
+    total = project_sum(refs, terms)
+    if len(refs) - 1 > 1 + max(term[3] for term in terms):
+        total = total + refs[-2][...]
+    out_ref[...] = total
+
+
+def project_part(terms, *operands):
+    shape = (operands[0].shape[0], operands[-1].shape[1])
+    kernel = functools.partial(project_kernel, terms)
+    return call(
+        kernel,
+        jax.ShapeDtypeStruct(shape, F32),
+        *operands,
+        flops=2 * shape[0] * shape[1] * sum(term[2] - term[1] for term in terms),
+    )
+
+
+def project_last_kernel(terms, *refs):
+    operands, (out_ref, tan_ref, held_ref, sems) = refs[:-4], refs[-4:]
+    rows, columns = out_ref.shape
+    copies = []
+    for place, start in enumerate(range(0, columns, 2 * HD)):
+        lanes = slice(start, start + 2 * HD)
+        total = operands[-1][:, lanes] + project_sum(operands, terms, lanes)
+        held_ref[:, lanes] = total.astype(BF16)
+        for half, ref in enumerate((out_ref, tan_ref)):
+            source = held_ref.at[half * rows : (half + 1) * rows, lanes]
+            copy = pltpu.make_async_copy(source, ref.at[:, lanes], sems.at[half, place])
+            copy.start()
+            copies.append(copy)
+    for copy in copies:
+        copy.wait()
+
+
+def project_last(terms, *operands):
     rows, columns = operands[-1].shape
-    tile = 256
-    half = pl.BlockSpec((rows // 2, tile), lambda j: (0, j))
     return pl.pallas_call(
-        project_last_kernel,
-        grid=(columns // tile,),
+        functools.partial(project_last_kernel, terms),
         in_specs=[VMEM] * len(operands),
-        out_specs=[half, half],
+        out_specs=[HBM, HBM],
         out_shape=[jax.ShapeDtypeStruct((rows // 2, columns), BF16)] * 2,
+        scratch_shapes=[
+            pltpu.VMEM((rows, columns), BF16),
+            pltpu.SemaphoreType.DMA((2, columns // (2 * HD))),
+        ],
         name="project_last",
         compiler_params=pltpu.CompilerParams(vmem_limit_bytes=16 << 20),
     )(*operands)
@@ -312,7 +322,8 @@
         specs=[SMEM, HBM, HBM],
         scratch_shapes=[pltpu.VMEM((2, rows, width), BF16), pltpu.SemaphoreType.DMA((2,))],
     )
-    blocks = [sends[0]] + [shift(sends[k], swap=k) for k in (1, 2, 3)] + [sends[NY]]
+    others = [shift(sends[k], swap=k) for k in (1, 2, 3)]
+    blocks = [jnp.concatenate([*others, sends[0]]), sends[NY]]
 
     place, _ = lax.optimization_barrier((place, sends[1]))
     cuts = call(
@@ -352,12 +363,26 @@
     right = [shift(own[0], ring=-1), shift(own[1], ring=-1)]
     opposite = [shift(left[0], ring=1), shift(right[1], ring=-1)]
 
-    state = attend_step(blocks, own[0], own[1], None)
-    state = attend_step(blocks, left[0], right[1], state)
-    state = attend_step(blocks, right[0], left[1], state)
-    others = attend_step(blocks, opposite[0], opposite[0], state, (1, 2, 3), False)
+    state = attend_step(blocks, own, ())
+    state = attend_step(blocks, (left[0], right[1]), state)
+    state = attend_step(blocks, (right[0], left[1]), state)
+    others = call(
+        attend_others_kernel,
+        [jax.ShapeDtypeStruct((2 * rows, HD), BF16)] * (NY - 1),
+        blocks[0],
+        opposite[0],
+        state[0],
+        flops=3 * rows * opposite[0].shape[0] * 1792,
+    )
     opposite[1], _ = lax.optimization_barrier((opposite[1], others[0]))
-    kept = attend_step(blocks, opposite[0], opposite[1], state, (0, NY), True)
+    kept = call(
+        attend_kept_kernel,
+        jax.ShapeDtypeStruct((2 * rows, 2 * HD), BF16),
+        *blocks,
+        *opposite,
+        *state,
+        flops=2 * rows * opposite[0].shape[0] * 1792,
+    )
 
     near = [
         shift(kept, zl=1),
@@ -366,21 +391,41 @@
     mine = [kept, jnp.concatenate([shift(others[k - 1], swap=-k) for k in (1, 2, 3)], axis=1)]
     sibling = [shift(mine[n], core=1) for n in range(2)]
     far = [shift(near[n], core=1) for n in range(2)]
-    weights = (cuts[0], weight_core, weight_near)
-    partial = call(
-        project_first_kernel,
-        jax.ShapeDtypeStruct((2 * rows, columns), F32),
+    own, rest, cut = 2 * HD, 3 * HD, width - HD
+    partial = project_part(
+        (
+            (0, 0, own, 3, 0),
+            (1, 0, own, 4, 0),
+            (2, 0, cut - own, 5, own),
+            (2, cut - own, rest, 6, 0),
+        ),
         mine[0],
         sibling[0],
         near[1],
+        cuts[0],
+        weight_core,
+        weight_near,
+        weight_more,
+    )
+    partial = project_part(
+        ((0, 0, rest, 3, own), (1, 0, rest, 4, own), (2, 0, own, 5, 0)),
         far[1],
-        *weights,
-        weight_more,
+        mine[1],
+        near[0],
         weight_far,
-        flops=8 * rows * width * columns,
+        cuts[0],
+        weight_near,
+        partial,
     )
     return tuple(
-        project_last(mine[1], sibling[1], near[0], far[0], *weights, weight_far, partial)
+        project_last(
+            ((0, 0, rest, 2, own), (1, 0, own, 3, 0)),
+            sibling[1],
+            far[0],
+            weight_core,
+            weight_far,
+            partial,
+        )
     )
 
 

time: 132 us -> 135 us (1.023)
  waiting for transfers between devices: 47.5 us -> 55.3 us
  starting transfers between devices: 61.8 us -> 58.9 us
  Pallas kernels: 21.8 us -> 19.1 us
    ppermute x28, waiting for transfers between devices: 18.7 us -> 22.8 us  [shift(): return lax.ppermute(array, AXES, pairs)]
    ppermute x2, waiting for transfers between devices: 28.8 us -> 32.5 us  [across(): return lax.ppermute(array, AXES, pairs)]
    ppermute x28, starting transfers between devices: 59 us -> 56.1 us  [shift(): return lax.ppermute(array, AXES, pairs)]
    pallas_call x1, Pallas kernels: 3.82 us -> 2.08 us  [project_last(): pl.pallas_call(functools.partial(project_last_kernel, terms), in_specs=[V...]
    pallas_call x11 -> x12, Pallas kernels: 18 us -> 17 us  [called(): pl.pallas_call(kernel, out_shape=outs, in_specs=specs or [VMEM] * len(ope...]
  transfers between devices with their start and end apart: 30 -> 30, of which waited for: 11 -> 12; matrix products, arithmetic and copies ran while one was open for 0% -> 0% of each run, Pallas kernels for 13% -> 12%
where the time goes in v4:
time: 135 us
  starting transfers between devices  58.9 us (44%)
  waiting for transfers between devices  55.3 us (41%)
  Pallas kernels  19.1 us (14%)
    ppermute x28, starting transfers between devices, shift(): return lax.ppermute(array, AXES, pairs)  56.1 us
    ppermute x2, waiting for transfers between devices, across(): return lax.ppermute(array, AXES, pairs)  32.5 us
    ppermute x28, waiting for transfers between devices, shift(): return lax.ppermute(array, AXES, pairs)  22.8 us
    pallas_call x12, Pallas kernels, called(): pl.pallas_call(kernel, out_shape=outs, in_specs=specs or [VMEM] * len(ope...  17 us
    ppermute x2, starting transfers between devices, across(): return lax.ppermute(array, AXES, pairs)  2.84 us
  transfers between devices with their start and end apart: 30, of which 12 were waited for; matrix products, arithmetic and copies ran while one was open for 0% of the time, Pallas kernels for 12%

profile of v4, /device:TPU:1, one launch (start us, length us, event | category | flops | bytes accessed | tf_op | source)
XLA Modules:
  0.0 134.6 jit_solution(12525641214119039429)
XLA Ops:
  0.6 0.9 shard_map.87.refs_0_
  1.5 3.9 %collective-permute-start.3 = (bf16[5,32,512]{2,1,0:T(8,128)(2,1)S(1)}, bf16[5,32,512]{2,1,0:T(8,128)(2,1)S(1)}, u32[]{:S(2)}, u32[]{:S(2)}) collective-permute-start(bf16[5,32,512]{2,1,0:T(8,128)(2,1)S(1)} %shard_map.87.refs_0_), channel_id=1, source_target_pairs={{0,64},{1,65},{2,66},{3,67},{4,68},{5,69},{6,70},{7,71},{8,72},{9,... | collective-permute-start | bytes 491528 | tf_op jit(solution)/shard_map/ppermute | solution.py:38
  5.4 3.1 %collective-permute-start.4 = (bf16[5,32,512]{2,1,0:T(8,128)(2,1)S(1)}, bf16[5,32,512]{2,1,0:T(8,128)(2,1)S(1)}, u32[]{:S(2)}, u32[]{:S(2)}) collective-permute-start(bf16[5,32,512]{2,1,0:T(8,128)(2,1)S(1)} %shard_map.87.refs_0_), channel_id=1, source_target_pairs={{0,192},{1,193},{2,194},{3,195},{4,196},{5,197},{6,198},{7,199},{8... | collective-permute-start | bytes 491528 | tf_op jit(solution)/shard_map/ppermute | solution.py:38
  8.5 4.4 %collective-permute-start.5 = (bf16[5,32,512]{2,1,0:T(8,128)(2,1)S(1)}, bf16[5,32,512]{2,1,0:T(8,128)(2,1)S(1)}, u32[]{:S(2)}, u32[]{:S(2)}) collective-permute-start(bf16[5,32,512]{2,1,0:T(8,128)(2,1)S(1)} %shard_map.87.refs_0_), channel_id=1, source_target_pairs={{0,128},{1,129},{2,130},{3,131},{4,132},{5,133},{6,134},{7,135},{8... | collective-permute-start | bytes 491528 | tf_op jit(solution)/shard_map/ppermute | solution.py:38
  12.9 1.2 shard_map.86
  14.1 3.1 %shard_map.88 = (bf16[640,1280]{1,0:T(8,128)(2,1)S(1)}, bf16[640,1280]{1,0:T(8,128)(2,1)S(1)}, bf16[512,1280]{1,0:T(8,128)(2,1)S(1)}, bf16[640,1280]{1,0:T(8,128)(2,1)S(1)}, bf16[128,1280]{1,0:T(8,128)(2,1)S(1)}) custom-call(s32[1]{0:T(128)S(6)} %select_n.27.y_ref, s32[1]{0:T(128)} %bitcast.place_ref, bf16[640,5120]{1,0:T(8,128)(2,1)} %w_ref.1), custom_call_target="tpu_custom_call" | custom-call | bytes 6553608 | tf_op jit(solution)/shard_map/pallas_call | solution.py:57
  17.2 3.7 %collective-permute-done.4.refs_2_ = bf16[5,32,512]{2,1,0:T(8,128)(2,1)S(1)} collective-permute-done((bf16[5,32,512]{2,1,0:T(8,128)(2,1)S(1)}, bf16[5,32,512]{2,1,0:T(8,128)(2,1)S(1)}, u32[]{:S(2)}, u32[]{:S(2)}) %collective-permute-start.4) | collective-permute-done | bytes 163872 | tf_op jit(solution)/shard_map/ppermute | solution.py:38
  21.0 0.9 collective-permute-done.5.refs_3_
  21.9 1.3 collective-permute-start.6
  23.2 1.5 %collective-permute-start.7 = (bf16[256,512]{1,0:T(8,128)(2,1)S(1)}, bf16[256,512]{1,0:T(8,128)(2,1)S(1)}, u32[]{:S(2)}, u32[]{:S(2)}) collective-permute-start(bf16[256,512]{1,0:T(8,128)(2,1)S(1)} %get-tuple-element.59), channel_id=1, source_target_pairs={{0,12},{1,49},{2,14},{3,51},{4,0},{5,53},{6,2},{7,55},{8,4},{9,57}... | collective-permute-start | bytes 786440 | tf_op jit(solution)/shard_map/ppermute | solution.py:38
  24.6 1.5 %collective-permute-start.8 = (bf16[256,512]{1,0:T(8,128)(2,1)S(1)}, bf16[256,512]{1,0:T(8,128)(2,1)S(1)}, u32[]{:S(2)}, u32[]{:S(2)}) collective-permute-start(bf16[256,512]{1,0:T(8,128)(2,1)S(1)} %get-tuple-element.60), channel_id=1, source_target_pairs={{0,8},{1,33},{2,10},{3,35},{4,12},{5,37},{6,14},{7,39},{8,0},{9,41... | collective-permute-start | bytes 786440 | tf_op jit(solution)/shard_map/ppermute | solution.py:38
  26.2 2.2 %collective-permute-done.6.refs_1_ = bf16[256,512]{1,0:T(8,128)(2,1)S(1)} collective-permute-done((bf16[256,512]{1,0:T(8,128)(2,1)S(1)}, bf16[256,512]{1,0:T(8,128)(2,1)S(1)}, u32[]{:S(2)}, u32[]{:S(2)}) %collective-permute-start.6) | collective-permute-done | bytes 262176 | tf_op jit(solution)/shard_map/ppermute | solution.py:38
  28.4 3.8 %collective-permute-done.8.refs_3_ = bf16[256,512]{1,0:T(8,128)(2,1)S(1)} collective-permute-done((bf16[256,512]{1,0:T(8,128)(2,1)S(1)}, bf16[256,512]{1,0:T(8,128)(2,1)S(1)}, u32[]{:S(2)}, u32[]{:S(2)}) %collective-permute-start.8) | collective-permute-done | bytes 262176 | tf_op jit(solution)/shard_map/ppermute | solution.py:38
  32.3 1.4 %collective-permute-start.9 = (bf16[512,512]{1,0:T(8,128)(2,1)S(1)}, bf16[512,512]{1,0:T(8,128)(2,1)S(1)}, u32[]{:S(2)}, u32[]{:S(2)}) collective-permute-start(bf16[512,512]{1,0:T(8,128)(2,1)S(1)} %get-tuple-element.61.shared_keys), channel_id=1, source_target_pairs={{0,16},{1,5},{2,18},{3,7},{4,20},{5,9},{6,22},{7,11},{8,24},{9,13}... | collective-permute-start | bytes 1572872 | tf_op jit(solution)/shard_map/ppermute | solution.py:38
  33.6 0.9 collective-permute-start
  34.5 1.8 %collective-permute-start.13 = (bf16[512,512]{1,0:T(8,128)(2,1)S(1)}, bf16[512,512]{1,0:T(8,128)(2,1)S(1)}, u32[]{:S(2)}, u32[]{:S(2)}) collective-permute-start(bf16[512,512]{1,0:T(8,128)(2,1)S(1)} %get-tuple-element.63.own_keys), channel_id=1, source_target_pairs={{0,48},{1,13},{2,50},{3,15},{4,52},{5,1},{6,54},{7,3},{8,56},{9,5}... | collective-permute-start | bytes 1572872 | tf_op jit(solution)/shard_map/ppermute | solution.py:38
  36.3 2.0 %collective-permute-start.1 = (bf16[256,256]{1,0:T(8,128)(2,1)S(1)}, bf16[256,256]{1,0:T(8,128)(2,1)S(1)}, u32[]{:S(2)}, u32[]{:S(2)}) collective-permute-start(bf16[256,256]{1,0:T(8,128)(2,1)S(1)} %get-tuple-element.44), channel_id=1, source_target_pairs={{0,8},{1,33},{2,10},{3,35},{4,12},{5,37},{6,14},{7,39},{8,0},{9,41... | collective-permute-start | bytes 393224 | tf_op jit(solution)/shard_map/ppermute | solution.py:38
  38.4 1.4 %collective-permute-start.11 = (bf16[512,512]{1,0:T(8,128)(2,1)S(1)}, bf16[512,512]{1,0:T(8,128)(2,1)S(1)}, u32[]{:S(2)}, u32[]{:S(2)}) collective-permute-start(bf16[512,512]{1,0:T(8,128)(2,1)S(1)} %get-tuple-element.61.shared_keys), channel_id=1, source_target_pairs={{0,48},{1,13},{2,50},{3,15},{4,52},{5,1},{6,54},{7,3},{8,56},{9,5}... | collective-permute-start | bytes 1572872 | tf_op jit(solution)/shard_map/ppermute | solution.py:38
  40.0 1.7 %collective-permute-done.1 = bf16[256,256]{1,0:T(8,128)(2,1)S(1)} collective-permute-done((bf16[256,256]{1,0:T(8,128)(2,1)S(1)}, bf16[256,256]{1,0:T(8,128)(2,1)S(1)}, u32[]{:S(2)}, u32[]{:S(2)}) %collective-permute-start.1) | collective-permute-done | bytes 131104 | tf_op jit(solution)/shard_map/ppermute | solution.py:38
  41.7 1.7 %collective-permute-start.2 = (bf16[256,256]{1,0:T(8,128)(2,1)S(1)}, bf16[256,256]{1,0:T(8,128)(2,1)S(1)}, u32[]{:S(2)}, u32[]{:S(2)}) collective-permute-start(bf16[256,256]{1,0:T(8,128)(2,1)S(1)} %get-tuple-element.45), channel_id=1, source_target_pairs={{0,12},{1,49},{2,14},{3,51},{4,0},{5,53},{6,2},{7,55},{8,4},{9,57}... | collective-permute-start | bytes 393224 | tf_op jit(solution)/shard_map/ppermute | solution.py:38
  43.5 3.8 %collective-permute-done.2 = bf16[256,256]{1,0:T(8,128)(2,1)S(1)} collective-permute-done((bf16[256,256]{1,0:T(8,128)(2,1)S(1)}, bf16[256,256]{1,0:T(8,128)(2,1)S(1)}, u32[]{:S(2)}, u32[]{:S(2)}) %collective-permute-start.2) | collective-permute-done | bytes 131104 | tf_op jit(solution)/shard_map/ppermute | solution.py:38
  47.2 7.1 %collective-permute-start.27 = (bf16[512,1280]{1,0:T(8,128)(2,1)S(1)}, bf16[512,1280]{1,0:T(8,128)(2,1)S(1)}, u32[]{:S(2)}, u32[]{:S(2)}) collective-permute-start(bf16[512,1280]{1,0:T(8,128)(2,1)S(1)} %get-tuple-element.82), channel_id=1, source_target_pairs={{0,2},{1,3},{2,0},{3,1},{4,6},{5,7},{6,4},{7,5},{8,10},{9,11},{10,... | collective-permute-start | bytes 3932168 | tf_op jit(solution)/shard_map/ppermute | solution.py:38
  54.3 0.4 collective-permute-start.10
  54.8 4.9 %collective-permute-start.21 = (bf16[640,1280]{1,0:T(8,128)(2,1)S(1)}, bf16[640,1280]{1,0:T(8,128)(2,1)S(1)}, u32[]{:S(2)}, u32[]{:S(2)}) collective-permute-start(bf16[640,1280]{1,0:T(8,128)(2,1)S(1)} %get-tuple-element.79), channel_id=1, source_target_pairs={{0,1},{1,0},{2,3},{3,2},{4,5},{5,4},{6,7},{7,6},{8,9},{9,8},{10,11... | collective-permute-start | bytes 4915208 | tf_op jit(solution)/shard_map/ppermute | solution.py:38
  59.7 0.3 collective-permute-start.22
  60.0 2.0 %collective-permute-start.18 = (bf16[512,512]{1,0:T(8,128)(2,1)S(1)}, bf16[512,512]{1,0:T(8,128)(2,1)S(1)}, u32[]{:S(2)}, u32[]{:S(2)}) collective-permute-start(bf16[512,512]{1,0:T(8,128)(2,1)S(1)} %collective-permute-done.13.own_keys), channel_id=1, source_target_pairs={{0,48},{1,13},{2,50},{3,15},{4,52},{5,1},{6,54},{7,3},{8,56},{9,5}... | collective-permute-start | bytes 1572872 | tf_op jit(solution)/shard_map/ppermute | solution.py:38
  62.1 1.8 %shard_map.91 = (f32[1024,768]{1,0:T(8,128)S(1)}, f32[256,768]{1,0:T(8,128)S(1)}) custom-call(bf16[1024,256]{1,0:T(8,128)(2,1)S(1)} %constant_dynamic-update-slice_fusion.shared_ref.query_ref, bf16[256,256]{1,0:T(8,128)(2,1)S(1)} %get-tuple-element.62.own_ref, bf16[512,512]{1,0:T(8,128)(2,1)S(1)} %get-tuple-element.61.shared_keys, ...), custom_call_target="tpu_custom_call" | custom-call | flops 1174405120 | bytes 1703936 | tf_op jit(solution)/shard_map/pallas_call | solution.py:57
  63.9 2.6 %collective-permute-start.29 = (bf16[128,1280]{1,0:T(8,128)(2,1)S(1)}, bf16[128,1280]{1,0:T(8,128)(2,1)S(1)}, u32[]{:S(2)}, u32[]{:S(2)}) collective-permute-start(bf16[128,1280]{1,0:T(8,128)(2,1)S(1)} %get-tuple-element.83), channel_id=1, source_target_pairs={{0,194},{1,195},{2,64},{3,65},{4,198},{5,199},{6,68},{7,69},{8,202... | collective-permute-start | bytes 983048 | tf_op jit(solution)/shard_map/ppermute | solution.py:49
  66.4 2.0 %shard_map.92 = (f32[1024,768]{1,0:T(8,128)S(1)}, f32[256,768]{1,0:T(8,128)S(1)}) custom-call(bf16[1024,256]{1,0:T(8,128)(2,1)S(1)} %constant_dynamic-update-slice_fusion.shared_ref.query_ref, bf16[256,256]{1,0:T(8,128)(2,1)S(1)} %get-tuple-element.62.own_ref, bf16[512,512]{1,0:T(8,128)(2,1)S(1)} %collective-permute-done.9.shared_keys, ...), custom_call_target="tpu_custom_call" | custom-call | flops 1174405120 | bytes 5636096 | tf_op jit(solution)/shard_map/pallas_call | solution.py:57
  68.4 2.0 %shard_map.93 = (f32[1024,768]{1,0:T(8,128)S(1)}, f32[256,768]{1,0:T(8,128)S(1)}) custom-call(bf16[1024,256]{1,0:T(8,128)(2,1)S(1)} %constant_dynamic-update-slice_fusion.shared_ref.query_ref, bf16[256,256]{1,0:T(8,128)(2,1)S(1)} %get-tuple-element.62.own_ref, bf16[512,512]{1,0:T(8,128)(2,1)S(1)} %collective-permute-done.11.shared_keys, ...), custom_call_target="tpu_custom_call" | custom-call | flops 1174405120 | bytes 5636096 | tf_op jit(solution)/shard_map/pallas_call | solution.py:57
  70.4 1.4 %shard_map.94 = (bf16[512,128]{1,0:T(8,128)(2,1)S(1)}, bf16[512,128]{1,0:T(8,128)(2,1)S(1)}, bf16[512,128]{1,0:T(8,128)(2,1)S(1)}) custom-call(bf16[1024,256]{1,0:T(8,128)(2,1)S(1)} %constant_dynamic-update-slice_fusion.shared_ref.query_ref, bf16[512,512]{1,0:T(8,128)(2,1)S(1)} %collective-permute-done.10.keys.shared_keys, ...), custom_call_target="tpu_custom_call" | custom-call | flops 704643072 | bytes 4194304 | tf_op jit(solution)/shard_map/pallas_call | solution.py:57
  71.8 1.0 collective-permute-start.23
  72.8 32.5 %collective-permute-done.29.refs_6_ = bf16[128,1280]{1,0:T(8,128)(2,1)S(1)} collective-permute-done((bf16[128,1280]{1,0:T(8,128)(2,1)S(1)}, bf16[128,1280]{1,0:T(8,128)(2,1)S(1)}, u32[]{:S(2)}, u32[]{:S(2)}) %collective-permute-start.29) | collective-permute-done | bytes 327712 | tf_op jit(solution)/shard_map/ppermute | solution.py:49
  105.3 1.9 %collective-permute-start.14 = (bf16[512,128]{1,0:T(8,128)(2,1)S(1)}, bf16[512,128]{1,0:T(8,128)(2,1)S(1)}, u32[]{:S(2)}, u32[]{:S(2)}) collective-permute-start(bf16[512,128]{1,0:T(8,128)(2,1)S(1)} %get-tuple-element.69), channel_id=1, source_target_pairs={{0,12},{1,49},{2,14},{3,51},{4,0},{5,53},{6,2},{7,55},{8,4},{9,57}... | collective-permute-start | bytes 393224 | tf_op jit(solution)/shard_map/ppermute | solution.py:38
  107.2 1.2 shard_map.95.refs_0_
  108.5 0.6 collective-permute-done.14
  109.1 1.0 collective-permute-start.25
  110.2 3.4 %collective-permute-start.15 = (bf16[512,128]{1,0:T(8,128)(2,1)S(1)}, bf16[512,128]{1,0:T(8,128)(2,1)S(1)}, u32[]{:S(2)}, u32[]{:S(2)}) collective-permute-start(bf16[512,128]{1,0:T(8,128)(2,1)S(1)} %get-tuple-element.70), channel_id=1, source_target_pairs={{0,8},{1,33},{2,10},{3,35},{4,12},{5,37},{6,14},{7,39},{8,0},{9,41... | collective-permute-start | bytes 393224 | tf_op jit(solution)/shard_map/ppermute | solution.py:38
  113.6 2.1 %collective-permute-done.24 = bf16[512,128]{1,0:T(8,128)(2,1)S(1)} collective-permute-done((bf16[512,128]{1,0:T(8,128)(2,1)S(1)}, bf16[512,128]{1,0:T(8,128)(2,1)S(1)}, u32[]{:S(2)}, u32[]{:S(2)}) %collective-permute-start.24) | collective-permute-done | bytes 131104 | tf_op jit(solution)/shard_map/ppermute | solution.py:38
  115.7 0.8 collective-permute-done.25
  116.5 3.5 %collective-permute-start.28 = (bf16[512,256]{1,0:T(8,128)(2,1)S(1)}, bf16[512,256]{1,0:T(8,128)(2,1)S(1)}, u32[]{:S(2)}, u32[]{:S(2)}) collective-permute-start(bf16[512,256]{1,0:T(8,128)(2,1)S(1)} %shard_map.95.refs_0_), channel_id=1, source_target_pairs={{0,1},{1,0},{2,3},{3,2},{4,5},{5,4},{6,7},{7,6},{8,9},{9,8},{10,11... | collective-permute-start | bytes 786440 | tf_op jit(solution)/shard_map/ppermute | solution.py:38
  120.2 0.5 collective-permute-done.16
  120.7 4.0 %collective-permute-start.26 = (bf16[512,384]{1,0:T(8,128)(2,1)S(1)}, bf16[512,384]{1,0:T(8,128)(2,1)S(1)}, u32[]{:S(2)}, u32[]{:S(2)}) collective-permute-start(bf16[512,384]{1,0:T(8,128)(2,1)S(1)} %constant_dynamic-update-slice_fusion.7.refs_2_), channel_id=1, source_target_pairs={{0,1},{1,0},{2,3},{3,2},{4,5},{5,4},{6,7},{7,6},{8,9},{9,8},{10,11... | collective-permute-start | bytes 1179656 | tf_op jit(solution)/shard_map/ppermute | solution.py:38
  124.9 2.6 %collective-permute-done.19.refs_2_ = bf16[512,256]{1,0:T(8,128)(2,1)S(1)} collective-permute-done((bf16[512,256]{1,0:T(8,128)(2,1)S(1)}, bf16[512,256]{1,0:T(8,128)(2,1)S(1)}, u32[]{:S(2)}, u32[]{:S(2)}) %collective-permute-start.19) | collective-permute-done | bytes 262176 | tf_op jit(solution)/shard_map/ppermute | solution.py:38
  127.5 1.4 %collective-permute-start.20 = (bf16[512,256]{1,0:T(8,128)(2,1)S(1)}, bf16[512,256]{1,0:T(8,128)(2,1)S(1)}, u32[]{:S(2)}, u32[]{:S(2)}) collective-permute-start(bf16[512,256]{1,0:T(8,128)(2,1)S(1)} %collective-permute-done.19.refs_2_), channel_id=1, source_target_pairs={{0,1},{1,0},{2,3},{3,2},{4,5},{5,4},{6,7},{7,6},{8,9},{9,8},{10,11... | collective-permute-start | bytes 786440 | tf_op jit(solution)/shard_map/ppermute | solution.py:38
  128.9 1.5 %shard_map.96.refs_6_ = f32[512,1280]{1,0:T(8,128)S(1)} custom-call(bf16[512,256]{1,0:T(8,128)(2,1)S(1)} %shard_map.95.refs_0_, bf16[512,256]{1,0:T(8,128)(2,1)S(1)} %collective-permute-done.28.refs_1_, bf16[512,384]{1,0:T(8,128)(2,1)S(1)} %constant_dynamic-update-slice_fusion.7.refs_2_, bf16[640,1280]{1,0:T(8,128)(2,1)S(1)} %get-tuple-element.81.refs_3_.refs_4_, ...), custom_call_target="tpu_custom_call" | custom-call | flops 1174405120 | bytes 5832704 | tf_op jit(solution)/shard_map/pallas_call | solution.py:57
  130.5 1.8 %shard_map.97.refs_4_ = f32[512,1280]{1,0:T(8,128)S(1)} custom-call(bf16[512,384]{1,0:T(8,128)(2,1)S(1)} %collective-permute-done.26.refs_0_, bf16[512,384]{1,0:T(8,128)(2,1)S(1)} %constant_dynamic-update-slice_fusion.4.refs_1_, bf16[512,256]{1,0:T(8,128)(2,1)S(1)} %collective-permute-done.19.refs_2_, bf16[640,1280]{1,0:T(8,128)(2,1)S(1)} %collective-permute-done.22.refs_3_, ...), custom_call_target="tpu_custom_call" | custom-call | flops 1342177280 | bytes 8257536 | tf_op jit(solution)/shard_map/pallas_call | solution.py:57
  132.3 2.1 %project_last.1 = (bf16[256,1280]{1,0:T(8,128)(2,1)}, bf16[256,1280]{1,0:T(8,128)(2,1)}) custom-call(bf16[512,384]{1,0:T(8,128)(2,1)S(1)} %collective-permute-done.17.refs_0_, bf16[512,256]{1,0:T(8,128)(2,1)S(1)} %collective-permute-done.20.refs_1_, bf16[640,1280]{1,0:T(8,128)(2,1)S(1)} %collective-permute-done.21.refs_4_.refs_2_, ...), custom_call_target="tpu_custom_call" | custom-call | tf_op jit(solution)/shard_map/project_last/pallas_call | solution.py:275
  (35 shorter events, 0.9 us)
Async XLA Ops:
  1.5 15.7 %collective-permute-start.3 = (bf16[5,32,512]{2,1,0:T(8,128)(2,1)S(1)}, bf16[5,32,512]{2,1,0:T(8,128)(2,1)S(1)}, u32[]{:S(2)}, u32[]{:S(2)}) collective-permute-start(bf16[5,32,512]{2,1,0:T(8,128)(2,1)S(1)} %shard_map.87.refs_0_), channel_id=1, source_target_pairs={{0,64},{1,65},{2,66},{3,67},{4,68},{5,69},{6,70},{7,71},{8,72},{9,... | collective-permute-start | bytes 491528 | tf_op jit(solution)/shard_map/ppermute | solution.py:38
  5.4 15.5 %collective-permute-start.4 = (bf16[5,32,512]{2,1,0:T(8,128)(2,1)S(1)}, bf16[5,32,512]{2,1,0:T(8,128)(2,1)S(1)}, u32[]{:S(2)}, u32[]{:S(2)}) collective-permute-start(bf16[5,32,512]{2,1,0:T(8,128)(2,1)S(1)} %shard_map.87.refs_0_), channel_id=1, source_target_pairs={{0,192},{1,193},{2,194},{3,195},{4,196},{5,197},{6,198},{7,199},{8... | collective-permute-start | bytes 491528 | tf_op jit(solution)/shard_map/ppermute | solution.py:38
  8.5 13.3 %collective-permute-start.5 = (bf16[5,32,512]{2,1,0:T(8,128)(2,1)S(1)}, bf16[5,32,512]{2,1,0:T(8,128)(2,1)S(1)}, u32[]{:S(2)}, u32[]{:S(2)}) collective-permute-start(bf16[5,32,512]{2,1,0:T(8,128)(2,1)S(1)} %shard_map.87.refs_0_), channel_id=1, source_target_pairs={{0,128},{1,129},{2,130},{3,131},{4,132},{5,133},{6,134},{7,135},{8... | collective-permute-start | bytes 491528 | tf_op jit(solution)/shard_map/ppermute | solution.py:38
  21.9 6.5 %collective-permute-start.6 = (bf16[256,512]{1,0:T(8,128)(2,1)S(1)}, bf16[256,512]{1,0:T(8,128)(2,1)S(1)}, u32[]{:S(2)}, u32[]{:S(2)}) collective-permute-start(bf16[256,512]{1,0:T(8,128)(2,1)S(1)} %get-tuple-element.58), channel_id=1, source_target_pairs={{0,4},{1,17},{2,6},{3,19},{4,8},{5,21},{6,10},{7,23},{8,12},{9,25}... | collective-permute-start | bytes 786440 | tf_op jit(solution)/shard_map/ppermute | solution.py:38
  23.2 5.2 %collective-permute-start.7 = (bf16[256,512]{1,0:T(8,128)(2,1)S(1)}, bf16[256,512]{1,0:T(8,128)(2,1)S(1)}, u32[]{:S(2)}, u32[]{:S(2)}) collective-permute-start(bf16[256,512]{1,0:T(8,128)(2,1)S(1)} %get-tuple-element.59), channel_id=1, source_target_pairs={{0,12},{1,49},{2,14},{3,51},{4,0},{5,53},{6,2},{7,55},{8,4},{9,57}... | collective-permute-start | bytes 786440 | tf_op jit(solution)/shard_map/ppermute | solution.py:38
  24.6 7.5 %collective-permute-start.8 = (bf16[256,512]{1,0:T(8,128)(2,1)S(1)}, bf16[256,512]{1,0:T(8,128)(2,1)S(1)}, u32[]{:S(2)}, u32[]{:S(2)}) collective-permute-start(bf16[256,512]{1,0:T(8,128)(2,1)S(1)} %get-tuple-element.60), channel_id=1, source_target_pairs={{0,8},{1,33},{2,10},{3,35},{4,12},{5,37},{6,14},{7,39},{8,0},{9,41... | collective-permute-start | bytes 786440 | tf_op jit(solution)/shard_map/ppermute | solution.py:38
  32.3 22.1 %collective-permute-start.9 = (bf16[512,512]{1,0:T(8,128)(2,1)S(1)}, bf16[512,512]{1,0:T(8,128)(2,1)S(1)}, u32[]{:S(2)}, u32[]{:S(2)}) collective-permute-start(bf16[512,512]{1,0:T(8,128)(2,1)S(1)} %get-tuple-element.61.shared_keys), channel_id=1, source_target_pairs={{0,16},{1,5},{2,18},{3,7},{4,20},{5,9},{6,22},{7,11},{8,24},{9,13}... | collective-permute-start | bytes 1572872 | tf_op jit(solution)/shard_map/ppermute | solution.py:38
  33.6 6.1 %collective-permute-start = (bf16[256,256]{1,0:T(8,128)(2,1)S(1)}, bf16[256,256]{1,0:T(8,128)(2,1)S(1)}, u32[]{:S(2)}, u32[]{:S(2)}) collective-permute-start(bf16[256,256]{1,0:T(8,128)(2,1)S(1)} %get-tuple-element.43), channel_id=1, source_target_pairs={{0,4},{1,17},{2,6},{3,19},{4,8},{5,21},{6,10},{7,23},{8,12},{9,25}... | collective-permute-start | bytes 393224 | tf_op jit(solution)/shard_map/ppermute | solution.py:38
  34.5 20.3 %collective-permute-start.13 = (bf16[512,512]{1,0:T(8,128)(2,1)S(1)}, bf16[512,512]{1,0:T(8,128)(2,1)S(1)}, u32[]{:S(2)}, u32[]{:S(2)}) collective-permute-start(bf16[512,512]{1,0:T(8,128)(2,1)S(1)} %get-tuple-element.63.own_keys), channel_id=1, source_target_pairs={{0,48},{1,13},{2,50},{3,15},{4,52},{5,1},{6,54},{7,3},{8,56},{9,5}... | collective-permute-start | bytes 1572872 | tf_op jit(solution)/shard_map/ppermute | solution.py:38
  36.3 5.4 %collective-permute-start.1 = (bf16[256,256]{1,0:T(8,128)(2,1)S(1)}, bf16[256,256]{1,0:T(8,128)(2,1)S(1)}, u32[]{:S(2)}, u32[]{:S(2)}) collective-permute-start(bf16[256,256]{1,0:T(8,128)(2,1)S(1)} %get-tuple-element.44), channel_id=1, source_target_pairs={{0,8},{1,33},{2,10},{3,35},{4,12},{5,37},{6,14},{7,39},{8,0},{9,41... | collective-permute-start | bytes 393224 | tf_op jit(solution)/shard_map/ppermute | solution.py:38
  38.4 21.3 %collective-permute-start.11 = (bf16[512,512]{1,0:T(8,128)(2,1)S(1)}, bf16[512,512]{1,0:T(8,128)(2,1)S(1)}, u32[]{:S(2)}, u32[]{:S(2)}) collective-permute-start(bf16[512,512]{1,0:T(8,128)(2,1)S(1)} %get-tuple-element.61.shared_keys), channel_id=1, source_target_pairs={{0,48},{1,13},{2,50},{3,15},{4,52},{5,1},{6,54},{7,3},{8,56},{9,5}... | collective-permute-start | bytes 1572872 | tf_op jit(solution)/shard_map/ppermute | solution.py:38
  39.7 20.3 %collective-permute-start.12 = (bf16[512,512]{1,0:T(8,128)(2,1)S(1)}, bf16[512,512]{1,0:T(8,128)(2,1)S(1)}, u32[]{:S(2)}, u32[]{:S(2)}) collective-permute-start(bf16[512,512]{1,0:T(8,128)(2,1)S(1)} %get-tuple-element.63.own_keys), channel_id=1, source_target_pairs={{0,16},{1,5},{2,18},{3,7},{4,20},{5,9},{6,22},{7,11},{8,24},{9,13}... | collective-permute-start | bytes 1572872 | tf_op jit(solution)/shard_map/ppermute | solution.py:38
  41.7 5.5 %collective-permute-start.2 = (bf16[256,256]{1,0:T(8,128)(2,1)S(1)}, bf16[256,256]{1,0:T(8,128)(2,1)S(1)}, u32[]{:S(2)}, u32[]{:S(2)}) collective-permute-start(bf16[256,256]{1,0:T(8,128)(2,1)S(1)} %get-tuple-element.45), channel_id=1, source_target_pairs={{0,12},{1,49},{2,14},{3,51},{4,0},{5,53},{6,2},{7,55},{8,4},{9,57}... | collective-permute-start | bytes 393224 | tf_op jit(solution)/shard_map/ppermute | solution.py:38
  47.2 62.9 %collective-permute-start.27 = (bf16[512,1280]{1,0:T(8,128)(2,1)S(1)}, bf16[512,1280]{1,0:T(8,128)(2,1)S(1)}, u32[]{:S(2)}, u32[]{:S(2)}) collective-permute-start(bf16[512,1280]{1,0:T(8,128)(2,1)S(1)} %get-tuple-element.82), channel_id=1, source_target_pairs={{0,2},{1,3},{2,0},{3,1},{4,6},{5,7},{6,4},{7,5},{8,10},{9,11},{10,... | collective-permute-start | bytes 3932168 | tf_op jit(solution)/shard_map/ppermute | solution.py:38
  54.3 9.5 %collective-permute-start.10 = (bf16[512,512]{1,0:T(8,128)(2,1)S(1)}, bf16[512,512]{1,0:T(8,128)(2,1)S(1)}, u32[]{:S(2)}, u32[]{:S(2)}) collective-permute-start(bf16[512,512]{1,0:T(8,128)(2,1)S(1)} %collective-permute-done.9.shared_keys), channel_id=1, source_target_pairs={{0,16},{1,5},{2,18},{3,7},{4,20},{5,9},{6,22},{7,11},{8,24},{9,13}... | collective-permute-start | bytes 1572872 | tf_op jit(solution)/shard_map/ppermute | solution.py:38
  54.8 74.1 %collective-permute-start.21 = (bf16[640,1280]{1,0:T(8,128)(2,1)S(1)}, bf16[640,1280]{1,0:T(8,128)(2,1)S(1)}, u32[]{:S(2)}, u32[]{:S(2)}) collective-permute-start(bf16[640,1280]{1,0:T(8,128)(2,1)S(1)} %get-tuple-element.79), channel_id=1, source_target_pairs={{0,1},{1,0},{2,3},{3,2},{4,5},{5,4},{6,7},{7,6},{8,9},{9,8},{10,11... | collective-permute-start | bytes 4915208 | tf_op jit(solution)/shard_map/ppermute | solution.py:38
  59.7 70.7 %collective-permute-start.22 = (bf16[640,1280]{1,0:T(8,128)(2,1)S(1)}, bf16[640,1280]{1,0:T(8,128)(2,1)S(1)}, u32[]{:S(2)}, u32[]{:S(2)}) collective-permute-start(bf16[640,1280]{1,0:T(8,128)(2,1)S(1)} %get-tuple-element.80), channel_id=1, source_target_pairs={{0,195},{1,194},{2,65},{3,64},{4,199},{5,198},{6,69},{7,68},{8,203... | collective-permute-start | bytes 4915208 | tf_op jit(solution)/shard_map/ppermute | solution.py:49
  60.0 11.8 %collective-permute-start.18 = (bf16[512,512]{1,0:T(8,128)(2,1)S(1)}, bf16[512,512]{1,0:T(8,128)(2,1)S(1)}, u32[]{:S(2)}, u32[]{:S(2)}) collective-permute-start(bf16[512,512]{1,0:T(8,128)(2,1)S(1)} %collective-permute-done.13.own_keys), channel_id=1, source_target_pairs={{0,48},{1,13},{2,50},{3,15},{4,52},{5,1},{6,54},{7,3},{8,56},{9,5}... | collective-permute-start | bytes 1572872 | tf_op jit(solution)/shard_map/ppermute | solution.py:38
  63.9 41.4 %collective-permute-start.29 = (bf16[128,1280]{1,0:T(8,128)(2,1)S(1)}, bf16[128,1280]{1,0:T(8,128)(2,1)S(1)}, u32[]{:S(2)}, u32[]{:S(2)}) collective-permute-start(bf16[128,1280]{1,0:T(8,128)(2,1)S(1)} %get-tuple-element.83), channel_id=1, source_target_pairs={{0,194},{1,195},{2,64},{3,65},{4,198},{5,199},{6,68},{7,69},{8,202... | collective-permute-start | bytes 983048 | tf_op jit(solution)/shard_map/ppermute | solution.py:49
  71.8 36.6 %collective-permute-start.23 = (bf16[512,128]{1,0:T(8,128)(2,1)S(1)}, bf16[512,128]{1,0:T(8,128)(2,1)S(1)}, u32[]{:S(2)}, u32[]{:S(2)}) collective-permute-start(bf16[512,128]{1,0:T(8,128)(2,1)S(1)} %get-tuple-element.69), channel_id=1, source_target_pairs={{0,14},{1,51},{2,12},{3,49},{4,2},{5,55},{6,0},{7,53},{8,6},{9,59}... | collective-permute-start | bytes 393224 | tf_op jit(solution)/shard_map/ppermute | solution.py:38
  105.3 3.8 %collective-permute-start.14 = (bf16[512,128]{1,0:T(8,128)(2,1)S(1)}, bf16[512,128]{1,0:T(8,128)(2,1)S(1)}, u32[]{:S(2)}, u32[]{:S(2)}) collective-permute-start(bf16[512,128]{1,0:T(8,128)(2,1)S(1)} %get-tuple-element.69), channel_id=1, source_target_pairs={{0,12},{1,49},{2,14},{3,51},{4,0},{5,53},{6,2},{7,55},{8,4},{9,57}... | collective-permute-start | bytes 393224 | tf_op jit(solution)/shard_map/ppermute | solution.py:38
  108.4 7.3 %collective-permute-start.24 = (bf16[512,128]{1,0:T(8,128)(2,1)S(1)}, bf16[512,128]{1,0:T(8,128)(2,1)S(1)}, u32[]{:S(2)}, u32[]{:S(2)}) collective-permute-start(bf16[512,128]{1,0:T(8,128)(2,1)S(1)} %get-tuple-element.70), channel_id=1, source_target_pairs={{0,10},{1,35},{2,8},{3,33},{4,14},{5,39},{6,12},{7,37},{8,2},{9,43... | collective-permute-start | bytes 393224 | tf_op jit(solution)/shard_map/ppermute | solution.py:38
  109.1 7.4 %collective-permute-start.25 = (bf16[512,128]{1,0:T(8,128)(2,1)S(1)}, bf16[512,128]{1,0:T(8,128)(2,1)S(1)}, u32[]{:S(2)}, u32[]{:S(2)}) collective-permute-start(bf16[512,128]{1,0:T(8,128)(2,1)S(1)} %get-tuple-element.71), channel_id=1, source_target_pairs={{0,6},{1,19},{2,4},{3,17},{4,10},{5,23},{6,8},{7,21},{8,14},{9,27}... | collective-permute-start | bytes 393224 | tf_op jit(solution)/shard_map/ppermute | solution.py:38
  110.2 9.9 %collective-permute-start.15 = (bf16[512,128]{1,0:T(8,128)(2,1)S(1)}, bf16[512,128]{1,0:T(8,128)(2,1)S(1)}, u32[]{:S(2)}, u32[]{:S(2)}) collective-permute-start(bf16[512,128]{1,0:T(8,128)(2,1)S(1)} %get-tuple-element.70), channel_id=1, source_target_pairs={{0,8},{1,33},{2,10},{3,35},{4,12},{5,37},{6,14},{7,39},{8,0},{9,41... | collective-permute-start | bytes 393224 | tf_op jit(solution)/shard_map/ppermute | solution.py:38
  115.7 5.0 %collective-permute-start.16 = (bf16[512,128]{1,0:T(8,128)(2,1)S(1)}, bf16[512,128]{1,0:T(8,128)(2,1)S(1)}, u32[]{:S(2)}, u32[]{:S(2)}) collective-permute-start(bf16[512,128]{1,0:T(8,128)(2,1)S(1)} %get-tuple-element.71), channel_id=1, source_target_pairs={{0,4},{1,17},{2,6},{3,19},{4,8},{5,21},{6,10},{7,23},{8,12},{9,25}... | collective-permute-start | bytes 393224 | tf_op jit(solution)/shard_map/ppermute | solution.py:38
  116.5 8.3 %collective-permute-start.28 = (bf16[512,256]{1,0:T(8,128)(2,1)S(1)}, bf16[512,256]{1,0:T(8,128)(2,1)S(1)}, u32[]{:S(2)}, u32[]{:S(2)}) collective-permute-start(bf16[512,256]{1,0:T(8,128)(2,1)S(1)} %shard_map.95.refs_0_), channel_id=1, source_target_pairs={{0,1},{1,0},{2,3},{3,2},{4,5},{5,4},{6,7},{7,6},{8,9},{9,8},{10,11... | collective-permute-start | bytes 786440 | tf_op jit(solution)/shard_map/ppermute | solution.py:38
  120.1 7.4 %collective-permute-start.19 = (bf16[512,256]{1,0:T(8,128)(2,1)S(1)}, bf16[512,256]{1,0:T(8,128)(2,1)S(1)}, u32[]{:S(2)}, u32[]{:S(2)}) collective-permute-start(bf16[512,256]{1,0:T(8,128)(2,1)S(1)} %shard_map.95.refs_0_), channel_id=1, source_target_pairs={{0,2},{1,3},{2,0},{3,1},{4,6},{5,7},{6,4},{7,5},{8,10},{9,11},{10,... | collective-permute-start | bytes 786440 | tf_op jit(solution)/shard_map/ppermute | solution.py:38
  120.7 9.7 %collective-permute-start.26 = (bf16[512,384]{1,0:T(8,128)(2,1)S(1)}, bf16[512,384]{1,0:T(8,128)(2,1)S(1)}, u32[]{:S(2)}, u32[]{:S(2)}) collective-permute-start(bf16[512,384]{1,0:T(8,128)(2,1)S(1)} %constant_dynamic-update-slice_fusion.7.refs_2_), channel_id=1, source_target_pairs={{0,1},{1,0},{2,3},{3,2},{4,5},{5,4},{6,7},{7,6},{8,9},{9,8},{10,11... | collective-permute-start | bytes 1179656 | tf_op jit(solution)/shard_map/ppermute | solution.py:38
  124.8 7.6 %collective-permute-start.17 = (bf16[512,384]{1,0:T(8,128)(2,1)S(1)}, bf16[512,384]{1,0:T(8,128)(2,1)S(1)}, u32[]{:S(2)}, u32[]{:S(2)}) collective-permute-start(bf16[512,384]{1,0:T(8,128)(2,1)S(1)} %constant_dynamic-update-slice_fusion.4.refs_1_), channel_id=1, source_target_pairs={{0,1},{1,0},{2,3},{3,2},{4,5},{5,4},{6,7},{7,6},{8,9},{9,8},{10,11... | collective-permute-start | bytes 1179656 | tf_op jit(solution)/shard_map/ppermute | solution.py:38
  127.5 4.8 %collective-permute-start.20 = (bf16[512,256]{1,0:T(8,128)(2,1)S(1)}, bf16[512,256]{1,0:T(8,128)(2,1)S(1)}, u32[]{:S(2)}, u32[]{:S(2)}) collective-permute-start(bf16[512,256]{1,0:T(8,128)(2,1)S(1)} %collective-permute-done.19.refs_2_), channel_id=1, source_target_pairs={{0,1},{1,0},{2,3},{3,2},{4,5},{5,4},{6,7},{7,6},{8,9},{9,8},{10,11... | collective-permute-start | bytes 786440 | tf_op jit(solution)/shard_map/ppermute | solution.py:38

commit v5 on v4

--- a/solution.py
+++ b/solution.py
@@ -38,14 +38,14 @@
     return lax.ppermute(array, AXES, pairs)
 
 
-def across(array, core=0):
+def across(array):
     pairs = []
     for index in range(ZH * NX * NY * ZL * CORES):
         rest, c = divmod(index, CORES)
         rest, b = divmod(rest, ZL)
         a, xy = divmod(rest, NX * NY)
         to = (a + 1) % ZH if b else (a - 1) % ZH
-        pairs.append((index, ((to * NX * NY + xy) * ZL + 1 - b) * CORES + (c + core) % CORES))
+        pairs.append((index, ((to * NX * NY + xy) * ZL + 1 - b) * CORES + 1 - c))
     return lax.ppermute(array, AXES, pairs)
 
 
@@ -159,46 +159,55 @@
     return (*cut, ref[rows, 3 * HD : 5 * HD], ref[rows, 5 * HD :])
 
 
-def attend_kernel(first, shared_ref, own_ref, shared_keys, own_keys, *refs):
-    sides = ((shared_ref, shared_keys, refs[-2]), (own_ref, own_keys, refs[-1]))
-    for side, (query, keys, out_ref) in enumerate(sides):
-        state = None if first else load_state(refs[side], slice(None))
-        out_ref[...] = jnp.concatenate(attend(query[...], keys, state), axis=1)
-
-
-def attend_step(queries, keys, state):
-    rows = [query.shape[0] for query in queries]
+def attend_begin_kernel(shared_ref, own_ref, shared_keys, own_keys, *out_refs):
+    sides = ((shared_ref, shared_keys), (own_ref, own_keys))
+    for (query, keys), out_ref in zip(sides, out_refs):
+        out_ref[...] = jnp.concatenate(attend(query[...], keys, None), axis=1)
+
+
+def attend_more_kernel(query_ref, keys, state_ref, out_ref):
+    state = load_state(state_ref, slice(None))
+    out_ref[...] = jnp.concatenate(attend(query_ref[...], keys, state), axis=1)
+
+
+def attend_more(query, keys, state):
     return call(
-        functools.partial(attend_kernel, not state),
-        [jax.ShapeDtypeStruct((n, 6 * HD), F32) for n in rows],
-        *queries,
-        *keys,
-        *state,
-        flops=sum(rows) * keys[0].shape[0] * 1792,
-    )
-
-
-def attend_others_kernel(query_ref, keys, state_ref, *out_refs):
+        attend_more_kernel,
+        jax.ShapeDtypeStruct(state.shape, F32),
+        query,
+        keys,
+        state,
+        flops=query.shape[0] * keys.shape[0] * 1792,
+    )
+
+
+def attend_done_kernel(start, query_ref, keys, state_ref, *out_refs):
     rows = out_refs[0].shape[0] // 2
-    most = slice(0, rows * len(out_refs))
-    attended, attended_tan = finish(attend(query_ref[most, :], keys, load_state(state_ref, most)))
+    part = slice(start, start + rows * len(out_refs))
+    attended, attended_tan = finish(attend(query_ref[part, :], keys, load_state(state_ref, part)))
     for place, ref in enumerate(out_refs):
         ref[:rows, :] = attended[place * rows : (place + 1) * rows]
         ref[rows:, :] = attended_tan[place * rows : (place + 1) * rows]
 
 
-def attend_kept_kernel(shared_ref, own_ref, shared_keys, own_keys, shared_state, own_state, out_ref):
-    rows = own_ref.shape[0]
-    start = shared_ref.shape[0] - rows
-    sides = (
-        (shared_ref, shared_keys, shared_state, slice(start, start + rows)),
-        (own_ref, own_keys, own_state, slice(0, rows)),
-    )
-    for side, (query, keys, state, part) in enumerate(sides):
-        lanes = slice(side * HD, (side + 1) * HD)
-        attended, attended_tan = finish(attend(query[part, :], keys, load_state(state, part)))
-        out_ref[:rows, lanes] = attended
-        out_ref[rows:, lanes] = attended_tan
+def attend_done(query, keys, state, start, rows, count):
+    return call(
+        functools.partial(attend_done_kernel, start),
+        [jax.ShapeDtypeStruct((2 * rows, HD), BF16)] * count,
+        query,
+        keys,
+        state,
+        flops=count * rows * keys.shape[0] * 1792,
+    )
+
+
+def attend_last_kernel(query_ref, b_keys, c_keys, d_keys, state_ref, done_ref, out_ref):
+    rows = query_ref.shape[0]
+    state = load_state(state_ref, slice(None))
+    for keys in (b_keys, c_keys, d_keys):
+        state = attend(query_ref[...], keys, state)
+    out_ref[:, :HD] = done_ref[...]
+    out_ref[:rows, HD:], out_ref[rows:, HD:] = finish(state)
 
 
 def cut_weight_kernel(y_ref, place_ref, w_ref, *refs):
@@ -211,10 +220,7 @@
         for slot, k in enumerate(SLOTS):
             head = lax.rem(y_ref[0] + k, NY) if k < NY else NY
             source = w_ref.at[pl.ds(pl.multiple_of(head * HD, HD), HD), lanes]
-            if flip == ZL and slot == NY:
-                target = out_refs[-1]
-            else:
-                target = out_refs[flip].at[slot * HD : (slot + 1) * HD]
+            target = out_refs[flip].at[slot * HD : (slot + 1) * HD]
             copies.append(pltpu.make_async_copy(source, target, sems.at[flip, slot]))
     for copy in copies:
         copy.start()
@@ -328,10 +334,7 @@
     place, _ = lax.optimization_barrier((place, sends[1]))
     cuts = call(
         cut_weight_kernel,
-        [
-            jax.ShapeDtypeStruct((depth, columns), BF16)
-            for depth in (width, width, width - HD, width, HD)
-        ],
+        [jax.ShapeDtypeStruct((width, columns), BF16)] * (ZL * CORES),
         y,
         place,
         out_weight,
@@ -349,8 +352,7 @@
     )
     cuts, _ = lax.optimization_barrier((cuts, split[0]))
     weight_near = shift(cuts[2], zl=1)
-    weight_far = across(cuts[3], core=1)
-    weight_more = across(cuts[4])
+    weight_far = across(cuts[3])
     weight_core = shift(cuts[1], core=1)
 
     own = call(
@@ -363,25 +365,29 @@
     right = [shift(own[0], ring=-1), shift(own[1], ring=-1)]
     opposite = [shift(left[0], ring=1), shift(right[1], ring=-1)]
 
-    state = attend_step(blocks, own, ())
-    state = attend_step(blocks, (left[0], right[1]), state)
-    state = attend_step(blocks, (right[0], left[1]), state)
-    others = call(
-        attend_others_kernel,
-        [jax.ShapeDtypeStruct((2 * rows, HD), BF16)] * (NY - 1),
-        blocks[0],
-        opposite[0],
-        state[0],
-        flops=3 * rows * opposite[0].shape[0] * 1792,
-    )
-    opposite[1], _ = lax.optimization_barrier((opposite[1], others[0]))
+    state, own_state = call(
+        attend_begin_kernel,
+        [jax.ShapeDtypeStruct((block.shape[0], 6 * HD), F32) for block in blocks],
+        *blocks,
+        *own,
+        flops=(NY + 1) * rows * own[0].shape[0] * 1792,
+    )
+    state = attend_more(blocks[0], left[0], state)
+    state = attend_more(blocks[0], right[0], state)
+    peers = NY - 1
+    others = attend_done(blocks[0], opposite[0], state, 0, rows, peers)
+    last_keys, _ = lax.optimization_barrier((opposite[0], others[0]))
+    kept = attend_done(blocks[0], last_keys, state, peers * rows, rows, 1)
     kept = call(
-        attend_kept_kernel,
+        attend_last_kernel,
         jax.ShapeDtypeStruct((2 * rows, 2 * HD), BF16),
-        *blocks,
-        *opposite,
-        *state,
-        flops=2 * rows * opposite[0].shape[0] * 1792,
+        blocks[1],
+        right[1],
+        left[1],
+        opposite[1],
+        own_state,
+        *kept,
+        flops=3 * rows * opposite[1].shape[0] * 1792,
     )
 
     near = [
@@ -391,13 +397,12 @@
     mine = [kept, jnp.concatenate([shift(others[k - 1], swap=-k) for k in (1, 2, 3)], axis=1)]
     sibling = [shift(mine[n], core=1) for n in range(2)]
     far = [shift(near[n], core=1) for n in range(2)]
-    own, rest, cut = 2 * HD, 3 * HD, width - HD
+    own, rest = 2 * HD, 3 * HD
     partial = project_part(
         (
             (0, 0, own, 3, 0),
             (1, 0, own, 4, 0),
-            (2, 0, cut - own, 5, own),
-            (2, cut - own, rest, 6, 0),
+            (2, 0, rest, 5, own),
         ),
         mine[0],
         sibling[0],
@@ -405,7 +410,6 @@
         cuts[0],
         weight_core,
         weight_near,
-        weight_more,
     )
     partial = project_part(
         ((0, 0, rest, 3, own), (1, 0, rest, 4, own), (2, 0, own, 5, 0)),

time: 135 us -> 132 us (0.978)
  waiting for transfers between devices: 55.3 us -> 52.3 us
    ppermute x2 -> x1, waiting for transfers between devices: 32.5 us -> 0.01 us  [across(): return lax.ppermute(array, AXES, pairs)]
    ppermute x28, waiting for transfers between devices: 22.8 us -> 52.3 us  [shift(): return lax.ppermute(array, AXES, pairs)]
    ppermute x2 -> x1, starting transfers between devices: 2.84 us -> 0.17 us  [across(): return lax.ppermute(array, AXES, pairs)]
    ppermute x28, starting transfers between devices: 56.1 us -> 58.4 us  [shift(): return lax.ppermute(array, AXES, pairs)]
    pallas_call x12 -> x13, Pallas kernels: 17 us -> 17.1 us  [called(): pl.pallas_call(kernel, out_shape=outs, in_specs=specs or [VMEM] * len(ope...]
  transfers between devices with their start and end apart: 30 -> 29, of which waited for: 12 -> 12; matrix products, arithmetic and copies ran while one was open for 0% -> 0% of each run, Pallas kernels for 12% -> 12%
where the time goes in v5:
time: 132 us; the launch traced here: 131 us
  starting transfers between devices  58.6 us (44%)
  waiting for transfers between devices  52.3 us (40%)
  Pallas kernels  19.2 us (15%)
    ppermute x28, starting transfers between devices, shift(): return lax.ppermute(array, AXES, pairs)  58.4 us
    ppermute x28, waiting for transfers between devices, shift(): return lax.ppermute(array, AXES, pairs)  52.3 us
    pallas_call x13, Pallas kernels, called(): pl.pallas_call(kernel, out_shape=outs, in_specs=specs or [VMEM] * len(ope...  17.1 us
  transfers between devices with their start and end apart: 29, of which 12 were waited for; matrix products, arithmetic and copies ran while one was open for 0% of the time, Pallas kernels for 12%

profile of v5, /device:TPU:1, one launch (start us, length us, event | category | flops | bytes accessed | tf_op | source)
XLA Modules:
  0.0 131.4 jit_solution(6020722219600834441)
XLA Ops:
  0.6 0.9 shard_map.87.refs_0_
  1.5 3.9 %collective-permute-start.3 = (bf16[5,32,512]{2,1,0:T(8,128)(2,1)S(1)}, bf16[5,32,512]{2,1,0:T(8,128)(2,1)S(1)}, u32[]{:S(2)}, u32[]{:S(2)}) collective-permute-start(bf16[5,32,512]{2,1,0:T(8,128)(2,1)S(1)} %shard_map.87.refs_0_), channel_id=1, source_target_pairs={{0,64},{1,65},{2,66},{3,67},{4,68},{5,69},{6,70},{7,71},{8,72},{9,... | collective-permute-start | bytes 491528 | tf_op jit(solution)/shard_map/ppermute | solution.py:38
  5.4 3.1 %collective-permute-start.4 = (bf16[5,32,512]{2,1,0:T(8,128)(2,1)S(1)}, bf16[5,32,512]{2,1,0:T(8,128)(2,1)S(1)}, u32[]{:S(2)}, u32[]{:S(2)}) collective-permute-start(bf16[5,32,512]{2,1,0:T(8,128)(2,1)S(1)} %shard_map.87.refs_0_), channel_id=1, source_target_pairs={{0,192},{1,193},{2,194},{3,195},{4,196},{5,197},{6,198},{7,199},{8... | collective-permute-start | bytes 491528 | tf_op jit(solution)/shard_map/ppermute | solution.py:38
  8.5 4.4 %collective-permute-start.5 = (bf16[5,32,512]{2,1,0:T(8,128)(2,1)S(1)}, bf16[5,32,512]{2,1,0:T(8,128)(2,1)S(1)}, u32[]{:S(2)}, u32[]{:S(2)}) collective-permute-start(bf16[5,32,512]{2,1,0:T(8,128)(2,1)S(1)} %shard_map.87.refs_0_), channel_id=1, source_target_pairs={{0,128},{1,129},{2,130},{3,131},{4,132},{5,133},{6,134},{7,135},{8... | collective-permute-start | bytes 491528 | tf_op jit(solution)/shard_map/ppermute | solution.py:38
  12.9 1.2 shard_map.86
  14.1 3.1 %shard_map.88 = (bf16[640,1280]{1,0:T(8,128)(2,1)S(1)}, bf16[640,1280]{1,0:T(8,128)(2,1)S(1)}, bf16[640,1280]{1,0:T(8,128)(2,1)S(1)}, bf16[640,1280]{1,0:T(8,128)(2,1)S(1)}) custom-call(s32[1]{0:T(128)S(6)} %select_n.27.y_ref, s32[1]{0:T(128)} %bitcast.place_ref, bf16[640,5120]{1,0:T(8,128)(2,1)} %w_ref.1), custom_call_target="tpu_custom_call" | custom-call | bytes 6553608 | tf_op jit(solution)/shard_map/pallas_call | solution.py:57
  17.2 3.8 %collective-permute-done.4.refs_2_ = bf16[5,32,512]{2,1,0:T(8,128)(2,1)S(1)} collective-permute-done((bf16[5,32,512]{2,1,0:T(8,128)(2,1)S(1)}, bf16[5,32,512]{2,1,0:T(8,128)(2,1)S(1)}, u32[]{:S(2)}, u32[]{:S(2)}) %collective-permute-start.4) | collective-permute-done | bytes 163872 | tf_op jit(solution)/shard_map/ppermute | solution.py:38
  21.0 0.9 collective-permute-done.5.refs_3_
  21.9 1.3 collective-permute-start.6
  23.2 1.5 %collective-permute-start.7 = (bf16[256,512]{1,0:T(8,128)(2,1)S(1)}, bf16[256,512]{1,0:T(8,128)(2,1)S(1)}, u32[]{:S(2)}, u32[]{:S(2)}) collective-permute-start(bf16[256,512]{1,0:T(8,128)(2,1)S(1)} %get-tuple-element.51), channel_id=1, source_target_pairs={{0,12},{1,49},{2,14},{3,51},{4,0},{5,53},{6,2},{7,55},{8,4},{9,57}... | collective-permute-start | bytes 786440 | tf_op jit(solution)/shard_map/ppermute | solution.py:38
  24.6 1.5 %collective-permute-start.8 = (bf16[256,512]{1,0:T(8,128)(2,1)S(1)}, bf16[256,512]{1,0:T(8,128)(2,1)S(1)}, u32[]{:S(2)}, u32[]{:S(2)}) collective-permute-start(bf16[256,512]{1,0:T(8,128)(2,1)S(1)} %get-tuple-element.52), channel_id=1, source_target_pairs={{0,8},{1,33},{2,10},{3,35},{4,12},{5,37},{6,14},{7,39},{8,0},{9,41... | collective-permute-start | bytes 786440 | tf_op jit(solution)/shard_map/ppermute | solution.py:38
  26.2 2.2 %collective-permute-done.6.refs_1_ = bf16[256,512]{1,0:T(8,128)(2,1)S(1)} collective-permute-done((bf16[256,512]{1,0:T(8,128)(2,1)S(1)}, bf16[256,512]{1,0:T(8,128)(2,1)S(1)}, u32[]{:S(2)}, u32[]{:S(2)}) %collective-permute-start.6) | collective-permute-done | bytes 262176 | tf_op jit(solution)/shard_map/ppermute | solution.py:38
  28.4 3.8 %collective-permute-done.8.refs_3_ = bf16[256,512]{1,0:T(8,128)(2,1)S(1)} collective-permute-done((bf16[256,512]{1,0:T(8,128)(2,1)S(1)}, bf16[256,512]{1,0:T(8,128)(2,1)S(1)}, u32[]{:S(2)}, u32[]{:S(2)}) %collective-permute-start.8) | collective-permute-done | bytes 262176 | tf_op jit(solution)/shard_map/ppermute | solution.py:38
  32.3 1.4 %collective-permute-start.9 = (bf16[512,512]{1,0:T(8,128)(2,1)S(1)}, bf16[512,512]{1,0:T(8,128)(2,1)S(1)}, u32[]{:S(2)}, u32[]{:S(2)}) collective-permute-start(bf16[512,512]{1,0:T(8,128)(2,1)S(1)} %get-tuple-element.53.shared_keys), channel_id=1, source_target_pairs={{0,16},{1,5},{2,18},{3,7},{4,20},{5,9},{6,22},{7,11},{8,24},{9,13}... | collective-permute-start | bytes 1572872 | tf_op jit(solution)/shard_map/ppermute | solution.py:38
  33.6 1.8 %collective-permute-start.11 = (bf16[512,512]{1,0:T(8,128)(2,1)S(1)}, bf16[512,512]{1,0:T(8,128)(2,1)S(1)}, u32[]{:S(2)}, u32[]{:S(2)}) collective-permute-start(bf16[512,512]{1,0:T(8,128)(2,1)S(1)} %get-tuple-element.53.shared_keys), channel_id=1, source_target_pairs={{0,48},{1,13},{2,50},{3,15},{4,52},{5,1},{6,54},{7,3},{8,56},{9,5}... | collective-permute-start | bytes 1572872 | tf_op jit(solution)/shard_map/ppermute | solution.py:38
  35.5 1.4 %collective-permute-start.16 = (bf16[512,512]{1,0:T(8,128)(2,1)S(1)}, bf16[512,512]{1,0:T(8,128)(2,1)S(1)}, u32[]{:S(2)}, u32[]{:S(2)}) collective-permute-start(bf16[512,512]{1,0:T(8,128)(2,1)S(1)} %get-tuple-element.55.own_keys), channel_id=1, source_target_pairs={{0,48},{1,13},{2,50},{3,15},{4,52},{5,1},{6,54},{7,3},{8,56},{9,5}... | collective-permute-start | bytes 1572872 | tf_op jit(solution)/shard_map/ppermute | solution.py:38
  36.8 0.9 collective-permute-start
  37.7 4.5 %collective-permute-done.9.keys = bf16[512,512]{1,0:T(8,128)(2,1)S(1)} collective-permute-done((bf16[512,512]{1,0:T(8,128)(2,1)S(1)}, bf16[512,512]{1,0:T(8,128)(2,1)S(1)}, u32[]{:S(2)}, u32[]{:S(2)}) %collective-permute-start.9) | collective-permute-done | bytes 524320 | tf_op jit(solution)/shard_map/ppermute | solution.py:38
  42.2 2.2 %collective-permute-start.1 = (bf16[256,256]{1,0:T(8,128)(2,1)S(1)}, bf16[256,256]{1,0:T(8,128)(2,1)S(1)}, u32[]{:S(2)}, u32[]{:S(2)}) collective-permute-start(bf16[256,256]{1,0:T(8,128)(2,1)S(1)} %get-tuple-element.37), channel_id=1, source_target_pairs={{0,8},{1,33},{2,10},{3,35},{4,12},{5,37},{6,14},{7,39},{8,0},{9,41... | collective-permute-start | bytes 393224 | tf_op jit(solution)/shard_map/ppermute | solution.py:38
  44.5 0.9 collective-permute-start.2
  45.3 3.6 %collective-permute-done.1 = bf16[256,256]{1,0:T(8,128)(2,1)S(1)} collective-permute-done((bf16[256,256]{1,0:T(8,128)(2,1)S(1)}, bf16[256,256]{1,0:T(8,128)(2,1)S(1)}, u32[]{:S(2)}, u32[]{:S(2)}) %collective-permute-start.1) | collective-permute-done | bytes 131104 | tf_op jit(solution)/shard_map/ppermute | solution.py:38
  49.0 7.1 %collective-permute-start.21 = (bf16[640,1280]{1,0:T(8,128)(2,1)S(1)}, bf16[640,1280]{1,0:T(8,128)(2,1)S(1)}, u32[]{:S(2)}, u32[]{:S(2)}) collective-permute-start(bf16[640,1280]{1,0:T(8,128)(2,1)S(1)} %get-tuple-element.66), channel_id=1, source_target_pairs={{0,1},{1,0},{2,3},{3,2},{4,5},{5,4},{6,7},{7,6},{8,9},{9,8},{10,11... | collective-permute-start | bytes 4915208 | tf_op jit(solution)/shard_map/ppermute | solution.py:38
  56.1 0.7 collective-permute-start.17
  56.8 4.4 %collective-permute-start.27 = (bf16[640,1280]{1,0:T(8,128)(2,1)S(1)}, bf16[640,1280]{1,0:T(8,128)(2,1)S(1)}, u32[]{:S(2)}, u32[]{:S(2)}) collective-permute-start(bf16[640,1280]{1,0:T(8,128)(2,1)S(1)} %get-tuple-element.69), channel_id=1, source_target_pairs={{0,2},{1,3},{2,0},{3,1},{4,6},{5,7},{6,4},{7,5},{8,10},{9,11},{10,... | collective-permute-start | bytes 4915208 | tf_op jit(solution)/shard_map/ppermute | solution.py:38
  61.3 1.9 %collective-permute-start.18 = (bf16[512,512]{1,0:T(8,128)(2,1)S(1)}, bf16[512,512]{1,0:T(8,128)(2,1)S(1)}, u32[]{:S(2)}, u32[]{:S(2)}) collective-permute-start(bf16[512,512]{1,0:T(8,128)(2,1)S(1)} %collective-permute-done.16.b_keys), channel_id=1, source_target_pairs={{0,48},{1,13},{2,50},{3,15},{4,52},{5,1},{6,54},{7,3},{8,56},{9,5}... | collective-permute-start | bytes 1572872 | tf_op jit(solution)/shard_map/ppermute | solution.py:38
  63.3 1.8 %shard_map.91 = (f32[1024,768]{1,0:T(8,128)S(1)}, f32[256,768]{1,0:T(8,128)S(1)}) custom-call(bf16[1024,256]{1,0:T(8,128)(2,1)S(1)} %constant_dynamic-update-slice_fusion.shared_ref.query_ref, bf16[256,256]{1,0:T(8,128)(2,1)S(1)} %get-tuple-element.54.own_ref.query_ref, bf16[512,512]{1,0:T(8,128)(2,1)S(1)} %get-tuple-element.53.shared_keys, ...), custom_call_target="tpu_custom_call" | custom-call | flops 1174405120 | bytes 1703936 | tf_op jit(solution)/shard_map/pallas_call | solution.py:57
  65.1 1.5 %shard_map.92.state_ref = f32[1024,768]{1,0:T(8,128)S(1)} custom-call(bf16[1024,256]{1,0:T(8,128)(2,1)S(1)} %constant_dynamic-update-slice_fusion.shared_ref.query_ref, bf16[512,512]{1,0:T(8,128)(2,1)S(1)} %collective-permute-done.9.keys, f32[1024,768]{1,0:T(8,128)S(1)} %get-tuple-element.56.state_ref), custom_call_target="tpu_custom_call" | custom-call | flops 939524096 | bytes 4194304 | tf_op jit(solution)/shard_map/pallas_call | solution.py:57
  66.6 1.5 %shard_map.93.state_ref = f32[1024,768]{1,0:T(8,128)S(1)} custom-call(bf16[1024,256]{1,0:T(8,128)(2,1)S(1)} %constant_dynamic-update-slice_fusion.shared_ref.query_ref, bf16[512,512]{1,0:T(8,128)(2,1)S(1)} %collective-permute-done.11.keys, f32[1024,768]{1,0:T(8,128)S(1)} %shard_map.92.state_ref), custom_call_target="tpu_custom_call" | custom-call | flops 939524096 | bytes 4194304 | tf_op jit(solution)/shard_map/pallas_call | solution.py:57
  68.0 1.4 %shard_map.94 = (bf16[512,128]{1,0:T(8,128)(2,1)S(1)}, bf16[512,128]{1,0:T(8,128)(2,1)S(1)}, bf16[512,128]{1,0:T(8,128)(2,1)S(1)}) custom-call(bf16[1024,256]{1,0:T(8,128)(2,1)S(1)} %constant_dynamic-update-slice_fusion.shared_ref.query_ref, bf16[512,512]{1,0:T(8,128)(2,1)S(1)} %collective-permute-done.10.keys, f32[1024,768]{1,0:T(8,128)S(1)} %shard_map.93.state_ref), custom_call_target="tpu_custom_call" | custom-call | flops 704643072 | bytes 4194304 | tf_op jit(solution)/shard_map/pallas_call | solution.py:57
  69.4 2.7 %collective-permute-start.23 = (bf16[512,128]{1,0:T(8,128)(2,1)S(1)}, bf16[512,128]{1,0:T(8,128)(2,1)S(1)}, u32[]{:S(2)}, u32[]{:S(2)}) collective-permute-start(bf16[512,128]{1,0:T(8,128)(2,1)S(1)} %get-tuple-element.57), channel_id=1, source_target_pairs={{0,14},{1,51},{2,12},{3,49},{4,2},{5,55},{6,0},{7,53},{8,6},{9,59}... | collective-permute-start | bytes 393224 | tf_op jit(solution)/shard_map/ppermute | solution.py:38
  72.2 0.9 collective-permute-start.24
  73.1 25.6 %collective-permute-done.23 = bf16[512,128]{1,0:T(8,128)(2,1)S(1)} collective-permute-done((bf16[512,128]{1,0:T(8,128)(2,1)S(1)}, bf16[512,128]{1,0:T(8,128)(2,1)S(1)}, u32[]{:S(2)}, u32[]{:S(2)}) %collective-permute-start.23) | collective-permute-done | bytes 131104 | tf_op jit(solution)/shard_map/ppermute | solution.py:38
  98.7 3.2 %collective-permute-start.25 = (bf16[512,128]{1,0:T(8,128)(2,1)S(1)}, bf16[512,128]{1,0:T(8,128)(2,1)S(1)}, u32[]{:S(2)}, u32[]{:S(2)}) collective-permute-start(bf16[512,128]{1,0:T(8,128)(2,1)S(1)} %get-tuple-element.59), channel_id=1, source_target_pairs={{0,6},{1,19},{2,4},{3,17},{4,10},{5,23},{6,8},{7,21},{8,14},{9,27}... | collective-permute-start | bytes 393224 | tf_op jit(solution)/shard_map/ppermute | solution.py:38
  101.9 0.7 shard_map.95.done_ref
  102.6 1.5 %collective-permute-done.24 = bf16[512,128]{1,0:T(8,128)(2,1)S(1)} collective-permute-done((bf16[512,128]{1,0:T(8,128)(2,1)S(1)}, bf16[512,128]{1,0:T(8,128)(2,1)S(1)}, u32[]{:S(2)}, u32[]{:S(2)}) %collective-permute-start.24) | collective-permute-done | bytes 131104 | tf_op jit(solution)/shard_map/ppermute | solution.py:38
  104.1 2.1 %collective-permute-done.25 = bf16[512,128]{1,0:T(8,128)(2,1)S(1)} collective-permute-done((bf16[512,128]{1,0:T(8,128)(2,1)S(1)}, bf16[512,128]{1,0:T(8,128)(2,1)S(1)}, u32[]{:S(2)}, u32[]{:S(2)}) %collective-permute-start.25) | collective-permute-done | bytes 131104 | tf_op jit(solution)/shard_map/ppermute | solution.py:38
  106.2 3.3 %collective-permute-start.13 = (bf16[512,128]{1,0:T(8,128)(2,1)S(1)}, bf16[512,128]{1,0:T(8,128)(2,1)S(1)}, u32[]{:S(2)}, u32[]{:S(2)}) collective-permute-start(bf16[512,128]{1,0:T(8,128)(2,1)S(1)} %get-tuple-element.58), channel_id=1, source_target_pairs={{0,8},{1,33},{2,10},{3,35},{4,12},{5,37},{6,14},{7,39},{8,0},{9,41... | collective-permute-start | bytes 393224 | tf_op jit(solution)/shard_map/ppermute | solution.py:38
  109.5 1.7 %shard_map.96.refs_0_ = bf16[512,256]{1,0:T(8,128)(2,1)S(1)} custom-call(bf16[256,256]{1,0:T(8,128)(2,1)S(1)} %get-tuple-element.54.own_ref.query_ref, bf16[512,512]{1,0:T(8,128)(2,1)S(1)} %collective-permute-done.16.b_keys, bf16[512,512]{1,0:T(8,128)(2,1)S(1)} %collective-permute-done.17.c_keys, bf16[512,512]{1,0:T(8,128)(2,1)S(1)} %collective-permute-done.18.d_keys, ...), custom_call_target="tpu_custom_call" | custom-call | flops 704643072 | bytes 2621440 | tf_op jit(solution)/shard_map/pallas_call | solution.py:57
  111.3 0.3 collective-permute-start.14
  111.9 3.6 %collective-permute-start.28 = (bf16[512,256]{1,0:T(8,128)(2,1)S(1)}, bf16[512,256]{1,0:T(8,128)(2,1)S(1)}, u32[]{:S(2)}, u32[]{:S(2)}) collective-permute-start(bf16[512,256]{1,0:T(8,128)(2,1)S(1)} %shard_map.96.refs_0_), channel_id=1, source_target_pairs={{0,1},{1,0},{2,3},{3,2},{4,5},{5,4},{6,7},{7,6},{8,9},{9,8},{10,11... | collective-permute-start | bytes 786440 | tf_op jit(solution)/shard_map/ppermute | solution.py:38
  115.5 1.4 %collective-permute-done.14 = bf16[512,128]{1,0:T(8,128)(2,1)S(1)} collective-permute-done((bf16[512,128]{1,0:T(8,128)(2,1)S(1)}, bf16[512,128]{1,0:T(8,128)(2,1)S(1)}, u32[]{:S(2)}, u32[]{:S(2)}) %collective-permute-start.14) | collective-permute-done | bytes 131104 | tf_op jit(solution)/shard_map/ppermute | solution.py:38
  116.9 0.4 collective-permute-start.19
  117.4 3.2 %collective-permute-start.26 = (bf16[512,384]{1,0:T(8,128)(2,1)S(1)}, bf16[512,384]{1,0:T(8,128)(2,1)S(1)}, u32[]{:S(2)}, u32[]{:S(2)}) collective-permute-start(bf16[512,384]{1,0:T(8,128)(2,1)S(1)} %constant_dynamic-update-slice_fusion.7.refs_2_), channel_id=1, source_target_pairs={{0,1},{1,0},{2,3},{3,2},{4,5},{5,4},{6,7},{7,6},{8,9},{9,8},{10,11... | collective-permute-start | bytes 1179656 | tf_op jit(solution)/shard_map/ppermute | solution.py:38
  120.7 2.5 %collective-permute-done.19.refs_2_ = bf16[512,256]{1,0:T(8,128)(2,1)S(1)} collective-permute-done((bf16[512,256]{1,0:T(8,128)(2,1)S(1)}, bf16[512,256]{1,0:T(8,128)(2,1)S(1)}, u32[]{:S(2)}, u32[]{:S(2)}) %collective-permute-start.19) | collective-permute-done | bytes 262176 | tf_op jit(solution)/shard_map/ppermute | solution.py:38
  123.2 2.4 %collective-permute-start.15 = (bf16[512,384]{1,0:T(8,128)(2,1)S(1)}, bf16[512,384]{1,0:T(8,128)(2,1)S(1)}, u32[]{:S(2)}, u32[]{:S(2)}) collective-permute-start(bf16[512,384]{1,0:T(8,128)(2,1)S(1)} %constant_dynamic-update-slice_fusion.4.refs_1_), channel_id=1, source_target_pairs={{0,1},{1,0},{2,3},{3,2},{4,5},{5,4},{6,7},{7,6},{8,9},{9,8},{10,11... | collective-permute-start | bytes 1179656 | tf_op jit(solution)/shard_map/ppermute | solution.py:38
  125.7 1.5 %shard_map.97.refs_6_ = f32[512,1280]{1,0:T(8,128)S(1)} custom-call(bf16[512,256]{1,0:T(8,128)(2,1)S(1)} %shard_map.96.refs_0_, bf16[512,256]{1,0:T(8,128)(2,1)S(1)} %collective-permute-done.28.refs_1_, bf16[512,384]{1,0:T(8,128)(2,1)S(1)} %constant_dynamic-update-slice_fusion.7.refs_2_, bf16[640,1280]{1,0:T(8,128)(2,1)S(1)} %get-tuple-element.68.refs_3_.refs_4_, ...), custom_call_target="tpu_custom_call" | custom-call | flops 1174405120 | bytes 5832704 | tf_op jit(solution)/shard_map/pallas_call | solution.py:57
  127.2 1.8 %shard_map.98.refs_4_ = f32[512,1280]{1,0:T(8,128)S(1)} custom-call(bf16[512,384]{1,0:T(8,128)(2,1)S(1)} %collective-permute-done.26.refs_0_, bf16[512,384]{1,0:T(8,128)(2,1)S(1)} %constant_dynamic-update-slice_fusion.4.refs_1_, bf16[512,256]{1,0:T(8,128)(2,1)S(1)} %collective-permute-done.19.refs_2_, bf16[640,1280]{1,0:T(8,128)(2,1)S(1)} %collective-permute-done.22.refs_3_, ...), custom_call_target="tpu_custom_call" | custom-call | flops 1342177280 | bytes 8585216 | tf_op jit(solution)/shard_map/pallas_call | solution.py:57
  129.1 2.1 %project_last.1 = (bf16[256,1280]{1,0:T(8,128)(2,1)}, bf16[256,1280]{1,0:T(8,128)(2,1)}) custom-call(bf16[512,384]{1,0:T(8,128)(2,1)S(1)} %collective-permute-done.15.refs_0_, bf16[512,256]{1,0:T(8,128)(2,1)S(1)} %collective-permute-done.20.refs_1_, bf16[640,1280]{1,0:T(8,128)(2,1)S(1)} %collective-permute-done.21.refs_4_.refs_2_, ...), custom_call_target="tpu_custom_call" | custom-call | tf_op jit(solution)/shard_map/project_last/pallas_call | solution.py:281
  (34 shorter events, 0.9 us)
Async XLA Ops:
  1.5 15.7 %collective-permute-start.3 = (bf16[5,32,512]{2,1,0:T(8,128)(2,1)S(1)}, bf16[5,32,512]{2,1,0:T(8,128)(2,1)S(1)}, u32[]{:S(2)}, u32[]{:S(2)}) collective-permute-start(bf16[5,32,512]{2,1,0:T(8,128)(2,1)S(1)} %shard_map.87.refs_0_), channel_id=1, source_target_pairs={{0,64},{1,65},{2,66},{3,67},{4,68},{5,69},{6,70},{7,71},{8,72},{9,... | collective-permute-start | bytes 491528 | tf_op jit(solution)/shard_map/ppermute | solution.py:38
  5.4 15.5 %collective-permute-start.4 = (bf16[5,32,512]{2,1,0:T(8,128)(2,1)S(1)}, bf16[5,32,512]{2,1,0:T(8,128)(2,1)S(1)}, u32[]{:S(2)}, u32[]{:S(2)}) collective-permute-start(bf16[5,32,512]{2,1,0:T(8,128)(2,1)S(1)} %shard_map.87.refs_0_), channel_id=1, source_target_pairs={{0,192},{1,193},{2,194},{3,195},{4,196},{5,197},{6,198},{7,199},{8... | collective-permute-start | bytes 491528 | tf_op jit(solution)/shard_map/ppermute | solution.py:38
  8.5 13.3 %collective-permute-start.5 = (bf16[5,32,512]{2,1,0:T(8,128)(2,1)S(1)}, bf16[5,32,512]{2,1,0:T(8,128)(2,1)S(1)}, u32[]{:S(2)}, u32[]{:S(2)}) collective-permute-start(bf16[5,32,512]{2,1,0:T(8,128)(2,1)S(1)} %shard_map.87.refs_0_), channel_id=1, source_target_pairs={{0,128},{1,129},{2,130},{3,131},{4,132},{5,133},{6,134},{7,135},{8... | collective-permute-start | bytes 491528 | tf_op jit(solution)/shard_map/ppermute | solution.py:38
  21.9 6.5 %collective-permute-start.6 = (bf16[256,512]{1,0:T(8,128)(2,1)S(1)}, bf16[256,512]{1,0:T(8,128)(2,1)S(1)}, u32[]{:S(2)}, u32[]{:S(2)}) collective-permute-start(bf16[256,512]{1,0:T(8,128)(2,1)S(1)} %get-tuple-element.50), channel_id=1, source_target_pairs={{0,4},{1,17},{2,6},{3,19},{4,8},{5,21},{6,10},{7,23},{8,12},{9,25}... | collective-permute-start | bytes 786440 | tf_op jit(solution)/shard_map/ppermute | solution.py:38
  23.2 5.2 %collective-permute-start.7 = (bf16[256,512]{1,0:T(8,128)(2,1)S(1)}, bf16[256,512]{1,0:T(8,128)(2,1)S(1)}, u32[]{:S(2)}, u32[]{:S(2)}) collective-permute-start(bf16[256,512]{1,0:T(8,128)(2,1)S(1)} %get-tuple-element.51), channel_id=1, source_target_pairs={{0,12},{1,49},{2,14},{3,51},{4,0},{5,53},{6,2},{7,55},{8,4},{9,57}... | collective-permute-start | bytes 786440 | tf_op jit(solution)/shard_map/ppermute | solution.py:38
  24.6 7.5 %collective-permute-start.8 = (bf16[256,512]{1,0:T(8,128)(2,1)S(1)}, bf16[256,512]{1,0:T(8,128)(2,1)S(1)}, u32[]{:S(2)}, u32[]{:S(2)}) collective-permute-start(bf16[256,512]{1,0:T(8,128)(2,1)S(1)} %get-tuple-element.52), channel_id=1, source_target_pairs={{0,8},{1,33},{2,10},{3,35},{4,12},{5,37},{6,14},{7,39},{8,0},{9,41... | collective-permute-start | bytes 786440 | tf_op jit(solution)/shard_map/ppermute | solution.py:38
  32.3 10.0 %collective-permute-start.9 = (bf16[512,512]{1,0:T(8,128)(2,1)S(1)}, bf16[512,512]{1,0:T(8,128)(2,1)S(1)}, u32[]{:S(2)}, u32[]{:S(2)}) collective-permute-start(bf16[512,512]{1,0:T(8,128)(2,1)S(1)} %get-tuple-element.53.shared_keys), channel_id=1, source_target_pairs={{0,16},{1,5},{2,18},{3,7},{4,20},{5,9},{6,22},{7,11},{8,24},{9,13}... | collective-permute-start | bytes 1572872 | tf_op jit(solution)/shard_map/ppermute | solution.py:38
  33.6 23.2 %collective-permute-start.11 = (bf16[512,512]{1,0:T(8,128)(2,1)S(1)}, bf16[512,512]{1,0:T(8,128)(2,1)S(1)}, u32[]{:S(2)}, u32[]{:S(2)}) collective-permute-start(bf16[512,512]{1,0:T(8,128)(2,1)S(1)} %get-tuple-element.53.shared_keys), channel_id=1, source_target_pairs={{0,48},{1,13},{2,50},{3,15},{4,52},{5,1},{6,54},{7,3},{8,56},{9,5}... | collective-permute-start | bytes 1572872 | tf_op jit(solution)/shard_map/ppermute | solution.py:38
  35.5 25.8 %collective-permute-start.16 = (bf16[512,512]{1,0:T(8,128)(2,1)S(1)}, bf16[512,512]{1,0:T(8,128)(2,1)S(1)}, u32[]{:S(2)}, u32[]{:S(2)}) collective-permute-start(bf16[512,512]{1,0:T(8,128)(2,1)S(1)} %get-tuple-element.55.own_keys), channel_id=1, source_target_pairs={{0,48},{1,13},{2,50},{3,15},{4,52},{5,1},{6,54},{7,3},{8,56},{9,5}... | collective-permute-start | bytes 1572872 | tf_op jit(solution)/shard_map/ppermute | solution.py:38
  36.8 7.6 %collective-permute-start = (bf16[256,256]{1,0:T(8,128)(2,1)S(1)}, bf16[256,256]{1,0:T(8,128)(2,1)S(1)}, u32[]{:S(2)}, u32[]{:S(2)}) collective-permute-start(bf16[256,256]{1,0:T(8,128)(2,1)S(1)} %get-tuple-element.36), channel_id=1, source_target_pairs={{0,4},{1,17},{2,6},{3,19},{4,8},{5,21},{6,10},{7,23},{8,12},{9,25}... | collective-permute-start | bytes 393224 | tf_op jit(solution)/shard_map/ppermute | solution.py:38
  42.2 20.9 %collective-permute-start.10 = (bf16[512,512]{1,0:T(8,128)(2,1)S(1)}, bf16[512,512]{1,0:T(8,128)(2,1)S(1)}, u32[]{:S(2)}, u32[]{:S(2)}) collective-permute-start(bf16[512,512]{1,0:T(8,128)(2,1)S(1)} %collective-permute-done.9.keys), channel_id=1, source_target_pairs={{0,16},{1,5},{2,18},{3,7},{4,20},{5,9},{6,22},{7,11},{8,24},{9,13}... | collective-permute-start | bytes 1572872 | tf_op jit(solution)/shard_map/ppermute | solution.py:38
  42.2 6.7 %collective-permute-start.1 = (bf16[256,256]{1,0:T(8,128)(2,1)S(1)}, bf16[256,256]{1,0:T(8,128)(2,1)S(1)}, u32[]{:S(2)}, u32[]{:S(2)}) collective-permute-start(bf16[256,256]{1,0:T(8,128)(2,1)S(1)} %get-tuple-element.37), channel_id=1, source_target_pairs={{0,8},{1,33},{2,10},{3,35},{4,12},{5,37},{6,14},{7,39},{8,0},{9,41... | collective-permute-start | bytes 393224 | tf_op jit(solution)/shard_map/ppermute | solution.py:38
  44.5 11.6 %collective-permute-start.2 = (bf16[256,256]{1,0:T(8,128)(2,1)S(1)}, bf16[256,256]{1,0:T(8,128)(2,1)S(1)}, u32[]{:S(2)}, u32[]{:S(2)}) collective-permute-start(bf16[256,256]{1,0:T(8,128)(2,1)S(1)} %get-tuple-element.38), channel_id=1, source_target_pairs={{0,12},{1,49},{2,14},{3,51},{4,0},{5,53},{6,2},{7,55},{8,4},{9,57}... | collective-permute-start | bytes 393224 | tf_op jit(solution)/shard_map/ppermute | solution.py:38
  49.0 76.7 %collective-permute-start.21 = (bf16[640,1280]{1,0:T(8,128)(2,1)S(1)}, bf16[640,1280]{1,0:T(8,128)(2,1)S(1)}, u32[]{:S(2)}, u32[]{:S(2)}) collective-permute-start(bf16[640,1280]{1,0:T(8,128)(2,1)S(1)} %get-tuple-element.66), channel_id=1, source_target_pairs={{0,1},{1,0},{2,3},{3,2},{4,5},{5,4},{6,7},{7,6},{8,9},{9,8},{10,11... | collective-permute-start | bytes 4915208 | tf_op jit(solution)/shard_map/ppermute | solution.py:38
  56.1 13.3 %collective-permute-start.17 = (bf16[512,512]{1,0:T(8,128)(2,1)S(1)}, bf16[512,512]{1,0:T(8,128)(2,1)S(1)}, u32[]{:S(2)}, u32[]{:S(2)}) collective-permute-start(bf16[512,512]{1,0:T(8,128)(2,1)S(1)} %get-tuple-element.55.own_keys), channel_id=1, source_target_pairs={{0,16},{1,5},{2,18},{3,7},{4,20},{5,9},{6,22},{7,11},{8,24},{9,13}... | collective-permute-start | bytes 1572872 | tf_op jit(solution)/shard_map/ppermute | solution.py:38
  56.8 68.8 %collective-permute-start.27 = (bf16[640,1280]{1,0:T(8,128)(2,1)S(1)}, bf16[640,1280]{1,0:T(8,128)(2,1)S(1)}, u32[]{:S(2)}, u32[]{:S(2)}) collective-permute-start(bf16[640,1280]{1,0:T(8,128)(2,1)S(1)} %get-tuple-element.69), channel_id=1, source_target_pairs={{0,2},{1,3},{2,0},{3,1},{4,6},{5,7},{6,4},{7,5},{8,10},{9,11},{10,... | collective-permute-start | bytes 4915208 | tf_op jit(solution)/shard_map/ppermute | solution.py:38
  61.3 10.9 %collective-permute-start.18 = (bf16[512,512]{1,0:T(8,128)(2,1)S(1)}, bf16[512,512]{1,0:T(8,128)(2,1)S(1)}, u32[]{:S(2)}, u32[]{:S(2)}) collective-permute-start(bf16[512,512]{1,0:T(8,128)(2,1)S(1)} %collective-permute-done.16.b_keys), channel_id=1, source_target_pairs={{0,48},{1,13},{2,50},{3,15},{4,52},{5,1},{6,54},{7,3},{8,56},{9,5}... | collective-permute-start | bytes 1572872 | tf_op jit(solution)/shard_map/ppermute | solution.py:38
  63.2 64.0 %collective-permute-start.22 = (bf16[640,1280]{1,0:T(8,128)(2,1)S(1)}, bf16[640,1280]{1,0:T(8,128)(2,1)S(1)}, u32[]{:S(2)}, u32[]{:S(2)}) collective-permute-start(bf16[640,1280]{1,0:T(8,128)(2,1)S(1)} %get-tuple-element.67), channel_id=1, source_target_pairs={{0,195},{1,194},{2,65},{3,64},{4,199},{5,198},{6,69},{7,68},{8,203... | collective-permute-start | bytes 4915208 | tf_op jit(solution)/shard_map/ppermute | solution.py:49
  69.4 29.3 %collective-permute-start.23 = (bf16[512,128]{1,0:T(8,128)(2,1)S(1)}, bf16[512,128]{1,0:T(8,128)(2,1)S(1)}, u32[]{:S(2)}, u32[]{:S(2)}) collective-permute-start(bf16[512,128]{1,0:T(8,128)(2,1)S(1)} %get-tuple-element.57), channel_id=1, source_target_pairs={{0,14},{1,51},{2,12},{3,49},{4,2},{5,55},{6,0},{7,53},{8,6},{9,59}... | collective-permute-start | bytes 393224 | tf_op jit(solution)/shard_map/ppermute | solution.py:38
  72.2 31.9 %collective-permute-start.24 = (bf16[512,128]{1,0:T(8,128)(2,1)S(1)}, bf16[512,128]{1,0:T(8,128)(2,1)S(1)}, u32[]{:S(2)}, u32[]{:S(2)}) collective-permute-start(bf16[512,128]{1,0:T(8,128)(2,1)S(1)} %get-tuple-element.58), channel_id=1, source_target_pairs={{0,10},{1,35},{2,8},{3,33},{4,14},{5,39},{6,12},{7,37},{8,2},{9,43... | collective-permute-start | bytes 393224 | tf_op jit(solution)/shard_map/ppermute | solution.py:38
  98.7 7.5 %collective-permute-start.25 = (bf16[512,128]{1,0:T(8,128)(2,1)S(1)}, bf16[512,128]{1,0:T(8,128)(2,1)S(1)}, u32[]{:S(2)}, u32[]{:S(2)}) collective-permute-start(bf16[512,128]{1,0:T(8,128)(2,1)S(1)} %get-tuple-element.59), channel_id=1, source_target_pairs={{0,6},{1,19},{2,4},{3,17},{4,10},{5,23},{6,8},{7,21},{8,14},{9,27}... | collective-permute-start | bytes 393224 | tf_op jit(solution)/shard_map/ppermute | solution.py:38
  104.1 7.2 %collective-permute-start.12 = (bf16[512,128]{1,0:T(8,128)(2,1)S(1)}, bf16[512,128]{1,0:T(8,128)(2,1)S(1)}, u32[]{:S(2)}, u32[]{:S(2)}) collective-permute-start(bf16[512,128]{1,0:T(8,128)(2,1)S(1)} %get-tuple-element.57), channel_id=1, source_target_pairs={{0,12},{1,49},{2,14},{3,51},{4,0},{5,53},{6,2},{7,55},{8,4},{9,57}... | collective-permute-start | bytes 393224 | tf_op jit(solution)/shard_map/ppermute | solution.py:38
  106.2 5.7 %collective-permute-start.13 = (bf16[512,128]{1,0:T(8,128)(2,1)S(1)}, bf16[512,128]{1,0:T(8,128)(2,1)S(1)}, u32[]{:S(2)}, u32[]{:S(2)}) collective-permute-start(bf16[512,128]{1,0:T(8,128)(2,1)S(1)} %get-tuple-element.58), channel_id=1, source_target_pairs={{0,8},{1,33},{2,10},{3,35},{4,12},{5,37},{6,14},{7,39},{8,0},{9,41... | collective-permute-start | bytes 393224 | tf_op jit(solution)/shard_map/ppermute | solution.py:38
  111.3 5.6 %collective-permute-start.14 = (bf16[512,128]{1,0:T(8,128)(2,1)S(1)}, bf16[512,128]{1,0:T(8,128)(2,1)S(1)}, u32[]{:S(2)}, u32[]{:S(2)}) collective-permute-start(bf16[512,128]{1,0:T(8,128)(2,1)S(1)} %get-tuple-element.59), channel_id=1, source_target_pairs={{0,4},{1,17},{2,6},{3,19},{4,8},{5,21},{6,10},{7,23},{8,12},{9,25}... | collective-permute-start | bytes 393224 | tf_op jit(solution)/shard_map/ppermute | solution.py:38
  111.9 5.5 %collective-permute-start.28 = (bf16[512,256]{1,0:T(8,128)(2,1)S(1)}, bf16[512,256]{1,0:T(8,128)(2,1)S(1)}, u32[]{:S(2)}, u32[]{:S(2)}) collective-permute-start(bf16[512,256]{1,0:T(8,128)(2,1)S(1)} %shard_map.96.refs_0_), channel_id=1, source_target_pairs={{0,1},{1,0},{2,3},{3,2},{4,5},{5,4},{6,7},{7,6},{8,9},{9,8},{10,11... | collective-permute-start | bytes 786440 | tf_op jit(solution)/shard_map/ppermute | solution.py:38
  116.9 6.3 %collective-permute-start.19 = (bf16[512,256]{1,0:T(8,128)(2,1)S(1)}, bf16[512,256]{1,0:T(8,128)(2,1)S(1)}, u32[]{:S(2)}, u32[]{:S(2)}) collective-permute-start(bf16[512,256]{1,0:T(8,128)(2,1)S(1)} %shard_map.96.refs_0_), channel_id=1, source_target_pairs={{0,2},{1,3},{2,0},{3,1},{4,6},{5,7},{6,4},{7,5},{8,10},{9,11},{10,... | collective-permute-start | bytes 786440 | tf_op jit(solution)/shard_map/ppermute | solution.py:38
  117.4 9.8 %collective-permute-start.26 = (bf16[512,384]{1,0:T(8,128)(2,1)S(1)}, bf16[512,384]{1,0:T(8,128)(2,1)S(1)}, u32[]{:S(2)}, u32[]{:S(2)}) collective-permute-start(bf16[512,384]{1,0:T(8,128)(2,1)S(1)} %constant_dynamic-update-slice_fusion.7.refs_2_), channel_id=1, source_target_pairs={{0,1},{1,0},{2,3},{3,2},{4,5},{5,4},{6,7},{7,6},{8,9},{9,8},{10,11... | collective-permute-start | bytes 1179656 | tf_op jit(solution)/shard_map/ppermute | solution.py:38
  123.2 5.8 %collective-permute-start.15 = (bf16[512,384]{1,0:T(8,128)(2,1)S(1)}, bf16[512,384]{1,0:T(8,128)(2,1)S(1)}, u32[]{:S(2)}, u32[]{:S(2)}) collective-permute-start(bf16[512,384]{1,0:T(8,128)(2,1)S(1)} %constant_dynamic-update-slice_fusion.4.refs_1_), channel_id=1, source_target_pairs={{0,1},{1,0},{2,3},{3,2},{4,5},{5,4},{6,7},{7,6},{8,9},{9,8},{10,11... | collective-permute-start | bytes 1179656 | tf_op jit(solution)/shard_map/ppermute | solution.py:38
  125.6 3.4 %collective-permute-start.20 = (bf16[512,256]{1,0:T(8,128)(2,1)S(1)}, bf16[512,256]{1,0:T(8,128)(2,1)S(1)}, u32[]{:S(2)}, u32[]{:S(2)}) collective-permute-start(bf16[512,256]{1,0:T(8,128)(2,1)S(1)} %collective-permute-done.19.refs_2_), channel_id=1, source_target_pairs={{0,1},{1,0},{2,3},{3,2},{4,5},{5,4},{6,7},{7,6},{8,9},{9,8},{10,11... | collective-permute-start | bytes 786440 | tf_op jit(solution)/shard_map/ppermute | solution.py:38

commit v6 on v4

--- a/solution.py
+++ b/solution.py
@@ -38,14 +38,14 @@
     return lax.ppermute(array, AXES, pairs)
 
 
-def across(array, core=0):
+def across(array):
     pairs = []
     for index in range(ZH * NX * NY * ZL * CORES):
         rest, c = divmod(index, CORES)
         rest, b = divmod(rest, ZL)
         a, xy = divmod(rest, NX * NY)
         to = (a + 1) % ZH if b else (a - 1) % ZH
-        pairs.append((index, ((to * NX * NY + xy) * ZL + 1 - b) * CORES + (c + core) % CORES))
+        pairs.append((index, ((to * NX * NY + xy) * ZL + 1 - b) * CORES + 1 - c))
     return lax.ppermute(array, AXES, pairs)
 
 
@@ -178,13 +178,24 @@
     )
 
 
-def attend_others_kernel(query_ref, keys, state_ref, *out_refs):
+def attend_done_kernel(start, query_ref, keys, state_ref, *out_refs):
     rows = out_refs[0].shape[0] // 2
-    most = slice(0, rows * len(out_refs))
-    attended, attended_tan = finish(attend(query_ref[most, :], keys, load_state(state_ref, most)))
+    part = slice(start, start + rows * len(out_refs))
+    attended, attended_tan = finish(attend(query_ref[part, :], keys, load_state(state_ref, part)))
     for place, ref in enumerate(out_refs):
         ref[:rows, :] = attended[place * rows : (place + 1) * rows]
         ref[rows:, :] = attended_tan[place * rows : (place + 1) * rows]
+
+
+def attend_done(query, keys, state, start, rows, count):
+    return call(
+        functools.partial(attend_done_kernel, start),
+        [jax.ShapeDtypeStruct((2 * rows, HD), BF16)] * count,
+        query,
+        keys,
+        state,
+        flops=count * rows * keys.shape[0] * 1792,
+    )
 
 
 def attend_kept_kernel(shared_ref, own_ref, shared_keys, own_keys, shared_state, own_state, out_ref):
@@ -211,10 +222,7 @@
         for slot, k in enumerate(SLOTS):
             head = lax.rem(y_ref[0] + k, NY) if k < NY else NY
             source = w_ref.at[pl.ds(pl.multiple_of(head * HD, HD), HD), lanes]
-            if flip == ZL and slot == NY:
-                target = out_refs[-1]
-            else:
-                target = out_refs[flip].at[slot * HD : (slot + 1) * HD]
+            target = out_refs[flip].at[slot * HD : (slot + 1) * HD]
             copies.append(pltpu.make_async_copy(source, target, sems.at[flip, slot]))
     for copy in copies:
         copy.start()
@@ -328,10 +336,7 @@
     place, _ = lax.optimization_barrier((place, sends[1]))
     cuts = call(
         cut_weight_kernel,
-        [
-            jax.ShapeDtypeStruct((depth, columns), BF16)
-            for depth in (width, width, width - HD, width, HD)
-        ],
+        [jax.ShapeDtypeStruct((width, columns), BF16)] * (ZL * CORES),
         y,
         place,
         out_weight,
@@ -349,8 +354,7 @@
     )
     cuts, _ = lax.optimization_barrier((cuts, split[0]))
     weight_near = shift(cuts[2], zl=1)
-    weight_far = across(cuts[3], core=1)
-    weight_more = across(cuts[4])
+    weight_far = across(cuts[3])
     weight_core = shift(cuts[1], core=1)
 
     own = call(
@@ -366,15 +370,10 @@
     state = attend_step(blocks, own, ())
     state = attend_step(blocks, (left[0], right[1]), state)
     state = attend_step(blocks, (right[0], left[1]), state)
-    others = call(
-        attend_others_kernel,
-        [jax.ShapeDtypeStruct((2 * rows, HD), BF16)] * (NY - 1),
-        blocks[0],
-        opposite[0],
-        state[0],
-        flops=3 * rows * opposite[0].shape[0] * 1792,
-    )
-    opposite[1], _ = lax.optimization_barrier((opposite[1], others[0]))
+    others = attend_done(blocks[0], opposite[0], state[0], 0, rows, 1)
+    opposite[0], _ = lax.optimization_barrier((opposite[0], others[0]))
+    others += attend_done(blocks[0], opposite[0], state[0], rows, rows, NY - 2)
+    opposite[1], _ = lax.optimization_barrier((opposite[1], others[-1]))
     kept = call(
         attend_kept_kernel,
         jax.ShapeDtypeStruct((2 * rows, 2 * HD), BF16),
@@ -391,13 +390,12 @@
     mine = [kept, jnp.concatenate([shift(others[k - 1], swap=-k) for k in (1, 2, 3)], axis=1)]
     sibling = [shift(mine[n], core=1) for n in range(2)]
     far = [shift(near[n], core=1) for n in range(2)]
-    own, rest, cut = 2 * HD, 3 * HD, width - HD
+    own, rest = 2 * HD, 3 * HD
     partial = project_part(
         (
             (0, 0, own, 3, 0),
             (1, 0, own, 4, 0),
-            (2, 0, cut - own, 5, own),
-            (2, cut - own, rest, 6, 0),
+            (2, 0, rest, 5, own),
         ),
         mine[0],
         sibling[0],
@@ -405,7 +403,6 @@
         cuts[0],
         weight_core,
         weight_near,
-        weight_more,
     )
     partial = project_part(
         ((0, 0, rest, 3, own), (1, 0, rest, 4, own), (2, 0, own, 5, 0)),

time: 135 us -> 128 us (0.948)
  waiting for transfers between devices: 55.3 us -> 48 us
    ppermute x2 -> x1, waiting for transfers between devices: 32.5 us -> 0.01 us  [across(): return lax.ppermute(array, AXES, pairs)]
    ppermute x28, waiting for transfers between devices: 22.8 us -> 47.9 us  [shift(): return lax.ppermute(array, AXES, pairs)]
    ppermute x28, starting transfers between devices: 56.1 us -> 58.7 us  [shift(): return lax.ppermute(array, AXES, pairs)]
    ppermute x2 -> x1, starting transfers between devices: 2.84 us -> 0.27 us  [across(): return lax.ppermute(array, AXES, pairs)]
    pallas_call x12 -> x13, Pallas kernels: 17 us -> 17.4 us  [called(): pl.pallas_call(kernel, out_shape=outs, in_specs=specs or [VMEM] * len(ope...]
  transfers between devices with their start and end apart: 30 -> 29, of which waited for: 12 -> 11; matrix products, arithmetic and copies ran while one was open for 0% -> 0% of each run, Pallas kernels for 12% -> 13%
where the time goes in v6:
time: 128 us
  starting transfers between devices  59 us (46%)
  waiting for transfers between devices  48 us (38%)
  Pallas kernels  19.5 us (15%)
    ppermute x28, starting transfers between devices, shift(): return lax.ppermute(array, AXES, pairs)  58.7 us
    ppermute x28, waiting for transfers between devices, shift(): return lax.ppermute(array, AXES, pairs)  47.9 us
    pallas_call x13, Pallas kernels, called(): pl.pallas_call(kernel, out_shape=outs, in_specs=specs or [VMEM] * len(ope...  17.4 us
  transfers between devices with their start and end apart: 29, of which 11 were waited for; matrix products, arithmetic and copies ran while one was open for 0% of the time, Pallas kernels for 13%

profile of v6, /device:TPU:1, one launch (start us, length us, event | category | flops | bytes accessed | tf_op | source)
XLA Modules:
  0.0 127.7 jit_solution(17916772339860524694)
XLA Ops:
  0.6 0.9 shard_map.87.refs_0_
  1.5 3.9 %collective-permute-start.3 = (bf16[5,32,512]{2,1,0:T(8,128)(2,1)S(1)}, bf16[5,32,512]{2,1,0:T(8,128)(2,1)S(1)}, u32[]{:S(2)}, u32[]{:S(2)}) collective-permute-start(bf16[5,32,512]{2,1,0:T(8,128)(2,1)S(1)} %shard_map.87.refs_0_), channel_id=1, source_target_pairs={{0,64},{1,65},{2,66},{3,67},{4,68},{5,69},{6,70},{7,71},{8,72},{9,... | collective-permute-start | bytes 491528 | tf_op jit(solution)/shard_map/ppermute | solution.py:38
  5.4 3.1 %collective-permute-start.4 = (bf16[5,32,512]{2,1,0:T(8,128)(2,1)S(1)}, bf16[5,32,512]{2,1,0:T(8,128)(2,1)S(1)}, u32[]{:S(2)}, u32[]{:S(2)}) collective-permute-start(bf16[5,32,512]{2,1,0:T(8,128)(2,1)S(1)} %shard_map.87.refs_0_), channel_id=1, source_target_pairs={{0,192},{1,193},{2,194},{3,195},{4,196},{5,197},{6,198},{7,199},{8... | collective-permute-start | bytes 491528 | tf_op jit(solution)/shard_map/ppermute | solution.py:38
  8.5 4.4 %collective-permute-start.5 = (bf16[5,32,512]{2,1,0:T(8,128)(2,1)S(1)}, bf16[5,32,512]{2,1,0:T(8,128)(2,1)S(1)}, u32[]{:S(2)}, u32[]{:S(2)}) collective-permute-start(bf16[5,32,512]{2,1,0:T(8,128)(2,1)S(1)} %shard_map.87.refs_0_), channel_id=1, source_target_pairs={{0,128},{1,129},{2,130},{3,131},{4,132},{5,133},{6,134},{7,135},{8... | collective-permute-start | bytes 491528 | tf_op jit(solution)/shard_map/ppermute | solution.py:38
  12.9 1.2 shard_map.86
  14.1 3.1 %shard_map.88 = (bf16[640,1280]{1,0:T(8,128)(2,1)S(1)}, bf16[640,1280]{1,0:T(8,128)(2,1)S(1)}, bf16[640,1280]{1,0:T(8,128)(2,1)S(1)}, bf16[640,1280]{1,0:T(8,128)(2,1)S(1)}) custom-call(s32[1]{0:T(128)S(6)} %select_n.27.y_ref, s32[1]{0:T(128)} %bitcast.place_ref, bf16[640,5120]{1,0:T(8,128)(2,1)} %w_ref.1), custom_call_target="tpu_custom_call" | custom-call | bytes 6553608 | tf_op jit(solution)/shard_map/pallas_call | solution.py:57
  17.2 3.8 %collective-permute-done.4.refs_2_ = bf16[5,32,512]{2,1,0:T(8,128)(2,1)S(1)} collective-permute-done((bf16[5,32,512]{2,1,0:T(8,128)(2,1)S(1)}, bf16[5,32,512]{2,1,0:T(8,128)(2,1)S(1)}, u32[]{:S(2)}, u32[]{:S(2)}) %collective-permute-start.4) | collective-permute-done | bytes 163872 | tf_op jit(solution)/shard_map/ppermute | solution.py:38
  21.0 0.9 collective-permute-done.5.refs_3_
  21.9 1.3 %collective-permute-start.6 = (bf16[256,512]{1,0:T(8,128)(2,1)S(1)}, bf16[256,512]{1,0:T(8,128)(2,1)S(1)}, u32[]{:S(2)}, u32[]{:S(2)}) collective-permute-start(bf16[256,512]{1,0:T(8,128)(2,1)S(1)} %get-tuple-element.54), channel_id=1, source_target_pairs={{0,4},{1,17},{2,6},{3,19},{4,8},{5,21},{6,10},{7,23},{8,12},{9,25}... | collective-permute-start | bytes 786440 | tf_op jit(solution)/shard_map/ppermute | solution.py:38
  23.2 1.5 %collective-permute-start.7 = (bf16[256,512]{1,0:T(8,128)(2,1)S(1)}, bf16[256,512]{1,0:T(8,128)(2,1)S(1)}, u32[]{:S(2)}, u32[]{:S(2)}) collective-permute-start(bf16[256,512]{1,0:T(8,128)(2,1)S(1)} %get-tuple-element.55), channel_id=1, source_target_pairs={{0,12},{1,49},{2,14},{3,51},{4,0},{5,53},{6,2},{7,55},{8,4},{9,57}... | collective-permute-start | bytes 786440 | tf_op jit(solution)/shard_map/ppermute | solution.py:38
  24.6 1.5 %collective-permute-start.8 = (bf16[256,512]{1,0:T(8,128)(2,1)S(1)}, bf16[256,512]{1,0:T(8,128)(2,1)S(1)}, u32[]{:S(2)}, u32[]{:S(2)}) collective-permute-start(bf16[256,512]{1,0:T(8,128)(2,1)S(1)} %get-tuple-element.56), channel_id=1, source_target_pairs={{0,8},{1,33},{2,10},{3,35},{4,12},{5,37},{6,14},{7,39},{8,0},{9,41... | collective-permute-start | bytes 786440 | tf_op jit(solution)/shard_map/ppermute | solution.py:38
  26.2 2.2 %collective-permute-done.6.refs_1_ = bf16[256,512]{1,0:T(8,128)(2,1)S(1)} collective-permute-done((bf16[256,512]{1,0:T(8,128)(2,1)S(1)}, bf16[256,512]{1,0:T(8,128)(2,1)S(1)}, u32[]{:S(2)}, u32[]{:S(2)}) %collective-permute-start.6) | collective-permute-done | bytes 262176 | tf_op jit(solution)/shard_map/ppermute | solution.py:38
  28.4 3.8 %collective-permute-done.8.refs_3_ = bf16[256,512]{1,0:T(8,128)(2,1)S(1)} collective-permute-done((bf16[256,512]{1,0:T(8,128)(2,1)S(1)}, bf16[256,512]{1,0:T(8,128)(2,1)S(1)}, u32[]{:S(2)}, u32[]{:S(2)}) %collective-permute-start.8) | collective-permute-done | bytes 262176 | tf_op jit(solution)/shard_map/ppermute | solution.py:38
  32.3 1.4 %collective-permute-start.9 = (bf16[512,512]{1,0:T(8,128)(2,1)S(1)}, bf16[512,512]{1,0:T(8,128)(2,1)S(1)}, u32[]{:S(2)}, u32[]{:S(2)}) collective-permute-start(bf16[512,512]{1,0:T(8,128)(2,1)S(1)} %get-tuple-element.57.shared_keys), channel_id=1, source_target_pairs={{0,16},{1,5},{2,18},{3,7},{4,20},{5,9},{6,22},{7,11},{8,24},{9,13}... | collective-permute-start | bytes 1572872 | tf_op jit(solution)/shard_map/ppermute | solution.py:38
  33.6 0.9 collective-permute-start
  34.5 1.8 %collective-permute-start.13 = (bf16[512,512]{1,0:T(8,128)(2,1)S(1)}, bf16[512,512]{1,0:T(8,128)(2,1)S(1)}, u32[]{:S(2)}, u32[]{:S(2)}) collective-permute-start(bf16[512,512]{1,0:T(8,128)(2,1)S(1)} %get-tuple-element.59.own_keys), channel_id=1, source_target_pairs={{0,48},{1,13},{2,50},{3,15},{4,52},{5,1},{6,54},{7,3},{8,56},{9,5}... | collective-permute-start | bytes 1572872 | tf_op jit(solution)/shard_map/ppermute | solution.py:38
  36.3 2.0 %collective-permute-start.1 = (bf16[256,256]{1,0:T(8,128)(2,1)S(1)}, bf16[256,256]{1,0:T(8,128)(2,1)S(1)}, u32[]{:S(2)}, u32[]{:S(2)}) collective-permute-start(bf16[256,256]{1,0:T(8,128)(2,1)S(1)} %get-tuple-element.41), channel_id=1, source_target_pairs={{0,8},{1,33},{2,10},{3,35},{4,12},{5,37},{6,14},{7,39},{8,0},{9,41... | collective-permute-start | bytes 393224 | tf_op jit(solution)/shard_map/ppermute | solution.py:38
  38.4 1.4 %collective-permute-start.11 = (bf16[512,512]{1,0:T(8,128)(2,1)S(1)}, bf16[512,512]{1,0:T(8,128)(2,1)S(1)}, u32[]{:S(2)}, u32[]{:S(2)}) collective-permute-start(bf16[512,512]{1,0:T(8,128)(2,1)S(1)} %get-tuple-element.57.shared_keys), channel_id=1, source_target_pairs={{0,48},{1,13},{2,50},{3,15},{4,52},{5,1},{6,54},{7,3},{8,56},{9,5}... | collective-permute-start | bytes 1572872 | tf_op jit(solution)/shard_map/ppermute | solution.py:38
  40.0 1.7 %collective-permute-done.1 = bf16[256,256]{1,0:T(8,128)(2,1)S(1)} collective-permute-done((bf16[256,256]{1,0:T(8,128)(2,1)S(1)}, bf16[256,256]{1,0:T(8,128)(2,1)S(1)}, u32[]{:S(2)}, u32[]{:S(2)}) %collective-permute-start.1) | collective-permute-done | bytes 131104 | tf_op jit(solution)/shard_map/ppermute | solution.py:38
  41.7 1.7 %collective-permute-start.2 = (bf16[256,256]{1,0:T(8,128)(2,1)S(1)}, bf16[256,256]{1,0:T(8,128)(2,1)S(1)}, u32[]{:S(2)}, u32[]{:S(2)}) collective-permute-start(bf16[256,256]{1,0:T(8,128)(2,1)S(1)} %get-tuple-element.42), channel_id=1, source_target_pairs={{0,12},{1,49},{2,14},{3,51},{4,0},{5,53},{6,2},{7,55},{8,4},{9,57}... | collective-permute-start | bytes 393224 | tf_op jit(solution)/shard_map/ppermute | solution.py:38
  43.6 3.6 %collective-permute-done.2 = bf16[256,256]{1,0:T(8,128)(2,1)S(1)} collective-permute-done((bf16[256,256]{1,0:T(8,128)(2,1)S(1)}, bf16[256,256]{1,0:T(8,128)(2,1)S(1)}, u32[]{:S(2)}, u32[]{:S(2)}) %collective-permute-start.2) | collective-permute-done | bytes 131104 | tf_op jit(solution)/shard_map/ppermute | solution.py:38
  47.3 7.3 %collective-permute-start.21 = (bf16[640,1280]{1,0:T(8,128)(2,1)S(1)}, bf16[640,1280]{1,0:T(8,128)(2,1)S(1)}, u32[]{:S(2)}, u32[]{:S(2)}) collective-permute-start(bf16[640,1280]{1,0:T(8,128)(2,1)S(1)} %get-tuple-element.74), channel_id=1, source_target_pairs={{0,1},{1,0},{2,3},{3,2},{4,5},{5,4},{6,7},{7,6},{8,9},{9,8},{10,11... | collective-permute-start | bytes 4915208 | tf_op jit(solution)/shard_map/ppermute | solution.py:38
  54.6 3.8 %collective-permute-start.27 = (bf16[640,1280]{1,0:T(8,128)(2,1)S(1)}, bf16[640,1280]{1,0:T(8,128)(2,1)S(1)}, u32[]{:S(2)}, u32[]{:S(2)}) collective-permute-start(bf16[640,1280]{1,0:T(8,128)(2,1)S(1)} %get-tuple-element.77), channel_id=1, source_target_pairs={{0,2},{1,3},{2,0},{3,1},{4,6},{5,7},{6,4},{7,5},{8,10},{9,11},{10,... | collective-permute-start | bytes 4915208 | tf_op jit(solution)/shard_map/ppermute | solution.py:38
  58.4 0.3 collective-permute-start.22
  58.6 2.8 %collective-permute-start.18 = (bf16[512,512]{1,0:T(8,128)(2,1)S(1)}, bf16[512,512]{1,0:T(8,128)(2,1)S(1)}, u32[]{:S(2)}, u32[]{:S(2)}) collective-permute-start(bf16[512,512]{1,0:T(8,128)(2,1)S(1)} %collective-permute-done.13.own_keys), channel_id=1, source_target_pairs={{0,48},{1,13},{2,50},{3,15},{4,52},{5,1},{6,54},{7,3},{8,56},{9,5}... | collective-permute-start | bytes 1572872 | tf_op jit(solution)/shard_map/ppermute | solution.py:38
  61.5 1.8 %shard_map.91 = (f32[1024,768]{1,0:T(8,128)S(1)}, f32[256,768]{1,0:T(8,128)S(1)}) custom-call(bf16[1024,256]{1,0:T(8,128)(2,1)S(1)} %constant_dynamic-update-slice_fusion.shared_ref.query_ref, bf16[256,256]{1,0:T(8,128)(2,1)S(1)} %get-tuple-element.58.own_ref, bf16[512,512]{1,0:T(8,128)(2,1)S(1)} %get-tuple-element.57.shared_keys, ...), custom_call_target="tpu_custom_call" | custom-call | flops 1174405120 | bytes 1703936 | tf_op jit(solution)/shard_map/pallas_call | solution.py:57
  63.3 2.0 %shard_map.92 = (f32[1024,768]{1,0:T(8,128)S(1)}, f32[256,768]{1,0:T(8,128)S(1)}) custom-call(bf16[1024,256]{1,0:T(8,128)(2,1)S(1)} %constant_dynamic-update-slice_fusion.shared_ref.query_ref, bf16[256,256]{1,0:T(8,128)(2,1)S(1)} %get-tuple-element.58.own_ref, bf16[512,512]{1,0:T(8,128)(2,1)S(1)} %collective-permute-done.9.shared_keys, ...), custom_call_target="tpu_custom_call" | custom-call | flops 1174405120 | bytes 5636096 | tf_op jit(solution)/shard_map/pallas_call | solution.py:57
  65.2 2.0 %shard_map.93 = (f32[1024,768]{1,0:T(8,128)S(1)}, f32[256,768]{1,0:T(8,128)S(1)}) custom-call(bf16[1024,256]{1,0:T(8,128)(2,1)S(1)} %constant_dynamic-update-slice_fusion.shared_ref.query_ref, bf16[256,256]{1,0:T(8,128)(2,1)S(1)} %get-tuple-element.58.own_ref, bf16[512,512]{1,0:T(8,128)(2,1)S(1)} %collective-permute-done.11.shared_keys, ...), custom_call_target="tpu_custom_call" | custom-call | flops 1174405120 | bytes 5636096 | tf_op jit(solution)/shard_map/pallas_call | solution.py:57
  67.2 0.7 shard_map.94
  67.9 1.1 shard_map.95
  69.0 2.9 %collective-permute-start.24 = (bf16[512,128]{1,0:T(8,128)(2,1)S(1)}, bf16[512,128]{1,0:T(8,128)(2,1)S(1)}, u32[]{:S(2)}, u32[]{:S(2)}) collective-permute-start(bf16[512,128]{1,0:T(8,128)(2,1)S(1)} %get-tuple-element.66), channel_id=1, source_target_pairs={{0,10},{1,35},{2,8},{3,33},{4,14},{5,39},{6,12},{7,37},{8,2},{9,43... | collective-permute-start | bytes 393224 | tf_op jit(solution)/shard_map/ppermute | solution.py:38
  72.0 0.5 collective-permute-start.23
  72.4 26.5 %collective-permute-done.24 = bf16[512,128]{1,0:T(8,128)(2,1)S(1)} collective-permute-done((bf16[512,128]{1,0:T(8,128)(2,1)S(1)}, bf16[512,128]{1,0:T(8,128)(2,1)S(1)}, u32[]{:S(2)}, u32[]{:S(2)}) %collective-permute-start.24) | collective-permute-done | bytes 131104 | tf_op jit(solution)/shard_map/ppermute | solution.py:38
  98.9 0.7 collective-permute-start.25
  99.7 0.8 collective-permute-done.23
  100.5 1.7 %collective-permute-start.15 = (bf16[512,128]{1,0:T(8,128)(2,1)S(1)}, bf16[512,128]{1,0:T(8,128)(2,1)S(1)}, u32[]{:S(2)}, u32[]{:S(2)}) collective-permute-start(bf16[512,128]{1,0:T(8,128)(2,1)S(1)} %get-tuple-element.66), channel_id=1, source_target_pairs={{0,8},{1,33},{2,10},{3,35},{4,12},{5,37},{6,14},{7,39},{8,0},{9,41... | collective-permute-start | bytes 393224 | tf_op jit(solution)/shard_map/ppermute | solution.py:38
  102.2 3.1 %collective-permute-done.25 = bf16[512,128]{1,0:T(8,128)(2,1)S(1)} collective-permute-done((bf16[512,128]{1,0:T(8,128)(2,1)S(1)}, bf16[512,128]{1,0:T(8,128)(2,1)S(1)}, u32[]{:S(2)}, u32[]{:S(2)}) %collective-permute-start.25) | collective-permute-done | bytes 131104 | tf_op jit(solution)/shard_map/ppermute | solution.py:38
  105.3 1.2 shard_map.96.refs_0_
  106.5 1.8 %collective-permute-start.16 = (bf16[512,128]{1,0:T(8,128)(2,1)S(1)}, bf16[512,128]{1,0:T(8,128)(2,1)S(1)}, u32[]{:S(2)}, u32[]{:S(2)}) collective-permute-start(bf16[512,128]{1,0:T(8,128)(2,1)S(1)} %get-tuple-element.67), channel_id=1, source_target_pairs={{0,4},{1,17},{2,6},{3,19},{4,8},{5,21},{6,10},{7,23},{8,12},{9,25}... | collective-permute-start | bytes 393224 | tf_op jit(solution)/shard_map/ppermute | solution.py:38
  108.3 0.8 collective-permute-done.14
  109.1 3.0 %collective-permute-start.28 = (bf16[512,256]{1,0:T(8,128)(2,1)S(1)}, bf16[512,256]{1,0:T(8,128)(2,1)S(1)}, u32[]{:S(2)}, u32[]{:S(2)}) collective-permute-start(bf16[512,256]{1,0:T(8,128)(2,1)S(1)} %shard_map.96.refs_0_), channel_id=1, source_target_pairs={{0,1},{1,0},{2,3},{3,2},{4,5},{5,4},{6,7},{7,6},{8,9},{9,8},{10,11... | collective-permute-start | bytes 786440 | tf_op jit(solution)/shard_map/ppermute | solution.py:38
  112.1 2.3 %collective-permute-start.19 = (bf16[512,256]{1,0:T(8,128)(2,1)S(1)}, bf16[512,256]{1,0:T(8,128)(2,1)S(1)}, u32[]{:S(2)}, u32[]{:S(2)}) collective-permute-start(bf16[512,256]{1,0:T(8,128)(2,1)S(1)} %shard_map.96.refs_0_), channel_id=1, source_target_pairs={{0,2},{1,3},{2,0},{3,1},{4,6},{5,7},{6,4},{7,5},{8,10},{9,11},{10,... | collective-permute-start | bytes 786440 | tf_op jit(solution)/shard_map/ppermute | solution.py:38
  114.4 3.0 %collective-permute-start.26 = (bf16[512,384]{1,0:T(8,128)(2,1)S(1)}, bf16[512,384]{1,0:T(8,128)(2,1)S(1)}, u32[]{:S(2)}, u32[]{:S(2)}) collective-permute-start(bf16[512,384]{1,0:T(8,128)(2,1)S(1)} %constant_dynamic-update-slice_fusion.7.refs_2_), channel_id=1, source_target_pairs={{0,1},{1,0},{2,3},{3,2},{4,5},{5,4},{6,7},{7,6},{8,9},{9,8},{10,11... | collective-permute-start | bytes 1179656 | tf_op jit(solution)/shard_map/ppermute | solution.py:38
  117.5 0.7 collective-permute-done.19.refs_2_
  118.1 3.9 %collective-permute-start.17 = (bf16[512,384]{1,0:T(8,128)(2,1)S(1)}, bf16[512,384]{1,0:T(8,128)(2,1)S(1)}, u32[]{:S(2)}, u32[]{:S(2)}) collective-permute-start(bf16[512,384]{1,0:T(8,128)(2,1)S(1)} %constant_dynamic-update-slice_fusion.4.refs_1_), channel_id=1, source_target_pairs={{0,1},{1,0},{2,3},{3,2},{4,5},{5,4},{6,7},{7,6},{8,9},{9,8},{10,11... | collective-permute-start | bytes 1179656 | tf_op jit(solution)/shard_map/ppermute | solution.py:38
  122.0 1.5 %shard_map.97.refs_6_ = f32[512,1280]{1,0:T(8,128)S(1)} custom-call(bf16[512,256]{1,0:T(8,128)(2,1)S(1)} %shard_map.96.refs_0_, bf16[512,256]{1,0:T(8,128)(2,1)S(1)} %collective-permute-done.28.refs_1_, bf16[512,384]{1,0:T(8,128)(2,1)S(1)} %constant_dynamic-update-slice_fusion.7.refs_2_, bf16[640,1280]{1,0:T(8,128)(2,1)S(1)} %get-tuple-element.76.refs_3_.refs_4_, ...), custom_call_target="tpu_custom_call" | custom-call | flops 1174405120 | bytes 5832704 | tf_op jit(solution)/shard_map/pallas_call | solution.py:57
  123.6 1.8 %shard_map.98.refs_4_ = f32[512,1280]{1,0:T(8,128)S(1)} custom-call(bf16[512,384]{1,0:T(8,128)(2,1)S(1)} %collective-permute-done.26.refs_0_, bf16[512,384]{1,0:T(8,128)(2,1)S(1)} %constant_dynamic-update-slice_fusion.4.refs_1_, bf16[512,256]{1,0:T(8,128)(2,1)S(1)} %collective-permute-done.19.refs_2_, bf16[640,1280]{1,0:T(8,128)(2,1)S(1)} %collective-permute-done.22.refs_3_, ...), custom_call_target="tpu_custom_call" | custom-call | flops 1342177280 | bytes 8585216 | tf_op jit(solution)/shard_map/pallas_call | solution.py:57
  125.4 2.1 %project_last.1 = (bf16[256,1280]{1,0:T(8,128)(2,1)}, bf16[256,1280]{1,0:T(8,128)(2,1)}) custom-call(bf16[512,384]{1,0:T(8,128)(2,1)S(1)} %collective-permute-done.17.refs_0_, bf16[512,256]{1,0:T(8,128)(2,1)S(1)} %collective-permute-done.20.refs_1_, bf16[640,1280]{1,0:T(8,128)(2,1)S(1)} %collective-permute-done.21.refs_4_.refs_2_, ...), custom_call_target="tpu_custom_call" | custom-call | tf_op jit(solution)/shard_map/project_last/pallas_call | solution.py:283
  (34 shorter events, 0.7 us)
Async XLA Ops:
  1.5 15.7 %collective-permute-start.3 = (bf16[5,32,512]{2,1,0:T(8,128)(2,1)S(1)}, bf16[5,32,512]{2,1,0:T(8,128)(2,1)S(1)}, u32[]{:S(2)}, u32[]{:S(2)}) collective-permute-start(bf16[5,32,512]{2,1,0:T(8,128)(2,1)S(1)} %shard_map.87.refs_0_), channel_id=1, source_target_pairs={{0,64},{1,65},{2,66},{3,67},{4,68},{5,69},{6,70},{7,71},{8,72},{9,... | collective-permute-start | bytes 491528 | tf_op jit(solution)/shard_map/ppermute | solution.py:38
  5.4 15.5 %collective-permute-start.4 = (bf16[5,32,512]{2,1,0:T(8,128)(2,1)S(1)}, bf16[5,32,512]{2,1,0:T(8,128)(2,1)S(1)}, u32[]{:S(2)}, u32[]{:S(2)}) collective-permute-start(bf16[5,32,512]{2,1,0:T(8,128)(2,1)S(1)} %shard_map.87.refs_0_), channel_id=1, source_target_pairs={{0,192},{1,193},{2,194},{3,195},{4,196},{5,197},{6,198},{7,199},{8... | collective-permute-start | bytes 491528 | tf_op jit(solution)/shard_map/ppermute | solution.py:38
  8.5 13.3 %collective-permute-start.5 = (bf16[5,32,512]{2,1,0:T(8,128)(2,1)S(1)}, bf16[5,32,512]{2,1,0:T(8,128)(2,1)S(1)}, u32[]{:S(2)}, u32[]{:S(2)}) collective-permute-start(bf16[5,32,512]{2,1,0:T(8,128)(2,1)S(1)} %shard_map.87.refs_0_), channel_id=1, source_target_pairs={{0,128},{1,129},{2,130},{3,131},{4,132},{5,133},{6,134},{7,135},{8... | collective-permute-start | bytes 491528 | tf_op jit(solution)/shard_map/ppermute | solution.py:38
  21.9 6.5 %collective-permute-start.6 = (bf16[256,512]{1,0:T(8,128)(2,1)S(1)}, bf16[256,512]{1,0:T(8,128)(2,1)S(1)}, u32[]{:S(2)}, u32[]{:S(2)}) collective-permute-start(bf16[256,512]{1,0:T(8,128)(2,1)S(1)} %get-tuple-element.54), channel_id=1, source_target_pairs={{0,4},{1,17},{2,6},{3,19},{4,8},{5,21},{6,10},{7,23},{8,12},{9,25}... | collective-permute-start | bytes 786440 | tf_op jit(solution)/shard_map/ppermute | solution.py:38
  23.2 5.2 %collective-permute-start.7 = (bf16[256,512]{1,0:T(8,128)(2,1)S(1)}, bf16[256,512]{1,0:T(8,128)(2,1)S(1)}, u32[]{:S(2)}, u32[]{:S(2)}) collective-permute-start(bf16[256,512]{1,0:T(8,128)(2,1)S(1)} %get-tuple-element.55), channel_id=1, source_target_pairs={{0,12},{1,49},{2,14},{3,51},{4,0},{5,53},{6,2},{7,55},{8,4},{9,57}... | collective-permute-start | bytes 786440 | tf_op jit(solution)/shard_map/ppermute | solution.py:38
  24.6 7.5 %collective-permute-start.8 = (bf16[256,512]{1,0:T(8,128)(2,1)S(1)}, bf16[256,512]{1,0:T(8,128)(2,1)S(1)}, u32[]{:S(2)}, u32[]{:S(2)}) collective-permute-start(bf16[256,512]{1,0:T(8,128)(2,1)S(1)} %get-tuple-element.56), channel_id=1, source_target_pairs={{0,8},{1,33},{2,10},{3,35},{4,12},{5,37},{6,14},{7,39},{8,0},{9,41... | collective-permute-start | bytes 786440 | tf_op jit(solution)/shard_map/ppermute | solution.py:38
  32.3 11.2 %collective-permute-start.9 = (bf16[512,512]{1,0:T(8,128)(2,1)S(1)}, bf16[512,512]{1,0:T(8,128)(2,1)S(1)}, u32[]{:S(2)}, u32[]{:S(2)}) collective-permute-start(bf16[512,512]{1,0:T(8,128)(2,1)S(1)} %get-tuple-element.57.shared_keys), channel_id=1, source_target_pairs={{0,16},{1,5},{2,18},{3,7},{4,20},{5,9},{6,22},{7,11},{8,24},{9,13}... | collective-permute-start | bytes 1572872 | tf_op jit(solution)/shard_map/ppermute | solution.py:38
  33.6 6.1 %collective-permute-start = (bf16[256,256]{1,0:T(8,128)(2,1)S(1)}, bf16[256,256]{1,0:T(8,128)(2,1)S(1)}, u32[]{:S(2)}, u32[]{:S(2)}) collective-permute-start(bf16[256,256]{1,0:T(8,128)(2,1)S(1)} %get-tuple-element.40), channel_id=1, source_target_pairs={{0,4},{1,17},{2,6},{3,19},{4,8},{5,21},{6,10},{7,23},{8,12},{9,25}... | collective-permute-start | bytes 393224 | tf_op jit(solution)/shard_map/ppermute | solution.py:38
  34.5 20.0 %collective-permute-start.13 = (bf16[512,512]{1,0:T(8,128)(2,1)S(1)}, bf16[512,512]{1,0:T(8,128)(2,1)S(1)}, u32[]{:S(2)}, u32[]{:S(2)}) collective-permute-start(bf16[512,512]{1,0:T(8,128)(2,1)S(1)} %get-tuple-element.59.own_keys), channel_id=1, source_target_pairs={{0,48},{1,13},{2,50},{3,15},{4,52},{5,1},{6,54},{7,3},{8,56},{9,5}... | collective-permute-start | bytes 1572872 | tf_op jit(solution)/shard_map/ppermute | solution.py:38
  36.3 5.4 %collective-permute-start.1 = (bf16[256,256]{1,0:T(8,128)(2,1)S(1)}, bf16[256,256]{1,0:T(8,128)(2,1)S(1)}, u32[]{:S(2)}, u32[]{:S(2)}) collective-permute-start(bf16[256,256]{1,0:T(8,128)(2,1)S(1)} %get-tuple-element.41), channel_id=1, source_target_pairs={{0,8},{1,33},{2,10},{3,35},{4,12},{5,37},{6,14},{7,39},{8,0},{9,41... | collective-permute-start | bytes 393224 | tf_op jit(solution)/shard_map/ppermute | solution.py:38
  38.4 20.0 %collective-permute-start.11 = (bf16[512,512]{1,0:T(8,128)(2,1)S(1)}, bf16[512,512]{1,0:T(8,128)(2,1)S(1)}, u32[]{:S(2)}, u32[]{:S(2)}) collective-permute-start(bf16[512,512]{1,0:T(8,128)(2,1)S(1)} %get-tuple-element.57.shared_keys), channel_id=1, source_target_pairs={{0,48},{1,13},{2,50},{3,15},{4,52},{5,1},{6,54},{7,3},{8,56},{9,5}... | collective-permute-start | bytes 1572872 | tf_op jit(solution)/shard_map/ppermute | solution.py:38
  39.7 18.9 %collective-permute-start.12 = (bf16[512,512]{1,0:T(8,128)(2,1)S(1)}, bf16[512,512]{1,0:T(8,128)(2,1)S(1)}, u32[]{:S(2)}, u32[]{:S(2)}) collective-permute-start(bf16[512,512]{1,0:T(8,128)(2,1)S(1)} %get-tuple-element.59.own_keys), channel_id=1, source_target_pairs={{0,16},{1,5},{2,18},{3,7},{4,20},{5,9},{6,22},{7,11},{8,24},{9,13}... | collective-permute-start | bytes 1572872 | tf_op jit(solution)/shard_map/ppermute | solution.py:38
  41.7 5.5 %collective-permute-start.2 = (bf16[256,256]{1,0:T(8,128)(2,1)S(1)}, bf16[256,256]{1,0:T(8,128)(2,1)S(1)}, u32[]{:S(2)}, u32[]{:S(2)}) collective-permute-start(bf16[256,256]{1,0:T(8,128)(2,1)S(1)} %get-tuple-element.42), channel_id=1, source_target_pairs={{0,12},{1,49},{2,14},{3,51},{4,0},{5,53},{6,2},{7,55},{8,4},{9,57}... | collective-permute-start | bytes 393224 | tf_op jit(solution)/shard_map/ppermute | solution.py:38
  43.5 23.7 %collective-permute-start.10 = (bf16[512,512]{1,0:T(8,128)(2,1)S(1)}, bf16[512,512]{1,0:T(8,128)(2,1)S(1)}, u32[]{:S(2)}, u32[]{:S(2)}) collective-permute-start(bf16[512,512]{1,0:T(8,128)(2,1)S(1)} %collective-permute-done.9.shared_keys), channel_id=1, source_target_pairs={{0,16},{1,5},{2,18},{3,7},{4,20},{5,9},{6,22},{7,11},{8,24},{9,13}... | collective-permute-start | bytes 1572872 | tf_op jit(solution)/shard_map/ppermute | solution.py:38
  47.3 74.7 %collective-permute-start.21 = (bf16[640,1280]{1,0:T(8,128)(2,1)S(1)}, bf16[640,1280]{1,0:T(8,128)(2,1)S(1)}, u32[]{:S(2)}, u32[]{:S(2)}) collective-permute-start(bf16[640,1280]{1,0:T(8,128)(2,1)S(1)} %get-tuple-element.74), channel_id=1, source_target_pairs={{0,1},{1,0},{2,3},{3,2},{4,5},{5,4},{6,7},{7,6},{8,9},{9,8},{10,11... | collective-permute-start | bytes 4915208 | tf_op jit(solution)/shard_map/ppermute | solution.py:38
  54.6 67.4 %collective-permute-start.27 = (bf16[640,1280]{1,0:T(8,128)(2,1)S(1)}, bf16[640,1280]{1,0:T(8,128)(2,1)S(1)}, u32[]{:S(2)}, u32[]{:S(2)}) collective-permute-start(bf16[640,1280]{1,0:T(8,128)(2,1)S(1)} %get-tuple-element.77), channel_id=1, source_target_pairs={{0,2},{1,3},{2,0},{3,1},{4,6},{5,7},{6,4},{7,5},{8,10},{9,11},{10,... | collective-permute-start | bytes 4915208 | tf_op jit(solution)/shard_map/ppermute | solution.py:38
  58.4 65.2 %collective-permute-start.22 = (bf16[640,1280]{1,0:T(8,128)(2,1)S(1)}, bf16[640,1280]{1,0:T(8,128)(2,1)S(1)}, u32[]{:S(2)}, u32[]{:S(2)}) collective-permute-start(bf16[640,1280]{1,0:T(8,128)(2,1)S(1)} %get-tuple-element.75), channel_id=1, source_target_pairs={{0,195},{1,194},{2,65},{3,64},{4,199},{5,198},{6,69},{7,68},{8,203... | collective-permute-start | bytes 4915208 | tf_op jit(solution)/shard_map/ppermute | solution.py:49
  58.6 13.3 %collective-permute-start.18 = (bf16[512,512]{1,0:T(8,128)(2,1)S(1)}, bf16[512,512]{1,0:T(8,128)(2,1)S(1)}, u32[]{:S(2)}, u32[]{:S(2)}) collective-permute-start(bf16[512,512]{1,0:T(8,128)(2,1)S(1)} %collective-permute-done.13.own_keys), channel_id=1, source_target_pairs={{0,48},{1,13},{2,50},{3,15},{4,52},{5,1},{6,54},{7,3},{8,56},{9,5}... | collective-permute-start | bytes 1572872 | tf_op jit(solution)/shard_map/ppermute | solution.py:38
  69.0 29.9 %collective-permute-start.24 = (bf16[512,128]{1,0:T(8,128)(2,1)S(1)}, bf16[512,128]{1,0:T(8,128)(2,1)S(1)}, u32[]{:S(2)}, u32[]{:S(2)}) collective-permute-start(bf16[512,128]{1,0:T(8,128)(2,1)S(1)} %get-tuple-element.66), channel_id=1, source_target_pairs={{0,10},{1,35},{2,8},{3,33},{4,14},{5,39},{6,12},{7,37},{8,2},{9,43... | collective-permute-start | bytes 393224 | tf_op jit(solution)/shard_map/ppermute | solution.py:38
  72.0 28.6 %collective-permute-start.23 = (bf16[512,128]{1,0:T(8,128)(2,1)S(1)}, bf16[512,128]{1,0:T(8,128)(2,1)S(1)}, u32[]{:S(2)}, u32[]{:S(2)}) collective-permute-start(bf16[512,128]{1,0:T(8,128)(2,1)S(1)} %shard_map.94), channel_id=1, source_target_pairs={{0,14},{1,51},{2,12},{3,49},{4,2},{5,55},{6,0},{7,53},{8,6},{9,59}... | collective-permute-start | bytes 393224 | tf_op jit(solution)/shard_map/ppermute | solution.py:38
  98.9 6.3 %collective-permute-start.25 = (bf16[512,128]{1,0:T(8,128)(2,1)S(1)}, bf16[512,128]{1,0:T(8,128)(2,1)S(1)}, u32[]{:S(2)}, u32[]{:S(2)}) collective-permute-start(bf16[512,128]{1,0:T(8,128)(2,1)S(1)} %get-tuple-element.67), channel_id=1, source_target_pairs={{0,6},{1,19},{2,4},{3,17},{4,10},{5,23},{6,8},{7,21},{8,14},{9,27}... | collective-permute-start | bytes 393224 | tf_op jit(solution)/shard_map/ppermute | solution.py:38
  100.5 6.0 %collective-permute-start.15 = (bf16[512,128]{1,0:T(8,128)(2,1)S(1)}, bf16[512,128]{1,0:T(8,128)(2,1)S(1)}, u32[]{:S(2)}, u32[]{:S(2)}) collective-permute-start(bf16[512,128]{1,0:T(8,128)(2,1)S(1)} %get-tuple-element.66), channel_id=1, source_target_pairs={{0,8},{1,33},{2,10},{3,35},{4,12},{5,37},{6,14},{7,39},{8,0},{9,41... | collective-permute-start | bytes 393224 | tf_op jit(solution)/shard_map/ppermute | solution.py:38
  105.3 3.8 %collective-permute-start.14 = (bf16[512,128]{1,0:T(8,128)(2,1)S(1)}, bf16[512,128]{1,0:T(8,128)(2,1)S(1)}, u32[]{:S(2)}, u32[]{:S(2)}) collective-permute-start(bf16[512,128]{1,0:T(8,128)(2,1)S(1)} %shard_map.94), channel_id=1, source_target_pairs={{0,12},{1,49},{2,14},{3,51},{4,0},{5,53},{6,2},{7,55},{8,4},{9,57}... | collective-permute-start | bytes 393224 | tf_op jit(solution)/shard_map/ppermute | solution.py:38
  106.5 5.6 %collective-permute-start.16 = (bf16[512,128]{1,0:T(8,128)(2,1)S(1)}, bf16[512,128]{1,0:T(8,128)(2,1)S(1)}, u32[]{:S(2)}, u32[]{:S(2)}) collective-permute-start(bf16[512,128]{1,0:T(8,128)(2,1)S(1)} %get-tuple-element.67), channel_id=1, source_target_pairs={{0,4},{1,17},{2,6},{3,19},{4,8},{5,21},{6,10},{7,23},{8,12},{9,25}... | collective-permute-start | bytes 393224 | tf_op jit(solution)/shard_map/ppermute | solution.py:38
  109.1 5.3 %collective-permute-start.28 = (bf16[512,256]{1,0:T(8,128)(2,1)S(1)}, bf16[512,256]{1,0:T(8,128)(2,1)S(1)}, u32[]{:S(2)}, u32[]{:S(2)}) collective-permute-start(bf16[512,256]{1,0:T(8,128)(2,1)S(1)} %shard_map.96.refs_0_), channel_id=1, source_target_pairs={{0,1},{1,0},{2,3},{3,2},{4,5},{5,4},{6,7},{7,6},{8,9},{9,8},{10,11... | collective-permute-start | bytes 786440 | tf_op jit(solution)/shard_map/ppermute | solution.py:38
  112.1 6.0 %collective-permute-start.19 = (bf16[512,256]{1,0:T(8,128)(2,1)S(1)}, bf16[512,256]{1,0:T(8,128)(2,1)S(1)}, u32[]{:S(2)}, u32[]{:S(2)}) collective-permute-start(bf16[512,256]{1,0:T(8,128)(2,1)S(1)} %shard_map.96.refs_0_), channel_id=1, source_target_pairs={{0,2},{1,3},{2,0},{3,1},{4,6},{5,7},{6,4},{7,5},{8,10},{9,11},{10,... | collective-permute-start | bytes 786440 | tf_op jit(solution)/shard_map/ppermute | solution.py:38
  114.4 9.1 %collective-permute-start.26 = (bf16[512,384]{1,0:T(8,128)(2,1)S(1)}, bf16[512,384]{1,0:T(8,128)(2,1)S(1)}, u32[]{:S(2)}, u32[]{:S(2)}) collective-permute-start(bf16[512,384]{1,0:T(8,128)(2,1)S(1)} %constant_dynamic-update-slice_fusion.7.refs_2_), channel_id=1, source_target_pairs={{0,1},{1,0},{2,3},{3,2},{4,5},{5,4},{6,7},{7,6},{8,9},{9,8},{10,11... | collective-permute-start | bytes 1179656 | tf_op jit(solution)/shard_map/ppermute | solution.py:38
  118.1 7.3 %collective-permute-start.17 = (bf16[512,384]{1,0:T(8,128)(2,1)S(1)}, bf16[512,384]{1,0:T(8,128)(2,1)S(1)}, u32[]{:S(2)}, u32[]{:S(2)}) collective-permute-start(bf16[512,384]{1,0:T(8,128)(2,1)S(1)} %constant_dynamic-update-slice_fusion.4.refs_1_), channel_id=1, source_target_pairs={{0,1},{1,0},{2,3},{3,2},{4,5},{5,4},{6,7},{7,6},{8,9},{9,8},{10,11... | collective-permute-start | bytes 1179656 | tf_op jit(solution)/shard_map/ppermute | solution.py:38
  122.0 3.4 %collective-permute-start.20 = (bf16[512,256]{1,0:T(8,128)(2,1)S(1)}, bf16[512,256]{1,0:T(8,128)(2,1)S(1)}, u32[]{:S(2)}, u32[]{:S(2)}) collective-permute-start(bf16[512,256]{1,0:T(8,128)(2,1)S(1)} %collective-permute-done.19.refs_2_), channel_id=1, source_target_pairs={{0,1},{1,0},{2,3},{3,2},{4,5},{5,4},{6,7},{7,6},{8,9},{9,8},{10,11... | collective-permute-start | bytes 786440 | tf_op jit(solution)/shard_map/ppermute | solution.py:38

commit v7 on v4

--- a/solution.py
+++ b/solution.py
@@ -38,14 +38,14 @@
     return lax.ppermute(array, AXES, pairs)
 
 
-def across(array, core=0):
+def across(array):
     pairs = []
     for index in range(ZH * NX * NY * ZL * CORES):
         rest, c = divmod(index, CORES)
         rest, b = divmod(rest, ZL)
         a, xy = divmod(rest, NX * NY)
         to = (a + 1) % ZH if b else (a - 1) % ZH
-        pairs.append((index, ((to * NX * NY + xy) * ZL + 1 - b) * CORES + (c + core) % CORES))
+        pairs.append((index, ((to * NX * NY + xy) * ZL + 1 - b) * CORES + 1 - c))
     return lax.ppermute(array, AXES, pairs)
 
 
@@ -211,10 +211,7 @@
         for slot, k in enumerate(SLOTS):
             head = lax.rem(y_ref[0] + k, NY) if k < NY else NY
             source = w_ref.at[pl.ds(pl.multiple_of(head * HD, HD), HD), lanes]
-            if flip == ZL and slot == NY:
-                target = out_refs[-1]
-            else:
-                target = out_refs[flip].at[slot * HD : (slot + 1) * HD]
+            target = out_refs[flip].at[slot * HD : (slot + 1) * HD]
             copies.append(pltpu.make_async_copy(source, target, sems.at[flip, slot]))
     for copy in copies:
         copy.start()
@@ -328,10 +325,7 @@
     place, _ = lax.optimization_barrier((place, sends[1]))
     cuts = call(
         cut_weight_kernel,
-        [
-            jax.ShapeDtypeStruct((depth, columns), BF16)
-            for depth in (width, width, width - HD, width, HD)
-        ],
+        [jax.ShapeDtypeStruct((width, columns), BF16)] * (ZL * CORES),
         y,
         place,
         out_weight,
@@ -349,8 +343,7 @@
     )
     cuts, _ = lax.optimization_barrier((cuts, split[0]))
     weight_near = shift(cuts[2], zl=1)
-    weight_far = across(cuts[3], core=1)
-    weight_more = across(cuts[4])
+    weight_far = across(cuts[3])
     weight_core = shift(cuts[1], core=1)
 
     own = call(
@@ -391,13 +384,12 @@
     mine = [kept, jnp.concatenate([shift(others[k - 1], swap=-k) for k in (1, 2, 3)], axis=1)]
     sibling = [shift(mine[n], core=1) for n in range(2)]
     far = [shift(near[n], core=1) for n in range(2)]
-    own, rest, cut = 2 * HD, 3 * HD, width - HD
+    own, rest = 2 * HD, 3 * HD
     partial = project_part(
         (
             (0, 0, own, 3, 0),
             (1, 0, own, 4, 0),
-            (2, 0, cut - own, 5, own),
-            (2, cut - own, rest, 6, 0),
+            (2, 0, rest, 5, own),
         ),
         mine[0],
         sibling[0],
@@ -405,7 +397,6 @@
         cuts[0],
         weight_core,
         weight_near,
-        weight_more,
     )
     partial = project_part(
         ((0, 0, rest, 3, own), (1, 0, rest, 4, own), (2, 0, own, 5, 0)),

time: 135 us -> 128 us (0.948)
  waiting for transfers between devices: 55.3 us -> 48.2 us
    ppermute x2 -> x1, waiting for transfers between devices: 32.5 us -> 0.01 us  [across(): return lax.ppermute(array, AXES, pairs)]
    ppermute x28, waiting for transfers between devices: 22.8 us -> 48.2 us  [shift(): return lax.ppermute(array, AXES, pairs)]
    ppermute x28, starting transfers between devices: 56.1 us -> 59 us  [shift(): return lax.ppermute(array, AXES, pairs)]
    ppermute x2 -> x1, starting transfers between devices: 2.84 us -> 0.27 us  [across(): return lax.ppermute(array, AXES, pairs)]
  transfers between devices with their start and end apart: 30 -> 29, of which waited for: 12 -> 12; matrix products, arithmetic and copies ran while one was open for 0% -> 0% of each run, Pallas kernels for 12% -> 12%
where the time goes in v7:
time: 128 us
  starting transfers between devices  59.3 us (46%)
  waiting for transfers between devices  48.2 us (38%)
  Pallas kernels  19.1 us (15%)
    ppermute x28, starting transfers between devices, shift(): return lax.ppermute(array, AXES, pairs)  59 us
    ppermute x28, waiting for transfers between devices, shift(): return lax.ppermute(array, AXES, pairs)  48.2 us
    pallas_call x12, Pallas kernels, called(): pl.pallas_call(kernel, out_shape=outs, in_specs=specs or [VMEM] * len(ope...  17 us
  transfers between devices with their start and end apart: 29, of which 12 were waited for; matrix products, arithmetic and copies ran while one was open for 0% of the time, Pallas kernels for 12%

profile of v7, /device:TPU:1, one launch (start us, length us, event | category | flops | bytes accessed | tf_op | source)
XLA Modules:
  0.0 127.8 jit_solution(5337234892797359070)
XLA Ops:
  0.6 0.9 shard_map.87.refs_0_
  1.5 3.9 %collective-permute-start.3 = (bf16[5,32,512]{2,1,0:T(8,128)(2,1)S(1)}, bf16[5,32,512]{2,1,0:T(8,128)(2,1)S(1)}, u32[]{:S(2)}, u32[]{:S(2)}) collective-permute-start(bf16[5,32,512]{2,1,0:T(8,128)(2,1)S(1)} %shard_map.87.refs_0_), channel_id=1, source_target_pairs={{0,64},{1,65},{2,66},{3,67},{4,68},{5,69},{6,70},{7,71},{8,72},{9,... | collective-permute-start | bytes 491528 | tf_op jit(solution)/shard_map/ppermute | solution.py:38
  5.4 3.1 %collective-permute-start.4 = (bf16[5,32,512]{2,1,0:T(8,128)(2,1)S(1)}, bf16[5,32,512]{2,1,0:T(8,128)(2,1)S(1)}, u32[]{:S(2)}, u32[]{:S(2)}) collective-permute-start(bf16[5,32,512]{2,1,0:T(8,128)(2,1)S(1)} %shard_map.87.refs_0_), channel_id=1, source_target_pairs={{0,192},{1,193},{2,194},{3,195},{4,196},{5,197},{6,198},{7,199},{8... | collective-permute-start | bytes 491528 | tf_op jit(solution)/shard_map/ppermute | solution.py:38
  8.5 4.4 %collective-permute-start.5 = (bf16[5,32,512]{2,1,0:T(8,128)(2,1)S(1)}, bf16[5,32,512]{2,1,0:T(8,128)(2,1)S(1)}, u32[]{:S(2)}, u32[]{:S(2)}) collective-permute-start(bf16[5,32,512]{2,1,0:T(8,128)(2,1)S(1)} %shard_map.87.refs_0_), channel_id=1, source_target_pairs={{0,128},{1,129},{2,130},{3,131},{4,132},{5,133},{6,134},{7,135},{8... | collective-permute-start | bytes 491528 | tf_op jit(solution)/shard_map/ppermute | solution.py:38
  12.9 1.2 shard_map.86
  14.1 3.1 %shard_map.88 = (bf16[640,1280]{1,0:T(8,128)(2,1)S(1)}, bf16[640,1280]{1,0:T(8,128)(2,1)S(1)}, bf16[640,1280]{1,0:T(8,128)(2,1)S(1)}, bf16[640,1280]{1,0:T(8,128)(2,1)S(1)}) custom-call(s32[1]{0:T(128)S(6)} %select_n.27.y_ref, s32[1]{0:T(128)} %bitcast.place_ref, bf16[640,5120]{1,0:T(8,128)(2,1)} %w_ref.1), custom_call_target="tpu_custom_call" | custom-call | bytes 6553608 | tf_op jit(solution)/shard_map/pallas_call | solution.py:57
  17.2 3.8 %collective-permute-done.4.refs_2_ = bf16[5,32,512]{2,1,0:T(8,128)(2,1)S(1)} collective-permute-done((bf16[5,32,512]{2,1,0:T(8,128)(2,1)S(1)}, bf16[5,32,512]{2,1,0:T(8,128)(2,1)S(1)}, u32[]{:S(2)}, u32[]{:S(2)}) %collective-permute-start.4) | collective-permute-done | bytes 163872 | tf_op jit(solution)/shard_map/ppermute | solution.py:38
  21.0 0.9 collective-permute-done.5.refs_3_
  21.9 1.3 %collective-permute-start.6 = (bf16[256,512]{1,0:T(8,128)(2,1)S(1)}, bf16[256,512]{1,0:T(8,128)(2,1)S(1)}, u32[]{:S(2)}, u32[]{:S(2)}) collective-permute-start(bf16[256,512]{1,0:T(8,128)(2,1)S(1)} %get-tuple-element.54), channel_id=1, source_target_pairs={{0,4},{1,17},{2,6},{3,19},{4,8},{5,21},{6,10},{7,23},{8,12},{9,25}... | collective-permute-start | bytes 786440 | tf_op jit(solution)/shard_map/ppermute | solution.py:38
  23.2 1.5 %collective-permute-start.7 = (bf16[256,512]{1,0:T(8,128)(2,1)S(1)}, bf16[256,512]{1,0:T(8,128)(2,1)S(1)}, u32[]{:S(2)}, u32[]{:S(2)}) collective-permute-start(bf16[256,512]{1,0:T(8,128)(2,1)S(1)} %get-tuple-element.55), channel_id=1, source_target_pairs={{0,12},{1,49},{2,14},{3,51},{4,0},{5,53},{6,2},{7,55},{8,4},{9,57}... | collective-permute-start | bytes 786440 | tf_op jit(solution)/shard_map/ppermute | solution.py:38
  24.6 1.5 %collective-permute-start.8 = (bf16[256,512]{1,0:T(8,128)(2,1)S(1)}, bf16[256,512]{1,0:T(8,128)(2,1)S(1)}, u32[]{:S(2)}, u32[]{:S(2)}) collective-permute-start(bf16[256,512]{1,0:T(8,128)(2,1)S(1)} %get-tuple-element.56), channel_id=1, source_target_pairs={{0,8},{1,33},{2,10},{3,35},{4,12},{5,37},{6,14},{7,39},{8,0},{9,41... | collective-permute-start | bytes 786440 | tf_op jit(solution)/shard_map/ppermute | solution.py:38
  26.2 2.2 %collective-permute-done.6.refs_1_ = bf16[256,512]{1,0:T(8,128)(2,1)S(1)} collective-permute-done((bf16[256,512]{1,0:T(8,128)(2,1)S(1)}, bf16[256,512]{1,0:T(8,128)(2,1)S(1)}, u32[]{:S(2)}, u32[]{:S(2)}) %collective-permute-start.6) | collective-permute-done | bytes 262176 | tf_op jit(solution)/shard_map/ppermute | solution.py:38
  28.4 3.8 %collective-permute-done.8.refs_3_ = bf16[256,512]{1,0:T(8,128)(2,1)S(1)} collective-permute-done((bf16[256,512]{1,0:T(8,128)(2,1)S(1)}, bf16[256,512]{1,0:T(8,128)(2,1)S(1)}, u32[]{:S(2)}, u32[]{:S(2)}) %collective-permute-start.8) | collective-permute-done | bytes 262176 | tf_op jit(solution)/shard_map/ppermute | solution.py:38
  32.3 1.4 %collective-permute-start.9 = (bf16[512,512]{1,0:T(8,128)(2,1)S(1)}, bf16[512,512]{1,0:T(8,128)(2,1)S(1)}, u32[]{:S(2)}, u32[]{:S(2)}) collective-permute-start(bf16[512,512]{1,0:T(8,128)(2,1)S(1)} %get-tuple-element.57.shared_keys), channel_id=1, source_target_pairs={{0,16},{1,5},{2,18},{3,7},{4,20},{5,9},{6,22},{7,11},{8,24},{9,13}... | collective-permute-start | bytes 1572872 | tf_op jit(solution)/shard_map/ppermute | solution.py:38
  33.6 0.9 collective-permute-start
  34.5 1.8 %collective-permute-start.13 = (bf16[512,512]{1,0:T(8,128)(2,1)S(1)}, bf16[512,512]{1,0:T(8,128)(2,1)S(1)}, u32[]{:S(2)}, u32[]{:S(2)}) collective-permute-start(bf16[512,512]{1,0:T(8,128)(2,1)S(1)} %get-tuple-element.59.own_keys), channel_id=1, source_target_pairs={{0,48},{1,13},{2,50},{3,15},{4,52},{5,1},{6,54},{7,3},{8,56},{9,5}... | collective-permute-start | bytes 1572872 | tf_op jit(solution)/shard_map/ppermute | solution.py:38
  36.3 2.0 %collective-permute-start.1 = (bf16[256,256]{1,0:T(8,128)(2,1)S(1)}, bf16[256,256]{1,0:T(8,128)(2,1)S(1)}, u32[]{:S(2)}, u32[]{:S(2)}) collective-permute-start(bf16[256,256]{1,0:T(8,128)(2,1)S(1)} %get-tuple-element.41), channel_id=1, source_target_pairs={{0,8},{1,33},{2,10},{3,35},{4,12},{5,37},{6,14},{7,39},{8,0},{9,41... | collective-permute-start | bytes 393224 | tf_op jit(solution)/shard_map/ppermute | solution.py:38
  38.4 1.4 %collective-permute-start.11 = (bf16[512,512]{1,0:T(8,128)(2,1)S(1)}, bf16[512,512]{1,0:T(8,128)(2,1)S(1)}, u32[]{:S(2)}, u32[]{:S(2)}) collective-permute-start(bf16[512,512]{1,0:T(8,128)(2,1)S(1)} %get-tuple-element.57.shared_keys), channel_id=1, source_target_pairs={{0,48},{1,13},{2,50},{3,15},{4,52},{5,1},{6,54},{7,3},{8,56},{9,5}... | collective-permute-start | bytes 1572872 | tf_op jit(solution)/shard_map/ppermute | solution.py:38
  39.7 0.2 collective-permute-start.12
  40.0 1.7 %collective-permute-done.1 = bf16[256,256]{1,0:T(8,128)(2,1)S(1)} collective-permute-done((bf16[256,256]{1,0:T(8,128)(2,1)S(1)}, bf16[256,256]{1,0:T(8,128)(2,1)S(1)}, u32[]{:S(2)}, u32[]{:S(2)}) %collective-permute-start.1) | collective-permute-done | bytes 131104 | tf_op jit(solution)/shard_map/ppermute | solution.py:38
  41.7 1.7 %collective-permute-start.2 = (bf16[256,256]{1,0:T(8,128)(2,1)S(1)}, bf16[256,256]{1,0:T(8,128)(2,1)S(1)}, u32[]{:S(2)}, u32[]{:S(2)}) collective-permute-start(bf16[256,256]{1,0:T(8,128)(2,1)S(1)} %get-tuple-element.42), channel_id=1, source_target_pairs={{0,12},{1,49},{2,14},{3,51},{4,0},{5,53},{6,2},{7,55},{8,4},{9,57}... | collective-permute-start | bytes 393224 | tf_op jit(solution)/shard_map/ppermute | solution.py:38
  43.6 3.6 %collective-permute-done.2 = bf16[256,256]{1,0:T(8,128)(2,1)S(1)} collective-permute-done((bf16[256,256]{1,0:T(8,128)(2,1)S(1)}, bf16[256,256]{1,0:T(8,128)(2,1)S(1)}, u32[]{:S(2)}, u32[]{:S(2)}) %collective-permute-start.2) | collective-permute-done | bytes 131104 | tf_op jit(solution)/shard_map/ppermute | solution.py:38
  47.3 7.3 %collective-permute-start.21 = (bf16[640,1280]{1,0:T(8,128)(2,1)S(1)}, bf16[640,1280]{1,0:T(8,128)(2,1)S(1)}, u32[]{:S(2)}, u32[]{:S(2)}) collective-permute-start(bf16[640,1280]{1,0:T(8,128)(2,1)S(1)} %get-tuple-element.74), channel_id=1, source_target_pairs={{0,1},{1,0},{2,3},{3,2},{4,5},{5,4},{6,7},{7,6},{8,9},{9,8},{10,11... | collective-permute-start | bytes 4915208 | tf_op jit(solution)/shard_map/ppermute | solution.py:38
  54.6 3.8 %collective-permute-start.27 = (bf16[640,1280]{1,0:T(8,128)(2,1)S(1)}, bf16[640,1280]{1,0:T(8,128)(2,1)S(1)}, u32[]{:S(2)}, u32[]{:S(2)}) collective-permute-start(bf16[640,1280]{1,0:T(8,128)(2,1)S(1)} %get-tuple-element.77), channel_id=1, source_target_pairs={{0,2},{1,3},{2,0},{3,1},{4,6},{5,7},{6,4},{7,5},{8,10},{9,11},{10,... | collective-permute-start | bytes 4915208 | tf_op jit(solution)/shard_map/ppermute | solution.py:38
  58.4 0.3 collective-permute-start.22
  58.6 2.8 %collective-permute-start.18 = (bf16[512,512]{1,0:T(8,128)(2,1)S(1)}, bf16[512,512]{1,0:T(8,128)(2,1)S(1)}, u32[]{:S(2)}, u32[]{:S(2)}) collective-permute-start(bf16[512,512]{1,0:T(8,128)(2,1)S(1)} %collective-permute-done.13.own_keys), channel_id=1, source_target_pairs={{0,48},{1,13},{2,50},{3,15},{4,52},{5,1},{6,54},{7,3},{8,56},{9,5}... | collective-permute-start | bytes 1572872 | tf_op jit(solution)/shard_map/ppermute | solution.py:38
  61.5 1.8 %shard_map.91 = (f32[1024,768]{1,0:T(8,128)S(1)}, f32[256,768]{1,0:T(8,128)S(1)}) custom-call(bf16[1024,256]{1,0:T(8,128)(2,1)S(1)} %constant_dynamic-update-slice_fusion.shared_ref.query_ref, bf16[256,256]{1,0:T(8,128)(2,1)S(1)} %get-tuple-element.58.own_ref, bf16[512,512]{1,0:T(8,128)(2,1)S(1)} %get-tuple-element.57.shared_keys, ...), custom_call_target="tpu_custom_call" | custom-call | flops 1174405120 | bytes 1703936 | tf_op jit(solution)/shard_map/pallas_call | solution.py:57
  63.3 2.0 %shard_map.92 = (f32[1024,768]{1,0:T(8,128)S(1)}, f32[256,768]{1,0:T(8,128)S(1)}) custom-call(bf16[1024,256]{1,0:T(8,128)(2,1)S(1)} %constant_dynamic-update-slice_fusion.shared_ref.query_ref, bf16[256,256]{1,0:T(8,128)(2,1)S(1)} %get-tuple-element.58.own_ref, bf16[512,512]{1,0:T(8,128)(2,1)S(1)} %collective-permute-done.9.shared_keys, ...), custom_call_target="tpu_custom_call" | custom-call | flops 1174405120 | bytes 5636096 | tf_op jit(solution)/shard_map/pallas_call | solution.py:57
  65.2 2.0 %shard_map.93 = (f32[1024,768]{1,0:T(8,128)S(1)}, f32[256,768]{1,0:T(8,128)S(1)}) custom-call(bf16[1024,256]{1,0:T(8,128)(2,1)S(1)} %constant_dynamic-update-slice_fusion.shared_ref.query_ref, bf16[256,256]{1,0:T(8,128)(2,1)S(1)} %get-tuple-element.58.own_ref, bf16[512,512]{1,0:T(8,128)(2,1)S(1)} %collective-permute-done.11.shared_keys, ...), custom_call_target="tpu_custom_call" | custom-call | flops 1174405120 | bytes 5636096 | tf_op jit(solution)/shard_map/pallas_call | solution.py:57
  67.2 1.4 %shard_map.94 = (bf16[512,128]{1,0:T(8,128)(2,1)S(1)}, bf16[512,128]{1,0:T(8,128)(2,1)S(1)}, bf16[512,128]{1,0:T(8,128)(2,1)S(1)}) custom-call(bf16[1024,256]{1,0:T(8,128)(2,1)S(1)} %constant_dynamic-update-slice_fusion.shared_ref.query_ref, bf16[512,512]{1,0:T(8,128)(2,1)S(1)} %collective-permute-done.10.keys.shared_keys, ...), custom_call_target="tpu_custom_call" | custom-call | flops 704643072 | bytes 4194304 | tf_op jit(solution)/shard_map/pallas_call | solution.py:57
  68.6 2.7 %collective-permute-start.23 = (bf16[512,128]{1,0:T(8,128)(2,1)S(1)}, bf16[512,128]{1,0:T(8,128)(2,1)S(1)}, u32[]{:S(2)}, u32[]{:S(2)}) collective-permute-start(bf16[512,128]{1,0:T(8,128)(2,1)S(1)} %get-tuple-element.65), channel_id=1, source_target_pairs={{0,14},{1,51},{2,12},{3,49},{4,2},{5,55},{6,0},{7,53},{8,6},{9,59}... | collective-permute-start | bytes 393224 | tf_op jit(solution)/shard_map/ppermute | solution.py:38
  71.3 0.4 collective-permute-start.24
  71.6 26.1 %collective-permute-done.23 = bf16[512,128]{1,0:T(8,128)(2,1)S(1)} collective-permute-done((bf16[512,128]{1,0:T(8,128)(2,1)S(1)}, bf16[512,128]{1,0:T(8,128)(2,1)S(1)}, u32[]{:S(2)}, u32[]{:S(2)}) %collective-permute-start.23) | collective-permute-done | bytes 131104 | tf_op jit(solution)/shard_map/ppermute | solution.py:38
  97.7 1.8 %collective-permute-start.25 = (bf16[512,128]{1,0:T(8,128)(2,1)S(1)}, bf16[512,128]{1,0:T(8,128)(2,1)S(1)}, u32[]{:S(2)}, u32[]{:S(2)}) collective-permute-start(bf16[512,128]{1,0:T(8,128)(2,1)S(1)} %get-tuple-element.67), channel_id=1, source_target_pairs={{0,6},{1,19},{2,4},{3,17},{4,10},{5,23},{6,8},{7,21},{8,14},{9,27}... | collective-permute-start | bytes 393224 | tf_op jit(solution)/shard_map/ppermute | solution.py:38
  99.5 2.2 %collective-permute-done.24 = bf16[512,128]{1,0:T(8,128)(2,1)S(1)} collective-permute-done((bf16[512,128]{1,0:T(8,128)(2,1)S(1)}, bf16[512,128]{1,0:T(8,128)(2,1)S(1)}, u32[]{:S(2)}, u32[]{:S(2)}) %collective-permute-start.24) | collective-permute-done | bytes 131104 | tf_op jit(solution)/shard_map/ppermute | solution.py:38
  101.8 1.2 collective-permute-start.14
  102.9 0.7 collective-permute-done.25
  103.6 0.8 collective-permute-start.15
  104.4 1.2 shard_map.95.refs_0_
  105.9 0.3 collective-permute-start.16
  106.2 2.8 %collective-permute-done.15 = bf16[512,128]{1,0:T(8,128)(2,1)S(1)} collective-permute-done((bf16[512,128]{1,0:T(8,128)(2,1)S(1)}, bf16[512,128]{1,0:T(8,128)(2,1)S(1)}, u32[]{:S(2)}, u32[]{:S(2)}) %collective-permute-start.15) | collective-permute-done | bytes 131104 | tf_op jit(solution)/shard_map/ppermute | solution.py:38
  109.0 3.7 %collective-permute-start.28 = (bf16[512,256]{1,0:T(8,128)(2,1)S(1)}, bf16[512,256]{1,0:T(8,128)(2,1)S(1)}, u32[]{:S(2)}, u32[]{:S(2)}) collective-permute-start(bf16[512,256]{1,0:T(8,128)(2,1)S(1)} %shard_map.95.refs_0_), channel_id=1, source_target_pairs={{0,1},{1,0},{2,3},{3,2},{4,5},{5,4},{6,7},{7,6},{8,9},{9,8},{10,11... | collective-permute-start | bytes 786440 | tf_op jit(solution)/shard_map/ppermute | solution.py:38
  112.8 1.4 %collective-permute-start.19 = (bf16[512,256]{1,0:T(8,128)(2,1)S(1)}, bf16[512,256]{1,0:T(8,128)(2,1)S(1)}, u32[]{:S(2)}, u32[]{:S(2)}) collective-permute-start(bf16[512,256]{1,0:T(8,128)(2,1)S(1)} %shard_map.95.refs_0_), channel_id=1, source_target_pairs={{0,2},{1,3},{2,0},{3,1},{4,6},{5,7},{6,4},{7,5},{8,10},{9,11},{10,... | collective-permute-start | bytes 786440 | tf_op jit(solution)/shard_map/ppermute | solution.py:38
  114.2 3.7 %collective-permute-start.26 = (bf16[512,384]{1,0:T(8,128)(2,1)S(1)}, bf16[512,384]{1,0:T(8,128)(2,1)S(1)}, u32[]{:S(2)}, u32[]{:S(2)}) collective-permute-start(bf16[512,384]{1,0:T(8,128)(2,1)S(1)} %constant_dynamic-update-slice_fusion.7.refs_2_), channel_id=1, source_target_pairs={{0,1},{1,0},{2,3},{3,2},{4,5},{5,4},{6,7},{7,6},{8,9},{9,8},{10,11... | collective-permute-start | bytes 1179656 | tf_op jit(solution)/shard_map/ppermute | solution.py:38
  118.1 4.0 %collective-permute-start.17 = (bf16[512,384]{1,0:T(8,128)(2,1)S(1)}, bf16[512,384]{1,0:T(8,128)(2,1)S(1)}, u32[]{:S(2)}, u32[]{:S(2)}) collective-permute-start(bf16[512,384]{1,0:T(8,128)(2,1)S(1)} %constant_dynamic-update-slice_fusion.4.refs_1_), channel_id=1, source_target_pairs={{0,1},{1,0},{2,3},{3,2},{4,5},{5,4},{6,7},{7,6},{8,9},{9,8},{10,11... | collective-permute-start | bytes 1179656 | tf_op jit(solution)/shard_map/ppermute | solution.py:38
  122.1 1.5 %shard_map.96.refs_6_ = f32[512,1280]{1,0:T(8,128)S(1)} custom-call(bf16[512,256]{1,0:T(8,128)(2,1)S(1)} %shard_map.95.refs_0_, bf16[512,256]{1,0:T(8,128)(2,1)S(1)} %collective-permute-done.28.refs_1_, bf16[512,384]{1,0:T(8,128)(2,1)S(1)} %constant_dynamic-update-slice_fusion.7.refs_2_, bf16[640,1280]{1,0:T(8,128)(2,1)S(1)} %get-tuple-element.76.refs_3_.refs_4_, ...), custom_call_target="tpu_custom_call" | custom-call | flops 1174405120 | bytes 5832704 | tf_op jit(solution)/shard_map/pallas_call | solution.py:57
  123.7 1.8 %shard_map.97.refs_4_ = f32[512,1280]{1,0:T(8,128)S(1)} custom-call(bf16[512,384]{1,0:T(8,128)(2,1)S(1)} %collective-permute-done.26.refs_0_, bf16[512,384]{1,0:T(8,128)(2,1)S(1)} %constant_dynamic-update-slice_fusion.4.refs_1_, bf16[512,256]{1,0:T(8,128)(2,1)S(1)} %collective-permute-done.19.refs_2_, bf16[640,1280]{1,0:T(8,128)(2,1)S(1)} %collective-permute-done.22.refs_3_, ...), custom_call_target="tpu_custom_call" | custom-call | flops 1342177280 | bytes 8585216 | tf_op jit(solution)/shard_map/pallas_call | solution.py:57
  125.5 2.1 %project_last.1 = (bf16[256,1280]{1,0:T(8,128)(2,1)}, bf16[256,1280]{1,0:T(8,128)(2,1)}) custom-call(bf16[512,384]{1,0:T(8,128)(2,1)S(1)} %collective-permute-done.17.refs_0_, bf16[512,256]{1,0:T(8,128)(2,1)S(1)} %collective-permute-done.20.refs_1_, bf16[640,1280]{1,0:T(8,128)(2,1)S(1)} %collective-permute-done.21.refs_4_.refs_2_, ...), custom_call_target="tpu_custom_call" | custom-call | tf_op jit(solution)/shard_map/project_last/pallas_call | solution.py:272
  (33 shorter events, 0.8 us)
Async XLA Ops:
  1.5 15.7 %collective-permute-start.3 = (bf16[5,32,512]{2,1,0:T(8,128)(2,1)S(1)}, bf16[5,32,512]{2,1,0:T(8,128)(2,1)S(1)}, u32[]{:S(2)}, u32[]{:S(2)}) collective-permute-start(bf16[5,32,512]{2,1,0:T(8,128)(2,1)S(1)} %shard_map.87.refs_0_), channel_id=1, source_target_pairs={{0,64},{1,65},{2,66},{3,67},{4,68},{5,69},{6,70},{7,71},{8,72},{9,... | collective-permute-start | bytes 491528 | tf_op jit(solution)/shard_map/ppermute | solution.py:38
  5.4 15.5 %collective-permute-start.4 = (bf16[5,32,512]{2,1,0:T(8,128)(2,1)S(1)}, bf16[5,32,512]{2,1,0:T(8,128)(2,1)S(1)}, u32[]{:S(2)}, u32[]{:S(2)}) collective-permute-start(bf16[5,32,512]{2,1,0:T(8,128)(2,1)S(1)} %shard_map.87.refs_0_), channel_id=1, source_target_pairs={{0,192},{1,193},{2,194},{3,195},{4,196},{5,197},{6,198},{7,199},{8... | collective-permute-start | bytes 491528 | tf_op jit(solution)/shard_map/ppermute | solution.py:38
  8.5 13.3 %collective-permute-start.5 = (bf16[5,32,512]{2,1,0:T(8,128)(2,1)S(1)}, bf16[5,32,512]{2,1,0:T(8,128)(2,1)S(1)}, u32[]{:S(2)}, u32[]{:S(2)}) collective-permute-start(bf16[5,32,512]{2,1,0:T(8,128)(2,1)S(1)} %shard_map.87.refs_0_), channel_id=1, source_target_pairs={{0,128},{1,129},{2,130},{3,131},{4,132},{5,133},{6,134},{7,135},{8... | collective-permute-start | bytes 491528 | tf_op jit(solution)/shard_map/ppermute | solution.py:38
  21.9 6.5 %collective-permute-start.6 = (bf16[256,512]{1,0:T(8,128)(2,1)S(1)}, bf16[256,512]{1,0:T(8,128)(2,1)S(1)}, u32[]{:S(2)}, u32[]{:S(2)}) collective-permute-start(bf16[256,512]{1,0:T(8,128)(2,1)S(1)} %get-tuple-element.54), channel_id=1, source_target_pairs={{0,4},{1,17},{2,6},{3,19},{4,8},{5,21},{6,10},{7,23},{8,12},{9,25}... | collective-permute-start | bytes 786440 | tf_op jit(solution)/shard_map/ppermute | solution.py:38
  23.2 5.2 %collective-permute-start.7 = (bf16[256,512]{1,0:T(8,128)(2,1)S(1)}, bf16[256,512]{1,0:T(8,128)(2,1)S(1)}, u32[]{:S(2)}, u32[]{:S(2)}) collective-permute-start(bf16[256,512]{1,0:T(8,128)(2,1)S(1)} %get-tuple-element.55), channel_id=1, source_target_pairs={{0,12},{1,49},{2,14},{3,51},{4,0},{5,53},{6,2},{7,55},{8,4},{9,57}... | collective-permute-start | bytes 786440 | tf_op jit(solution)/shard_map/ppermute | solution.py:38
  24.6 7.5 %collective-permute-start.8 = (bf16[256,512]{1,0:T(8,128)(2,1)S(1)}, bf16[256,512]{1,0:T(8,128)(2,1)S(1)}, u32[]{:S(2)}, u32[]{:S(2)}) collective-permute-start(bf16[256,512]{1,0:T(8,128)(2,1)S(1)} %get-tuple-element.56), channel_id=1, source_target_pairs={{0,8},{1,33},{2,10},{3,35},{4,12},{5,37},{6,14},{7,39},{8,0},{9,41... | collective-permute-start | bytes 786440 | tf_op jit(solution)/shard_map/ppermute | solution.py:38
  32.3 11.2 %collective-permute-start.9 = (bf16[512,512]{1,0:T(8,128)(2,1)S(1)}, bf16[512,512]{1,0:T(8,128)(2,1)S(1)}, u32[]{:S(2)}, u32[]{:S(2)}) collective-permute-start(bf16[512,512]{1,0:T(8,128)(2,1)S(1)} %get-tuple-element.57.shared_keys), channel_id=1, source_target_pairs={{0,16},{1,5},{2,18},{3,7},{4,20},{5,9},{6,22},{7,11},{8,24},{9,13}... | collective-permute-start | bytes 1572872 | tf_op jit(solution)/shard_map/ppermute | solution.py:38
  33.6 6.1 %collective-permute-start = (bf16[256,256]{1,0:T(8,128)(2,1)S(1)}, bf16[256,256]{1,0:T(8,128)(2,1)S(1)}, u32[]{:S(2)}, u32[]{:S(2)}) collective-permute-start(bf16[256,256]{1,0:T(8,128)(2,1)S(1)} %get-tuple-element.40), channel_id=1, source_target_pairs={{0,4},{1,17},{2,6},{3,19},{4,8},{5,21},{6,10},{7,23},{8,12},{9,25}... | collective-permute-start | bytes 393224 | tf_op jit(solution)/shard_map/ppermute | solution.py:38
  34.5 20.0 %collective-permute-start.13 = (bf16[512,512]{1,0:T(8,128)(2,1)S(1)}, bf16[512,512]{1,0:T(8,128)(2,1)S(1)}, u32[]{:S(2)}, u32[]{:S(2)}) collective-permute-start(bf16[512,512]{1,0:T(8,128)(2,1)S(1)} %get-tuple-element.59.own_keys), channel_id=1, source_target_pairs={{0,48},{1,13},{2,50},{3,15},{4,52},{5,1},{6,54},{7,3},{8,56},{9,5}... | collective-permute-start | bytes 1572872 | tf_op jit(solution)/shard_map/ppermute | solution.py:38
  36.3 5.4 %collective-permute-start.1 = (bf16[256,256]{1,0:T(8,128)(2,1)S(1)}, bf16[256,256]{1,0:T(8,128)(2,1)S(1)}, u32[]{:S(2)}, u32[]{:S(2)}) collective-permute-start(bf16[256,256]{1,0:T(8,128)(2,1)S(1)} %get-tuple-element.41), channel_id=1, source_target_pairs={{0,8},{1,33},{2,10},{3,35},{4,12},{5,37},{6,14},{7,39},{8,0},{9,41... | collective-permute-start | bytes 393224 | tf_op jit(solution)/shard_map/ppermute | solution.py:38
  38.4 20.0 %collective-permute-start.11 = (bf16[512,512]{1,0:T(8,128)(2,1)S(1)}, bf16[512,512]{1,0:T(8,128)(2,1)S(1)}, u32[]{:S(2)}, u32[]{:S(2)}) collective-permute-start(bf16[512,512]{1,0:T(8,128)(2,1)S(1)} %get-tuple-element.57.shared_keys), channel_id=1, source_target_pairs={{0,48},{1,13},{2,50},{3,15},{4,52},{5,1},{6,54},{7,3},{8,56},{9,5}... | collective-permute-start | bytes 1572872 | tf_op jit(solution)/shard_map/ppermute | solution.py:38
  39.7 18.9 %collective-permute-start.12 = (bf16[512,512]{1,0:T(8,128)(2,1)S(1)}, bf16[512,512]{1,0:T(8,128)(2,1)S(1)}, u32[]{:S(2)}, u32[]{:S(2)}) collective-permute-start(bf16[512,512]{1,0:T(8,128)(2,1)S(1)} %get-tuple-element.59.own_keys), channel_id=1, source_target_pairs={{0,16},{1,5},{2,18},{3,7},{4,20},{5,9},{6,22},{7,11},{8,24},{9,13}... | collective-permute-start | bytes 1572872 | tf_op jit(solution)/shard_map/ppermute | solution.py:38
  41.7 5.5 %collective-permute-start.2 = (bf16[256,256]{1,0:T(8,128)(2,1)S(1)}, bf16[256,256]{1,0:T(8,128)(2,1)S(1)}, u32[]{:S(2)}, u32[]{:S(2)}) collective-permute-start(bf16[256,256]{1,0:T(8,128)(2,1)S(1)} %get-tuple-element.42), channel_id=1, source_target_pairs={{0,12},{1,49},{2,14},{3,51},{4,0},{5,53},{6,2},{7,55},{8,4},{9,57}... | collective-permute-start | bytes 393224 | tf_op jit(solution)/shard_map/ppermute | solution.py:38
  43.5 23.7 %collective-permute-start.10 = (bf16[512,512]{1,0:T(8,128)(2,1)S(1)}, bf16[512,512]{1,0:T(8,128)(2,1)S(1)}, u32[]{:S(2)}, u32[]{:S(2)}) collective-permute-start(bf16[512,512]{1,0:T(8,128)(2,1)S(1)} %collective-permute-done.9.shared_keys), channel_id=1, source_target_pairs={{0,16},{1,5},{2,18},{3,7},{4,20},{5,9},{6,22},{7,11},{8,24},{9,13}... | collective-permute-start | bytes 1572872 | tf_op jit(solution)/shard_map/ppermute | solution.py:38
  47.3 74.8 %collective-permute-start.21 = (bf16[640,1280]{1,0:T(8,128)(2,1)S(1)}, bf16[640,1280]{1,0:T(8,128)(2,1)S(1)}, u32[]{:S(2)}, u32[]{:S(2)}) collective-permute-start(bf16[640,1280]{1,0:T(8,128)(2,1)S(1)} %get-tuple-element.74), channel_id=1, source_target_pairs={{0,1},{1,0},{2,3},{3,2},{4,5},{5,4},{6,7},{7,6},{8,9},{9,8},{10,11... | collective-permute-start | bytes 4915208 | tf_op jit(solution)/shard_map/ppermute | solution.py:38
  54.6 67.5 %collective-permute-start.27 = (bf16[640,1280]{1,0:T(8,128)(2,1)S(1)}, bf16[640,1280]{1,0:T(8,128)(2,1)S(1)}, u32[]{:S(2)}, u32[]{:S(2)}) collective-permute-start(bf16[640,1280]{1,0:T(8,128)(2,1)S(1)} %get-tuple-element.77), channel_id=1, source_target_pairs={{0,2},{1,3},{2,0},{3,1},{4,6},{5,7},{6,4},{7,5},{8,10},{9,11},{10,... | collective-permute-start | bytes 4915208 | tf_op jit(solution)/shard_map/ppermute | solution.py:38
  58.4 65.3 %collective-permute-start.22 = (bf16[640,1280]{1,0:T(8,128)(2,1)S(1)}, bf16[640,1280]{1,0:T(8,128)(2,1)S(1)}, u32[]{:S(2)}, u32[]{:S(2)}) collective-permute-start(bf16[640,1280]{1,0:T(8,128)(2,1)S(1)} %get-tuple-element.75), channel_id=1, source_target_pairs={{0,195},{1,194},{2,65},{3,64},{4,199},{5,198},{6,69},{7,68},{8,203... | collective-permute-start | bytes 4915208 | tf_op jit(solution)/shard_map/ppermute | solution.py:49
  58.6 12.6 %collective-permute-start.18 = (bf16[512,512]{1,0:T(8,128)(2,1)S(1)}, bf16[512,512]{1,0:T(8,128)(2,1)S(1)}, u32[]{:S(2)}, u32[]{:S(2)}) collective-permute-start(bf16[512,512]{1,0:T(8,128)(2,1)S(1)} %collective-permute-done.13.own_keys), channel_id=1, source_target_pairs={{0,48},{1,13},{2,50},{3,15},{4,52},{5,1},{6,54},{7,3},{8,56},{9,5}... | collective-permute-start | bytes 1572872 | tf_op jit(solution)/shard_map/ppermute | solution.py:38
  68.6 29.1 %collective-permute-start.23 = (bf16[512,128]{1,0:T(8,128)(2,1)S(1)}, bf16[512,128]{1,0:T(8,128)(2,1)S(1)}, u32[]{:S(2)}, u32[]{:S(2)}) collective-permute-start(bf16[512,128]{1,0:T(8,128)(2,1)S(1)} %get-tuple-element.65), channel_id=1, source_target_pairs={{0,14},{1,51},{2,12},{3,49},{4,2},{5,55},{6,0},{7,53},{8,6},{9,59}... | collective-permute-start | bytes 393224 | tf_op jit(solution)/shard_map/ppermute | solution.py:38
  71.3 30.5 %collective-permute-start.24 = (bf16[512,128]{1,0:T(8,128)(2,1)S(1)}, bf16[512,128]{1,0:T(8,128)(2,1)S(1)}, u32[]{:S(2)}, u32[]{:S(2)}) collective-permute-start(bf16[512,128]{1,0:T(8,128)(2,1)S(1)} %get-tuple-element.66), channel_id=1, source_target_pairs={{0,10},{1,35},{2,8},{3,33},{4,14},{5,39},{6,12},{7,37},{8,2},{9,43... | collective-permute-start | bytes 393224 | tf_op jit(solution)/shard_map/ppermute | solution.py:38
  97.7 5.9 %collective-permute-start.25 = (bf16[512,128]{1,0:T(8,128)(2,1)S(1)}, bf16[512,128]{1,0:T(8,128)(2,1)S(1)}, u32[]{:S(2)}, u32[]{:S(2)}) collective-permute-start(bf16[512,128]{1,0:T(8,128)(2,1)S(1)} %get-tuple-element.67), channel_id=1, source_target_pairs={{0,6},{1,19},{2,4},{3,17},{4,10},{5,23},{6,8},{7,21},{8,14},{9,27}... | collective-permute-start | bytes 393224 | tf_op jit(solution)/shard_map/ppermute | solution.py:38
  101.8 4.1 %collective-permute-start.14 = (bf16[512,128]{1,0:T(8,128)(2,1)S(1)}, bf16[512,128]{1,0:T(8,128)(2,1)S(1)}, u32[]{:S(2)}, u32[]{:S(2)}) collective-permute-start(bf16[512,128]{1,0:T(8,128)(2,1)S(1)} %get-tuple-element.65), channel_id=1, source_target_pairs={{0,12},{1,49},{2,14},{3,51},{4,0},{5,53},{6,2},{7,55},{8,4},{9,57}... | collective-permute-start | bytes 393224 | tf_op jit(solution)/shard_map/ppermute | solution.py:38
  103.6 5.3 %collective-permute-start.15 = (bf16[512,128]{1,0:T(8,128)(2,1)S(1)}, bf16[512,128]{1,0:T(8,128)(2,1)S(1)}, u32[]{:S(2)}, u32[]{:S(2)}) collective-permute-start(bf16[512,128]{1,0:T(8,128)(2,1)S(1)} %get-tuple-element.66), channel_id=1, source_target_pairs={{0,8},{1,33},{2,10},{3,35},{4,12},{5,37},{6,14},{7,39},{8,0},{9,41... | collective-permute-start | bytes 393224 | tf_op jit(solution)/shard_map/ppermute | solution.py:38
  105.9 6.9 %collective-permute-start.16 = (bf16[512,128]{1,0:T(8,128)(2,1)S(1)}, bf16[512,128]{1,0:T(8,128)(2,1)S(1)}, u32[]{:S(2)}, u32[]{:S(2)}) collective-permute-start(bf16[512,128]{1,0:T(8,128)(2,1)S(1)} %get-tuple-element.67), channel_id=1, source_target_pairs={{0,4},{1,17},{2,6},{3,19},{4,8},{5,21},{6,10},{7,23},{8,12},{9,25}... | collective-permute-start | bytes 393224 | tf_op jit(solution)/shard_map/ppermute | solution.py:38
  109.0 5.2 %collective-permute-start.28 = (bf16[512,256]{1,0:T(8,128)(2,1)S(1)}, bf16[512,256]{1,0:T(8,128)(2,1)S(1)}, u32[]{:S(2)}, u32[]{:S(2)}) collective-permute-start(bf16[512,256]{1,0:T(8,128)(2,1)S(1)} %shard_map.95.refs_0_), channel_id=1, source_target_pairs={{0,1},{1,0},{2,3},{3,2},{4,5},{5,4},{6,7},{7,6},{8,9},{9,8},{10,11... | collective-permute-start | bytes 786440 | tf_op jit(solution)/shard_map/ppermute | solution.py:38
  112.8 5.3 %collective-permute-start.19 = (bf16[512,256]{1,0:T(8,128)(2,1)S(1)}, bf16[512,256]{1,0:T(8,128)(2,1)S(1)}, u32[]{:S(2)}, u32[]{:S(2)}) collective-permute-start(bf16[512,256]{1,0:T(8,128)(2,1)S(1)} %shard_map.95.refs_0_), channel_id=1, source_target_pairs={{0,2},{1,3},{2,0},{3,1},{4,6},{5,7},{6,4},{7,5},{8,10},{9,11},{10,... | collective-permute-start | bytes 786440 | tf_op jit(solution)/shard_map/ppermute | solution.py:38
  114.2 9.5 %collective-permute-start.26 = (bf16[512,384]{1,0:T(8,128)(2,1)S(1)}, bf16[512,384]{1,0:T(8,128)(2,1)S(1)}, u32[]{:S(2)}, u32[]{:S(2)}) collective-permute-start(bf16[512,384]{1,0:T(8,128)(2,1)S(1)} %constant_dynamic-update-slice_fusion.7.refs_2_), channel_id=1, source_target_pairs={{0,1},{1,0},{2,3},{3,2},{4,5},{5,4},{6,7},{7,6},{8,9},{9,8},{10,11... | collective-permute-start | bytes 1179656 | tf_op jit(solution)/shard_map/ppermute | solution.py:38
  118.1 7.4 %collective-permute-start.17 = (bf16[512,384]{1,0:T(8,128)(2,1)S(1)}, bf16[512,384]{1,0:T(8,128)(2,1)S(1)}, u32[]{:S(2)}, u32[]{:S(2)}) collective-permute-start(bf16[512,384]{1,0:T(8,128)(2,1)S(1)} %constant_dynamic-update-slice_fusion.4.refs_1_), channel_id=1, source_target_pairs={{0,1},{1,0},{2,3},{3,2},{4,5},{5,4},{6,7},{7,6},{8,9},{9,8},{10,11... | collective-permute-start | bytes 1179656 | tf_op jit(solution)/shard_map/ppermute | solution.py:38
  122.1 3.4 %collective-permute-start.20 = (bf16[512,256]{1,0:T(8,128)(2,1)S(1)}, bf16[512,256]{1,0:T(8,128)(2,1)S(1)}, u32[]{:S(2)}, u32[]{:S(2)}) collective-permute-start(bf16[512,256]{1,0:T(8,128)(2,1)S(1)} %collective-permute-done.19.refs_2_), channel_id=1, source_target_pairs={{0,1},{1,0},{2,3},{3,2},{4,5},{5,4},{6,7},{7,6},{8,9},{9,8},{10,11... | collective-permute-start | bytes 786440 | tf_op jit(solution)/shard_map/ppermute | solution.py:38
